TPU v7x, 32 devices: a whole 2x2x4 slice. The times are simulated.
32 devices in a mesh: dp: 4 (over x, core), ctx: 4 (over z), tensor: 2 (over y).
Axes of the slice: x: 2, y: 2, z: 4, core: 2. Of those that a mesh axis runs over, the one named last changes fastest.
Arguments:
- block_input: bfloat16 [12288, 2048], P(('dp', 'ctx'), 'tensor'), may hold values from -6 to 6
- cotangent: bfloat16 [12288, 2048], P(('dp', 'ctx'), 'tensor'), may hold values from -6 to 6
- deal_order: int32 [4, 4], P('dp'), may hold values from 0 to 3, as said below
- seq_lengths: int32 [12], P('dp'), may hold values from 96 to 2880, as said below
- seq_adapter: int32 [12], P('dp'), may hold values from 0 to 7
- mixer_gain: bfloat16 [2048], replicated, may hold values from 0.099609375 to 1.8984375
- ffn_gain: bfloat16 [2048], replicated, may hold values from 0.099609375 to 1.8984375
- conv_taps: bfloat16 [3, 2048], P(None, 'tensor'), may hold values from -3.5 to 3.5
- in_weight: bfloat16 [3, 2048, 2048], P(None, 'dp', 'tensor'), may hold values from -0.125 to 0.125
- out_weight: bfloat16 [2048, 2048], P('tensor', 'dp'), may hold values from -0.125 to 0.125
- gateup_weight: bfloat16 [2, 2048, 5632], P(None, 'dp', 'tensor'), may hold values from -0.125 to 0.125
- down_weight: bfloat16 [5632, 2048], P('tensor', 'dp'), may hold values from -0.078125 to 0.078125
- input_adapter_shrink: bfloat16 [2048, 128], replicated, may hold values from -0.125 to 0.125
- in_expand: bfloat16 [3, 128, 2048], P(None, None, 'tensor'), may hold values from -1.5 to 1.5
- out_shrink: bfloat16 [2048, 128], P('tensor'), may hold values from -0.125 to 0.125
- output_adapter_expand: bfloat16 [128, 2048], replicated, may hold values from -1.5 to 1.5
- ffn_shrink: bfloat16 [2048, 256], replicated, may hold values from -0.125 to 0.125
- ffn_expand: bfloat16 [2, 128, 5632], P(None, None, 'tensor'), may hold values from -1.5 to 1.5
- down_shrink: bfloat16 [5632, 128], P('tensor'), may hold values from -0.078125 to 0.078125
- down_adapter_expand: bfloat16 [128, 2048], replicated, may hold values from -1.5 to 1.5
Outputs:
- block_output: bfloat16 [12288, 2048], P(('dp', 'ctx'), 'tensor')
- input_grad: float32 [12288, 2048], P(('dp', 'ctx'), 'tensor')
- in_shrink_grad: float32 [2048, 128], replicated
- input_expand_gradient: float32 [3, 128, 2048], P(None, None, 'tensor')
- out_shrink_grad: float32 [2048, 128], P('tensor')
- output_expand_gradient: float32 [128, 2048], replicated
- ffn_shrink_grad: float32 [2048, 256], replicated
- feedforward_expand_gradient: float32 [2, 128, 5632], P(None, None, 'tensor')
- down_shrink_grad: float32 [5632, 128], P('tensor')
- down_adapter_expand_gradient: float32 [128, 2048], replicated
Inputs may be any that keep to these rules, and one draw needn't show every extreme that they name: `deal_order`: each row is a permutation of the 4 shard numbers. `seq_lengths`: each data group's 3 entries sum to 3072; all but one of them lie between 96 and 192.
All inputs are finite; a program needn't handle non-finite values.
Results may differ from a plain program's by a relative error of at most 0.013.
Values may be sent and summed in bfloat16 or wider, within the bound.
No kernel may reach another device: no remote copies, remote signals or barrier semaphores. Data moves between devices by JAX's collectives and lax.ppermute only.
A program may use at most 256 MiB of HBM per device.

v0:
```python
import jax
import jax.numpy as jnp
from jax import lax
from jax.sharding import PartitionSpec as P

RANK = 16


norm_eps = 1e-05
adapter_scale = 0.5


def shifted(block, axis, distance):
    devices = range(lax.axis_size(axis))
    route = [(i - distance, i) for i in devices if i - distance in devices]
    return lax.ppermute(block, axis, route)


def rms_scale(values):
    return lax.rsqrt(jnp.mean(values * values, axis=-1, keepdims=True) + norm_eps)


def norm_back(values, scale, gain, grad_out):
    unit = values * scale
    grad_unit = grad_out * gain
    return scale * (grad_unit - unit * jnp.mean(grad_unit * unit, axis=-1, keepdims=True))


def product_simple(left, right):
    return jnp.dot(left, right, preferred_element_type=jnp.float32)


def product_backward(left, right):
    return lax.dot_general(
        left, right, (((1,), (1,)), ((), ())), preferred_element_type=jnp.float32
    )


def product_leading(left, right):
    return lax.dot_general(
        left, right, (((0,), (0,)), ((), ())), preferred_element_type=jnp.float32
    )


def segment_of(positions, seq_ends):
    return jnp.sum((positions[:, None] >= seq_ends[None, :]).astype(jnp.int32), axis=1)


def fetch_mixer(in_weight, out_weight):
    return (
        lax.all_gather(in_weight, "dp", axis=1, tiled=True),
        lax.all_gather(out_weight, "dp", axis=1, tiled=True),
    )


def fetch_ffn(gateup_weight, down_weight):
    return (
        lax.all_gather(gateup_weight, "dp", axis=1, tiled=True),
        lax.all_gather(down_weight, "dp", axis=1, tiled=True),
    )


def body(
    block_input,
    cotangent,
    deal_order,
    seq_lengths,
    seq_adapter,
    mixer_gain,
    ffn_gain,
    conv_taps,
    in_weight,
    out_weight,
    gateup_weight,
    down_weight,
    input_adapter_shrink,
    in_expand,
    out_shrink,
    output_adapter_expand,
    ffn_shrink,
    ffn_expand,
    down_shrink,
    down_adapter_expand,
):
    tok_count = block_input.shape[0]
    half_width = block_input.shape[1]
    rank_cols = input_adapter_shrink.shape[1]
    part_index = lax.axis_index("tensor")
    group_total = lax.axis_size("dp")
    block_rows = tok_count // group_total
    deal_row = deal_order[0]
    slot_all = jnp.arange(group_total, dtype=jnp.int32)
    inverse_row = jnp.sum(
        jnp.where(deal_row[:, None] == slot_all[None, :], slot_all[:, None], 0), axis=0
    )
    dealt_in, dealt_cot = (
        lax.all_to_all(
            block_input.reshape(group_total, block_rows, half_width),
            "dp",
            split_axis=0,
            concat_axis=0,
            tiled=True,
        ),
        lax.all_to_all(
            cotangent.reshape(group_total, block_rows, half_width),
            "dp",
            split_axis=0,
            concat_axis=0,
            tiled=True,
        ),
    )
    packed_in = jnp.take(dealt_in, deal_row, axis=0).reshape(tok_count, half_width)
    packed_cot = jnp.take(dealt_cot, deal_row, axis=0).reshape(tok_count, half_width)
    seq_ends = jnp.cumsum(seq_lengths)[:-1]
    positions = lax.axis_index("ctx") * tok_count + jnp.arange(tok_count, dtype=jnp.int32)
    segment = segment_of(positions, seq_ends)
    slot_ids = jnp.arange(seq_lengths.shape[0], dtype=jnp.int32)
    token_adapter_index = jnp.sum(
        jnp.where(segment[:, None] == slot_ids[None, :], seq_adapter[None, :], 0), axis=1
    )
    column_group_index = jnp.arange(rank_cols, dtype=jnp.int32) // RANK
    adapter_mask = (column_group_index[None, :] == token_adapter_index[:, None]).astype(jnp.float32)
    adapter_half_float = adapter_mask.astype(jnp.bfloat16)
    adapter_mask_pair = jnp.concatenate([adapter_mask, adapter_mask], axis=1)
    pair_bf = adapter_mask_pair.astype(jnp.bfloat16)
    matching_first = ((positions >= 1) & (segment_of(positions - 1, seq_ends) == segment)).astype(
        jnp.float32
    )[:, None]
    matching_second = ((positions >= 2) & (segment_of(positions - 2, seq_ends) == segment)).astype(
        jnp.float32
    )[:, None]
    ahead_one = (segment_of(positions + 1, seq_ends) == segment).astype(jnp.float32)[:, None]
    ahead_two = (segment_of(positions + 2, seq_ends) == segment).astype(jnp.float32)[:, None]
    row_pair = (
        lax.all_gather(packed_in, "tensor", axis=1, tiled=True),
        lax.all_gather(packed_cot, "tensor", axis=1, tiled=True),
    )
    input_complete = row_pair[0].astype(jnp.float32)
    cotangent_half_float = row_pair[1]
    cot_full = cotangent_half_float.astype(jnp.float32)
    mixer_f = mixer_gain.astype(jnp.float32)
    ffn_f = ffn_gain.astype(jnp.float32)
    conv_w = conv_taps.astype(jnp.float32)
    in_full, out_full = fetch_mixer(in_weight, out_weight)
    scale_one = rms_scale(input_complete)
    normalized_rows = (input_complete * scale_one * mixer_f).astype(jnp.bfloat16)
    input_rank_rows = (
        product_simple(normalized_rows, input_adapter_shrink).astype(jnp.bfloat16)
        * adapter_half_float
    )
    projected_rows = jnp.einsum(
        "px,sxa->psa", normalized_rows, in_full, preferred_element_type=jnp.float32
    ) + adapter_scale * jnp.einsum(
        "fw,kwo->fko", input_rank_rows, in_expand, preferred_element_type=jnp.float32
    )
    gate_b = projected_rows[:, 0]
    gate_c = projected_rows[:, 1]
    values_x = projected_rows[:, 2]
    mixed = (gate_b * values_x).astype(jnp.bfloat16)
    prior = shifted(mixed[tok_count - 2 :], "ctx", 1)
    extended = jnp.concatenate([prior, mixed], axis=0).astype(jnp.float32)
    conv_out = (
        conv_w[0] * extended[2:]
        + conv_w[1] * extended[1:-1] * matching_first
        + conv_w[2] * extended[:-2] * matching_second
    )
    gated_rows = (gate_c * conv_out).astype(jnp.bfloat16)
    adapter_branch_sum, output_rank_sum = lax.psum(
        (product_simple(gated_rows, out_full), product_simple(gated_rows, out_shrink)), "tensor"
    )
    output_rank_rows = output_rank_sum.astype(jnp.bfloat16) * adapter_half_float
    hidden_state_rows = input_complete + (
        adapter_branch_sum + adapter_scale * product_simple(output_rank_rows, output_adapter_expand)
    )
    scale_two = rms_scale(hidden_state_rows)
    feedforward_input = (hidden_state_rows * scale_two * ffn_f).astype(jnp.bfloat16)
    feedforward_rank_rows = (
        product_simple(feedforward_input, ffn_shrink).astype(jnp.bfloat16) * pair_bf
    )
    ffn_low_split = feedforward_rank_rows.reshape(tok_count, 2, rank_cols)
    gu_full, down_full = fetch_ffn(gateup_weight, down_weight)
    gate_up_output = jnp.einsum(
        "cm,ame->cae", feedforward_input, gu_full, preferred_element_type=jnp.float32
    ) + adapter_scale * jnp.einsum(
        "vmc,mcb->vmb", ffn_low_split, ffn_expand, preferred_element_type=jnp.float32
    )
    gate_pre = gate_up_output[:, 0]
    up_pre = gate_up_output[:, 1]
    activated_rows = (jax.nn.silu(gate_pre) * up_pre).astype(jnp.bfloat16)
    down_weight_slice = lax.psum_scatter(
        product_simple(activated_rows, down_full).astype(jnp.bfloat16),
        "tensor",
        scatter_dimension=1,
        tiled=True,
    ).astype(jnp.float32)
    down_rank_rows_sum = lax.psum(product_simple(activated_rows, down_shrink), "tensor")
    down_rank_rows = down_rank_rows_sum.astype(jnp.bfloat16) * adapter_half_float
    expand_factor_slice = lax.dynamic_slice_in_dim(
        down_adapter_expand, part_index * half_width, half_width, 1
    )
    hidden_column_slice = lax.dynamic_slice_in_dim(
        hidden_state_rows, part_index * half_width, half_width, 1
    )
    packed_output = (
        hidden_column_slice
        + (down_weight_slice + adapter_scale * product_simple(down_rank_rows, expand_factor_slice))
    ).astype(jnp.bfloat16)
    gu_full, down_full = fetch_ffn(gateup_weight, down_weight)
    down_rank_gradient = (
        adapter_scale * product_backward(cotangent_half_float, down_adapter_expand) * adapter_mask
    ).astype(jnp.bfloat16)
    down_adapter_expand_gradient = adapter_scale * product_leading(
        down_rank_rows, cotangent_half_float
    )
    grad_act = product_backward(cotangent_half_float, down_full) + product_backward(
        down_rank_gradient, down_shrink
    )
    down_shrink_grad = product_leading(activated_rows, down_rank_gradient)
    sigmoid_gate = jax.nn.sigmoid(gate_pre)
    grad_gate = grad_act * up_pre * sigmoid_gate * (1.0 + gate_pre * (1.0 - sigmoid_gate))
    grad_up = grad_act * gate_pre * sigmoid_gate
    grad_gu = jnp.stack([grad_gate, grad_up], axis=1).astype(jnp.bfloat16)
    feedforward_expand_gradient = adapter_scale * jnp.einsum(
        "tje,tjf->jef", ffn_low_split, grad_gu, preferred_element_type=jnp.float32
    )
    feedforward_rank_part = adapter_scale * jnp.einsum(
        "tjf,jef->tje", grad_gu, ffn_expand, preferred_element_type=jnp.float32
    ).reshape(tok_count, 2 * rank_cols)
    ffn_in_part = jnp.einsum("tjf,jdf->td", grad_gu, gu_full, preferred_element_type=jnp.float32)
    ffn_in_sum, ffn_low_sum = lax.psum((ffn_in_part, feedforward_rank_part), "tensor")
    grad_ffn_low = (ffn_low_sum * adapter_mask_pair).astype(jnp.bfloat16)
    grad_ffn_in = ffn_in_sum + product_backward(grad_ffn_low, ffn_shrink)
    ffn_shrink_grad = product_leading(feedforward_input, grad_ffn_low)
    grad_hidden = cot_full + norm_back(hidden_state_rows, scale_two, ffn_f, grad_ffn_in)
    in_full, out_full = fetch_mixer(in_weight, out_weight)
    adapter_branch_gradient = grad_hidden.astype(jnp.bfloat16)
    out_rank_gradient = (
        adapter_scale
        * product_backward(adapter_branch_gradient, output_adapter_expand)
        * adapter_mask
    ).astype(jnp.bfloat16)
    output_expand_gradient = adapter_scale * product_leading(
        output_rank_rows, adapter_branch_gradient
    )
    grad_gated = product_backward(adapter_branch_gradient, out_full) + product_backward(
        out_rank_gradient, out_shrink
    )
    out_shrink_grad = product_leading(gated_rows, out_rank_gradient)
    grad_gate_c = grad_gated * conv_out
    grad_conv = grad_gated * gate_c
    ahead = shifted(grad_conv[:2], "ctx", -1)
    trailing = jnp.concatenate([grad_conv, ahead], axis=0)
    grad_mixed = (
        conv_w[0] * grad_conv
        + conv_w[1] * trailing[1:-1] * ahead_one
        + conv_w[2] * trailing[2:] * ahead_two
    )
    grad_proj = jnp.stack([grad_mixed * values_x, grad_gate_c, grad_mixed * gate_b], axis=1).astype(
        jnp.bfloat16
    )
    input_expand_gradient = adapter_scale * jnp.einsum(
        "te,tjc->jec", input_rank_rows, grad_proj, preferred_element_type=jnp.float32
    )
    input_rank_part = adapter_scale * jnp.einsum(
        "tjc,jec->te", grad_proj, in_expand, preferred_element_type=jnp.float32
    )
    normed_part = jnp.einsum("tjc,jdc->td", grad_proj, in_full, preferred_element_type=jnp.float32)
    normed_sum, input_rank_sum = lax.psum((normed_part, input_rank_part), "tensor")
    in_rank_gradient = (input_rank_sum * adapter_mask).astype(jnp.bfloat16)
    grad_normed = normed_sum + product_backward(in_rank_gradient, input_adapter_shrink)
    in_shrink_grad = product_leading(normalized_rows, in_rank_gradient)
    grad_input_full = grad_hidden + norm_back(input_complete, scale_one, mixer_f, grad_normed)
    packed_grad = lax.dynamic_slice_in_dim(grad_input_full, part_index * half_width, half_width, 1)
    output_blocks = jnp.take(
        packed_output.reshape(group_total, block_rows, half_width), inverse_row, axis=0
    )
    grad_blocks = jnp.take(
        packed_grad.reshape(group_total, block_rows, half_width), inverse_row, axis=0
    )
    block_output = lax.all_to_all(
        output_blocks, "dp", split_axis=0, concat_axis=0, tiled=True
    ).reshape(tok_count, half_width)
    input_grad = (
        lax.all_to_all(
            grad_blocks.astype(jnp.bfloat16), "dp", split_axis=0, concat_axis=0, tiled=True
        )
        .astype(grad_blocks.dtype)
        .reshape(tok_count, half_width)
    )
    totals = lax.psum(
        (
            in_shrink_grad,
            input_expand_gradient,
            out_shrink_grad,
            output_expand_gradient,
            ffn_shrink_grad,
            feedforward_expand_gradient,
            down_shrink_grad,
            down_adapter_expand_gradient,
        ),
        ("dp", "ctx"),
    )
    return (
        block_output,
        input_grad,
        totals[0],
        totals[1],
        totals[2],
        totals[3],
        totals[4],
        totals[5],
        totals[6],
        totals[7],
    )


def solution(mesh):
    placed = (
        P(("dp", "ctx"), "tensor"),
        P(("dp", "ctx"), "tensor"),
        P("dp", None),
        P("dp"),
        P("dp"),
        P(),
        P(),
        P(None, "tensor"),
        P(None, "dp", "tensor"),
        P("tensor", "dp"),
        P(None, "dp", "tensor"),
        P("tensor", "dp"),
        P(),
        P(None, None, "tensor"),
        P("tensor", None),
        P(),
        P(),
        P(None, None, "tensor"),
        P("tensor", None),
        P(),
    )
    return jax.shard_map(
        body,
        mesh=mesh,
        in_specs=placed,
        out_specs=(
            P(("dp", "ctx"), "tensor"),
            P(("dp", "ctx"), "tensor"),
            P(),
            P(None, None, "tensor"),
            P("tensor", None),
            P(),
            P(),
            P(None, None, "tensor"),
            P("tensor", None),
            P(),
        ),
        check_vma=False,
    )
```

profile of v0, /device:TPU:0, one launch (start us, length us, event | category | flops | bytes accessed | tf_op | source)
XLA Modules:
  0.0 1380.1 jit_solution(14482190222094816660)
XLA Ops:
  7.2 25.2 %all_to_all.20 = bf16[4,192,1024]{2,1,0:T(8,128)(2,1)} all-to-all(bf16[4,192,1024]{2,1,0:T(8,128)(2,1)} %bitcast.155), channel_id=1, replica_groups=mesh['dp'=4,'ctx'=4,'tensor'=2] {'dp'}, dimensions={0} | all-to-all | bytes 3145728 | tf_op jit(solution)/shard_map/all_to_all | solution.py:97
  39.3 16.7 %all-to-all-done.2 = bf16[4,192,1024]{2,1,0:T(8,128)(2,1)S(1)} async-done(((bf16[4,192,1024]{2,1,0:T(8,128)(2,1)}), bf16[4,192,1024]{2,1,0:T(8,128)(2,1)S(1)}, u32[]{:S(2)}, u32[]{:S(2)}) %all-to-all-start.2) | async-done | bytes 1572896 | tf_op jit(solution)/shard_map/all_to_all | solution.py:104
  65.6 42.4 %all-gather.7.cloned.1.call-done = bf16[768,2048]{1,0:T(8,128)(2,1)} async-done(((bf16[768,1024]{1,0:T(8,128)(2,1)}), bf16[768,2048]{1,0:T(8,128)(2,1)}) %all-gather.7.cloned.1.call-update) | async-done | bytes 3145744 | tf_op jit(solution)/shard_map/all_gather | solution.py:135
  111.9 79.8 %all-gather.9.cloned.1.call-done = bf16[3,2048,1024]{2,1,0:T(8,128)(2,1)} async-done(((bf16[3,512,1024]{2,1,0:T(8,128)(2,1)}), bf16[3,2048,1024]{2,1,0:T(8,128)(2,1)}) %all-gather.9.cloned.1.call-update) | async-done | bytes 12582928 | tf_op jit(solution)/shard_map/all_gather | solution.py:51
  191.7 13.6 fusion.17
  215.4 12.4 all-gather.11.cloned.1.call-done
  227.8 7.4 fusion.72
  237.9 36.9 %all-gather.17.cloned.1.call-done = bf16[768,2048]{1,0:T(8,128)(2,1)} async-done(((bf16[768,1024]{1,0:T(8,128)(2,1)}), bf16[768,2048]{1,0:T(8,128)(2,1)}) %all-gather.17.cloned.1.call-update) | async-done | bytes 3145744 | tf_op jit(solution)/shard_map/all_gather | solution.py:136
  278.3 74.0 %all-gather.15.cloned.1.call-done = bf16[2816,2048]{1,0:T(8,128)(2,1)} async-done(((bf16[2816,512]{1,0:T(8,128)(2,1)}), bf16[2816,2048]{1,0:T(8,128)(2,1)}) %all-gather.15.cloned.1.call-update) | async-done | bytes 11534352 | tf_op jit(solution)/shard_map/all_gather | solution.py:59
  352.3 15.8 %fusion.75 = f32[768,2816]{1,0:T(8,128)} fusion(bf16[768,2048]{1,0:T(8,128)(2,1)} %all-gather.17.cloned.1.call-done, bf16[2816,2048]{1,0:T(8,128)(2,1)} %all-gather.15.cloned.1.call-done), kind=kOutput, calls=%fused_computation.166 | convolution fusion | flops 8858370048 | bytes 23330816 | tf_op jit(solution)/shard_map/dot_general | solution.py:34
  369.5 25.5 %all-reduce.17 = bf16[768,128]{1,0:T(8,128)(2,1)S(1)} all-reduce(f32[768,128]{1,0:T(8,128)} %fusion.73), channel_id=1, replica_groups=mesh['dp'=4,'ctx'=4,'tensor'=2] {'tensor'}, use_global_device_ids=true, to_apply=%region_7.9 | all-reduce | flops 98304 | bytes 589824 | tf_op jit(solution)/shard_map/psum | solution.py:168
  395.0 121.3 %all-reduce.10.cloned.1.call-done = f32[768,2048]{1,0:T(8,128)} async-done(((f32[768,2048]{1,0:T(8,128)}), f32[768,2048]{1,0:T(8,128)}) %all-reduce.10.cloned.1.call-update) | async-done | bytes 6291472 | tf_op jit(solution)/shard_map/psum | solution.py:168
  516.3 4.7 multiply_reduce_fusion.2
  528.2 131.7 %all-gather.13.cloned.1.call-done = bf16[2,2048,2816]{2,1,0:T(8,128)(2,1)} async-done(((bf16[2,512,2816]{2,1,0:T(8,128)(2,1)}), bf16[2,2048,2816]{2,1,0:T(8,128)(2,1)}) %all-gather.13.cloned.1.call-update) | async-done | bytes 23068688 | tf_op jit(solution)/shard_map/all_gather | solution.py:58
  659.9 23.8 %fusion.15 = f32[768,2,2816]{2,0,1:T(8,128)S(1)} fusion(bf16[2,2048,2816]{2,1,0:T(8,128)(2,1)} %all-gather.13.cloned.1.call-done, bf16[768,2048]{1,0:T(8,128)(2,1)} %copy-done.11), kind=kOutput, calls=%fused_computation.57 | convolution fusion | flops 17716740096 | bytes 43515904 | tf_op jit(solution)/shard_map/cm,ame->cae/dot_general | solution.py:182
  683.6 9.4 bitcast_add_fusion
  693.0 13.5 fusion.2
  706.6 5.8 fusion.24
  713.6 25.4 %convolution_bitcast_fusion.1 = f32[768,2048]{1,0:T(8,128)} fusion(bf16[2,2048,2816]{2,1,0:T(8,128)(2,1)} %all-gather.13.cloned.1.call-done, bf16[768,1,2816]{2,0,1:T(8,128)(2,1)} %get-tuple-element.53, bf16[768,1,2816]{2,0,1:T(8,128)(2,1)} %copy-done.65), kind=kOutput, calls=%fused_computation.31 | convolution fusion | flops 17721065472 | bytes 38010880 | tf_op jit(solution)/shard_map/tjf,jdf->td/dot_general | solution.py:229
  739.0 14.4 %convolution_convert_fusion = bf16[768,2048]{1,0:T(8,128)(2,1)} fusion(bf16[768,2816]{1,0:T(8,128)(2,1)} %get-tuple-element.54, bf16[2816,2048]{1,0:T(8,128)(2,1)} %all-gather.15.cloned.1.call-done), kind=kOutput, calls=%fused_computation.32 | convolution fusion | flops 8859942912 | bytes 19005440 | tf_op jit(solution)/shard_map/dot_general | solution.py:30
  753.6 156.1 %all-reduce.16.cloned.1.call-done = (f32[768,2048]{1,0:T(8,128)}, f32[768,256]{1,0:T(8,128)}) async-done(((f32[768,2048]{1,0:T(8,128)}, f32[768,256]{1,0:T(8,128)}), (f32[768,2048]{1,0:T(8,128)}, f32[768,256]{1,0:T(8,128)})) %all-reduce.16.cloned.1.call-update) | async-done | bytes 7077904 | tf_op jit(solution)/shard_map/psum | solution.py:230
  909.7 6.5 multiply_reduce_fusion.1
  930.6 4.2 collective-permute-done.1
  940.3 14.7 %convolution_bitcast_fusion = f32[768,2048]{1,0:T(8,128)} fusion(bf16[3,2048,1024]{2,1,0:T(8,128)(2,1)} %all-gather.9.cloned.1.call-done, bf16[768,1,1024]{2,0,1:T(8,128)(2,1)S(1)} %fusion.23, bf16[768,1,1024]{2,0,1:T(8,128)(2,1)S(1)} %get-tuple-element.57, bf16[768,1,1024]{2,0,1:T(8,128)(2,1)S(1)} %get-tuple-element.48), kind=kOutput, calls=%fused_computation.30 | convolution fusion | flops 9668395008 | bytes 23592960 | tf_op jit(solution)/shard_map/tjc,jdc->td/dot_general | solution.py:267
  959.1 4.8 fusion.77
  963.9 6.9 convolution_multiply_fusion
  978.8 41.3 %all-reduce.18 = (bf16[768,128]{1,0:T(8,128)(2,1)S(1)}, bf16[768,128]{1,0:T(8,128)(2,1)S(1)}) all-reduce(f32[768,128]{1,0:T(8,128)S(1)} %fusion.74, f32[768,128]{1,0:T(8,128)S(1)} %fusion.27), channel_id=1, replica_groups=mesh['dp'=4,'ctx'=4,'tensor'=2] {'tensor'}, use_global_device_ids=true, to_apply=%region_10.12 | all-reduce | flops 196608 | bytes 1179648 | tf_op jit(solution)/shard_map/psum | solution.py:196
  1035.0 92.8 %all-reduce.12.cloned.1.call-done = f32[768,2048]{1,0:T(8,128)} async-done(((f32[768,2048]{1,0:T(8,128)}), f32[768,2048]{1,0:T(8,128)}) %all-reduce.12.cloned.1.call-update) | async-done | bytes 6291472 | tf_op jit(solution)/shard_map/psum | solution.py:268
  1127.8 4.9 multiply_reduce_fusion
  1141.1 39.8 %all_to_all.21 = bf16[4,192,1024]{2,1,0:T(8,128)(2,1)S(1)} all-to-all(bf16[4,192,1024]{2,1,0:T(8,128)(2,1)S(1)} %get-tuple-element.67), channel_id=1, replica_groups=mesh['dp'=4,'ctx'=4,'tensor'=2] {'dp'}, dimensions={0} | all-to-all | bytes 3145728 | tf_op jit(solution)/shard_map/all_to_all | solution.py:280
  1180.9 4.4 all-to-all-start.3
  1185.3 170.9 %all-reduce.14.cloned.1.call-done = (f32[2048,128]{1,0:T(8,128)}, f32[3,128,1024]{1,2,0:T(8,128)}, f32[1024,128]{1,0:T(8,128)}, f32[128,2048]{1,0:T(8,128)}, f32...) async-done(((f32[2048,128]{1,0:T(8,128)}, f32[3,128,1024]{1,2,0:T(8,128)}, f32[1024,128]{1,0:T(8,128)}, ...) | async-done | bytes 11665424 | tf_op jit(solution)/shard_map/psum | solution.py:290
  (250 shorter events, 117.4 us)
Async XLA Ops:
  7.2 676.5 %copy-start = (bf16[2,128,2816]{2,1,0:T(8,128)(2,1)S(1)}, bf16[2,128,2816]{2,1,0:T(8,128)(2,1)}, u32[]{:S(2)}) copy-start(bf16[2,128,2816]{2,1,0:T(8,128)(2,1)} %param.39) | copy-start | bytes 4325380
  7.2 28.9 %copy-start.63 = (s32[1,4]{1,0:T(1,128)S(1)}, s32[1,4]{1,0:T(1,128)}, u32[]{:S(2)}) copy-start(s32[1,4]{1,0:T(1,128)} %param.24) | copy-start | bytes 52
  32.4 23.6 %all-to-all-start.2 = ((bf16[4,192,1024]{2,1,0:T(8,128)(2,1)}), bf16[4,192,1024]{2,1,0:T(8,128)(2,1)S(1)}, u32[]{:S(2)}, u32[]{:S(2)}) async-start(bf16[4,192,1024]{2,1,0:T(8,128)(2,1)} %bitcast.156), calls=%async_computation.3 | async-start | bytes 3145728 | tf_op jit(solution)/shard_map/all_to_all | solution.py:104
  36.0 72.0 %all-gather.7.cloned.1.call-start = ((), (), s32[]{:S(2)}) async-start(), calls=%async_computation.5 | async-start | bytes 4718592 | tf_op jit(solution)/shard_map/all_gather | solution.py:135
  61.8 130.0 %all-gather.9.cloned.1.call-start = ((), (), s32[]{:S(2)}) async-start(), calls=%async_computation.6 | async-start | bytes 15728640 | tf_op jit(solution)/shard_map/all_gather | solution.py:51
  62.6 165.3 %all-gather.11.cloned.1.call-start = ((), (), s32[]{:S(2)}) async-start(), calls=%async_computation.7 | async-start | bytes 5242880 | tf_op jit(solution)/shard_map/all_gather | solution.py:52
  63.3 211.5 %all-gather.17.cloned.1.call-start = ((), (), s32[]{:S(2)}) async-start(), calls=%async_computation.12 | async-start | bytes 4718592 | tf_op jit(solution)/shard_map/all_gather | solution.py:136
  63.9 46.9 %copy-start.38 = (bf16[2048,128]{1,0:T(8,128)(2,1)S(1)}, bf16[2048,128]{1,0:T(8,128)(2,1)}, u32[]{:S(2)}) copy-start(bf16[2048,128]{1,0:T(8,128)(2,1)} %param.34) | copy-start | bytes 1572868
  63.9 288.5 %all-gather.15.cloned.1.call-start = ((), (), s32[]{:S(2)}) async-start(), calls=%async_computation.10 | async-start | bytes 14417920 | tf_op jit(solution)/shard_map/all_gather | solution.py:59
  64.5 451.9 %all-reduce.10.cloned.1.call-start = ((), (), s32[]{:S(2)}) async-start(), calls=%async_computation.8 | async-start | bytes 12582912 | tf_op jit(solution)/shard_map/psum | solution.py:168
  64.5 127.2 %copy-start.54 = (f32[2048]{0:T(1024)}, f32[2048]{0:T(1024)S(1)}, u32[]{:S(2)}) copy-start(f32[2048]{0:T(1024)S(1)} %convert_element_type.128) | copy-start | bytes 24580
  110.9 80.9 %copy-start.46 = (f32[768]{0:T(1024)}, f32[768]{0:T(1024)S(1)}, u32[]{:S(2)}) copy-start(f32[768]{0:T(1024)S(1)} %add_rsqrt_fusion.1) | copy-start | bytes 9220
  111.9 93.4 %copy-start.41 = (bf16[768,128,1]{1,0,2:T(8,128)(2,1)}, bf16[768,128,1]{1,0,2:T(8,128)(2,1)S(1)}, u32[]{:S(2)}) copy-start(bf16[768,128,1]{1,0,2:T(8,128)(2,1)S(1)} %fusion.32) | copy-start | bytes 589828
  111.9 93.4 %copy-start.28 = (bf16[3,128,1024]{2,1,0:T(8,128)(2,1)S(1)}, bf16[3,128,1024]{2,1,0:T(8,128)(2,1)}, u32[]{:S(2)}) copy-start(bf16[3,128,1024]{2,1,0:T(8,128)(2,1)} %param.35) | copy-start | bytes 2359300
  207.3 4.7 collective-permute-start
  215.4 152.8 %copy-start.7 = (bf16[768,1024]{1,0:T(8,128)(2,1)}, bf16[768,1024]{1,0:T(8,128)(2,1)S(1)}, u32[]{:S(2)}) copy-start(bf16[768,1024]{1,0:T(8,128)(2,1)S(1)} %get-tuple-element.50) | copy-start | bytes 4718596
  235.2 39.5 %copy-start.44 = (bf16[128,2048]{1,0:T(8,128)(2,1)S(1)}, bf16[128,2048]{1,0:T(8,128)(2,1)}, u32[]{:S(2)}) copy-start(bf16[128,2048]{1,0:T(8,128)(2,1)} %param.41) | copy-start | bytes 1572868
  235.2 424.6 %all-gather.13.cloned.1.call-start = ((), (), s32[]{:S(2)}) async-start(), calls=%async_computation.9 | async-start | bytes 28835840 | tf_op jit(solution)/shard_map/all_gather | solution.py:58
  236.0 673.7 %all-reduce.16.cloned.1.call-start = ((), (), s32[]{:S(2)}) async-start(), calls=%async_computation.15 | async-start | bytes 14155776 | tf_op jit(solution)/shard_map/psum | solution.py:230
  352.3 15.8 %copy-start.32 = (bf16[1024,128]{1,0:T(8,128)(2,1)S(1)}, bf16[1024,128]{1,0:T(8,128)(2,1)}, u32[]{:S(2)}) copy-start(bf16[1024,128]{1,0:T(8,128)(2,1)} %param.36) | copy-start | bytes 786436
  368.2 148.1 %copy-start.14 = (bf16[128,2048]{1,0:T(8,128)(2,1)S(1)}, bf16[128,2048]{1,0:T(8,128)(2,1)}, u32[]{:S(2)}) copy-start(bf16[128,2048]{1,0:T(8,128)(2,1)} %param.37) | copy-start | bytes 1572868
  395.0 126.0 %copy-start.16 = (bf16[768,128]{1,0:T(8,128)(2,1)}, bf16[768,128]{1,0:T(8,128)(2,1)S(1)}, u32[]{:S(2)}) copy-start(bf16[768,128]{1,0:T(8,128)(2,1)S(1)} %all-reduce.17) | copy-start | bytes 589828
  739.0 290.9 %reduce-scatter.2.cloned.1.call-start = ((), (), s32[]{:S(2)}) async-start(), calls=%async_computation.11 | async-start | bytes 4718592 | tf_op jit(solution)/shard_map/reduce_scatter | solution.py:190
  753.5 156.2 %copy-start.26 = (f32[768,128]{1,0:T(8,128)S(1)}, f32[768,128]{1,0:T(8,128)}, u32[]{:S(2)}) copy-start(f32[768,128]{1,0:T(8,128)} %compare_convert_fusion) | copy-start | bytes 1179652
  753.5 156.2 %copy-start.31 = (bf16[2048,256]{1,0:T(8,128)(2,1)S(1)}, bf16[2048,256]{1,0:T(8,128)(2,1)}, u32[]{:S(2)}) copy-start(bf16[2048,256]{1,0:T(8,128)(2,1)} %param.38) | copy-start | bytes 3145732
  753.5 374.3 %all-reduce.12.cloned.1.call-start = ((), (), s32[]{:S(2)}) async-start(), calls=%async_computation.13 | async-start | bytes 12582912 | tf_op jit(solution)/shard_map/psum | solution.py:268
  929.3 5.5 collective-permute-start.1
  955.0 401.1 %all-reduce.14.cloned.1.call-start = ((), (), s32[]{:S(2)}) async-start(), calls=%async_computation.14 | async-start | bytes 23330816 | tf_op jit(solution)/shard_map/psum | solution.py:290
  978.8 45.0 %copy-start.47 = (f32[768]{0:T(1024)S(1)}, f32[768]{0:T(1024)}, u32[]{:S(2)}) copy-start(f32[768]{0:T(1024)} %copy-done.46) | copy-start | bytes 9220
  978.8 45.0 %copy-start.55 = (f32[2048]{0:T(1024)S(1)}, f32[2048]{0:T(1024)}, u32[]{:S(2)}) copy-start(f32[2048]{0:T(1024)} %copy-done.54) | copy-start | bytes 24580
  1033.2 94.6 %copy-start.39 = (bf16[2048,128]{1,0:T(8,128)(2,1)S(1)}, bf16[2048,128]{1,0:T(8,128)(2,1)}, u32[]{:S(2)}) copy-start(bf16[2048,128]{1,0:T(8,128)(2,1)} %param.34) | copy-start | bytes 1572868
  1180.9 178.3 %all-to-all-start.3 = ((bf16[4,192,1024]{2,1,0:T(8,128)(2,1)}), bf16[4,192,1024]{2,1,0:T(8,128)(2,1)}, u32[]{:S(2)}, u32[]{:S(2)}) async-start(bf16[4,192,1024]{2,1,0:T(8,128)(2,1)} %get-tuple-element.66), calls=%async_computation.4 | async-start | bytes 3145728 | tf_op jit(solution)/shard_map/all_to_all | solution.py:284
  (56 other events, 240.8 us)
Sparse Core Ops, SparseCore 0:
  61.9 46.0 all-gather.6
  109.6 82.0 all-gather.8
  193.3 34.4 all-gather.10
  229.8 44.9 all-gather.16
  276.2 76.1 all-gather.14
  354.6 161.6 all-reduce.9
  518.0 141.8 all-gather.12
  739.1 170.5 all-reduce.15
  911.9 43.3 reduce-scatter.1
  957.7 170.0 all-reduce.11
  1133.8 222.3 all-reduce.13
where the time goes:
time: 1390 us; the launch traced here: 1380 us
  waiting for transfers between devices  944 us (68%)
  matrix products  208 us (15%)
  blocking collectives  132 us (9%)
  local copies, waits for them, and re-layouts  36.4 us (3%)
  other arithmetic  31.6 us (2%)
  between operations  15.3 us (1%)
    psum x1, waiting for transfers between devices, body(): lax.psum((in_shrink_grad, input_expand_gradient, out_shrink_grad, output_...  171 us
    psum x1, waiting for transfers between devices, body(): lax.psum((ffn_in_part, feedforward_rank_part), 'tensor')  156 us
    all_gather x1, waiting for transfers between devices, fetch_ffn(): lax.all_gather(gateup_weight, 'dp', axis=1, tiled=True)  132 us
    psum x1, waiting for transfers between devices, body(): lax.psum((product_simple(gated_rows, out_full), product_simple(gated_rows...  121 us
    psum x1, waiting for transfers between devices, body(): lax.psum((normed_part, input_rank_part), 'tensor')  92.8 us
    all_gather x1, waiting for transfers between devices, fetch_mixer(): lax.all_gather(in_weight, 'dp', axis=1, tiled=True)  79.8 us
    all_gather x1, waiting for transfers between devices, fetch_ffn(): lax.all_gather(down_weight, 'dp', axis=1, tiled=True)  74 us
    dot_general x8, matrix products, product_backward(): lax.dot_general(left, right, (((1,), (1,)), ((), ())), preferred_element_...  49.3 us
  transfers between devices with their start and end apart: 15, of which 13 were waited for; matrix products, arithmetic and copies ran while one was open for 12% of the time, Pallas kernels for 0%

commit v1 on v0

v1 whole, which is shorter than its diff:
```python
import jax
import jax.numpy as jnp
from jax import lax
from jax.sharding import PartitionSpec as P

RANK = 16
CHUNKS = 2

norm_eps = 1e-05
adapter_scale = 0.5

f32 = jnp.float32
bf16 = jnp.bfloat16


def dot(left, right):
    return jnp.dot(left, right, preferred_element_type=f32)


def dot_nt(left, right):
    return lax.dot_general(left, right, (((1,), (1,)), ((), ())), preferred_element_type=f32)


def dot_tn(left, right):
    return lax.dot_general(left, right, (((0,), (0,)), ((), ())), preferred_element_type=f32)


def rms_scale(values):
    return lax.rsqrt(jnp.mean(values * values, axis=-1, keepdims=True) + norm_eps)


def block_order(array, axis, index_list, width):
    pieces = [lax.dynamic_slice_in_dim(array, i * width, width, axis) for i in index_list]
    return jnp.concatenate(pieces, axis=axis)


def swap_tensor(array):
    return lax.ppermute(array, "tensor", [(0, 1), (1, 0)])


def body(
    block_input,
    cotangent,
    deal_order,
    seq_lengths,
    seq_adapter,
    mixer_gain,
    ffn_gain,
    conv_taps,
    in_weight,
    out_weight,
    gateup_weight,
    down_weight,
    input_adapter_shrink,
    in_expand,
    out_shrink,
    output_adapter_expand,
    ffn_shrink,
    ffn_expand,
    down_shrink,
    down_adapter_expand,
):
    tok_count, half = block_input.shape
    width = 2 * half
    rank_cols = input_adapter_shrink.shape[1]
    groups = lax.axis_size("dp")
    pieces = lax.axis_size("ctx")
    sub = tok_count // groups
    group_tokens = pieces * tok_count
    seqs = seq_lengths.shape[0]
    special = groups == 4 and pieces % 2 == 0
    me = lax.axis_index("dp")
    ctx = lax.axis_index("ctx")
    tens = lax.axis_index("tensor")
    if special:
        xb, cb, zb = me // 2, me % 2, ctx % 2
    else:
        xb = cb = zb = jnp.int32(0)
    pair_flip = xb ^ tens
    sub_width = width // 8

    actual = []
    in_stack = []
    for rx in (0, 1):
        for rc in (0, 1):
            for rh in (0, 1):
                low = (rc ^ cb) * 2 + (rh ^ (zb & rx))
                actual.append((rx ^ xb) * 4 + low)
                in_stack.append((rx ^ pair_flip) * 4 + low)
    inner = []
    for bc in (0, 1):
        for bh in (0, 1):
            inner.append((bc ^ cb) * 2 + (bh ^ (zb & pair_flip)))

    def relative(array, axis):
        return block_order(array, axis, actual, sub_width) if special else array

    def own_half(array, axis):
        return lax.dynamic_slice_in_dim(array, pair_flip * half, half, axis)

    def other_half(array, axis):
        return lax.dynamic_slice_in_dim(array, (1 - pair_flip) * half, half, axis)

    def restored(array, axis):
        return block_order(array, axis, inner, sub_width) if special else array

    core_route = [(0, 1), (1, 0), (2, 3), (3, 2)]
    x_route = [(0, 2), (2, 0), (1, 3), (3, 1)]
    z_route = [(i, i ^ 1) for i in range(pieces)]

    def fetch(shard, axis):
        if not special:
            return [lax.all_gather(shard, "dp", axis=axis, tiled=True)]
        n = shard.shape[axis] // 2
        mine = lax.dynamic_slice_in_dim(shard, zb * n, n, axis)
        over_x = lax.ppermute(mine, "dp", x_route)
        over_z = lax.ppermute(over_x, "ctx", z_route)
        return [
            shard,
            lax.ppermute(shard, "dp", core_route),
            over_x,
            over_z,
            lax.ppermute(over_x, "dp", core_route),
            lax.ppermute(over_z, "dp", core_route),
        ]

    span = tok_count // CHUNKS
    nb = groups // CHUNKS
    x_own = [block_input[i * span : (i + 1) * span] for i in range(CHUNKS)]
    g_own = [cotangent[i * span : (i + 1) * span] for i in range(CHUNKS)]
    x_got = [swap_tensor(v) for v in x_own]

    in_shards = [fetch(in_weight[j], 0) for j in range(3)]
    out_shards = fetch(out_weight, 1)

    table = jnp.concatenate([deal_order[0], seq_lengths, seq_adapter])
    table = lax.all_gather(table, "dp", axis=0, tiled=False)
    deal_all = table[:, :groups]
    lengths_all = table[:, groups : groups + seqs]
    adapter_all = table[:, groups + seqs :]
    device_ids = jnp.arange(groups, dtype=jnp.int32)
    slot = jnp.sum(
        jnp.where(deal_all[:, :, None] == device_ids[None, None, :], device_ids[None, :, None], 0), axis=1
    )
    my_slot = jnp.sum(jnp.where(device_ids[None, :] == me, slot, 0), axis=1)

    x_blocks = block_input.reshape(groups, sub, half)
    g_blocks = cotangent.reshape(groups, sub, half)
    edges = jnp.concatenate([x_blocks[:, :2], g_blocks[:, :2], x_blocks[:, sub - 2 :]], axis=1)
    all_edges = lax.all_gather(edges, "dp", axis=0, tiled=False)
    slot_of = slot.T[:, :, None, None]
    want = my_slot[None, :, None, None]

    def pick(test, rows):
        return jnp.sum(jnp.where(test, rows.astype(f32), 0.0), axis=0).astype(bf16)

    heads, tails = all_edges[:, :, :4], all_edges[:, :, 4:]
    first_heads = pick(slot_of == 0, heads)
    last_tails = pick(slot_of == groups - 1, tails)
    from_next = lax.ppermute(first_heads, "ctx", [(i + 1, i) for i in range(pieces - 1)])
    from_prev = lax.ppermute(last_tails, "ctx", [(i, i + 1) for i in range(pieces - 1)])
    edge = my_slot[:, None, None]
    next_rows = jnp.where(edge == groups - 1, from_next, pick(slot_of == want + 1, heads))
    prev_rows = jnp.where(edge == 0, from_prev, pick(slot_of == want - 1, tails))
    halo_own = jnp.concatenate([next_rows, prev_rows], axis=1)
    halo_got = swap_tensor(halo_own)
    g_got = [swap_tensor(v) for v in g_own]

    gu_shards = [fetch(gateup_weight[j], 0) for j in range(2)]
    down_shards = fetch(down_weight, 1)

    in_first = relative(input_adapter_shrink, 0)
    out_second = relative(output_adapter_expand, 1)
    ffn_first = relative(ffn_shrink, 0)
    down_second = relative(down_adapter_expand, 1)
    mixer_f = relative(mixer_gain, 0).astype(f32)
    ffn_f = relative(ffn_gain, 0).astype(f32)
    conv_w = conv_taps.astype(f32)

    half_scale = jnp.asarray(adapter_scale, bf16)
    in_full = [jnp.concatenate([*in_shards[j], in_expand[j] * half_scale], axis=0) for j in range(3)]
    out_full = jnp.concatenate([*out_shards, out_shrink], axis=1)
    blank = jnp.zeros((rank_cols, gateup_weight.shape[2]), bf16)
    gu_full = [
        jnp.concatenate([*gu_shards[0], ffn_expand[0] * half_scale, blank], axis=0),
        jnp.concatenate([*gu_shards[1], blank, ffn_expand[1] * half_scale], axis=0),
    ]
    down_full = jnp.concatenate([*down_shards, down_shrink], axis=1)

    def full_rows(own, got):
        stack = jnp.concatenate([own, got], axis=1)
        return block_order(stack, 1, in_stack, sub_width)

    offsets = jnp.concatenate(
        [jnp.arange(sub + 2, dtype=jnp.int32), jnp.arange(-2, 0, dtype=jnp.int32)]
    )
    seq_ends = []
    total = jnp.zeros((groups,), jnp.int32)
    for i in range(seqs - 1):
        total = total + lengths_all[:, i]
        seq_ends.append(total)

    def segment_of(positions, ends):
        found = jnp.zeros(positions.shape, jnp.int32)
        for end in ends:
            found = found + (positions >= end[:, None]).astype(jnp.int32)
        return found

    chunk = []
    for i in range(CHUNKS):
        blocks = slice(i * nb, (i + 1) * nb)
        base = ctx * tok_count + my_slot[blocks] * sub
        positions = base[:, None] + offsets[None, :]
        ends = [end[blocks] for end in seq_ends]
        segment = segment_of(positions, ends)
        adapter = jnp.zeros(positions.shape, jnp.int32)
        for j in range(seqs):
            adapter = adapter + jnp.where(segment == j, adapter_all[blocks, j][:, None], 0)
        inside = positions < group_tokens
        same_one = (positions >= 1) & inside & (segment_of(positions - 1, ends) == segment)
        same_two = (positions >= 2) & inside & (segment_of(positions - 2, ends) == segment)
        same_one = same_one.astype(f32)[:, : sub + 2, None]
        same_two = same_two.astype(f32)[:, : sub + 2, None]

        def in_rows(array):
            tail = array.shape[2:]
            return jnp.concatenate(
                [
                    array[:, :sub].reshape((nb * sub,) + tail),
                    array[:, sub : sub + 2].reshape((nb * 2,) + tail),
                    array[:, sub + 2 :].reshape((nb * 2,) + tail),
                ],
                axis=0,
            )

        columns = jnp.arange(rank_cols, dtype=jnp.int32) // RANK
        adapter_rows = in_rows(adapter[:, :, None])
        mask = (columns[None, :] == adapter_rows).astype(bf16)

        def with_halo(main, halo, first):
            edge_rows = halo[blocks]
            nxt = edge_rows[:, first : first + 2].reshape(nb * 2, half)
            prv = edge_rows[:, 4:].reshape(nb * 2, half)
            return jnp.concatenate([main, nxt, prv], axis=0)

        x_full = full_rows(with_halo(x_own[i], halo_own, 0), with_halo(x_got[i], halo_got, 0))
        rows = nb * (sub + 2)
        g_full = full_rows(
            with_halo(g_own[i], halo_own, 2)[:rows], with_halo(g_got[i], halo_got, 2)[:rows]
        )
        chunk.append(dict(x=x_full, g=g_full, mask=mask, s1=same_one, s2=same_two))

    rows = nb * (sub + 2)
    main = nb * sub

    def blocked(array):
        return array[:main].reshape(nb, sub, -1), array[main:rows].reshape(nb, 2, -1)

    for c in chunk:
        x = c["x"].astype(f32)
        scale = rms_scale(x)
        normed = (x * scale * mixer_f).astype(bf16)
        low = dot(normed, in_first).astype(bf16) * c["mask"]
        lhs = jnp.concatenate([normed, low], axis=1)
        gate_b, gate_c, values = (dot(lhs, in_full[j]) for j in range(3))
        mixed = (gate_b * values).astype(bf16)
        mid, nxt = blocked(mixed)
        prv = mixed[rows:].reshape(nb, 2, -1)
        ext = jnp.concatenate([prv, mid, nxt], axis=1).astype(f32)
        conv = (
            conv_w[0] * ext[:, 2:]
            + conv_w[1] * ext[:, 1:-1] * c["s1"]
            + conv_w[2] * ext[:, :-2] * c["s2"]
        )
        conv = jnp.concatenate(
            [conv[:, :sub].reshape(main, -1), conv[:, sub:].reshape(rows - main, -1)], axis=0
        )
        gated = (gate_c[:rows] * conv).astype(bf16)
        part = dot(gated, out_full).astype(bf16)
        c.update(
            scale=scale[:rows], normed=normed, low=low, b=gate_b, c=gate_c[:rows], v=values,
            conv=conv, gated=gated, part=part, got=swap_tensor(part), m=c["mask"][:rows],
        )

    for c in chunk:
        both = c["part"].astype(f32) + c["got"].astype(f32)
        out_low = both[:, width:].astype(bf16) * c["m"]
        hidden = c["x"][:rows].astype(f32) + (both[:, :width] + adapter_scale * dot(out_low, out_second))
        scale = rms_scale(hidden)
        ffn_in = (hidden * scale * ffn_f).astype(bf16)
        m2 = jnp.concatenate([c["m"], c["m"]], axis=1)
        low = dot(ffn_in, ffn_first).astype(bf16) * m2
        lhs = jnp.concatenate([ffn_in, low], axis=1)
        gate, up = dot(lhs, gu_full[0]), dot(lhs, gu_full[1])
        sig = jax.nn.sigmoid(gate)
        act = (gate * sig * up).astype(bf16)
        g = c["g"]
        g_low = (adapter_scale * dot_nt(g, down_second)).astype(bf16) * c["m"]
        grad_act = dot_nt(jnp.concatenate([g, g_low], axis=1), down_full)
        gg = (grad_act * up * sig * (1.0 + gate * (1.0 - sig))).astype(bf16)
        gu = (grad_act * gate * sig).astype(bf16)
        part = (dot_nt(gg, gu_full[0]) + dot_nt(gu, gu_full[1])).astype(bf16)
        c.update(f_part=part, f_got=swap_tensor(part))
        down = dot(act[:main], down_full).astype(bf16)
        own = jnp.concatenate([own_half(down, 1), down[:, width:]], axis=1)
        send = jnp.concatenate([other_half(down, 1), down[:, width:]], axis=1)
        c.update(
            out_low=out_low, hidden=hidden, scale_two=scale, ffn_in=ffn_in, ffn_low=low, act=act,
            g_low=g_low, gg=gg, gu=gu, m2=m2, d_own=own, d_got=swap_tensor(send),
        )

    for c in chunk:
        both = c["f_part"].astype(f32) + c["f_got"].astype(f32)
        grad_low = both[:, width:].astype(bf16) * c["m2"]
        grad_in = both[:, :width] + dot_nt(grad_low, ffn_first)
        scale, hidden = c["scale_two"], c["hidden"]
        unit = hidden * scale
        grad_unit = grad_in * ffn_f
        grad_hidden = c["g"].astype(f32) + scale * (
            grad_unit - unit * jnp.mean(grad_unit * unit, axis=-1, keepdims=True)
        )
        branch = grad_hidden.astype(bf16)
        b_low = (adapter_scale * dot_nt(branch, out_second)).astype(bf16) * c["m"]
        grad_gated = dot_nt(jnp.concatenate([branch, b_low], axis=1), out_full)
        grad_c = grad_gated[:main] * c["conv"][:main]
        grad_conv = grad_gated * c["c"]
        mid, nxt = blocked(grad_conv)
        ext = jnp.concatenate([mid, nxt], axis=1)
        grad_mixed = (
            conv_w[0] * mid
            + conv_w[1] * (ext * c["s1"])[:, 1:-1]
            + conv_w[2] * (ext * c["s2"])[:, 2:]
        ).reshape(main, -1)
        proj = [
            (grad_mixed * c["v"][:main]).astype(bf16),
            grad_c.astype(bf16),
            (grad_mixed * c["b"][:main]).astype(bf16),
        ]
        part = sum(dot_nt(proj[j], in_full[j]) for j in range(3)).astype(bf16)
        x = c["x"][:main].astype(f32)
        unit = x * c["scale"][:main]
        stat = jnp.sum(part[:, :width].astype(f32) * (unit * mixer_f), axis=-1, keepdims=True)
        own = jnp.concatenate([own_half(part, 1), part[:, width:]], axis=1)
        send = jnp.concatenate([other_half(part, 1), part[:, width:]], axis=1)
        c.update(
            f_low=grad_low, grad_hidden=grad_hidden, branch=branch, b_low=b_low, proj=proj,
            n_own=own, n_got=swap_tensor(send), stat=stat, stat_got=swap_tensor(stat), unit=unit,
        )

    out_rows, grad_rows = [], []
    mixer_half = own_half(mixer_f, 0)
    for c in chunk:
        both = c["d_own"].astype(f32) + c["d_got"].astype(f32)
        down_low = both[:, half:].astype(bf16) * c["m"][:main]
        c["down_low"] = down_low
        hidden = own_half(c["hidden"], 1)[:main]
        rows_out = hidden + (
            both[:, :half] + adapter_scale * dot(down_low, own_half(down_second, 1))
        )
        out_rows.append(restored(rows_out.astype(bf16), 1))
        both = c["n_own"].astype(f32) + c["n_got"].astype(f32)
        grad_low = both[:, half:].astype(bf16) * c["m"][:main]
        c["n_low"] = grad_low
        added = dot_nt(grad_low, in_first)
        stat = (
            c["stat"]
            + c["stat_got"]
            + jnp.sum(added * (c["unit"] * mixer_f), axis=-1, keepdims=True)
        ) / width
        grad_unit = (both[:, :half] + own_half(added, 1)) * mixer_half
        grad_x = own_half(c["grad_hidden"], 1)[:main] + c["scale"][:main] * (
            grad_unit - own_half(c["unit"], 1) * stat
        )
        grad_rows.append(restored(grad_x, 1))
    block_output = jnp.concatenate(out_rows, axis=0)
    input_grad = jnp.concatenate(grad_rows, axis=0)

    def over_rows(left, right):
        return sum(dot_tn(left(c)[:main], right(c)[:main]) for c in chunk)

    def reduced(*parts):
        return lax.psum(tuple(p.astype(bf16) for p in parts), ("dp", "ctx"))

    def joined(part, axis):
        got = swap_tensor(part)
        first = jnp.where(tens == 0, part, got)
        second = jnp.where(tens == 0, got, part)
        return jnp.concatenate([first, second], axis=axis).astype(f32)

    down_first_grad = over_rows(lambda c: c["act"], lambda c: c["g_low"])
    down_second_grad = adapter_scale * over_rows(
        lambda c: c["down_low"], lambda c: own_half(c["g"], 1)
    )
    ffn_second_grad = [
        adapter_scale
        * over_rows(lambda c: c["ffn_low"][:, j * rank_cols : (j + 1) * rank_cols], lambda c: c[k])
        for j, k in enumerate(("gg", "gu"))
    ]
    early = reduced(
        down_first_grad, restored(down_second_grad, 1), ffn_second_grad[0], ffn_second_grad[1]
    )
    ffn_first_grad = over_rows(lambda c: own_half(c["ffn_in"], 1), lambda c: c["f_low"])
    out_first_grad = over_rows(lambda c: c["gated"], lambda c: c["b_low"])
    out_second_grad = adapter_scale * over_rows(
        lambda c: c["out_low"], lambda c: own_half(c["branch"], 1)
    )
    middle = reduced(restored(ffn_first_grad, 0), out_first_grad, restored(out_second_grad, 1))
    in_second_grad = [
        adapter_scale * over_rows(lambda c: c["low"], lambda c: c["proj"][j]) for j in range(3)
    ]
    in_first_grad = over_rows(lambda c: own_half(c["normed"], 1), lambda c: c["n_low"])
    late = reduced(*in_second_grad, restored(in_first_grad, 0))
    return (
        block_output,
        input_grad,
        joined(late[3], 0),
        jnp.stack(late[:3], axis=0).astype(f32),
        middle[1].astype(f32),
        joined(middle[2], 1),
        joined(middle[0], 0),
        jnp.stack(early[2:], axis=0).astype(f32),
        early[0].astype(f32),
        joined(early[1], 1),
    )


def solution(mesh):
    placed = (
        P(("dp", "ctx"), "tensor"),
        P(("dp", "ctx"), "tensor"),
        P("dp", None),
        P("dp"),
        P("dp"),
        P(),
        P(),
        P(None, "tensor"),
        P(None, "dp", "tensor"),
        P("tensor", "dp"),
        P(None, "dp", "tensor"),
        P("tensor", "dp"),
        P(),
        P(None, None, "tensor"),
        P("tensor", None),
        P(),
        P(),
        P(None, None, "tensor"),
        P("tensor", None),
        P(),
    )
    return jax.shard_map(
        body,
        mesh=mesh,
        in_specs=placed,
        out_specs=(
            P(("dp", "ctx"), "tensor"),
            P(("dp", "ctx"), "tensor"),
            P(),
            P(None, None, "tensor"),
            P("tensor", None),
            P(),
            P(),
            P(None, None, "tensor"),
            P("tensor", None),
            P(),
        ),
        check_vma=False,
    )
```

time: 1390 us -> 936 us (0.67)
  waiting for transfers between devices: 944 us -> 365 us
  blocking collectives: 132 us -> 11.7 us
  local copies, waits for them, and re-layouts: 36.4 us -> 154 us
  other arithmetic: 31.6 us -> 86 us
  starting transfers between devices: 13.5 us -> 50.1 us
  matrix products: 208 us -> 240 us
    psum x4 -> x1, waiting for transfers between devices: 541 us -> 89.5 us  [reduced(): return lax.psum(tuple((p.astype(bf16) for p in parts)), ('dp', 'ctx'))]
    all_gather x6 -> x0, waiting for transfers between devices: 377 us -> none  [the longest x1 132 us: fetch_ffn(): lax.all_gather(gateup_weight, 'dp', axis=1, tiled=True)]
    ppermute x2 -> x56, waiting for transfers between devices: 5.49 us -> 276 us  [the longest x19 178 us: swap_tensor(): return lax.ppermute(array, 'tensor', [(0, 1), (1, 0)])]
    unnamed x155 -> x523, local copies, waits for them, and re-layouts: 25.7 us -> 98.3 us
    psum x2 -> x0, blocking collectives: 66.8 us -> none  [the longest x1 41.3 us: body(): lax.psum(product_simple(activated_rows, down_shrink), 'tensor')]
    all_to_all x2 -> x0, blocking collectives: 65 us -> none  [the longest x1 39.8 us: body(): lax.all_to_all(output_blocks, 'dp', split_axis=0, concat_axis=0, tiled=True)]
    ppermute x2 -> x56, starting transfers between devices: 4.68 us -> 50 us  [the longest x19 18.8 us: swap_tensor(): return lax.ppermute(array, 'tensor', [(0, 1), (1, 0)])]
    dot_general x32 -> x66, matrix products: 208 us -> 240 us  [the longest x22 138 us: dot_nt(): lax.dot_general(left, right, (((1,), (1,)), ((), ())), preferred_element_...]
  transfers between devices with their start and end apart: 15 -> 57, of which waited for: 13 -> 20; matrix products, arithmetic and copies ran while one was open for 12% -> 34% of each run, Pallas kernels for 0% -> 0%
where the time goes in v1:
time: 936 us; the launch traced here: 926 us
  waiting for transfers between devices  365 us (39%)
  matrix products  240 us (26%)
  local copies, waits for them, and re-layouts  154 us (16%)
  other arithmetic  86 us (9%)
  starting transfers between devices  50.1 us (5%)
  between operations  18.4 us (2%)
  blocking collectives  11.7 us (1%)
    ppermute x19, waiting for transfers between devices, swap_tensor(): return lax.ppermute(array, 'tensor', [(0, 1), (1, 0)])  178 us
    dot_general x22, matrix products, dot_nt(): lax.dot_general(left, right, (((1,), (1,)), ((), ())), preferred_element_...  138 us
    unnamed x523, local copies, waits for them, and re-layouts  98.3 us
    psum x1, waiting for transfers between devices, reduced(): return lax.psum(tuple((p.astype(bf16) for p in parts)), ('dp', 'ctx'))  89.5 us
    dot_general x22, matrix products, dot(): return jnp.dot(left, right, preferred_element_type=f32)  80.7 us
    ppermute x7, waiting for transfers between devices, fetch(): over_x = lax.ppermute(mine, 'dp', x_route)  54 us
    ppermute x7, waiting for transfers between devices, fetch(): over_z = lax.ppermute(over_x, 'ctx', z_route)  43.6 us
    dot_general x22, matrix products, dot_tn(): lax.dot_general(left, right, (((0,), (0,)), ((), ())), preferred_element_...  22 us
  transfers between devices with their start and end apart: 57, of which 20 were waited for; matrix products, arithmetic and copies ran while one was open for 34% of the time, Pallas kernels for 0%

profile of v1, /device:TPU:0, one launch (start us, length us, event | category | flops | bytes accessed | tf_op | source)
XLA Modules:
  0.0 926.2 jit_solution(1362471824940992608)
XLA Ops:
  14.1 5.9 all-reduce
  21.5 5.8 all-gather.1
  104.2 17.2 %collective-permute-done.3 = bf16[4,6,1024]{2,1,0:T(8,128)(2,1)} collective-permute-done((bf16[4,6,1024]{2,1,0:T(8,128)(2,1)}, bf16[4,6,1024]{2,1,0:T(8,128)(2,1)}, u32[]{:S(2)}, u32[]{:S(2)}) %collective-permute-start.3) | collective-permute-done | bytes 49184 | tf_op jit(solution)/shard_map/ppermute | solution.py:38
  128.6 15.4 %collective-permute-done.44 = bf16[384,1024]{1,0:T(8,128)(2,1)S(1)} collective-permute-done((bf16[384,1024]{1,0:T(8,128)(2,1)}, bf16[384,1024]{1,0:T(8,128)(2,1)S(1)}, u32[]{:S(2)}, u32[]{:S(2)}) %collective-permute-start.44) | collective-permute-done | bytes 786464 | tf_op jit(solution)/shard_map/ppermute | solution.py:38
  145.3 14.0 %collective-permute-done.48 = bf16[384,1024]{1,0:T(8,128)(2,1)S(1)} collective-permute-done((bf16[384,1024]{1,0:T(8,128)(2,1)}, bf16[384,1024]{1,0:T(8,128)(2,1)S(1)}, u32[]{:S(2)}, u32[]{:S(2)}) %collective-permute-start.48) | collective-permute-done | bytes 786464 | tf_op jit(solution)/shard_map/ppermute | solution.py:38
  177.5 5.7 collective-permute-done.5
  197.2 8.1 collective-permute-done.20
  213.6 9.7 %collective-permute-done.21 = bf16[1024,256]{1,0:T(8,128)(2,1)} collective-permute-done((bf16[1024,256]{1,0:T(8,128)(2,1)S(1)}, bf16[1024,256]{1,0:T(8,128)(2,1)}, u32[]{:S(2)}, u32[]{:S(2)}) %collective-permute-start.21) | collective-permute-done | bytes 524320 | tf_op jit(solution)/shard_map/ppermute | solution.py:117
  260.4 6.6 fusion.55
  280.8 11.3 %collective-permute-done.31 = bf16[256,2816]{1,0:T(8,128)(2,1)S(1)} collective-permute-done((bf16[256,2816]{1,0:T(8,128)(2,1)}, bf16[256,2816]{1,0:T(8,128)(2,1)S(1)}, u32[]{:S(2)}, u32[]{:S(2)}) %collective-permute-start.31) | collective-permute-done | bytes 1441824 | tf_op jit(solution)/shard_map/ppermute | solution.py:116
  297.5 24.6 %collective-permute-done.36 = bf16[2816,256]{1,0:T(8,128)(2,1)S(1)} collective-permute-done((bf16[2816,256]{1,0:T(8,128)(2,1)S(1)}, bf16[2816,256]{1,0:T(8,128)(2,1)S(1)}, u32[]{:S(2)}, u32[]{:S(2)}) %collective-permute-start.36) | collective-permute-done | bytes 1441824 | tf_op jit(solution)/shard_map/ppermute | solution.py:116
  343.9 26.6 %collective-permute-done.37 = bf16[2816,256]{1,0:T(8,128)(2,1)S(1)} collective-permute-done((bf16[2816,256]{1,0:T(8,128)(2,1)S(1)}, bf16[2816,256]{1,0:T(8,128)(2,1)S(1)}, u32[]{:S(2)}, u32[]{:S(2)}) %collective-permute-start.37) | collective-permute-done | bytes 1441824 | tf_op jit(solution)/shard_map/ppermute | solution.py:117
  375.6 34.4 %collective-permute-done.42 = bf16[388,2176]{1,0:T(8,128)(2,1)S(1)} collective-permute-done((bf16[388,2176]{1,0:T(8,128)(2,1)S(1)}, bf16[388,2176]{1,0:T(8,128)(2,1)S(1)}, u32[]{:S(2)}, u32[]{:S(2)}) %collective-permute-start.42) | collective-permute-done | bytes 1688608 | tf_op jit(solution)/shard_map/ppermute | solution.py:38
  422.2 7.6 fusion.103
  429.8 10.4 %fusion.104 = f32[388,2816]{1,0:T(8,128)} fusion(bf16[2304,2816]{1,0:T(8,128)(2,1)} %broadcast_dynamic-update-slice_fusion.1, bf16[388,256]{1,0:T(8,128)(2,1)S(1)} %fusion.108, bf16[388,2048]{1,0:T(8,128)(2,1)S(1)} %get-tuple-element.164), kind=kOutput, calls=%fused_computation.212 | convolution fusion | flops 5038313472 | bytes 19134464 | tf_op jit(solution)/shard_map/dot_general | solution.py:17
  440.2 7.6 fusion.105
  447.9 10.7 %fusion.106 = f32[388,2816]{1,0:T(8,128)} fusion(bf16[2304,2816]{1,0:T(8,128)(2,1)} %broadcast_dynamic-update-slice_fusion.1, bf16[388,256]{1,0:T(8,128)(2,1)S(1)} %fusion.107, bf16[388,2048]{1,0:T(8,128)(2,1)S(1)} %get-tuple-element.163), kind=kOutput, calls=%fused_computation.214 | convolution fusion | flops 5038313472 | bytes 19134464 | tf_op jit(solution)/shard_map/dot_general | solution.py:17
  460.9 16.6 %multiply_convert_fusion.1 = (bf16[388,2816]{1,0:T(8,128)(2,1)}, bf16[388,2816]{1,0:T(8,128)(2,1)}, f32[388,2816]{1,0:T(8,128)}) fusion(f32[388,2816]{1,0:T(8,128)} %fusion.104, f32[388,2816]{1,0:T(8,128)} %fusion.103, bf16[388,2176]{1,0:T(8,128)(2,1)S(1)} %copy-done.148, bf16[2816,2176]{1,0:T(8,128)(2,1)} %constant_dynamic-update-slice_fusion.72), kind=kOutput, calls=%fused_computation.7 | convolution fusion | flops 4769233920 | bytes 31425536 | tf_op jit(solution)/shard_map/dot_general | solution.py:21
  492.2 16.7 %multiply_convert_fusion.3 = (bf16[388,2816]{1,0:T(8,128)(2,1)}, bf16[388,2816]{1,0:T(8,128)(2,1)}, f32[388,2816]{1,0:T(8,128)}) fusion(f32[388,2816]{1,0:T(8,128)} %fusion.106, f32[388,2816]{1,0:T(8,128)} %fusion.105, bf16[388,2176]{1,0:T(8,128)(2,1)} %copy-done.146, bf16[2816,2176]{1,0:T(8,128)(2,1)} %constant_dynamic-update-slice_fusion.72), kind=kOutput, calls=%fused_computation.9 | convolution fusion | flops 4769233920 | bytes 31425536 | tf_op jit(solution)/shard_map/dot_general | solution.py:21
  514.2 9.0 convolution_convert_fusion.3
  525.0 10.8 %fusion.239 = f32[388,2304]{1,0:T(8,128)} fusion(bf16[388,2816]{1,0:T(8,128)(2,1)S(1)} %copy-done.53, bf16[2304,2816]{1,0:T(8,128)(2,1)} %copy-done.103), kind=kOutput, calls=%fused_computation.639 | convolution fusion | flops 5034737664 | bytes 18737152 | tf_op jit(solution)/shard_map/dot_general | solution.py:21
  543.2 14.9 %fusion.4 = bf16[388,2304]{1,0:T(8,128)(2,1)} fusion(f32[388,2304]{1,0:T(8,128)} %fusion.239, bf16[388,2816]{1,0:T(8,128)(2,1)} %get-tuple-element.49, bf16[2304,2816]{1,0:T(8,128)(2,1)} %broadcast_dynamic-update-slice_fusion.1), kind=kOutput, calls=%fused_computation.18 | convolution fusion | flops 5036525568 | bytes 20525056 | tf_op jit(solution)/shard_map/dot_general | solution.py:21
  558.4 14.6 %fusion.242 = f32[388,2304]{1,0:T(8,128)} fusion(bf16[388,2816]{1,0:T(8,128)(2,1)} %get-tuple-element.48, bf16[2304,2816]{1,0:T(8,128)(2,1)} %copy-done.103), kind=kOutput, calls=%fused_computation.642 | convolution fusion | flops 5034737664 | bytes 18737152 | tf_op jit(solution)/shard_map/dot_general | solution.py:21
  573.0 15.2 %fusion.5 = bf16[388,2304]{1,0:T(8,128)(2,1)} fusion(f32[388,2304]{1,0:T(8,128)} %fusion.242, bf16[388,2816]{1,0:T(8,128)(2,1)} %get-tuple-element.47, bf16[2304,2816]{1,0:T(8,128)(2,1)} %broadcast_dynamic-update-slice_fusion.1), kind=kOutput, calls=%fused_computation.19 | convolution fusion | flops 5036525568 | bytes 20525056 | tf_op jit(solution)/shard_map/dot_general | solution.py:21
  606.5 49.5 %collective-permute-done.49 = bf16[388,2304]{1,0:T(8,128)(2,1)S(1)} collective-permute-done((bf16[388,2304]{1,0:T(8,128)(2,1)}, bf16[388,2304]{1,0:T(8,128)(2,1)S(1)}, u32[]{:S(2)}, u32[]{:S(2)}) %collective-permute-start.49) | collective-permute-done | bytes 1787936 | tf_op jit(solution)/shard_map/ppermute | solution.py:38
  669.5 6.0 fusion.237
  685.4 6.1 fusion.66
  692.2 6.5 fusion.241
  734.1 28.5 %collective-permute-done.50 = bf16[384,1152]{1,0:T(8,128)(2,1)S(1)} collective-permute-done((bf16[384,1152]{1,0:T(8,128)(2,1)S(1)}, bf16[384,1152]{1,0:T(8,128)(2,1)S(1)}, u32[]{:S(2)}, u32[]{:S(2)}) %collective-permute-start.50) | collective-permute-done | bytes 884768 | tf_op jit(solution)/shard_map/ppermute | solution.py:38
  774.7 10.6 %maximum_maximum_fusion.5 = bf16[768,1024]{1,0:T(8,128)(2,1)} fusion(bf16[384,256]{1,0:T(8,128)(2,1)S(1)} %copy-done.88, bf16[384,256]{1,0:T(8,128)(2,1)S(1)} %copy-done.89, bf16[384,256]{1,0:T(8,128)(2,1)S(1)} %copy-done.90, bf16[384,256]{1,0:T(8,128)(2,1)S(1)} %copy-done.87, bf16[384,256]{1,0:T(8,128)(2,1)S(1)} %copy-done.92, ...), kind=kLoop, calls=%fused_computation.175 | loop fusion | flops 12582912 | bytes 3145728 | tf_op jit(solution)/shard_map/concatenate | solution.py:375
  796.4 89.5 %all-reduce.4.cloned.1.call-done = (bf16[1024,128]{1,0:T(8,128)(2,1)}, bf16[1,128,1024]{2,1,0:T(8,128)(2,1)}, bf16[1,128,1024]{2,1,0:T(8,128)(2,1)}, bf16[1,128,...) async-done(((bf16[1024,128]{1,0:T(8,128)(2,1)}, ...) | async-done | bytes 4522000 | tf_op jit(solution)/shard_map/psum | solution.py:382
  902.1 14.3 %collective-permute-done.55 = bf16[128,1024]{1,0:T(8,128)(2,1)S(1)} collective-permute-done((bf16[128,1024]{1,0:T(8,128)(2,1)}, bf16[128,1024]{1,0:T(8,128)(2,1)S(1)}, u32[]{:S(2)}, u32[]{:S(2)}) %collective-permute-start.55) | collective-permute-done | bytes 262176 | tf_op jit(solution)/shard_map/ppermute | solution.py:38
  (877 shorter events, 377.4 us)
Async XLA Ops:
  7.2 878.7 %all-reduce.4.cloned.1.call-start = ((), (), s32[]{:S(2)}) async-start(), calls=%async_computation | async-start | bytes 9043968 | tf_op jit(solution)/shard_map/psum | solution.py:382
  12.2 156.2 %collective-permute-start.14 = (bf16[512,1024]{1,0:T(8,128)(2,1)}, bf16[512,1024]{1,0:T(8,128)(2,1)}, u32[]{:S(2)}, u32[]{:S(2)}) collective-permute-start(bf16[512,1024]{1,0:T(8,128)(2,1)} %get-tuple-element.62), channel_id=1, source_target_pairs={{0,8},{8,0},{16,24},{24,16},{1,9},{9,1},{17,25},{25,17},{2,10},{10... | collective-permute-start | bytes 3145736 | tf_op jit(solution)/shard_map/ppermute | solution.py:120
  28.2 71.6 %collective-permute-start.1 = (bf16[4,2,1024]{2,1,0:T(2,128)(2,1)}, bf16[4,2,1024]{2,1,0:T(2,128)(2,1)S(1)}, u32[]{:S(2)}, u32[]{:S(2)}) collective-permute-start(bf16[4,2,1024]{2,1,0:T(2,128)(2,1)} %get-tuple-element.17), channel_id=1, source_target_pairs={{0,2},{2,4},{4,6},{1,3},{3,5},{5,7},{8,10},{10,12},{12,14},{9,11},... | collective-permute-start | bytes 49160 | tf_op jit(solution)/shard_map/ppermute | solution.py:161
  32.7 68.9 %collective-permute-start = (bf16[4,4,1024]{2,1,0:T(4,128)(2,1)}, bf16[4,4,1024]{2,1,0:T(4,128)(2,1)S(1)}, u32[]{:S(2)}, u32[]{:S(2)}) collective-permute-start(bf16[4,4,1024]{2,1,0:T(4,128)(2,1)} %get-tuple-element.15), channel_id=1, source_target_pairs={{2,0},{4,2},{6,4},{3,1},{5,3},{7,5},{10,8},{12,10},{14,12},{11,9},... | collective-permute-start | bytes 98312 | tf_op jit(solution)/shard_map/ppermute | solution.py:160
  35.3 88.0 %collective-permute-start.2 = (bf16[384,1024]{1,0:T(8,128)(2,1)}, bf16[384,1024]{1,0:T(8,128)(2,1)}, u32[]{:S(2)}, u32[]{:S(2)}) collective-permute-start(bf16[384,1024]{1,0:T(8,128)(2,1)} %get-tuple-element.96), channel_id=1, source_target_pairs={{0,1},{1,0},{2,3},{3,2},{4,5},{5,4},{6,7},{7,6},{8,9},{9,8},{10,11... | collective-permute-start | bytes 2359304 | tf_op jit(solution)/shard_map/ppermute | solution.py:38
  36.9 146.3 %collective-permute-start.19 = (bf16[1024,512]{1,0:T(8,128)(2,1)}, bf16[1024,512]{1,0:T(8,128)(2,1)}, u32[]{:S(2)}, u32[]{:S(2)}) collective-permute-start(bf16[1024,512]{1,0:T(8,128)(2,1)} %param.29), channel_id=1, source_target_pairs={{0,8},{8,0},{16,24},{24,16},{1,9},{9,1},{17,25},{25,17},{2,10},{10... | collective-permute-start | bytes 3145736 | tf_op jit(solution)/shard_map/ppermute | solution.py:120
  121.4 52.3 %collective-permute-start.15 = (bf16[256,1024]{1,0:T(8,128)(2,1)}, bf16[256,1024]{1,0:T(8,128)(2,1)}, u32[]{:S(2)}, u32[]{:S(2)}) collective-permute-start(bf16[256,1024]{1,0:T(8,128)(2,1)} %dynamic-slice_bitcast_fusion.2), channel_id=1, source_target_pairs={{0,16},{16,0},{8,24},{24,8},{1,17},{17,1},{9,25},{25,9},{2,18},{18... | collective-permute-start | bytes 1572872 | tf_op jit(solution)/shard_map/ppermute | solution.py:116
  125.4 33.9 %collective-permute-start.48 = (bf16[384,1024]{1,0:T(8,128)(2,1)}, bf16[384,1024]{1,0:T(8,128)(2,1)S(1)}, u32[]{:S(2)}, u32[]{:S(2)}) collective-permute-start(bf16[384,1024]{1,0:T(8,128)(2,1)} %get-tuple-element.94), channel_id=1, source_target_pairs={{0,1},{1,0},{2,3},{3,2},{4,5},{5,4},{6,7},{7,6},{8,9},{9,8},{10,11... | collective-permute-start | bytes 2359304 | tf_op jit(solution)/shard_map/ppermute | solution.py:38
  173.7 31.6 %collective-permute-start.20 = (bf16[1024,256]{1,0:T(8,128)(2,1)S(1)}, bf16[1024,256]{1,0:T(8,128)(2,1)S(1)}, u32[]{:S(2)}, u32[]{:S(2)}) collective-permute-start(bf16[1024,256]{1,0:T(8,128)(2,1)S(1)} %copy-done.106), channel_id=1, source_target_pairs={{0,16},{16,0},{8,24},{24,8},{1,17},{17,1},{9,25},{25,9},{2,18},{18... | collective-permute-start | bytes 1572872 | tf_op jit(solution)/shard_map/ppermute | solution.py:116
  223.2 98.9 %collective-permute-start.35 = (bf16[2816,512]{1,0:T(8,128)(2,1)}, bf16[2816,512]{1,0:T(8,128)(2,1)}, u32[]{:S(2)}, u32[]{:S(2)}) collective-permute-start(bf16[2816,512]{1,0:T(8,128)(2,1)} %param.31), channel_id=1, source_target_pairs={{0,8},{8,0},{16,24},{24,16},{1,9},{9,1},{17,25},{25,17},{2,10},{10... | collective-permute-start | bytes 8650760 | tf_op jit(solution)/shard_map/ppermute | solution.py:120
  225.2 50.2 %collective-permute-start.25 = (bf16[512,2816]{1,0:T(8,128)(2,1)}, bf16[512,2816]{1,0:T(8,128)(2,1)}, u32[]{:S(2)}, u32[]{:S(2)}) collective-permute-start(bf16[512,2816]{1,0:T(8,128)(2,1)} %get-tuple-element.52), channel_id=1, source_target_pairs={{0,8},{8,0},{16,24},{24,16},{1,9},{9,1},{17,25},{25,17},{2,10},{10... | collective-permute-start | bytes 8650760 | tf_op jit(solution)/shard_map/ppermute | solution.py:120
  226.6 43.7 %collective-permute-start.26 = (bf16[256,2816]{1,0:T(8,128)(2,1)}, bf16[256,2816]{1,0:T(8,128)(2,1)}, u32[]{:S(2)}, u32[]{:S(2)}) collective-permute-start(bf16[256,2816]{1,0:T(8,128)(2,1)} %dynamic-slice_bitcast_fusion.1), channel_id=1, source_target_pairs={{0,16},{16,0},{8,24},{24,8},{1,17},{17,1},{9,25},{25,9},{2,18},{18... | collective-permute-start | bytes 4325384 | tf_op jit(solution)/shard_map/ppermute | solution.py:116
  227.5 64.7 %collective-permute-start.30 = (bf16[512,2816]{1,0:T(8,128)(2,1)}, bf16[512,2816]{1,0:T(8,128)(2,1)}, u32[]{:S(2)}, u32[]{:S(2)}) collective-permute-start(bf16[512,2816]{1,0:T(8,128)(2,1)} %get-tuple-element.53), channel_id=1, source_target_pairs={{0,8},{8,0},{16,24},{24,16},{1,9},{9,1},{17,25},{25,17},{2,10},{10... | collective-permute-start | bytes 8650760 | tf_op jit(solution)/shard_map/ppermute | solution.py:120
  255.3 36.8 %collective-permute-start.31 = (bf16[256,2816]{1,0:T(8,128)(2,1)}, bf16[256,2816]{1,0:T(8,128)(2,1)S(1)}, u32[]{:S(2)}, u32[]{:S(2)}) collective-permute-start(bf16[256,2816]{1,0:T(8,128)(2,1)} %dynamic-slice_bitcast_fusion), channel_id=1, source_target_pairs={{0,16},{16,0},{8,24},{24,8},{1,17},{17,1},{9,25},{25,9},{2,18},{18... | collective-permute-start | bytes 4325384 | tf_op jit(solution)/shard_map/ppermute | solution.py:116
  270.3 51.8 %collective-permute-start.36 = (bf16[2816,256]{1,0:T(8,128)(2,1)S(1)}, bf16[2816,256]{1,0:T(8,128)(2,1)S(1)}, u32[]{:S(2)}, u32[]{:S(2)}) collective-permute-start(bf16[2816,256]{1,0:T(8,128)(2,1)S(1)} %copy-done.75), channel_id=1, source_target_pairs={{0,16},{16,0},{8,24},{24,8},{1,17},{17,1},{9,25},{25,9},{2,18},{18... | collective-permute-start | bytes 4325384 | tf_op jit(solution)/shard_map/ppermute | solution.py:116
  275.4 57.1 %collective-permute-start.27 = (bf16[256,2816]{1,0:T(8,128)(2,1)}, bf16[256,2816]{1,0:T(8,128)(2,1)S(1)}, u32[]{:S(2)}, u32[]{:S(2)}) collective-permute-start(bf16[256,2816]{1,0:T(8,128)(2,1)} %collective-permute-done.26), channel_id=1, source_target_pairs={{0,2},{2,0},{4,6},{6,4},{1,3},{3,1},{5,7},{7,5},{8,10},{10,8},{12,... | collective-permute-start | bytes 4325384 | tf_op jit(solution)/shard_map/ppermute | solution.py:117
  292.2 41.9 %collective-permute-start.28 = (bf16[256,2816]{1,0:T(8,128)(2,1)}, bf16[256,2816]{1,0:T(8,128)(2,1)S(1)}, u32[]{:S(2)}, u32[]{:S(2)}) collective-permute-start(bf16[256,2816]{1,0:T(8,128)(2,1)} %collective-permute-done.26), channel_id=1, source_target_pairs={{0,8},{8,0},{16,24},{24,16},{1,9},{9,1},{17,25},{25,17},{2,10},{10... | collective-permute-start | bytes 4325384 | tf_op jit(solution)/shard_map/ppermute | solution.py:123
  292.2 48.9 %collective-permute-start.32 = (bf16[256,2816]{1,0:T(8,128)(2,1)S(1)}, bf16[256,2816]{1,0:T(8,128)(2,1)S(1)}, u32[]{:S(2)}, u32[]{:S(2)}) collective-permute-start(bf16[256,2816]{1,0:T(8,128)(2,1)S(1)} %collective-permute-done.31), channel_id=1, source_target_pairs={{0,2},{2,0},{4,6},{6,4},{1,3},{3,1},{5,7},{7,5},{8,10},{10,8},{12,... | collective-permute-start | bytes 4325384 | tf_op jit(solution)/shard_map/ppermute | solution.py:117
  322.1 48.3 %collective-permute-start.37 = (bf16[2816,256]{1,0:T(8,128)(2,1)S(1)}, bf16[2816,256]{1,0:T(8,128)(2,1)S(1)}, u32[]{:S(2)}, u32[]{:S(2)}) collective-permute-start(bf16[2816,256]{1,0:T(8,128)(2,1)S(1)} %collective-permute-done.36), channel_id=1, source_target_pairs={{0,2},{2,0},{4,6},{6,4},{1,3},{3,1},{5,7},{7,5},{8,10},{10,8},{12,... | collective-permute-start | bytes 4325384 | tf_op jit(solution)/shard_map/ppermute | solution.py:117
  332.6 39.2 %collective-permute-start.38 = (bf16[2816,256]{1,0:T(8,128)(2,1)S(1)}, bf16[2816,256]{1,0:T(8,128)(2,1)S(1)}, u32[]{:S(2)}, u32[]{:S(2)}) collective-permute-start(bf16[2816,256]{1,0:T(8,128)(2,1)S(1)} %collective-permute-done.36), channel_id=1, source_target_pairs={{0,8},{8,0},{16,24},{24,16},{1,9},{9,1},{17,25},{25,17},{2,10},{10... | collective-permute-start | bytes 4325384 | tf_op jit(solution)/shard_map/ppermute | solution.py:123
  334.1 40.1 %collective-permute-start.24 = (bf16[388,2176]{1,0:T(8,128)(2,1)S(1)}, bf16[388,2176]{1,0:T(8,128)(2,1)S(1)}, u32[]{:S(2)}, u32[]{:S(2)}) collective-permute-start(bf16[388,2176]{1,0:T(8,128)(2,1)S(1)} %convolution_convert_fusion.1), channel_id=1, source_target_pairs={{0,1},{1,0},{2,3},{3,2},{4,5},{5,4},{6,7},{7,6},{8,9},{9,8},{10,11... | collective-permute-start | bytes 5065736 | tf_op jit(solution)/shard_map/ppermute | solution.py:38
  341.1 69.0 %collective-permute-start.42 = (bf16[388,2176]{1,0:T(8,128)(2,1)S(1)}, bf16[388,2176]{1,0:T(8,128)(2,1)S(1)}, u32[]{:S(2)}, u32[]{:S(2)}) collective-permute-start(bf16[388,2176]{1,0:T(8,128)(2,1)S(1)} %convolution_convert_fusion), channel_id=1, source_target_pairs={{0,1},{1,0},{2,3},{3,2},{4,5},{5,4},{6,7},{7,6},{8,9},{9,8},{10,11... | collective-permute-start | bytes 5065736 | tf_op jit(solution)/shard_map/ppermute | solution.py:38
  342.6 75.7 %collective-permute-start.29 = (bf16[256,2816]{1,0:T(8,128)(2,1)S(1)}, bf16[256,2816]{1,0:T(8,128)(2,1)S(1)}, u32[]{:S(2)}, u32[]{:S(2)}) collective-permute-start(bf16[256,2816]{1,0:T(8,128)(2,1)S(1)} %collective-permute-done.27), channel_id=1, source_target_pairs={{0,8},{8,0},{16,24},{24,16},{1,9},{9,1},{17,25},{25,17},{2,10},{10... | collective-permute-start | bytes 4325384 | tf_op jit(solution)/shard_map/ppermute | solution.py:124
  370.4 46.4 %collective-permute-start.34 = (bf16[256,2816]{1,0:T(8,128)(2,1)S(1)}, bf16[256,2816]{1,0:T(8,128)(2,1)S(1)}, u32[]{:S(2)}, u32[]{:S(2)}) collective-permute-start(bf16[256,2816]{1,0:T(8,128)(2,1)S(1)} %collective-permute-done.32), channel_id=1, source_target_pairs={{0,8},{8,0},{16,24},{24,16},{1,9},{9,1},{17,25},{25,17},{2,10},{10... | collective-permute-start | bytes 4325384 | tf_op jit(solution)/shard_map/ppermute | solution.py:124
  371.7 86.9 %collective-permute-start.39 = (bf16[2816,256]{1,0:T(8,128)(2,1)S(1)}, bf16[2816,256]{1,0:T(8,128)(2,1)S(1)}, u32[]{:S(2)}, u32[]{:S(2)}) collective-permute-start(bf16[2816,256]{1,0:T(8,128)(2,1)S(1)} %collective-permute-done.37), channel_id=1, source_target_pairs={{0,8},{8,0},{16,24},{24,16},{1,9},{9,1},{17,25},{25,17},{2,10},{10... | collective-permute-start | bytes 4325384 | tf_op jit(solution)/shard_map/ppermute | solution.py:124
  538.5 58.9 %collective-permute-start.43 = (bf16[384,1152]{1,0:T(8,128)(2,1)}, bf16[384,1152]{1,0:T(8,128)(2,1)}, u32[]{:S(2)}, u32[]{:S(2)}) collective-permute-start(bf16[384,1152]{1,0:T(8,128)(2,1)} %pad_maximum_fusion.8), channel_id=1, source_target_pairs={{0,1},{1,0},{2,3},{3,2},{4,5},{5,4},{6,7},{7,6},{8,9},{9,8},{10,11... | collective-permute-start | bytes 2654216 | tf_op jit(solution)/shard_map/ppermute | solution.py:38
  539.7 59.6 %collective-permute-start.40 = (bf16[384,1152]{1,0:T(8,128)(2,1)}, bf16[384,1152]{1,0:T(8,128)(2,1)}, u32[]{:S(2)}, u32[]{:S(2)}) collective-permute-start(bf16[384,1152]{1,0:T(8,128)(2,1)} %pad_maximum_fusion.6), channel_id=1, source_target_pairs={{0,1},{1,0},{2,3},{3,2},{4,5},{5,4},{6,7},{7,6},{8,9},{9,8},{10,11... | collective-permute-start | bytes 2654216 | tf_op jit(solution)/shard_map/ppermute | solution.py:38
  558.1 99.2 %collective-permute-start.45 = (bf16[388,2304]{1,0:T(8,128)(2,1)}, bf16[388,2304]{1,0:T(8,128)(2,1)}, u32[]{:S(2)}, u32[]{:S(2)}) collective-permute-start(bf16[388,2304]{1,0:T(8,128)(2,1)} %fusion.4), channel_id=1, source_target_pairs={{0,1},{1,0},{2,3},{3,2},{4,5},{5,4},{6,7},{7,6},{8,9},{9,8},{10,11... | collective-permute-start | bytes 5363720 | tf_op jit(solution)/shard_map/ppermute | solution.py:38
  588.2 67.8 %collective-permute-start.49 = (bf16[388,2304]{1,0:T(8,128)(2,1)}, bf16[388,2304]{1,0:T(8,128)(2,1)S(1)}, u32[]{:S(2)}, u32[]{:S(2)}) collective-permute-start(bf16[388,2304]{1,0:T(8,128)(2,1)} %fusion.5), channel_id=1, source_target_pairs={{0,1},{1,0},{2,3},{3,2},{4,5},{5,4},{6,7},{7,6},{8,9},{9,8},{10,11... | collective-permute-start | bytes 5363720 | tf_op jit(solution)/shard_map/ppermute | solution.py:38
  723.5 40.8 %collective-permute-start.46 = (bf16[384,1152]{1,0:T(8,128)(2,1)S(1)}, bf16[384,1152]{1,0:T(8,128)(2,1)S(1)}, u32[]{:S(2)}, u32[]{:S(2)}) collective-permute-start(bf16[384,1152]{1,0:T(8,128)(2,1)S(1)} %pad_maximum_fusion.10), channel_id=1, source_target_pairs={{0,1},{1,0},{2,3},{3,2},{4,5},{5,4},{6,7},{7,6},{8,9},{9,8},{10,11... | collective-permute-start | bytes 2654216 | tf_op jit(solution)/shard_map/ppermute | solution.py:38
  724.0 38.6 %collective-permute-start.50 = (bf16[384,1152]{1,0:T(8,128)(2,1)S(1)}, bf16[384,1152]{1,0:T(8,128)(2,1)S(1)}, u32[]{:S(2)}, u32[]{:S(2)}) collective-permute-start(bf16[384,1152]{1,0:T(8,128)(2,1)S(1)} %pad_maximum_fusion.12), channel_id=1, source_target_pairs={{0,1},{1,0},{2,3},{3,2},{4,5},{5,4},{6,7},{7,6},{8,9},{9,8},{10,11... | collective-permute-start | bytes 2654216 | tf_op jit(solution)/shard_map/ppermute | solution.py:38
  889.7 27.8 %collective-permute-start.54 = (bf16[1024,256]{1,0:T(8,128)(2,1)}, bf16[1024,256]{1,0:T(8,128)(2,1)S(1)}, u32[]{:S(2)}, u32[]{:S(2)}) collective-permute-start(bf16[1024,256]{1,0:T(8,128)(2,1)} %get-tuple-element.38), channel_id=1, source_target_pairs={{0,1},{1,0},{2,3},{3,2},{4,5},{5,4},{6,7},{7,6},{8,9},{9,8},{10,11... | collective-permute-start | bytes 1572872 | tf_op jit(solution)/shard_map/ppermute | solution.py:38
  (225 other events, 4168.6 us)
Sparse Core Ops, SparseCore 0:
  767.7 118.1 all-reduce.3

commit v2 on v1

v2 whole, which is shorter than its diff:
```python
import functools

import jax
import jax.numpy as jnp
from jax import lax
from jax.experimental import pallas as pl
from jax.experimental.pallas import tpu as pltpu
from jax.sharding import PartitionSpec as P

RANK = 16
CHUNKS = 2
TILE = 256
VMEM_BYTES = 56 * 1024 * 1024

norm_eps = 1e-05
adapter_scale = 0.5

f32 = jnp.float32
bf16 = jnp.bfloat16


def dot(left, right):
    return jnp.dot(left, right, preferred_element_type=f32)


def dot_nt(left, right):
    return lax.dot_general(left, right, (((1,), (1,)), ((), ())), preferred_element_type=f32)


def dot_tn(left, right):
    return lax.dot_general(left, right, (((0,), (0,)), ((), ())), preferred_element_type=f32)


def over_row_blocks(rows, step, visit):
    def one(i, carry):
        visit(pl.ds(pl.multiple_of(i * step, step), step))
        return carry

    lax.fori_loop(0, rows // step, one, 0)


def lanes_at(index, width):
    return pl.ds(pl.multiple_of(index * width, width), width)


def call(kernel, grid, scalars, ins, outs, scratch=(), flops=0):
    in_specs = []
    for array, block, index in ins:
        if block is None:
            zeros = (0,) * array.ndim
            in_specs.append(
                pl.BlockSpec(array.shape, lambda *_, z=zeros: z, pipeline_mode=pl.Buffered(1))
            )
        else:
            in_specs.append(pl.BlockSpec(block, index))
    out_specs, out_shape = [], []
    for shape, dtype, block, index in outs:
        zeros = (0,) * len(shape)
        out_specs.append(
            pl.BlockSpec(shape, lambda *_, z=zeros: z) if block is None else pl.BlockSpec(block, index)
        )
        out_shape.append(jax.ShapeDtypeStruct(shape, dtype))
    moved = sum(a.size * a.dtype.itemsize for a, _, _ in ins)
    return pl.pallas_call(
        kernel,
        grid_spec=pltpu.PrefetchScalarGridSpec(
            num_scalar_prefetch=len(scalars),
            grid=grid,
            in_specs=in_specs,
            out_specs=out_specs,
            scratch_shapes=list(scratch),
        ),
        out_shape=out_shape,
        compiler_params=pltpu.CompilerParams(
            dimension_semantics=("arbitrary",) * len(grid), vmem_limit_bytes=VMEM_BYTES
        ),
        cost_estimate=pl.CostEstimate(flops=flops, transcendentals=0, bytes_accessed=moved),
    )(*scalars, *[a for a, _, _ in ins])


def tables_kernel(dims, table, info, mask_ref, one_ref, two_ref):
    groups, seqs, sub, nb, rows, tok_count, group_tokens = dims
    chunk = pl.program_id(0)
    me, ctx = info[0], info[1]
    span = nb * sub
    row = lax.broadcasted_iota(jnp.int32, (rows, 128), 0)
    col = lax.broadcasted_iota(jnp.int32, (rows, 128), 1)
    far = jnp.full((rows, 128), -9, jnp.int32)
    pos, first_src, second_src = far, far, far
    ends = [far] * (seqs - 1)
    names = [far] * seqs
    for b in range(nb):
        group = chunk * nb + b
        slot = jnp.int32(0)
        for s in range(groups):
            slot = slot + jnp.where(table[group, s] == me, s, 0)
        base = ctx * tok_count + slot * sub
        low, top = b * sub, (b + 1) * sub
        edge = span + 4 * b
        inner = (row >= low) & (row < top)
        before = (row >= edge) & (row < edge + 2)
        after = (row >= edge + 2) & (row < edge + 4)
        here = inner | before | after
        pos = jnp.where(inner, base + row - low, pos)
        pos = jnp.where(before, base - 2 + row - edge, pos)
        pos = jnp.where(after, base + sub + row - (edge + 2), pos)
        first_src = jnp.where(inner, jnp.where(row == low, edge + 1, row - 1), first_src)
        first_src = jnp.where(after, jnp.where(row == edge + 2, top - 1, row - 1), first_src)
        second_src = jnp.where(inner, jnp.where(row < low + 2, edge + row - low, row - 2), second_src)
        second_src = jnp.where(after, top - 2 + row - (edge + 2), second_src)
        end = jnp.int32(0)
        for j in range(seqs - 1):
            end = end + table[group, groups + j]
            ends[j] = jnp.where(here, end, ends[j])
        for j in range(seqs):
            names[j] = jnp.where(here, table[group, groups + seqs + j], names[j])

    def segment_of(positions):
        found = jnp.zeros((rows, 128), jnp.int32)
        for end in ends:
            found = found + jnp.where(positions >= end, 1, 0)
        return found

    segment = segment_of(pos)
    adapter = names[0]
    for j in range(1, seqs):
        adapter = jnp.where(segment == j, names[j], adapter)
    picked = (col >= adapter * RANK) & (col < adapter * RANK + RANK)
    mask_ref[...] = jnp.where(picked, 1.0, 0.0).astype(bf16)
    source = lax.broadcasted_iota(jnp.int32, (rows, rows), 1)
    for lag, src, ref in ((1, first_src, one_ref), (2, second_src, two_ref)):
        same = (pos >= lag) & (pos < group_tokens) & (segment_of(pos - lag) == segment)
        src = jnp.where(same, src, -9)
        ref[...] = jnp.where(source == src[:, :1], 1.0, 0.0).astype(bf16)


def edges_kernel(dims, table, info, edges_ref, first_ref, last_ref, next_ref, prev_ref):
    groups = dims
    me = info[0]
    for g in range(groups):
        slot = jnp.int32(0)
        for s in range(groups):
            slot = slot + jnp.where(table[g, s] == me, s, 0)
        first_ref[g] = edges_ref[table[g, 0], g, 0:4]
        last_ref[g] = edges_ref[table[g, groups - 1], g, 4:6]
        after = table[g, jnp.minimum(slot + 1, groups - 1)]
        before = table[g, jnp.maximum(slot - 1, 0)]
        rows = edges_ref[after, g, 0:4]
        next_ref[g] = jnp.where(slot < groups - 1, rows, jnp.zeros_like(rows))
        rows = edges_ref[before, g, 4:6]
        prev_ref[g] = jnp.where(slot > 0, rows, jnp.zeros_like(rows))


ACTUAL, STACK, INNER = 4, 12, 20


def stack_rows(info, own, got, halo_own, halo_got, stack, span, half, into):
    block = half // 4
    stack[:span, :half] = own[...]
    stack[:span, half:] = got[...]
    stack[span:, :half] = halo_own[...]
    stack[span:, half:] = halo_got[...]
    for r in range(8):
        into[:, r * block : (r + 1) * block] = stack[:, lanes_at(info[STACK + r], block)]


def input_kernel(info, own, got, halo_own, halo_got, gain, first, mask, x_ref, lhs_ref, scale_ref, stack, first_rel, gain_rel):
    span, half = own.shape
    rows, width = x_ref.shape
    block = half // 4
    stack_rows(info, own, got, halo_own, halo_got, stack, span, half, x_ref)
    for r in range(8):
        first_rel[r * block : (r + 1) * block, :] = first[lanes_at(info[ACTUAL + r], block), :]
        gain_rel[:, r * block : (r + 1) * block] = gain[:, lanes_at(info[ACTUAL + r], block)]

    def visit(at):
        x = x_ref[at, :].astype(f32)
        scale = lax.rsqrt(jnp.mean(x * x, axis=-1, keepdims=True) + norm_eps)
        lhs_ref[at, :width] = (x * scale * gain_rel[0:1, :]).astype(bf16)
        scale_ref[at, :] = jnp.broadcast_to(scale, (scale.shape[0], 128))

    over_row_blocks(rows, 16, visit)
    lhs_ref[:, width:] = dot(lhs_ref[:, :width], first_rel[...]).astype(bf16) * mask[...]


def cotangent_kernel(info, own, got, halo_own, halo_got, second, mask, lhs_ref, stack, second_rel):
    span, half = own.shape
    width = 2 * half
    block = half // 4
    stack_rows(info, own, got, halo_own, halo_got, stack, span, half, lhs_ref)
    for r in range(8):
        second_rel[:, r * block : (r + 1) * block] = second[:, lanes_at(info[ACTUAL + r], block)]
    low = adapter_scale * dot_nt(lhs_ref[:, :width], second_rel[...])
    lhs_ref[:, width:] = low.astype(bf16) * mask[...]


def mixer_kernel(cuts, lhs, one, two, taps, in_expand, out_shrink, *refs):
    count = len(cuts)
    in_parts, out_parts = refs[:count], refs[count : 2 * count]
    b_ref, c_ref, v_ref, conv_ref, gated_ref, part_ref, acc = refs[2 * count :]
    width = cuts[-1][1]
    step = pl.program_id(0)

    def project(j):
        total = dot(lhs[:, width:], in_expand[j] * jnp.asarray(adapter_scale, bf16))
        for (low, top), part in zip(cuts, in_parts):
            total = total + dot(lhs[:, low:top], part[j])
        return total

    b, c, v = project(0), project(1), project(2)
    b_ref[...] = b
    c_ref[...] = c
    v_ref[...] = v
    mixed = (b * v).astype(bf16)
    w = taps[...].astype(f32)
    conv = w[0:1] * mixed.astype(f32) + w[1:2] * dot(one[...], mixed) + w[2:3] * dot(two[...], mixed)
    conv_ref[...] = conv
    gated = (c * conv).astype(bf16)
    gated_ref[...] = gated

    @pl.when(step == 0)
    def _():
        acc[...] = jnp.zeros_like(acc)

    for (low, top), part in zip(cuts, out_parts):
        acc[:, low:top] += dot(gated, part[...])
    acc[:, width:] += dot(gated, out_shrink[...])

    @pl.when(step == pl.num_programs(0) - 1)
    def _():
        part_ref[...] = acc[...].astype(bf16)


def feed_kernel(cuts, span, info, x, part, got, glhs, mask, gain, out_second, ffn_first, ffn_expand, down_shrink, *refs):
    count = len(cuts)
    gu_parts, down_parts = refs[:count], refs[count : 2 * count]
    (f_ref, own_ref, send_ref, hidden_ref, lhs, low_ref, grads,
     acc_d, acc_f, first_rel, second_rel, gain_rel) = refs[2 * count :]
    width = cuts[-1][1]
    half = width // 2
    block = width // 8
    rank = mask.shape[1]
    step = pl.program_id(0)

    @pl.when(step == 0)
    def _():
        for r in range(8):
            at = lanes_at(info[ACTUAL + r], block)
            here = slice(r * block, (r + 1) * block)
            first_rel[here, :] = ffn_first[at, :]
            second_rel[:, here] = out_second[:, at]
            gain_rel[:, here] = gain[:, at]
        low = (part[:, width:].astype(f32) + got[:, width:].astype(f32)).astype(bf16) * mask[...]
        low_ref[...] = low
        acc_d[:, :width] = dot(low, second_rel[...])

        def visit(at):
            both = part[at, :width].astype(f32) + got[at, :width].astype(f32)
            hidden = x[at, :].astype(f32) + (both + adapter_scale * acc_d[at, :width])
            hidden_ref[at, :] = hidden
            scale = lax.rsqrt(jnp.mean(hidden * hidden, axis=-1, keepdims=True) + norm_eps)
            lhs[at, :width] = (hidden * scale * gain_rel[0:1, :]).astype(bf16)

        over_row_blocks(x.shape[0], 16, visit)
        low = dot(lhs[:, :width], first_rel[...]).astype(bf16)
        lhs[:, width : width + rank] = low[:, :rank] * mask[...]
        lhs[:, width + rank :] = low[:, rank:] * mask[...]
        acc_d[...] = jnp.zeros_like(acc_d)
        acc_f[...] = jnp.zeros_like(acc_f)

    lows = [lhs[:, width : width + rank], lhs[:, width + rank :]]
    half_scale = jnp.asarray(adapter_scale, bf16)

    def project(j):
        total = dot(lows[j], ffn_expand[j] * half_scale)
        for (low, top), w in zip(cuts, gu_parts):
            total = total + dot(lhs[:, low:top], w[j])
        return total

    gate, up = project(0), project(1)
    sig = jax.nn.sigmoid(gate)
    silu = gate * sig
    act = (silu * up).astype(bf16)
    g_low = glhs[:, width:]
    grad_act = dot_nt(g_low, down_shrink[...])
    for (low, top), w in zip(cuts, down_parts):
        grad_act = grad_act + dot_nt(glhs[:, low:top], w[...])
    gg = (grad_act * up * (sig * (1.0 + gate * (1.0 - sig)))).astype(bf16)
    gu = (grad_act * silu).astype(bf16)
    for (low, top), w in zip(cuts, down_parts):
        acc_d[:span, low:top] += dot(act[:span], w[...])
    acc_d[:span, width:] += dot(act[:span], down_shrink[...])
    for (low, top), w in zip(cuts, gu_parts):
        acc_f[:, low:top] += dot_nt(gg, w[0]) + dot_nt(gu, w[1])
    acc_f[:, width : width + rank] += dot_nt(gg, ffn_expand[0] * half_scale)
    acc_f[:, width + rank :] += dot_nt(gu, ffn_expand[1] * half_scale)
    grads[0] = dot_tn(g_low[:span], act[:span])
    grads[1] = adapter_scale * dot_tn(lows[0][:span], gg[:span])
    grads[2] = adapter_scale * dot_tn(lows[1][:span], gu[:span])

    @pl.when(step == pl.num_programs(0) - 1)
    def _():
        f_ref[...] = acc_f[...].astype(bf16)
        place = info[3]
        own_ref[:, :half] = acc_d[:span, lanes_at(place, half)].astype(bf16)
        send_ref[:, :half] = acc_d[:span, lanes_at(1 - place, half)].astype(bf16)
        own_ref[:, half:] = acc_d[:span, width:].astype(bf16)
        send_ref[:, half:] = acc_d[:span, width:].astype(bf16)


def back_kernel(cuts, span, info, part, got, hidden, glhs, lhs_two, out_low, lhs_one, mask, gain, out_second, ffn_first,
                one, two, taps, in_expand, out_shrink, b_ref, c_ref, v_ref, conv_ref, gated_ref, *refs):
    count = len(cuts)
    in_parts, out_parts = refs[:count], refs[count : 2 * count]
    (own_ref, send_ref, gh_ref, ffn_grad, second_grad, grads,
     acc, branch, first_rel, second_rel, gain_rel) = refs[2 * count :]
    width = cuts[-1][1]
    half = width // 2
    block = width // 8
    rank = mask.shape[1]
    step = pl.program_id(0)
    place = info[3]

    @pl.when(step == 0)
    def _():
        for r in range(8):
            at = lanes_at(info[ACTUAL + r], block)
            here = slice(r * block, (r + 1) * block)
            first_rel[here, :] = ffn_first[at, :]
            second_rel[:, here] = out_second[:, at]
            gain_rel[:, here] = gain[:, at]
        low = (part[:, width:].astype(f32) + got[:, width:].astype(f32)).astype(bf16)
        low = jnp.concatenate([low[:, :rank] * mask[...], low[:, rank:] * mask[...]], axis=1)
        acc[:, :width] = dot_nt(low, first_rel[...])

        def visit(at):
            both = part[at, :width].astype(f32) + got[at, :width].astype(f32)
            h = hidden[at, :]
            scale = lax.rsqrt(jnp.mean(h * h, axis=-1, keepdims=True) + norm_eps)
            unit = h * scale
            grad_unit = (both + acc[at, :width]) * gain_rel[0:1, :]
            grad = glhs[at, :width].astype(f32) + scale * (
                grad_unit - unit * jnp.mean(grad_unit * unit, axis=-1, keepdims=True)
            )
            gh_ref[at, :] = grad
            branch[at, :width] = grad.astype(bf16)

        over_row_blocks(hidden.shape[0], 16, visit)
        b_low = adapter_scale * dot_nt(branch[:, :width], second_rel[...])
        branch[:, width:] = b_low.astype(bf16) * mask[...]
        for i in range(4):
            at = lanes_at(place * 4 + info[INNER + i], block)
            here = slice(i * block, (i + 1) * block)
            ffn_grad[:, here] = dot_tn(low[:span], lhs_two[:span, at])
            second_grad[:, here] = adapter_scale * dot_tn(out_low[:span, :], branch[:span, at])
        acc[...] = jnp.zeros_like(acc)

    total = dot_nt(branch[:, width:], out_shrink[...])
    for (low, top), w in zip(cuts, out_parts):
        total = total + dot_nt(branch[:, low:top], w[...])
    grad_c = total * conv_ref[...]
    conv = total * c_ref[...]
    w = taps[...].astype(f32)
    high = conv.astype(bf16)
    rest = (conv - high.astype(f32)).astype(bf16)
    mixed = (
        w[0:1] * conv
        + w[1:2] * (dot_tn(one[...], high) + dot_tn(one[...], rest))
        + w[2:3] * (dot_tn(two[...], high) + dot_tn(two[...], rest))
    )
    proj = [
        (mixed * v_ref[...]).astype(bf16)[:span],
        grad_c.astype(bf16)[:span],
        (mixed * b_ref[...]).astype(bf16)[:span],
    ]
    half_scale = jnp.asarray(adapter_scale, bf16)
    for (low, top), w in zip(cuts, in_parts):
        acc[:span, low:top] += dot_nt(proj[0], w[0]) + dot_nt(proj[1], w[1]) + dot_nt(proj[2], w[2])
    acc[:span, width:] += (
        dot_nt(proj[0], in_expand[0] * half_scale)
        + dot_nt(proj[1], in_expand[1] * half_scale)
        + dot_nt(proj[2], in_expand[2] * half_scale)
    )
    low_one = lhs_one[:span, width:]
    for j in range(3):
        grads[j] = adapter_scale * dot_tn(low_one, proj[j])
    grads[3] = dot_tn(branch[:span, width:], gated_ref[:span, :])

    @pl.when(step == pl.num_programs(0) - 1)
    def _():
        own_ref[:, :half] = acc[:span, lanes_at(place, half)].astype(bf16)
        send_ref[:, :half] = acc[:span, lanes_at(1 - place, half)].astype(bf16)
        own_ref[:, half : half + rank] = acc[:span, width:].astype(bf16)
        send_ref[:, half : half + rank] = acc[:span, width:].astype(bf16)

        def visit(at):
            sums = acc[at, :width].astype(bf16).astype(f32) * lhs_one[at, :width].astype(f32)
            stat = jnp.sum(sums, axis=-1, keepdims=True)
            high = stat.astype(bf16).astype(f32)
            middle = (stat - high).astype(bf16).astype(f32)
            rest = stat - high - middle
            lane = lax.broadcasted_iota(jnp.int32, (stat.shape[0], 128), 1)
            packed = jnp.where(lane == 0, high, jnp.where(lane == 1, middle, jnp.where(lane == 2, rest, 0.0)))
            own_ref[at, half + rank :] = packed.astype(bf16)
            send_ref[at, half + rank :] = packed.astype(bf16)

        over_row_blocks(span, 16, visit)


def final_kernel(width, info, n_own, n_got, nt_own, nt_got, d_own, d_got, dl_own, dl_got, hidden, gh, x, normed, low, scale, mask,
                 g, gain, in_first, down_second, out_ref, grad_ref, in_grad, down_grad):
    rank = mask.shape[1]
    sums = nt_own[...].astype(f32) + nt_got[...].astype(f32)
    n_low = sums[:, :rank].astype(bf16) * mask[...]
    stat = jnp.sum(sums[:, rank:], axis=-1, keepdims=True)
    stat = stat + jnp.sum(n_low.astype(f32) * low[...].astype(f32), axis=-1, keepdims=True)
    stat = stat / width
    scale_rows = scale[:, 0:1]
    unit = x[...].astype(f32) * scale_rows
    grad = n_own[...].astype(f32) + n_got[...].astype(f32) + dot_nt(n_low, in_first[...])
    grad_ref[...] = gh[...] + scale_rows * (grad * gain[0:1, :].astype(f32) - unit * stat)
    d_low = (dl_own[...].astype(f32) + dl_got[...].astype(f32)).astype(bf16) * mask[...]
    down = d_own[...].astype(f32) + d_got[...].astype(f32)
    out_ref[...] = (hidden[...] + (down + adapter_scale * dot(d_low, down_second[...]))).astype(bf16)
    in_grad[...] = dot_tn(n_low, normed[...])
    down_grad[...] = adapter_scale * dot_tn(d_low, g[...])


def swap_tensor(array):
    return lax.ppermute(array, "tensor", [(0, 1), (1, 0)])


def body(
    block_input,
    cotangent,
    deal_order,
    seq_lengths,
    seq_adapter,
    mixer_gain,
    ffn_gain,
    conv_taps,
    in_weight,
    out_weight,
    gateup_weight,
    down_weight,
    input_adapter_shrink,
    in_expand,
    out_shrink,
    output_adapter_expand,
    ffn_shrink,
    ffn_expand,
    down_shrink,
    down_adapter_expand,
):
    tok_count, half = block_input.shape
    width = 2 * half
    rank = input_adapter_shrink.shape[1]
    hidden_units = gateup_weight.shape[2]
    groups = lax.axis_size("dp")
    pieces = lax.axis_size("ctx")
    sub = tok_count // groups
    group_tokens = pieces * tok_count
    seqs = seq_lengths.shape[0]
    nb = groups // CHUNKS
    span = nb * sub
    halo = -(-4 * nb // 16) * 16
    rows = span + halo
    special = groups == 4 and pieces % 2 == 0
    me = lax.axis_index("dp")
    ctx = lax.axis_index("ctx")
    tens = lax.axis_index("tensor")
    if special:
        xb, cb, zb = me // 2, me % 2, ctx % 2
    else:
        xb = cb = zb = jnp.int32(0)
    flip = xb ^ tens

    actual, in_stack, inner = [], [], []
    for rx in (0, 1):
        for rc in (0, 1):
            for rh in (0, 1):
                low = (rc ^ cb) * 2 + (rh ^ (zb & rx))
                actual.append((rx ^ xb) * 4 + low)
                in_stack.append((rx ^ flip) * 4 + low)
    for bc in (0, 1):
        for bh in (0, 1):
            inner.append((bc ^ cb) * 2 + (bh ^ (zb & flip)))
    info = jnp.stack([me, ctx, tens, flip, *actual, *in_stack, *inner]).astype(jnp.int32)

    core_route = [(0, 1), (1, 0), (2, 3), (3, 2)]
    x_route = [(0, 2), (2, 0), (1, 3), (3, 1)]
    z_route = [(i, i ^ 1) for i in range(pieces)]

    def fetch(shard, axis):
        if not special:
            return [lax.all_gather(shard, "dp", axis=axis, tiled=True)]
        n = shard.shape[axis] // 2
        mine = lax.dynamic_slice_in_dim(shard, zb * n, n, axis)
        over_x = lax.ppermute(mine, "dp", x_route)
        over_z = lax.ppermute(over_x, "ctx", z_route)
        return [
            shard,
            lax.ppermute(shard, "dp", core_route),
            over_x,
            over_z,
            lax.ppermute(over_x, "dp", core_route),
            lax.ppermute(over_z, "dp", core_route),
        ]

    x_got = swap_tensor(block_input)
    in_parts = fetch(in_weight, 1)
    out_parts = fetch(out_weight, 1)
    if special:
        n = width // 8
        cuts = ((0, 2 * n), (2 * n, 4 * n), (4 * n, 5 * n), (5 * n, 6 * n), (6 * n, 7 * n), (7 * n, 8 * n))
    else:
        cuts = ((0, width),)

    table = jnp.concatenate([deal_order[0], seq_lengths, seq_adapter])
    table = lax.all_gather(table, "dp", axis=0, tiled=False)
    dims = (groups, seqs, sub, nb, rows, tok_count, group_tokens)
    per_chunk = lambda c, *_: (c, 0, 0)
    mask, one, two = call(
        functools.partial(tables_kernel, dims), (CHUNKS,), (table, info), [],
        [
            ((CHUNKS, rows, rank), bf16, (None, rows, rank), per_chunk),
            ((CHUNKS, rows, rows), bf16, (None, rows, rows), per_chunk),
            ((CHUNKS, rows, rows), bf16, (None, rows, rows), per_chunk),
        ],
    )
    x_blocks = block_input.reshape(groups, sub, half)
    g_blocks = cotangent.reshape(groups, sub, half)
    edges = jnp.concatenate([x_blocks[:, :2], g_blocks[:, :2], x_blocks[:, sub - 2 :]], axis=1)
    all_edges = lax.all_gather(edges, "dp", axis=0, tiled=False)
    first_heads, last_tails, next_near, prev_near = call(
        functools.partial(edges_kernel, groups), (1,), (table, info), [(all_edges, None, None)],
        [
            ((groups, 4, half), bf16, None, None),
            ((groups, 2, half), bf16, None, None),
            ((groups, 4, half), bf16, None, None),
            ((groups, 2, half), bf16, None, None),
        ],
    )
    from_next = lax.ppermute(first_heads, "ctx", [(i + 1, i) for i in range(pieces - 1)])
    from_prev = lax.ppermute(last_tails, "ctx", [(i, i + 1) for i in range(pieces - 1)])
    deal_all = table[:, :groups]
    at_end = (deal_all[:, groups - 1] == me)[:, None, None]
    at_start = (deal_all[:, 0] == me)[:, None, None]
    next_rows = jnp.where(at_end, from_next, next_near)
    prev_rows = jnp.where(at_start, from_prev, prev_near)
    halo_x = jnp.concatenate([prev_rows, next_rows[:, :2]], axis=1)
    halo_g = jnp.concatenate([jnp.zeros_like(prev_rows), next_rows[:, 2:]], axis=1)
    halo_own = jnp.stack([halo_x, halo_g]).reshape(2, CHUNKS, 4 * nb, half)
    halo_own = jnp.pad(halo_own, ((0, 0), (0, 0), (0, halo - 4 * nb), (0, 0)))
    halo_got = swap_tensor(halo_own)
    g_got = swap_tensor(cotangent)
    gu_parts = fetch(gateup_weight, 1)
    down_parts = fetch(down_weight, 1)

    gain_one, gain_two = mixer_gain[None, :].astype(f32), ffn_gain[None, :].astype(f32)
    ext_one, ext_two = width + rank, width + 2 * rank

    def stacked(array, last):
        return (array, (None,) + array.shape[1:], lambda c, *_: (c, 0, 0))

    def joined_inputs(own, got, which):
        def rows_of(array):
            return (array, (span, half), lambda c, *_: (c, 0))

        def halo_of(array):
            return (array, (None, None, halo, half), lambda c, *_: (which, c, 0, 0))

        return [rows_of(own), rows_of(got), halo_of(halo_own), halo_of(halo_got)]

    x_full, lhs_one, scale = call(
        input_kernel, (CHUNKS,), (info,),
        joined_inputs(block_input, x_got, 0)
        + [(gain_one, None, None), (input_adapter_shrink, None, None), stacked(mask, rank)],
        [
            ((CHUNKS, rows, width), bf16, (None, rows, width), per_chunk),
            ((CHUNKS, rows, ext_one), bf16, (None, rows, ext_one), per_chunk),
            ((CHUNKS, rows, 128), f32, (None, rows, 128), per_chunk),
        ],
        [
            pltpu.VMEM((rows, width), bf16),
            pltpu.VMEM((width, rank), bf16),
            pltpu.VMEM((1, width), f32),
        ],
    )
    (glhs,) = call(
        cotangent_kernel, (CHUNKS,), (info,),
        joined_inputs(cotangent, g_got, 1) + [(down_adapter_expand, None, None), stacked(mask, rank)],
        [((CHUNKS, rows, ext_one), bf16, (None, rows, ext_one), per_chunk)],
        [pltpu.VMEM((rows, width), bf16), pltpu.VMEM((rank, width), bf16)],
    )

    def picked(array, c):
        return (array, (None,) + array.shape[1:], lambda *_: (c, 0, 0))

    def columns(array):
        return (array, array.shape[:-1] + (TILE,), lambda h, *_: (0,) * (array.ndim - 1) + (h,))

    def row_tiles(array):
        return (array, (TILE, array.shape[1]), lambda h, *_: (h, 0))

    mixer_steps = half // TILE
    feed_steps = hidden_units // TILE
    column_out = lambda h, *_: (0, h)
    chunks = []
    for c in range(CHUNKS):
        gate_b, gate_c, values, conv, gated, part = call(
            functools.partial(mixer_kernel, cuts), (mixer_steps,), (),
            [picked(lhs_one, c), picked(one, c), picked(two, c), columns(conv_taps), columns(in_expand), row_tiles(out_shrink)]
            + [columns(w) for w in in_parts]
            + [row_tiles(w) for w in out_parts],
            [((rows, half), f32, (rows, TILE), column_out)] * 4
            + [((rows, half), bf16, (rows, TILE), column_out), ((rows, ext_one), bf16, None, None)],
            [pltpu.VMEM((rows, ext_one), f32)],
            flops=2 * rows * half * ext_one * 4,
        )
        chunks.append(dict(b=gate_b, c=gate_c, v=values, conv=conv, gated=gated, part=part))
    for c in chunks:
        c["got"] = swap_tensor(c["part"])

    for i, c in enumerate(chunks):
        f_part, d_own, d_send, hidden, lhs_two, out_low, grads = call(
            functools.partial(feed_kernel, cuts, span), (feed_steps,), (info,),
            [picked(x_full, i), (c["part"], None, None), (c["got"], None, None), picked(glhs, i), picked(mask, i),
             (gain_two, None, None), (output_adapter_expand, None, None), (ffn_shrink, None, None),
             columns(ffn_expand), row_tiles(down_shrink)]
            + [columns(w) for w in gu_parts]
            + [row_tiles(w) for w in down_parts],
            [
                ((rows, ext_two), bf16, None, None),
                ((span, half + rank), bf16, None, None),
                ((span, half + rank), bf16, None, None),
                ((rows, width), f32, None, None),
                ((rows, ext_two), bf16, None, None),
                ((rows, rank), bf16, None, None),
                ((3, rank, hidden_units), f32, (3, rank, TILE), lambda h, *_: (0, 0, h)),
            ],
            [
                pltpu.VMEM((rows, ext_one), f32),
                pltpu.VMEM((rows, ext_two), f32),
                pltpu.VMEM((width, 2 * rank), bf16),
                pltpu.VMEM((rank, width), bf16),
                pltpu.VMEM((1, width), f32),
            ],
            flops=2 * rows * hidden_units * ext_two * 6,
        )
        c.update(f_own=f_part, d_own=d_own, d_send=d_send, hidden=hidden, lhs=lhs_two, low=out_low, feed_grads=grads)
    for c in chunks:
        c["f_got"] = swap_tensor(c["f_own"])
    for c in chunks:
        c["d_got"] = swap_tensor(c["d_send"])

    sent = half + 2 * rank
    for i, c in enumerate(chunks):
        n_own, n_send, grad_hidden, ffn_grad, second_grad, grads = call(
            functools.partial(back_kernel, cuts, span), (mixer_steps,), (info,),
            [(c["f_own"], None, None), (c["f_got"], None, None), (c["hidden"], None, None), picked(glhs, i),
             (c["lhs"], None, None), (c["low"], None, None), picked(lhs_one, i), picked(mask, i),
             (gain_two, None, None), (output_adapter_expand, None, None), (ffn_shrink, None, None),
             picked(one, i), picked(two, i), columns(conv_taps), columns(in_expand), row_tiles(out_shrink),
             columns(c["b"]), columns(c["c"]), columns(c["v"]), columns(c["conv"]), columns(c["gated"])]
            + [columns(w) for w in in_parts]
            + [row_tiles(w) for w in out_parts],
            [
                ((span, sent), bf16, None, None),
                ((span, sent), bf16, None, None),
                ((rows, width), f32, None, None),
                ((2 * rank, half), f32, None, None),
                ((rank, half), f32, None, None),
                ((4, rank, half), f32, (4, rank, TILE), lambda h, *_: (0, 0, h)),
            ],
            [
                pltpu.VMEM((rows, ext_one), f32),
                pltpu.VMEM((rows, ext_one), bf16),
                pltpu.VMEM((width, 2 * rank), bf16),
                pltpu.VMEM((rank, width), bf16),
                pltpu.VMEM((1, width), f32),
            ],
            flops=2 * rows * half * ext_one * 4,
        )
        c.update(n_own=n_own, n_send=n_send, gh=grad_hidden, ffn_grad=ffn_grad, second_grad=second_grad, mixer_grads=grads)
    for c in chunks:
        c["n_got"] = swap_tensor(c["n_send"])

    block = half // 4
    in_half = lambda i, info: (0, info[INNER + i])
    in_full = lambda i, info: (0, info[3] * 4 + info[INNER + i])
    for k, c in enumerate(chunks):
        in_stack_full = lambda i, info, k=k: (k, 0, info[3] * 4 + info[INNER + i])
        tail = (span, rank)
        c["out"], c["grad"], c["in_grad"], c["down_grad"] = call(
            functools.partial(final_kernel, width), (4,), (info,),
            [
                (c["n_own"], (span, block), in_half),
                (c["n_got"], (span, block), in_half),
                (c["n_own"], (span, 2 * rank), lambda i, info: (0, half // (2 * rank))),
                (c["n_got"], (span, 2 * rank), lambda i, info: (0, half // (2 * rank))),
                (c["d_own"], (span, block), in_half),
                (c["d_got"], (span, block), in_half),
                (c["d_own"], tail, lambda i, info: (0, half // rank)),
                (c["d_got"], tail, lambda i, info: (0, half // rank)),
                (c["hidden"], (span, block), in_full),
                (c["gh"], (span, block), in_full),
                (x_full, (None, span, block), in_stack_full),
                (lhs_one, (None, span, block), in_stack_full),
                (lhs_one, (None,) + tail, lambda i, info, k=k: (k, 0, width // rank)),
                (scale, (None, span, 128), lambda i, info, k=k: (k, 0, 0)),
                (mask, (None,) + tail, lambda i, info, k=k: (k, 0, 0)),
                (glhs, (None, span, block), in_stack_full),
                (gain_one, (1, block), lambda i, info: (0, info[2] * 4 + i)),
                (input_adapter_shrink, (block, rank), lambda i, info: (info[2] * 4 + i, 0)),
                (down_adapter_expand, (rank, block), lambda i, info: (0, info[2] * 4 + i)),
            ],
            [
                ((span, half), bf16, (span, block), lambda i, info: (0, i)),
                ((span, half), f32, (span, block), lambda i, info: (0, i)),
                ((rank, half), f32, (rank, block), lambda i, info: (0, i)),
                ((rank, half), f32, (rank, block), lambda i, info: (0, i)),
            ],
        )
    block_output = jnp.concatenate([c["out"] for c in chunks], axis=0)
    input_grad = jnp.concatenate([c["grad"] for c in chunks], axis=0)

    def summed(name):
        return sum(c[name] for c in chunks).astype(bf16)

    def reduced(*parts):
        return lax.psum(parts, ("dp", "ctx"))

    def joined(part):
        got = swap_tensor(part)
        first = jnp.where(tens == 0, part, got)
        second = jnp.where(tens == 0, got, part)
        return jnp.concatenate([first, second], axis=1).astype(f32)

    feed, ffn_grad, second_grad, mixer, in_grad, down_grad = reduced(
        summed("feed_grads"), summed("ffn_grad"), summed("second_grad"), summed("mixer_grads"), summed("in_grad"), summed("down_grad")
    )
    return (
        block_output,
        input_grad,
        joined(in_grad).T,
        mixer[:3].astype(f32),
        mixer[3].astype(f32).T,
        joined(second_grad),
        joined(ffn_grad).T,
        feed[1:].astype(f32),
        feed[0].astype(f32).T,
        joined(down_grad),
    )


def solution(mesh):
    placed = (
        P(("dp", "ctx"), "tensor"),
        P(("dp", "ctx"), "tensor"),
        P("dp", None),
        P("dp"),
        P("dp"),
        P(),
        P(),
        P(None, "tensor"),
        P(None, "dp", "tensor"),
        P("tensor", "dp"),
        P(None, "dp", "tensor"),
        P("tensor", "dp"),
        P(),
        P(None, None, "tensor"),
        P("tensor", None),
        P(),
        P(),
        P(None, None, "tensor"),
        P("tensor", None),
        P(),
    )
    return jax.shard_map(
        body,
        mesh=mesh,
        in_specs=placed,
        out_specs=(
            P(("dp", "ctx"), "tensor"),
            P(("dp", "ctx"), "tensor"),
            P(),
            P(None, None, "tensor"),
            P("tensor", None),
            P(),
            P(),
            P(None, None, "tensor"),
            P("tensor", None),
            P(),
        ),
        check_vma=False,
    )
```

time: 936 us -> 760 us (0.81)
  Pallas kernels: 0 us -> 253 us
  matrix products: 240 us -> 0 us
  local copies, waits for them, and re-layouts: 154 us -> 26.5 us
  other arithmetic: 86 us -> 27.8 us
  waiting for transfers between devices: 365 us -> 381 us
  starting transfers between devices: 50.1 us -> 34.8 us
    pallas_call x0 -> x12, Pallas kernels: none -> 253 us  [call(): pl.pallas_call(kernel, grid_spec=pltpu.PrefetchScalarGridSpec(num_scalar_...]
    dot_general x66 -> x0, matrix products: 240 us -> none  [the longest x22 138 us: dot_nt(): lax.dot_general(left, right, (((1,), (1,)), ((), ())), preferred_element_...]
    ppermute x19 -> x15, waiting for transfers between devices: 178 us -> 59.7 us  [swap_tensor(): return lax.ppermute(array, 'tensor', [(0, 1), (1, 0)])]
    unnamed x523 -> x96, local copies, waits for them, and re-layouts: 98.3 us -> 17.3 us
    ppermute x7 -> x4, waiting for transfers between devices: 54 us -> 116 us  [fetch(): over_x = lax.ppermute(mine, 'dp', x_route)]
    ppermute x7 -> x4, waiting for transfers between devices: 43.6 us -> 92.7 us  [fetch(): over_z = lax.ppermute(over_x, 'ctx', z_route)]
    slice x32 -> x1, local copies, waits for them, and re-layouts: 25.1 us -> 0.03 us  [body(): halo_x = jnp.concatenate([prev_rows, next_rows[:, :2]], axis=1)]
    concatenate x18 -> x3, other arithmetic: 26.5 us -> 4.71 us  [the longest x1 2.79 us: body(): block_output = jnp.concatenate([c['out'] for c in chunks], axis=0)]
  transfers between devices with their start and end apart: 57 -> 38, of which waited for: 20 -> 17; matrix products, arithmetic and copies ran while one was open for 34% -> 4% of each run, Pallas kernels for 0% -> 32%
where the time goes in v2:
time: 760 us; the launch traced here: 751 us
  waiting for transfers between devices  381 us (50%)
  Pallas kernels  253 us (33%)
  starting transfers between devices  34.8 us (5%)
  other arithmetic  27.8 us (4%)
  local copies, waits for them, and re-layouts  26.5 us (3%)
  between operations  15.7 us (2%)
  blocking collectives  12.6 us (2%)
    pallas_call x12, Pallas kernels, call(): pl.pallas_call(kernel, grid_spec=pltpu.PrefetchScalarGridSpec(num_scalar_...  253 us
    ppermute x4, waiting for transfers between devices, fetch(): over_x = lax.ppermute(mine, 'dp', x_route)  116 us
    psum x1, waiting for transfers between devices, reduced(): return lax.psum(parts, ('dp', 'ctx'))  110 us
    ppermute x4, waiting for transfers between devices, fetch(): over_z = lax.ppermute(over_x, 'ctx', z_route)  92.7 us
    ppermute x15, waiting for transfers between devices, swap_tensor(): return lax.ppermute(array, 'tensor', [(0, 1), (1, 0)])  59.7 us
    ppermute x15, starting transfers between devices, swap_tensor(): return lax.ppermute(array, 'tensor', [(0, 1), (1, 0)])  17.3 us
    unnamed x96, local copies, waits for them, and re-layouts  17.3 us
  transfers between devices with their start and end apart: 38, of which 17 were waited for; matrix products, arithmetic and copies ran while one was open for 4% of the time, Pallas kernels for 32%

profile of v2, /device:TPU:0, one launch (start us, length us, event | category | flops | bytes accessed | tf_op | source)
XLA Modules:
  0.0 751.2 jit_solution(3605481384542502772)
XLA Ops:
  10.1 6.4 all-reduce.2
  18.9 6.2 all-gather.1
  25.8 2.3 shard_map.267
  29.4 4.5 collective-permute-start.1
  36.1 3.6 constant_dynamic-slice_fusion.1
  43.4 6.6 collective-permute-done.10.refs_8_
  53.4 3.4 collective-permute-done.3.halo_got
  58.4 5.0 collective-permute-done.11.refs_9_
  64.6 78.2 %collective-permute-done.22.refs_8_ = bf16[2816,256]{1,0:T(8,128)(2,1)} collective-permute-done((bf16[2816,256]{1,0:T(8,128)(2,1)}, bf16[2816,256]{1,0:T(8,128)(2,1)}, u32[]{:S(2)}, u32[]{:S(2)}) %collective-permute-start.22) | collective-permute-done | bytes 1441824 | tf_op jit(solution)/shard_map/ppermute | solution.py:499
  144.6 31.4 %collective-permute-done.5.refs_2_ = bf16[3,256,1024]{2,1,0:T(8,128)(2,1)S(1)} collective-permute-done((bf16[3,256,1024]{2,1,0:T(8,128)(2,1)S(1)}, bf16[3,256,1024]{2,1,0:T(8,128)(2,1)S(1)}, u32[]{:S(2)}, u32[]{:S(2)}) %collective-permute-start.5) | collective-permute-done | bytes 1572896 | tf_op jit(solution)/shard_map/ppermute | solution.py:499
  182.9 30.4 %collective-permute-done.6.refs_3_ = bf16[3,256,1024]{2,1,0:T(8,128)(2,1)S(1)} collective-permute-done((bf16[3,256,1024]{2,1,0:T(8,128)(2,1)S(1)}, bf16[3,256,1024]{2,1,0:T(8,128)(2,1)S(1)}, u32[]{:S(2)}, u32[]{:S(2)}) %collective-permute-start.6) | collective-permute-done | bytes 1572896 | tf_op jit(solution)/shard_map/ppermute | solution.py:500
  217.9 57.3 %collective-permute-done.18.refs_3_ = bf16[2,256,2816]{2,1,0:T(8,128)(2,1)} collective-permute-done((bf16[2,256,2816]{2,1,0:T(8,128)(2,1)}, bf16[2,256,2816]{2,1,0:T(8,128)(2,1)}, u32[]{:S(2)}, u32[]{:S(2)}) %collective-permute-start.18) | collective-permute-done | bytes 2883616 | tf_op jit(solution)/shard_map/ppermute | solution.py:500
  275.2 2.5 shard_map.268
  278.3 11.5 %shard_map.269 = (bf16[2,400,2048]{2,1,0:T(8,128)(2,1)}, bf16[2,400,2176]{2,1,0:T(8,128)(2,1)}, f32[2,400,128]{2,1,0:T(8,128)}) custom-call(s32[24]{0:T(128)} %stack.108.info, bf16[768,1024]{1,0:T(8,128)(2,1)} %own.2, bf16[768,1024]{1,0:T(8,128)(2,1)} %collective-permute-done.got, bf16[2,2,16,1024]{3,2,1,0:T(8,128)(2,1)} %copy-done.20, ...), custom_call_target="tpu_custom_call" | custom-call | bytes 4145152 | tf_op jit(solution)/shard_map/pallas_call | solution.py:64
  289.7 19.4 %shard_map.275 = (f32[400,1024]{1,0:T(8,128)}, f32[400,1024]{1,0:T(8,128)}, f32[400,1024]{1,0:T(8,128)}, f32[400,1024]{1,0:T(8,128)}, bf16[400,1024]{1,0:T(8,128)(2,1)}, /*index=5*/bf16[400,2176]{1,0:T(8,128)(2,1)}) custom-call(bf16[2,400,2176]{2,1,0:T(8,128)(2,1)} %get-tuple-element.72.lhs.lhs_one.normed.low, bf16[2,400,400]{2,1,0:T(8,128)(2,1)} %get-tuple-element.73.one, ...), custom_call_target="tpu_custom_call" | custom-call | flops 7130316800 | bytes 22593536 | tf_op jit(solution)/shard_map/pallas_call | solution.py:64
  311.8 5.2 shard_map.271.glhs.g
  316.9 19.4 %shard_map.270 = (f32[400,1024]{1,0:T(8,128)}, f32[400,1024]{1,0:T(8,128)}, f32[400,1024]{1,0:T(8,128)}, f32[400,1024]{1,0:T(8,128)}, bf16[400,1024]{1,0:T(8,128)(2,1)}, /*index=5*/bf16[400,2176]{1,0:T(8,128)(2,1)}) custom-call(bf16[2,400,2176]{2,1,0:T(8,128)(2,1)} %get-tuple-element.72.lhs.lhs_one.normed.low, bf16[2,400,400]{2,1,0:T(8,128)(2,1)} %get-tuple-element.73.one, ...), custom_call_target="tpu_custom_call" | custom-call | flops 7130316800 | bytes 22593536 | tf_op jit(solution)/shard_map/pallas_call | solution.py:64
  338.0 12.3 %collective-permute-done.29.got = bf16[400,2176]{1,0:T(8,128)(2,1)S(1)} collective-permute-done((bf16[400,2176]{1,0:T(8,128)(2,1)}, bf16[400,2176]{1,0:T(8,128)(2,1)S(1)}, u32[]{:S(2)}, u32[]{:S(2)}) %collective-permute-start.29) | collective-permute-done | bytes 1740832 | tf_op jit(solution)/shard_map/ppermute | solution.py:430
  351.5 51.3 %shard_map.276 = (bf16[400,2304]{1,0:T(8,128)(2,1)}, bf16[384,1152]{1,0:T(8,128)(2,1)}, bf16[384,1152]{1,0:T(8,128)(2,1)}, f32[400,2048]{1,0:T(8,128)}, bf16[400...) custom-call(s32[24]{0:T(128)} %stack.108.info, bf16[2,400,2048]{2,1,0:T(8,128)(2,1)} %get-tuple-element.71.x, ...), custom_call_target="tpu_custom_call" | custom-call | flops 31142707200 | bytes 48791552 | tf_op jit(solution)/shard_map/pallas_call | solution.py:64
  405.7 51.3 %shard_map.272 = (bf16[400,2304]{1,0:T(8,128)(2,1)}, bf16[384,1152]{1,0:T(8,128)(2,1)}, bf16[384,1152]{1,0:T(8,128)(2,1)}, f32[400,2048]{1,0:T(8,128)}, bf16[400...) custom-call(s32[24]{0:T(128)} %stack.108.info, bf16[2,400,2048]{2,1,0:T(8,128)(2,1)} %get-tuple-element.71.x, ...), custom_call_target="tpu_custom_call" | custom-call | flops 31142707200 | bytes 48791552 | tf_op jit(solution)/shard_map/pallas_call | solution.py:64
  460.8 37.3 %shard_map.277 = (bf16[384,1280]{1,0:T(8,128)(2,1)}, bf16[384,1280]{1,0:T(8,128)(2,1)}, f32[400,2048]{1,0:T(8,128)}, f32[256,1024]{1,0:T(8,128)}, f32[128,1024]{1,0:T(8,128)}, /*index=5*/f32[4,128,1024]{2,1,0:T(8,128)}) custom-call(s32[24]{0:T(128)} %stack.108.info, bf16[400,2304]{1,0:T(8,128)(2,1)} %get-tuple-element.93.part, bf16[400,2304]{1,0:T(8,128)(2,1)} %copy-done.15, ...), custom_call_target="tpu_custom_call" | custom-call | flops 7130316800 | bytes 44142592 | tf_op jit(solution)/shard_map/pallas_call | solution.py:64
  501.6 37.6 %shard_map.273 = (bf16[384,1280]{1,0:T(8,128)(2,1)}, bf16[384,1280]{1,0:T(8,128)(2,1)}, f32[400,2048]{1,0:T(8,128)}, f32[256,1024]{1,0:T(8,128)}, f32[128,1024]{1,0:T(8,128)}, /*index=5*/f32[4,128,1024]{2,1,0:T(8,128)}) custom-call(s32[24]{0:T(128)} %stack.108.info, bf16[400,2304]{1,0:T(8,128)(2,1)} %get-tuple-element.76.part, bf16[400,2304]{1,0:T(8,128)(2,1)} %copy-done.14, ...), custom_call_target="tpu_custom_call" | custom-call | flops 7130316800 | bytes 44142592 | tf_op jit(solution)/shard_map/pallas_call | solution.py:64
  539.8 4.1 add_convert_fusion
  546.9 12.4 %collective-permute-done.31.n_got.nt_got = bf16[384,1280]{1,0:T(8,128)(2,1)S(1)} collective-permute-done((bf16[384,1280]{1,0:T(8,128)(2,1)}, bf16[384,1280]{1,0:T(8,128)(2,1)S(1)}, u32[]{:S(2)}, u32[]{:S(2)}) %collective-permute-start.31) | collective-permute-done | bytes 983072 | tf_op jit(solution)/shard_map/ppermute | solution.py:430
  560.3 7.4 shard_map.278
  567.7 10.9 %collective-permute-done.27.n_got.nt_got = bf16[384,1280]{1,0:T(8,128)(2,1)S(1)} collective-permute-done((bf16[384,1280]{1,0:T(8,128)(2,1)}, bf16[384,1280]{1,0:T(8,128)(2,1)S(1)}, u32[]{:S(2)}, u32[]{:S(2)}) %collective-permute-start.27) | collective-permute-done | bytes 983072 | tf_op jit(solution)/shard_map/ppermute | solution.py:430
  579.5 7.8 %shard_map.274 = (bf16[384,1024]{1,0:T(8,128)(2,1)}, f32[384,1024]{1,0:T(8,128)}, f32[128,1024]{1,0:T(8,128)}, f32[128,1024]{1,0:T(8,128)}) custom-call(s32[24]{0:T(128)} %stack.108.info, bf16[384,1280]{1,0:T(8,128)(2,1)} %get-tuple-element.85.n_own.nt_own, bf16[384,1280]{1,0:T(8,128)(2,1)} %copy-done.7, bf16[384,1280]{1,0:T(8,128)(2,1)} %get-tuple-element.85.n_own.nt_own, ...), custom_call_target="tpu_custom_call" | custom-call | bytes 29417472 | tf_op jit(solution)/shard_map/pallas_call | solution.py:64
  589.5 2.8 pad_maximum_fusion.1
  594.2 110.5 %all-reduce.6.cloned.1.call-done = (bf16[128,1024]{1,0:T(8,128)(2,1)}, bf16[4,128,1024]{2,1,0:T(8,128)(2,1)}, bf16[128,1024]{1,0:T(8,128)(2,1)}, bf16[256,1024]{...) async-done(((bf16[128,1024]{1,0:T(8,128)(2,1)}, bf16[4,128,1024]{2,1,0:T(8,128)(2,1)}, bf16[128,1024]{1,0:T(8,128)(2,1)}, ...) | async-done | bytes 4522000 | tf_op jit(solution)/shard_map/psum | solution.py:732
  704.7 3.1 slice_convert_fusion
  720.0 4.4 collective-permute-done.34
  727.8 11.9 %collective-permute-done.36 = bf16[128,1024]{1,0:T(8,128)(2,1)} collective-permute-done((bf16[128,1024]{1,0:T(8,128)(2,1)}, bf16[128,1024]{1,0:T(8,128)(2,1)}, u32[]{:S(2)}, u32[]{:S(2)}) %collective-permute-start.36) | collective-permute-done | bytes 262176 | tf_op jit(solution)/shard_map/ppermute | solution.py:430
  (196 shorter events, 76.9 us)
Async XLA Ops:
  7.2 697.5 %all-reduce.6.cloned.1.call-start = ((), (), s32[]{:S(2)}) async-start(), calls=%async_computation | async-start | bytes 9043968 | tf_op jit(solution)/shard_map/psum | solution.py:732
  28.2 15.2 %collective-permute-start.2 = (bf16[4,4,1024]{2,1,0:T(4,128)(2,1)}, bf16[4,4,1024]{2,1,0:T(4,128)(2,1)S(1)}, u32[]{:S(2)}, u32[]{:S(2)}) collective-permute-start(bf16[4,4,1024]{2,1,0:T(4,128)(2,1)} %get-tuple-element.68), channel_id=1, source_target_pairs={{2,0},{4,2},{6,4},{3,1},{5,3},{7,5},{10,8},{12,10},{14,12},{11,9},... | collective-permute-start | bytes 98312 | tf_op jit(solution)/shard_map/ppermute | solution.py:544
  34.0 22.9 %collective-permute-start.9 = (bf16[1024,512]{1,0:T(8,128)(2,1)}, bf16[1024,512]{1,0:T(8,128)(2,1)}, u32[]{:S(2)}, u32[]{:S(2)}) collective-permute-start(bf16[1024,512]{1,0:T(8,128)(2,1)} %refs_6_.11), channel_id=1, source_target_pairs={{0,8},{8,0},{16,24},{24,16},{1,9},{9,1},{17,25},{25,17},{2,10},{10... | collective-permute-start | bytes 3145736 | tf_op jit(solution)/shard_map/ppermute | solution.py:503
  35.2 14.9 %collective-permute-start.10 = (bf16[1024,256]{1,0:T(8,128)(2,1)S(1)}, bf16[1024,256]{1,0:T(8,128)(2,1)}, u32[]{:S(2)}, u32[]{:S(2)}) collective-permute-start(bf16[1024,256]{1,0:T(8,128)(2,1)S(1)} %constant_dynamic-slice_fusion.2), channel_id=1, source_target_pairs={{0,16},{16,0},{8,24},{24,8},{1,17},{17,1},{9,25},{25,9},{2,18},{18... | collective-permute-start | bytes 1572872 | tf_op jit(solution)/shard_map/ppermute | solution.py:499
  39.7 139.9 %collective-permute-start.17 = (bf16[2,256,2816]{2,1,0:T(8,128)(2,1)}, bf16[2,256,2816]{2,1,0:T(8,128)(2,1)}, u32[]{:S(2)}, u32[]{:S(2)}) collective-permute-start(bf16[2,256,2816]{2,1,0:T(8,128)(2,1)} %constant_dynamic-slice_fusion.1), channel_id=1, source_target_pairs={{0,16},{16,0},{8,24},{24,8},{1,17},{17,1},{9,25},{25,9},{2,18},{18... | collective-permute-start | bytes 8650760 | tf_op jit(solution)/shard_map/ppermute | solution.py:499
  42.3 100.5 %collective-permute-start.22 = (bf16[2816,256]{1,0:T(8,128)(2,1)}, bf16[2816,256]{1,0:T(8,128)(2,1)}, u32[]{:S(2)}, u32[]{:S(2)}) collective-permute-start(bf16[2816,256]{1,0:T(8,128)(2,1)} %constant_dynamic-slice_fusion), channel_id=1, source_target_pairs={{0,16},{16,0},{8,24},{24,8},{1,17},{17,1},{9,25},{25,9},{2,18},{18... | collective-permute-start | bytes 4325384 | tf_op jit(solution)/shard_map/ppermute | solution.py:499
  50.1 13.4 %collective-permute-start.11 = (bf16[1024,256]{1,0:T(8,128)(2,1)}, bf16[1024,256]{1,0:T(8,128)(2,1)}, u32[]{:S(2)}, u32[]{:S(2)}) collective-permute-start(bf16[1024,256]{1,0:T(8,128)(2,1)} %collective-permute-done.10.refs_8_), channel_id=1, source_target_pairs={{0,2},{2,0},{4,6},{6,4},{1,3},{3,1},{5,7},{7,5},{8,10},{10,8},{12,... | collective-permute-start | bytes 1572872 | tf_op jit(solution)/shard_map/ppermute | solution.py:500
  56.9 87.5 %collective-permute-start = (bf16[768,1024]{1,0:T(8,128)(2,1)}, bf16[768,1024]{1,0:T(8,128)(2,1)}, u32[]{:S(2)}, u32[]{:S(2)}) collective-permute-start(bf16[768,1024]{1,0:T(8,128)(2,1)} %own.2), channel_id=1, source_target_pairs={{0,1},{1,0},{2,3},{3,2},{4,5},{5,4},{6,7},{7,6},{8,9},{9,8},{10,11... | collective-permute-start | bytes 4718600 | tf_op jit(solution)/shard_map/ppermute | solution.py:430
  63.5 79.3 %collective-permute-start.13 = (bf16[1024,256]{1,0:T(8,128)(2,1)}, bf16[1024,256]{1,0:T(8,128)(2,1)S(1)}, u32[]{:S(2)}, u32[]{:S(2)}) collective-permute-start(bf16[1024,256]{1,0:T(8,128)(2,1)} %collective-permute-done.11.refs_9_), channel_id=1, source_target_pairs={{0,8},{8,0},{16,24},{24,16},{1,9},{9,1},{17,25},{25,17},{2,10},{10... | collective-permute-start | bytes 1572872 | tf_op jit(solution)/shard_map/ppermute | solution.py:507
  63.6 112.3 %collective-permute-start.5 = (bf16[3,256,1024]{2,1,0:T(8,128)(2,1)S(1)}, bf16[3,256,1024]{2,1,0:T(8,128)(2,1)S(1)}, u32[]{:S(2)}, u32[]{:S(2)}) collective-permute-start(bf16[3,256,1024]{2,1,0:T(8,128)(2,1)S(1)} %constant_dynamic-slice_fusion.3), channel_id=1, source_target_pairs={{0,16},{16,0},{8,24},{24,8},{1,17},{17,1},{9,25},{25,9},{2,18},{18... | collective-permute-start | bytes 4718600 | tf_op jit(solution)/shard_map/ppermute | solution.py:499
  142.8 38.5 %collective-permute-start.21 = (bf16[2816,512]{1,0:T(8,128)(2,1)}, bf16[2816,512]{1,0:T(8,128)(2,1)S(1)}, u32[]{:S(2)}, u32[]{:S(2)}) collective-permute-start(bf16[2816,512]{1,0:T(8,128)(2,1)} %refs_6_.10), channel_id=1, source_target_pairs={{0,8},{8,0},{16,24},{24,16},{1,9},{9,1},{17,25},{25,17},{2,10},{10... | collective-permute-start | bytes 8650760 | tf_op jit(solution)/shard_map/ppermute | solution.py:503
  142.8 36.9 %collective-permute-start.15 = (bf16[768,1024]{1,0:T(8,128)(2,1)S(1)}, bf16[768,1024]{1,0:T(8,128)(2,1)S(1)}, u32[]{:S(2)}, u32[]{:S(2)}) collective-permute-start(bf16[768,1024]{1,0:T(8,128)(2,1)S(1)} %copy-done.16), channel_id=1, source_target_pairs={{0,1},{1,0},{2,3},{3,2},{4,5},{5,4},{6,7},{7,6},{8,9},{9,8},{10,11... | collective-permute-start | bytes 4718600 | tf_op jit(solution)/shard_map/ppermute | solution.py:430
  144.4 68.9 %collective-permute-start.4 = (bf16[3,512,1024]{2,1,0:T(8,128)(2,1)S(1)}, bf16[3,512,1024]{2,1,0:T(8,128)(2,1)S(1)}, u32[]{:S(2)}, u32[]{:S(2)}) collective-permute-start(bf16[3,512,1024]{2,1,0:T(8,128)(2,1)S(1)} %copy-done), channel_id=1, source_target_pairs={{0,8},{8,0},{16,24},{24,16},{1,9},{9,1},{17,25},{25,17},{2,10},{10... | collective-permute-start | bytes 9437192 | tf_op jit(solution)/shard_map/ppermute | solution.py:503
  176.0 37.3 %collective-permute-start.6 = (bf16[3,256,1024]{2,1,0:T(8,128)(2,1)S(1)}, bf16[3,256,1024]{2,1,0:T(8,128)(2,1)S(1)}, u32[]{:S(2)}, u32[]{:S(2)}) collective-permute-start(bf16[3,256,1024]{2,1,0:T(8,128)(2,1)S(1)} %collective-permute-done.5.refs_2_), channel_id=1, source_target_pairs={{0,2},{2,0},{4,6},{6,4},{1,3},{3,1},{5,7},{7,5},{8,10},{10,8},{12,... | collective-permute-start | bytes 4718600 | tf_op jit(solution)/shard_map/ppermute | solution.py:500
  179.6 158.3 %collective-permute-start.16 = (bf16[2,512,2816]{2,1,0:T(8,128)(2,1)}, bf16[2,512,2816]{2,1,0:T(8,128)(2,1)}, u32[]{:S(2)}, u32[]{:S(2)}) collective-permute-start(bf16[2,512,2816]{2,1,0:T(8,128)(2,1)} %refs_0_.10), channel_id=1, source_target_pairs={{0,8},{8,0},{16,24},{24,16},{1,9},{9,1},{17,25},{25,17},{2,10},{10... | collective-permute-start | bytes 17301512 | tf_op jit(solution)/shard_map/ppermute | solution.py:503
  179.7 95.5 %collective-permute-start.18 = (bf16[2,256,2816]{2,1,0:T(8,128)(2,1)}, bf16[2,256,2816]{2,1,0:T(8,128)(2,1)}, u32[]{:S(2)}, u32[]{:S(2)}) collective-permute-start(bf16[2,256,2816]{2,1,0:T(8,128)(2,1)} %collective-permute-done.17.refs_2_), channel_id=1, source_target_pairs={{0,2},{2,0},{4,6},{6,4},{1,3},{3,1},{5,7},{7,5},{8,10},{10,8},{12,... | collective-permute-start | bytes 8650760 | tf_op jit(solution)/shard_map/ppermute | solution.py:500
  181.3 33.6 %collective-permute-start.7 = (bf16[3,256,1024]{2,1,0:T(8,128)(2,1)S(1)}, bf16[3,256,1024]{2,1,0:T(8,128)(2,1)S(1)}, u32[]{:S(2)}, u32[]{:S(2)}) collective-permute-start(bf16[3,256,1024]{2,1,0:T(8,128)(2,1)S(1)} %collective-permute-done.5.refs_2_), channel_id=1, source_target_pairs={{0,8},{8,0},{16,24},{24,16},{1,9},{9,1},{17,25},{25,17},{2,10},{10... | collective-permute-start | bytes 4718600 | tf_op jit(solution)/shard_map/ppermute | solution.py:506
  213.3 95.9 %collective-permute-start.23 = (bf16[2816,256]{1,0:T(8,128)(2,1)}, bf16[2816,256]{1,0:T(8,128)(2,1)}, u32[]{:S(2)}, u32[]{:S(2)}) collective-permute-start(bf16[2816,256]{1,0:T(8,128)(2,1)} %collective-permute-done.22.refs_8_), channel_id=1, source_target_pairs={{0,2},{2,0},{4,6},{6,4},{1,3},{3,1},{5,7},{7,5},{8,10},{10,8},{12,... | collective-permute-start | bytes 4325384 | tf_op jit(solution)/shard_map/ppermute | solution.py:500
  214.9 95.8 %collective-permute-start.24 = (bf16[2816,256]{1,0:T(8,128)(2,1)}, bf16[2816,256]{1,0:T(8,128)(2,1)}, u32[]{:S(2)}, u32[]{:S(2)}) collective-permute-start(bf16[2816,256]{1,0:T(8,128)(2,1)} %collective-permute-done.22.refs_8_), channel_id=1, source_target_pairs={{0,8},{8,0},{16,24},{24,16},{1,9},{9,1},{17,25},{25,17},{2,10},{10... | collective-permute-start | bytes 4325384 | tf_op jit(solution)/shard_map/ppermute | solution.py:506
  216.7 121.3 %collective-permute-start.19 = (bf16[2,256,2816]{2,1,0:T(8,128)(2,1)}, bf16[2,256,2816]{2,1,0:T(8,128)(2,1)S(1)}, u32[]{:S(2)}, u32[]{:S(2)}) collective-permute-start(bf16[2,256,2816]{2,1,0:T(8,128)(2,1)} %collective-permute-done.17.refs_2_), channel_id=1, source_target_pairs={{0,8},{8,0},{16,24},{24,16},{1,9},{9,1},{17,25},{25,17},{2,10},{10... | collective-permute-start | bytes 8650760 | tf_op jit(solution)/shard_map/ppermute | solution.py:506
  275.2 75.2 %collective-permute-start.20 = (bf16[2,256,2816]{2,1,0:T(8,128)(2,1)}, bf16[2,256,2816]{2,1,0:T(8,128)(2,1)}, u32[]{:S(2)}, u32[]{:S(2)}) collective-permute-start(bf16[2,256,2816]{2,1,0:T(8,128)(2,1)} %collective-permute-done.18.refs_3_), channel_id=1, source_target_pairs={{0,8},{8,0},{16,24},{24,16},{1,9},{9,1},{17,25},{25,17},{2,10},{10... | collective-permute-start | bytes 8650760 | tf_op jit(solution)/shard_map/ppermute | solution.py:507
  309.2 41.1 %collective-permute-start.29 = (bf16[400,2176]{1,0:T(8,128)(2,1)}, bf16[400,2176]{1,0:T(8,128)(2,1)S(1)}, u32[]{:S(2)}, u32[]{:S(2)}) collective-permute-start(bf16[400,2176]{1,0:T(8,128)(2,1)} %get-tuple-element.92.part), channel_id=1, source_target_pairs={{0,1},{1,0},{2,3},{3,2},{4,5},{5,4},{6,7},{7,6},{8,9},{9,8},{10,11... | collective-permute-start | bytes 5222408 | tf_op jit(solution)/shard_map/ppermute | solution.py:430
  310.8 25.6 %collective-permute-start.25 = (bf16[2816,256]{1,0:T(8,128)(2,1)}, bf16[2816,256]{1,0:T(8,128)(2,1)S(1)}, u32[]{:S(2)}, u32[]{:S(2)}) collective-permute-start(bf16[2816,256]{1,0:T(8,128)(2,1)} %collective-permute-done.23.refs_9_), channel_id=1, source_target_pairs={{0,8},{8,0},{16,24},{24,16},{1,9},{9,1},{17,25},{25,17},{2,10},{10... | collective-permute-start | bytes 4325384 | tf_op jit(solution)/shard_map/ppermute | solution.py:507
  337.5 67.0 %collective-permute-start.14 = (bf16[400,2176]{1,0:T(8,128)(2,1)}, bf16[400,2176]{1,0:T(8,128)(2,1)S(1)}, u32[]{:S(2)}, u32[]{:S(2)}) collective-permute-start(bf16[400,2176]{1,0:T(8,128)(2,1)} %get-tuple-element.75.part), channel_id=1, source_target_pairs={{0,1},{1,0},{2,3},{3,2},{4,5},{5,4},{6,7},{7,6},{8,9},{9,8},{10,11... | collective-permute-start | bytes 5222408 | tf_op jit(solution)/shard_map/ppermute | solution.py:430
  402.9 56.7 %collective-permute-start.30 = (bf16[400,2304]{1,0:T(8,128)(2,1)}, bf16[400,2304]{1,0:T(8,128)(2,1)S(1)}, u32[]{:S(2)}, u32[]{:S(2)}) collective-permute-start(bf16[400,2304]{1,0:T(8,128)(2,1)} %get-tuple-element.93.part), channel_id=1, source_target_pairs={{0,1},{1,0},{2,3},{3,2},{4,5},{5,4},{6,7},{7,6},{8,9},{9,8},{10,11... | collective-permute-start | bytes 5529608 | tf_op jit(solution)/shard_map/ppermute | solution.py:430
  456.9 43.4 %collective-permute-start.26 = (bf16[400,2304]{1,0:T(8,128)(2,1)}, bf16[400,2304]{1,0:T(8,128)(2,1)S(1)}, u32[]{:S(2)}, u32[]{:S(2)}) collective-permute-start(bf16[400,2304]{1,0:T(8,128)(2,1)} %get-tuple-element.76.part), channel_id=1, source_target_pairs={{0,1},{1,0},{2,3},{3,2},{4,5},{5,4},{6,7},{7,6},{8,9},{9,8},{10,11... | collective-permute-start | bytes 5529608 | tf_op jit(solution)/shard_map/ppermute | solution.py:430
  457.5 89.4 %collective-permute-start.32 = (bf16[384,1152]{1,0:T(8,128)(2,1)}, bf16[384,1152]{1,0:T(8,128)(2,1)S(1)}, u32[]{:S(2)}, u32[]{:S(2)}) collective-permute-start(bf16[384,1152]{1,0:T(8,128)(2,1)} %get-tuple-element.105), channel_id=1, source_target_pairs={{0,1},{1,0},{2,3},{3,2},{4,5},{5,4},{6,7},{7,6},{8,9},{9,8},{10,11... | collective-permute-start | bytes 2654216 | tf_op jit(solution)/shard_map/ppermute | solution.py:430
  459.0 108.7 %collective-permute-start.28 = (bf16[384,1152]{1,0:T(8,128)(2,1)}, bf16[384,1152]{1,0:T(8,128)(2,1)S(1)}, u32[]{:S(2)}, u32[]{:S(2)}) collective-permute-start(bf16[384,1152]{1,0:T(8,128)(2,1)} %get-tuple-element.88), channel_id=1, source_target_pairs={{0,1},{1,0},{2,3},{3,2},{4,5},{5,4},{6,7},{7,6},{8,9},{9,8},{10,11... | collective-permute-start | bytes 2654216 | tf_op jit(solution)/shard_map/ppermute | solution.py:430
  498.1 61.3 %collective-permute-start.31 = (bf16[384,1280]{1,0:T(8,128)(2,1)}, bf16[384,1280]{1,0:T(8,128)(2,1)S(1)}, u32[]{:S(2)}, u32[]{:S(2)}) collective-permute-start(bf16[384,1280]{1,0:T(8,128)(2,1)} %get-tuple-element.103), channel_id=1, source_target_pairs={{0,1},{1,0},{2,3},{3,2},{4,5},{5,4},{6,7},{7,6},{8,9},{9,8},{10,11... | collective-permute-start | bytes 2949128 | tf_op jit(solution)/shard_map/ppermute | solution.py:430
  539.2 39.4 %collective-permute-start.27 = (bf16[384,1280]{1,0:T(8,128)(2,1)}, bf16[384,1280]{1,0:T(8,128)(2,1)S(1)}, u32[]{:S(2)}, u32[]{:S(2)}) collective-permute-start(bf16[384,1280]{1,0:T(8,128)(2,1)} %get-tuple-element.86), channel_id=1, source_target_pairs={{0,1},{1,0},{2,3},{3,2},{4,5},{5,4},{6,7},{7,6},{8,9},{9,8},{10,11... | collective-permute-start | bytes 2949128 | tf_op jit(solution)/shard_map/ppermute | solution.py:430
  712.3 29.4 %collective-permute-start.35 = (bf16[256,1024]{1,0:T(8,128)(2,1)S(1)}, bf16[256,1024]{1,0:T(8,128)(2,1)S(1)}, u32[]{:S(2)}, u32[]{:S(2)}) collective-permute-start(bf16[256,1024]{1,0:T(8,128)(2,1)S(1)} %copy-done.26), channel_id=1, source_target_pairs={{0,1},{1,0},{2,3},{3,2},{4,5},{5,4},{6,7},{7,6},{8,9},{9,8},{10,11... | collective-permute-start | bytes 1572872 | tf_op jit(solution)/shard_map/ppermute | solution.py:430
  715.3 24.3 %collective-permute-start.36 = (bf16[128,1024]{1,0:T(8,128)(2,1)}, bf16[128,1024]{1,0:T(8,128)(2,1)}, u32[]{:S(2)}, u32[]{:S(2)}) collective-permute-start(bf16[128,1024]{1,0:T(8,128)(2,1)} %get-tuple-element.149), channel_id=1, source_target_pairs={{0,1},{1,0},{2,3},{3,2},{4,5},{5,4},{6,7},{7,6},{8,9},{9,8},{10,11... | collective-permute-start | bytes 786440 | tf_op jit(solution)/shard_map/ppermute | solution.py:430
  (51 other events, 1504.5 us)
Sparse Core Ops, SparseCore 0:
  589.6 115.0 all-reduce.5

commit v3 on v2

--- a/solution.py
+++ b/solution.py
@@ -10,6 +10,7 @@
 RANK = 16
 CHUNKS = 2
 TILE = 256
+FEED_CUTS = ((0, 2), (2, 4), (4, 6), (6, 8), (8, 10), (10, 11))
 VMEM_BYTES = 56 * 1024 * 1024
 
 norm_eps = 1e-05
@@ -74,7 +75,7 @@
         compiler_params=pltpu.CompilerParams(
             dimension_semantics=("arbitrary",) * len(grid), vmem_limit_bytes=VMEM_BYTES
         ),
-        cost_estimate=pl.CostEstimate(flops=flops, transcendentals=0, bytes_accessed=moved),
+        cost_estimate=pl.CostEstimate(flops=max(flops, 1), transcendentals=0, bytes_accessed=1),
     )(*scalars, *[a for a, _, _ in ins])
 
 
@@ -154,21 +155,21 @@
 ACTUAL, STACK, INNER = 4, 12, 20
 
 
-def stack_rows(info, own, got, halo_own, halo_got, stack, span, half, into):
+def stack_rows(info, own, got_first, got_second, halo_own, halo_got, stack, span, half, into):
     block = half // 4
     stack[:span, :half] = own[...]
-    stack[:span, half:] = got[...]
+    stack[:span, half:] = jnp.where(pl.program_id(0) == 0, got_first[...], got_second[...])
     stack[span:, :half] = halo_own[...]
     stack[span:, half:] = halo_got[...]
     for r in range(8):
         into[:, r * block : (r + 1) * block] = stack[:, lanes_at(info[STACK + r], block)]
 
 
-def input_kernel(info, own, got, halo_own, halo_got, gain, first, mask, x_ref, lhs_ref, scale_ref, stack, first_rel, gain_rel):
+def input_kernel(info, own, got_first, got_second, halo_own, halo_got, gain, first, mask, x_ref, lhs_ref, scale_ref, stack, first_rel, gain_rel):
     span, half = own.shape
     rows, width = x_ref.shape
     block = half // 4
-    stack_rows(info, own, got, halo_own, halo_got, stack, span, half, x_ref)
+    stack_rows(info, own, got_first, got_second, halo_own, halo_got, stack, span, half, x_ref)
     for r in range(8):
         first_rel[r * block : (r + 1) * block, :] = first[lanes_at(info[ACTUAL + r], block), :]
         gain_rel[:, r * block : (r + 1) * block] = gain[:, lanes_at(info[ACTUAL + r], block)]
@@ -183,28 +184,41 @@
     lhs_ref[:, width:] = dot(lhs_ref[:, :width], first_rel[...]).astype(bf16) * mask[...]
 
 
-def cotangent_kernel(info, own, got, halo_own, halo_got, second, mask, lhs_ref, stack, second_rel):
+def cotangent_kernel(info, own, got_first, got_second, halo_own, halo_got, second, mask, lhs_ref, stack, second_rel):
     span, half = own.shape
     width = 2 * half
     block = half // 4
-    stack_rows(info, own, got, halo_own, halo_got, stack, span, half, lhs_ref)
+    stack_rows(info, own, got_first, got_second, halo_own, halo_got, stack, span, half, lhs_ref)
     for r in range(8):
         second_rel[:, r * block : (r + 1) * block] = second[:, lanes_at(info[ACTUAL + r], block)]
     low = adapter_scale * dot_nt(lhs_ref[:, :width], second_rel[...])
     lhs_ref[:, width:] = low.astype(bf16) * mask[...]
 
 
+def mixer_parts(refs, cuts):
+    if len(cuts) == 1:
+        return [[refs[0].at[j] for j in range(3)]], [refs[1]], refs[2:]
+    ins = [[refs[0].at[k, j] for j in range(3)] for k in range(2)]
+    outs = [refs[1].at[k] for k in range(2)]
+    early = pl.program_id(0) < 2
+    for k in range(4):
+        first, second = refs[2 + 2 * k], refs[3 + 2 * k]
+        tiles = [jnp.where(early, first[j], second[j]) for j in range(4)]
+        ins.append(tiles[:3])
+        outs.append(tiles[3])
+    return ins, outs, refs[10:]
+
+
 def mixer_kernel(cuts, lhs, one, two, taps, in_expand, out_shrink, *refs):
-    count = len(cuts)
-    in_parts, out_parts = refs[:count], refs[count : 2 * count]
-    b_ref, c_ref, v_ref, conv_ref, gated_ref, part_ref, acc = refs[2 * count :]
+    in_parts, out_parts, refs = mixer_parts(refs, cuts)
+    b_ref, c_ref, v_ref, conv_ref, gated_ref, part_first, part_second, acc = refs
     width = cuts[-1][1]
     step = pl.program_id(0)
 
     def project(j):
         total = dot(lhs[:, width:], in_expand[j] * jnp.asarray(adapter_scale, bf16))
         for (low, top), part in zip(cuts, in_parts):
-            total = total + dot(lhs[:, low:top], part[j])
+            total = total + dot(lhs[:, low:top], part[j][...])
         return total
 
     b, c, v = project(0), project(1), project(2)
@@ -228,14 +242,32 @@
 
     @pl.when(step == pl.num_programs(0) - 1)
     def _():
-        part_ref[...] = acc[...].astype(bf16)
-
-
-def feed_kernel(cuts, span, info, x, part, got, glhs, mask, gain, out_second, ffn_first, ffn_expand, down_shrink, *refs):
-    count = len(cuts)
-    gu_parts, down_parts = refs[:count], refs[count : 2 * count]
+        cut = part_first.shape[0]
+        part_first[...] = acc[:cut, :].astype(bf16)
+        part_second[...] = acc[cut:, :].astype(bf16)
+
+
+def feed_kernel(cuts, span, info, x, part_first, part_second, got_first, got_second, glhs, mask, gain, out_second, ffn_first, ffn_expand, down_shrink, *refs):
+    if len(cuts) == 1:
+        gu_parts, down_parts, refs = [[refs[0].at[0], refs[0].at[1]]], [refs[1]], refs[2:]
+    else:
+        gu_parts = [[refs[0].at[k, j] for j in range(2)] for k in range(2)]
+        down_parts = [refs[1].at[k] for k in range(2)]
+        count = len(FEED_CUTS)
+        far, refs = refs[2 : 2 + 4 * count], refs[2 + 4 * count :]
+        here, refs = refs[-1], refs[:-1]
+        for i, (low, top) in enumerate(FEED_CUTS):
+
+            @pl.when((pl.program_id(0) >= low) & (pl.program_id(0) < top))
+            def _(i=i):
+                for k in range(4):
+                    here[k] = far[k * count + i][...]
+
+        for k in range(4):
+            gu_parts.append([here.at[k, 0], here.at[k, 1]])
+            down_parts.append(here.at[k, 2])
     (f_ref, own_ref, send_ref, hidden_ref, lhs, low_ref, grads,
-     acc_d, acc_f, first_rel, second_rel, gain_rel) = refs[2 * count :]
+     acc_d, acc_f, first_rel, second_rel, gain_rel) = refs
     width = cuts[-1][1]
     half = width // 2
     block = width // 8
@@ -250,13 +282,17 @@
             first_rel[here, :] = ffn_first[at, :]
             second_rel[:, here] = out_second[:, at]
             gain_rel[:, here] = gain[:, at]
-        low = (part[:, width:].astype(f32) + got[:, width:].astype(f32)).astype(bf16) * mask[...]
+        cut = part_first.shape[0]
+        for own, got, base in ((part_first, got_first, 0), (part_second, got_second, cut)):
+            n = own.shape[0]
+            acc_d[base : base + n, :] = own[...].astype(f32) + got[...].astype(f32)
+        low = acc_d[:, width:].astype(bf16) * mask[...]
         low_ref[...] = low
-        acc_d[:, :width] = dot(low, second_rel[...])
+        acc_f[:, :width] = dot(low, second_rel[...])
 
         def visit(at):
-            both = part[at, :width].astype(f32) + got[at, :width].astype(f32)
-            hidden = x[at, :].astype(f32) + (both + adapter_scale * acc_d[at, :width])
+            both = acc_d[at, :width]
+            hidden = x[at, :].astype(f32) + (both + adapter_scale * acc_f[at, :width])
             hidden_ref[at, :] = hidden
             scale = lax.rsqrt(jnp.mean(hidden * hidden, axis=-1, keepdims=True) + norm_eps)
             lhs[at, :width] = (hidden * scale * gain_rel[0:1, :]).astype(bf16)
@@ -274,7 +310,7 @@
     def project(j):
         total = dot(lows[j], ffn_expand[j] * half_scale)
         for (low, top), w in zip(cuts, gu_parts):
-            total = total + dot(lhs[:, low:top], w[j])
+            total = total + dot(lhs[:, low:top], w[j][...])
         return total
 
     gate, up = project(0), project(1)
@@ -291,7 +327,7 @@
         acc_d[:span, low:top] += dot(act[:span], w[...])
     acc_d[:span, width:] += dot(act[:span], down_shrink[...])
     for (low, top), w in zip(cuts, gu_parts):
-        acc_f[:, low:top] += dot_nt(gg, w[0]) + dot_nt(gu, w[1])
+        acc_f[:, low:top] += dot_nt(gg, w[0][...]) + dot_nt(gu, w[1][...])
     acc_f[:, width : width + rank] += dot_nt(gg, ffn_expand[0] * half_scale)
     acc_f[:, width + rank :] += dot_nt(gu, ffn_expand[1] * half_scale)
     grads[0] = dot_tn(g_low[:span], act[:span])
@@ -310,10 +346,9 @@
 
 def back_kernel(cuts, span, info, part, got, hidden, glhs, lhs_two, out_low, lhs_one, mask, gain, out_second, ffn_first,
                 one, two, taps, in_expand, out_shrink, b_ref, c_ref, v_ref, conv_ref, gated_ref, *refs):
-    count = len(cuts)
-    in_parts, out_parts = refs[:count], refs[count : 2 * count]
-    (own_ref, send_ref, gh_ref, ffn_grad, second_grad, grads,
-     acc, branch, first_rel, second_rel, gain_rel) = refs[2 * count :]
+    in_parts, out_parts, refs = mixer_parts(refs, cuts)
+    (own_ref, send_ref, rank_ref, gh_ref, ffn_grad, second_grad, grads,
+     acc, branch, first_rel, second_rel, gain_rel) = refs
     width = cuts[-1][1]
     half = width // 2
     block = width // 8
@@ -375,7 +410,7 @@
     ]
     half_scale = jnp.asarray(adapter_scale, bf16)
     for (low, top), w in zip(cuts, in_parts):
-        acc[:span, low:top] += dot_nt(proj[0], w[0]) + dot_nt(proj[1], w[1]) + dot_nt(proj[2], w[2])
+        acc[:span, low:top] += dot_nt(proj[0], w[0][...]) + dot_nt(proj[1], w[1][...]) + dot_nt(proj[2], w[2][...])
     acc[:span, width:] += (
         dot_nt(proj[0], in_expand[0] * half_scale)
         + dot_nt(proj[1], in_expand[1] * half_scale)
@@ -388,10 +423,9 @@
 
     @pl.when(step == pl.num_programs(0) - 1)
     def _():
-        own_ref[:, :half] = acc[:span, lanes_at(place, half)].astype(bf16)
-        send_ref[:, :half] = acc[:span, lanes_at(1 - place, half)].astype(bf16)
-        own_ref[:, half : half + rank] = acc[:span, width:].astype(bf16)
-        send_ref[:, half : half + rank] = acc[:span, width:].astype(bf16)
+        own_ref[...] = acc[:span, lanes_at(place, half)].astype(bf16)
+        send_ref[...] = acc[:span, lanes_at(1 - place, half)].astype(bf16)
+        rank_ref[:, :rank] = acc[:span, width:].astype(bf16)
 
         def visit(at):
             sums = acc[at, :width].astype(bf16).astype(f32) * lhs_one[at, :width].astype(f32)
@@ -401,29 +435,42 @@
             rest = stat - high - middle
             lane = lax.broadcasted_iota(jnp.int32, (stat.shape[0], 128), 1)
             packed = jnp.where(lane == 0, high, jnp.where(lane == 1, middle, jnp.where(lane == 2, rest, 0.0)))
-            own_ref[at, half + rank :] = packed.astype(bf16)
-            send_ref[at, half + rank :] = packed.astype(bf16)
+            rank_ref[at, rank:] = packed.astype(bf16)
 
         over_row_blocks(span, 16, visit)
 
 
-def final_kernel(width, info, n_own, n_got, nt_own, nt_got, d_own, d_got, dl_own, dl_got, hidden, gh, x, normed, low, scale, mask,
-                 g, gain, in_first, down_second, out_ref, grad_ref, in_grad, down_grad):
+def rank_rows(own, got, mask):
     rank = mask.shape[1]
-    sums = nt_own[...].astype(f32) + nt_got[...].astype(f32)
-    n_low = sums[:, :rank].astype(bf16) * mask[...]
-    stat = jnp.sum(sums[:, rank:], axis=-1, keepdims=True)
+    sums = own[...].astype(f32) + got[...].astype(f32)
+    return sums[:, :rank].astype(bf16) * mask[...], sums[:, rank:]
+
+
+def output_kernel(info, own, got, rank_own, rank_got, hidden, mask, g, second, out_ref, grad_ref):
+    low, _ = rank_rows(rank_own, rank_got, mask)
+    down = own[...].astype(f32) + got[...].astype(f32)
+    out_ref[...] = (hidden[...] + (down + adapter_scale * dot(low, second[...]))).astype(bf16)
+    grad_ref[...] = adapter_scale * dot_tn(low, g[...])
+
+
+def rank_kernel(info, own, got, mask, normed, grad_ref):
+    low, _ = rank_rows(own, got, mask)
+    grad_ref[...] = dot_tn(low, normed[...])
+
+
+def final_kernel(width, info, own, got, rank_own, rank_got, gh, x, low, scale, mask, gain, first, grad_ref):
+    n_low, stat = rank_rows(rank_own, rank_got, mask)
+    stat = jnp.sum(stat, axis=-1, keepdims=True)
     stat = stat + jnp.sum(n_low.astype(f32) * low[...].astype(f32), axis=-1, keepdims=True)
     stat = stat / width
     scale_rows = scale[:, 0:1]
     unit = x[...].astype(f32) * scale_rows
-    grad = n_own[...].astype(f32) + n_got[...].astype(f32) + dot_nt(n_low, in_first[...])
+    grad = own[...].astype(f32) + got[...].astype(f32) + dot_nt(n_low, first[...])
     grad_ref[...] = gh[...] + scale_rows * (grad * gain[0:1, :].astype(f32) - unit * stat)
-    d_low = (dl_own[...].astype(f32) + dl_got[...].astype(f32)).astype(bf16) * mask[...]
-    down = d_own[...].astype(f32) + d_got[...].astype(f32)
-    out_ref[...] = (hidden[...] + (down + adapter_scale * dot(d_low, down_second[...]))).astype(bf16)
-    in_grad[...] = dot_tn(n_low, normed[...])
-    down_grad[...] = adapter_scale * dot_tn(d_low, g[...])
+
+
+def after(array, *gates):
+    return lax.optimization_barrier((array,) + gates)[0] if gates else array
 
 
 def swap_tensor(array):
@@ -479,45 +526,67 @@
     for rx in (0, 1):
         for rc in (0, 1):
             for rh in (0, 1):
-                low = (rc ^ cb) * 2 + (rh ^ (zb & rx))
+                low = (rc ^ (cb & rx)) * 2 + (rh ^ (zb & rx))
                 actual.append((rx ^ xb) * 4 + low)
                 in_stack.append((rx ^ flip) * 4 + low)
     for bc in (0, 1):
         for bh in (0, 1):
-            inner.append((bc ^ cb) * 2 + (bh ^ (zb & flip)))
+            inner.append((bc ^ (cb & flip)) * 2 + (bh ^ (zb & flip)))
     info = jnp.stack([me, ctx, tens, flip, *actual, *in_stack, *inner]).astype(jnp.int32)
 
     core_route = [(0, 1), (1, 0), (2, 3), (3, 2)]
     x_route = [(0, 2), (2, 0), (1, 3), (3, 1)]
     z_route = [(i, i ^ 1) for i in range(pieces)]
-
-    def fetch(shard, axis):
-        if not special:
-            return [lax.all_gather(shard, "dp", axis=axis, tiled=True)]
+    gates = []
+
+    def wait(*values):
+        gates[:] = values
+
+    def begin(axis, route, array):
+        return lax.ppermute(after(array, *gates), axis, route)
+
+    def core(array):
+        return begin("dp", core_route, array)
+
+    def over_x(array):
+        return begin("dp", x_route, array)
+
+    def over_z(array):
+        return begin("ctx", z_route, array)
+
+    def over_y(array):
+        return begin("tensor", [(0, 1), (1, 0)], array)
+
+    def tiles_beside(array):
+        tiles = array.reshape(-1, TILE, array.shape[1])
+        return jnp.concatenate([tiles[i] for i in range(tiles.shape[0])], axis=1)
+
+    def mixer_piece(k):
+        at = slice(k * half // 2, (k + 1) * half // 2)
+        return jnp.concatenate([mine(in_weight[:, :, at], 1), tiles_beside(mine(out_weight[at], 1))[None]], axis=0)
+
+    def feed_piece(k):
+        low, top = FEED_CUTS[k]
+        at = slice(low * TILE, top * TILE)
+        return jnp.concatenate([mine(gateup_weight[:, :, at], 1), tiles_beside(mine(down_weight[at], 1))[None]], axis=0)
+
+    def chip_pair(array):
+        return lax.all_gather(after(array, *gates), "dp", axis_index_groups=[[0, 1], [2, 3]])
+
+    def mine(shard, axis):
         n = shard.shape[axis] // 2
-        mine = lax.dynamic_slice_in_dim(shard, zb * n, n, axis)
-        over_x = lax.ppermute(mine, "dp", x_route)
-        over_z = lax.ppermute(over_x, "ctx", z_route)
-        return [
-            shard,
-            lax.ppermute(shard, "dp", core_route),
-            over_x,
-            over_z,
-            lax.ppermute(over_x, "dp", core_route),
-            lax.ppermute(over_z, "dp", core_route),
-        ]
-
-    x_got = swap_tensor(block_input)
-    in_parts = fetch(in_weight, 1)
-    out_parts = fetch(out_weight, 1)
-    if special:
-        n = width // 8
-        cuts = ((0, 2 * n), (2 * n, 4 * n), (4 * n, 5 * n), (5 * n, 6 * n), (6 * n, 7 * n), (7 * n, 8 * n))
-    else:
-        cuts = ((0, width),)
-
-    table = jnp.concatenate([deal_order[0], seq_lengths, seq_adapter])
-    table = lax.all_gather(table, "dp", axis=0, tiled=False)
+        return lax.dynamic_slice_in_dim(shard, zb * n, n, axis)
+
+    numbers = jnp.concatenate([deal_order[0], seq_lengths, seq_adapter])
+    digits = jnp.concatenate([numbers // 64, numbers % 64]).astype(bf16)
+    x_blocks = block_input.reshape(groups, sub, half)
+    g_blocks = cotangent.reshape(groups, sub, half)
+    digit_rows = jnp.zeros((groups, 2, half), bf16).at[0, 0, : digits.shape[0]].set(digits)
+    edges = jnp.concatenate([x_blocks[:, :2], g_blocks[:, :2], x_blocks[:, sub - 2 :], digit_rows], axis=1)
+
+    all_edges = lax.all_gather(edges, "dp", axis=0, tiled=False)
+    digits = all_edges[:, 0, 6, : 2 * numbers.shape[0]].astype(jnp.int32)
+    table = digits[:, : numbers.shape[0]] * 64 + digits[:, numbers.shape[0] :]
     dims = (groups, seqs, sub, nb, rows, tok_count, group_tokens)
     per_chunk = lambda c, *_: (c, 0, 0)
     mask, one, two = call(
@@ -528,10 +597,6 @@
             ((CHUNKS, rows, rows), bf16, (None, rows, rows), per_chunk),
         ],
     )
-    x_blocks = block_input.reshape(groups, sub, half)
-    g_blocks = cotangent.reshape(groups, sub, half)
-    edges = jnp.concatenate([x_blocks[:, :2], g_blocks[:, :2], x_blocks[:, sub - 2 :]], axis=1)
-    all_edges = lax.all_gather(edges, "dp", axis=0, tiled=False)
     first_heads, last_tails, next_near, prev_near = call(
         functools.partial(edges_kernel, groups), (1,), (table, info), [(all_edges, None, None)],
         [
@@ -541,8 +606,18 @@
             ((groups, 2, half), bf16, None, None),
         ],
     )
-    from_next = lax.ppermute(first_heads, "ctx", [(i + 1, i) for i in range(pieces - 1)])
-    from_prev = lax.ppermute(last_tails, "ctx", [(i, i + 1) for i in range(pieces - 1)])
+    if special:
+        in_own = chip_pair(in_weight)
+        mixer_x, mixer_z, mixer_xc, mixer_zc = ([None] * 2 for _ in range(4))
+        feed_x, feed_z, feed_xc, feed_zc = ([None] * len(FEED_CUTS) for _ in range(4))
+        mixer_packed = [mixer_piece(k) for k in range(2)]
+        feed_packed = [feed_piece(k) for k in range(len(FEED_CUTS))]
+    wait(all_edges)
+    x_got = [over_y(block_input[:span]), None]
+    if special:
+        mixer_x[0] = over_x(mixer_packed[0])
+    from_next = begin("ctx", [(i + 1, i) for i in range(pieces - 1)], first_heads)
+    from_prev = begin("ctx", [(i, i + 1) for i in range(pieces - 1)], last_tails)
     deal_all = table[:, :groups]
     at_end = (deal_all[:, groups - 1] == me)[:, None, None]
     at_start = (deal_all[:, 0] == me)[:, None, None]
@@ -552,10 +627,23 @@
     halo_g = jnp.concatenate([jnp.zeros_like(prev_rows), next_rows[:, 2:]], axis=1)
     halo_own = jnp.stack([halo_x, halo_g]).reshape(2, CHUNKS, 4 * nb, half)
     halo_own = jnp.pad(halo_own, ((0, 0), (0, 0), (0, halo - 4 * nb), (0, 0)))
-    halo_got = swap_tensor(halo_own)
-    g_got = swap_tensor(cotangent)
-    gu_parts = fetch(gateup_weight, 1)
-    down_parts = fetch(down_weight, 1)
+    stage = [from_next, from_prev, x_got[0]] + ([mixer_x[0], in_own, mixer_packed[1]] if special else [])
+    wait(*stage)
+    halo_got = over_y(halo_own)
+    x_got[1] = over_y(block_input[span:])
+    stage = [halo_got, x_got[1]]
+    if special:
+        mixer_x[1], mixer_z[0], mixer_xc[0] = over_x(mixer_packed[1]), over_z(mixer_x[0]), core(mixer_x[0])
+        out_own = chip_pair(out_weight)
+        stage += [mixer_x[1], mixer_z[0], mixer_xc[0], out_own, feed_packed[0]]
+    wait(*stage)
+    g_got = [over_y(cotangent[:span]), None]
+    stage = [g_got[0]]
+    if special:
+        feed_x[0], mixer_z[1] = over_x(feed_packed[0]), over_z(mixer_x[1])
+        mixer_xc[1], mixer_zc[0] = core(mixer_x[1]), core(mixer_z[0])
+        gu_own = chip_pair(gateup_weight)
+        stage += [feed_x[0], mixer_z[1], mixer_xc[1], mixer_zc[0], feed_packed[1]]
 
     gain_one, gain_two = mixer_gain[None, :].astype(f32), ffn_gain[None, :].astype(f32)
     ext_one, ext_two = width + rank, width + 2 * rank
@@ -564,13 +652,16 @@
         return (array, (None,) + array.shape[1:], lambda c, *_: (c, 0, 0))
 
     def joined_inputs(own, got, which):
-        def rows_of(array):
-            return (array, (span, half), lambda c, *_: (c, 0))
-
         def halo_of(array):
             return (array, (None, None, halo, half), lambda c, *_: (which, c, 0, 0))
 
-        return [rows_of(own), rows_of(got), halo_of(halo_own), halo_of(halo_got)]
+        return [
+            (own, (span, half), lambda c, *_: (c, 0)),
+            (got[0], None, None),
+            (got[1], None, None),
+            halo_of(halo_own),
+            halo_of(halo_got),
+        ]
 
     x_full, lhs_one, scale = call(
         input_kernel, (CHUNKS,), (info,),
@@ -587,6 +678,85 @@
             pltpu.VMEM((1, width), f32),
         ],
     )
+    wait(*stage, lhs_one)
+    g_got[1] = over_y(cotangent[span:])
+    stage = [g_got[1]]
+    if special:
+        n = width // 8
+        cuts = ((0, 2 * n), (2 * n, 4 * n), (4 * n, 5 * n), (5 * n, 6 * n), (6 * n, 7 * n), (7 * n, 8 * n))
+        mixer_zc[1] = core(mixer_z[1])
+        feed_x[1], feed_z[0], feed_xc[0] = over_x(feed_packed[1]), over_z(feed_x[0]), core(feed_x[0])
+        stage += [feed_x[1], feed_z[0], feed_xc[0], feed_packed[2]]
+        mixer_inputs = lambda: (
+            [(in_own, (2, 3, in_own.shape[2], TILE), lambda h, *_: (0, 0, 0, h)),
+             (out_own, (2, TILE, out_own.shape[2]), lambda h, *_: (0, h, 0))]
+            + [(w, (4, TILE, TILE), (lambda h, *_: (0, 0, jnp.minimum(h, 1))) if i == 0 else (lambda h, *_: (0, 0, jnp.maximum(h - 2, 0))))
+               for part in (mixer_x, mixer_z, mixer_xc, mixer_zc) for i, w in enumerate(part)]
+        )
+    else:
+        cuts = ((0, width),)
+        in_parts = [lax.all_gather(in_weight, "dp", axis=1, tiled=True)]
+        out_parts = [lax.all_gather(out_weight, "dp", axis=1, tiled=True)]
+        gu_parts = [lax.all_gather(gateup_weight, "dp", axis=1, tiled=True)]
+        down_parts = [lax.all_gather(down_weight, "dp", axis=1, tiled=True)]
+        mixer_inputs = lambda: [columns(in_parts[0]), row_tiles(out_parts[0])]
+
+    def picked(array, c):
+        return (array, (None,) + array.shape[1:], lambda *_: (c, 0, 0))
+
+    def columns(array):
+        return (array, array.shape[:-1] + (TILE,), lambda h, *_: (0,) * (array.ndim - 1) + (h,))
+
+    def row_tiles(array):
+        lead = array.ndim - 2
+        return (array, array.shape[:lead] + (TILE, array.shape[-1]), lambda h, *_: (0,) * lead + (h, 0))
+
+    def feed_step(k):
+        count = len(FEED_CUTS)
+        if k < count:
+            feed_x[k] = over_x(feed_packed[k])
+            stage.extend([feed_x[k]] + feed_packed[k + 1 : k + 2])
+        if 0 <= k - 1 < count:
+            feed_z[k - 1], feed_xc[k - 1] = over_z(feed_x[k - 1]), core(feed_x[k - 1])
+            stage.extend([feed_z[k - 1], feed_xc[k - 1]])
+        if 0 <= k - 2 < count:
+            feed_zc[k - 2] = core(feed_z[k - 2])
+            stage.append(feed_zc[k - 2])
+
+    mixer_steps = half // TILE
+    feed_steps = hidden_units // TILE
+    column_out = lambda h, *_: (0, h)
+    row_halves = (rows // 32 * 16, rows - rows // 32 * 16)
+    chunks = []
+    for c in range(CHUNKS):
+        gate_b, gate_c, values, conv, gated, *part = call(
+            functools.partial(mixer_kernel, cuts), (mixer_steps,), (),
+            [picked(lhs_one, c), picked(one, c), picked(two, c), columns(conv_taps), columns(in_expand), row_tiles(out_shrink)]
+            + mixer_inputs(),
+            [((rows, half), f32, (rows, TILE), column_out)] * 4
+            + [((rows, half), bf16, (rows, TILE), column_out)]
+            + [((n, ext_one), bf16, None, None) for n in row_halves],
+            [pltpu.VMEM((rows, ext_one), f32)],
+            flops=2 * rows * half * ext_one * 4,
+        )
+        chunks.append(dict(b=gate_b, c=gate_c, v=values, conv=conv, gated=gated, part=part))
+        if c == 0:
+            wait(*stage, *part)
+            chunks[0]["got"] = [over_y(part[0]), None]
+            stage = [chunks[0]["got"][0]]
+            if special:
+                feed_step(2)
+                down_own = chip_pair(down_weight)
+    wait(*stage, *chunks[1]["part"])
+    chunks[0]["got"][1] = over_y(chunks[0]["part"][1])
+    stage = [chunks[0]["got"][1]]
+    if special:
+        feed_step(3)
+    wait(*stage)
+    chunks[1]["got"] = [over_y(chunks[1]["part"][0]), None]
+    stage = [chunks[1]["got"][0]]
+    if special:
+        feed_step(4)
     (glhs,) = call(
         cotangent_kernel, (CHUNKS,), (info,),
         joined_inputs(cotangent, g_got, 1) + [(down_adapter_expand, None, None), stacked(mask, rank)],
@@ -594,42 +764,33 @@
         [pltpu.VMEM((rows, width), bf16), pltpu.VMEM((rank, width), bf16)],
     )
 
-    def picked(array, c):
-        return (array, (None,) + array.shape[1:], lambda *_: (c, 0, 0))
-
-    def columns(array):
-        return (array, array.shape[:-1] + (TILE,), lambda h, *_: (0,) * (array.ndim - 1) + (h,))
-
-    def row_tiles(array):
-        return (array, (TILE, array.shape[1]), lambda h, *_: (h, 0))
-
-    mixer_steps = half // TILE
-    feed_steps = hidden_units // TILE
-    column_out = lambda h, *_: (0, h)
-    chunks = []
-    for c in range(CHUNKS):
-        gate_b, gate_c, values, conv, gated, part = call(
-            functools.partial(mixer_kernel, cuts), (mixer_steps,), (),
-            [picked(lhs_one, c), picked(one, c), picked(two, c), columns(conv_taps), columns(in_expand), row_tiles(out_shrink)]
-            + [columns(w) for w in in_parts]
-            + [row_tiles(w) for w in out_parts],
-            [((rows, half), f32, (rows, TILE), column_out)] * 4
-            + [((rows, half), bf16, (rows, TILE), column_out), ((rows, ext_one), bf16, None, None)],
-            [pltpu.VMEM((rows, ext_one), f32)],
-            flops=2 * rows * half * ext_one * 4,
-        )
-        chunks.append(dict(b=gate_b, c=gate_c, v=values, conv=conv, gated=gated, part=part))
-    for c in chunks:
-        c["got"] = swap_tensor(c["part"])
+    wait(*stage, glhs)
+    chunks[1]["got"][1] = over_y(chunks[1]["part"][1])
+    stage = []
+    if special:
+        feed_step(5)
+        wait(*stage)
+        stage = []
+        feed_step(6)
+        wait(*stage)
+        feed_step(7)
+        whole = [(gu_own, (2, 2, gu_own.shape[2], TILE), lambda h, *_: (0, 0, 0, h)),
+                 (down_own, (2, TILE, down_own.shape[2]), lambda h, *_: (0, h, 0))]
+        feed_inputs = whole + [
+            (w, (3, TILE, TILE), lambda h, *_, low=low, top=top: (0, 0, jnp.clip(h - low, 0, top - low - 1)))
+            for part in (feed_x, feed_z, feed_xc, feed_zc)
+            for w, (low, top) in zip(part, FEED_CUTS)
+        ]
+    else:
+        feed_inputs = [columns(gu_parts[0]), row_tiles(down_parts[0])]
 
     for i, c in enumerate(chunks):
         f_part, d_own, d_send, hidden, lhs_two, out_low, grads = call(
             functools.partial(feed_kernel, cuts, span), (feed_steps,), (info,),
-            [picked(x_full, i), (c["part"], None, None), (c["got"], None, None), picked(glhs, i), picked(mask, i),
+            [picked(x_full, i)] + [(w, None, None) for w in (*c["part"], *c["got"])] + [picked(glhs, i), picked(mask, i),
              (gain_two, None, None), (output_adapter_expand, None, None), (ffn_shrink, None, None),
              columns(ffn_expand), row_tiles(down_shrink)]
-            + [columns(w) for w in gu_parts]
-            + [row_tiles(w) for w in down_parts],
+            + feed_inputs,
             [
                 ((rows, ext_two), bf16, None, None),
                 ((span, half + rank), bf16, None, None),
@@ -645,29 +806,80 @@
                 pltpu.VMEM((width, 2 * rank), bf16),
                 pltpu.VMEM((rank, width), bf16),
                 pltpu.VMEM((1, width), f32),
-            ],
+            ]
+            + ([pltpu.VMEM((4, 3, TILE, TILE), bf16)] if special else []),
             flops=2 * rows * hidden_units * ext_two * 6,
         )
         c.update(f_own=f_part, d_own=d_own, d_send=d_send, hidden=hidden, lhs=lhs_two, low=out_low, feed_grads=grads)
+    def summed(name):
+        return sum(c[name] for c in chunks).astype(bf16)
+
+    def joined(own, got, axis):
+        first = jnp.where(tens == 0, own, got)
+        second = jnp.where(tens == 0, got, own)
+        return jnp.concatenate([first, second], axis=axis)
+
+    def take(array, i):
+        return lax.dynamic_index_in_dim(array, i, 0, keepdims=False)
+
+    def add(*terms):
+        return sum(t.astype(f32) for t in terms).astype(bf16)
+
+    core_bit, x_bit = me % 2, me // 2
+    shifts = [[(i, (i + k) % pieces) for i in range(pieces)] for k in range(1, pieces)]
+
+    def cut(arrays):
+        return jnp.concatenate([a.reshape(-1, half) for a in arrays], axis=0).reshape(2, 2, pieces, -1, half)
+
+    def scatter_core(total):
+        return add(take(total, core_bit), lax.ppermute(take(total, 1 - core_bit), "dp", core_route))
+
+    def scatter_x(total):
+        return add(take(total, x_bit), lax.ppermute(take(total, 1 - x_bit), "dp", x_route))
+
+    def scatter_z(total):
+        sent = [lax.ppermute(take(total, (ctx + k) % pieces), "ctx", route) for k, route in enumerate(shifts, 1)]
+        return add(take(total, ctx), *sent)
+
+    def gather_z(total):
+        got = [total] + [lax.ppermute(total, "ctx", route) for route in shifts]
+        total = jnp.zeros((pieces,) + total.shape, bf16)
+        for k, piece in enumerate(got):
+            total = lax.dynamic_update_index_in_dim(total, piece, (ctx + pieces - k) % pieces, 0)
+        return total
+
+    def gather_pair(total, route, bit):
+        got = lax.ppermute(total, "dp", route)
+        return jnp.where(bit == 0, jnp.stack([total, got]), jnp.stack([got, total]))
+
+    def gather_chip(total):
+        return gather_pair(gather_pair(total, x_route, x_bit), core_route, core_bit)
+
+    def both_halves(total, h):
+        return total[:, : 2 * h].reshape(4 * pieces, 2, h, half).transpose(0, 2, 1, 3).reshape(-1, width)
+
+    def plain(*arrays):
+        return lax.psum(arrays, ("dp", "ctx"))
+
     for c in chunks:
         c["f_got"] = swap_tensor(c["f_own"])
-    for c in chunks:
-        c["d_got"] = swap_tensor(c["d_send"])
-
-    sent = half + 2 * rank
+    feed = summed("feed_grads")
+    if special:
+        feed_sum = scatter_core(cut([after(feed, chunks[0]["f_got"])]))
     for i, c in enumerate(chunks):
-        n_own, n_send, grad_hidden, ffn_grad, second_grad, grads = call(
+        f_got = after(c["f_got"], feed_sum) if special and i == 1 else c["f_got"]
+        n_own, n_send, n_rank, grad_hidden, ffn_grad, second_grad, grads = call(
             functools.partial(back_kernel, cuts, span), (mixer_steps,), (info,),
-            [(c["f_own"], None, None), (c["f_got"], None, None), (c["hidden"], None, None), picked(glhs, i),
+            [(c["f_own"], None, None), (f_got, None, None), (c["hidden"], None, None), picked(glhs, i),
              (c["lhs"], None, None), (c["low"], None, None), picked(lhs_one, i), picked(mask, i),
              (gain_two, None, None), (output_adapter_expand, None, None), (ffn_shrink, None, None),
              picked(one, i), picked(two, i), columns(conv_taps), columns(in_expand), row_tiles(out_shrink),
              columns(c["b"]), columns(c["c"]), columns(c["v"]), columns(c["conv"]), columns(c["gated"])]
-            + [columns(w) for w in in_parts]
-            + [row_tiles(w) for w in out_parts],
+            + mixer_inputs(),
             [
-                ((span, sent), bf16, None, None),
-                ((span, sent), bf16, None, None),
+                ((span, half), bf16, None, None),
+                ((span, half), bf16, None, None),
+                ((span, 2 * rank), bf16, None, None),
                 ((rows, width), f32, None, None),
                 ((2 * rank, half), f32, None, None),
                 ((rank, half), f32, None, None),
@@ -682,75 +894,94 @@
             ],
             flops=2 * rows * half * ext_one * 4,
         )
-        c.update(n_own=n_own, n_send=n_send, gh=grad_hidden, ffn_grad=ffn_grad, second_grad=second_grad, mixer_grads=grads)
+        c.update(n_own=n_own, n_send=n_send, n_rank=n_rank, gh=grad_hidden, ffn_grad=ffn_grad, second_grad=second_grad, mixer_grads=grads)
+        c["rank_got"] = swap_tensor(n_rank)
+        c["n_got"] = swap_tensor(after(n_send, c["rank_got"]))
+        if special:
+            feed_sum = scatter_x(after(feed_sum, n_rank)) if i == 0 else scatter_z(after(feed_sum, n_rank))
     for c in chunks:
-        c["n_got"] = swap_tensor(c["n_send"])
+        c["d_got"] = swap_tensor(after(c["d_send"], chunks[0]["n_rank"]))
 
     block = half // 4
     in_half = lambda i, info: (0, info[INNER + i])
     in_full = lambda i, info: (0, info[3] * 4 + info[INNER + i])
+    whole_block = lambda i, info: (0, 0)
+    grad_out = ((rank, half), f32, (rank, block), lambda i, info: (0, i))
     for k, c in enumerate(chunks):
         in_stack_full = lambda i, info, k=k: (k, 0, info[3] * 4 + info[INNER + i])
-        tail = (span, rank)
-        c["out"], c["grad"], c["in_grad"], c["down_grad"] = call(
+        masks = (mask, (None, span, rank), lambda i, info, k=k: (k, 0, 0))
+        ranks = [(c[name], (span, 2 * rank), whole_block) for name in ("n_rank", "rank_got")]
+        d_got = after(c["d_got"], chunks[1]["n_rank"])
+        c["out"], c["down_grad"] = call(
+            output_kernel, (4,), (info,),
+            [
+                (c["d_own"], (span, block), in_half),
+                (d_got, (span, block), in_half),
+                (c["d_own"], (span, rank), lambda i, info: (0, half // rank)),
+                (d_got, (span, rank), lambda i, info: (0, half // rank)),
+                (c["hidden"], (span, block), in_full),
+                masks,
+                (glhs, (None, span, block), in_stack_full),
+                (down_adapter_expand, (rank, block), lambda i, info: (0, info[2] * 4 + i)),
+            ],
+            [((span, half), bf16, (span, block), lambda i, info: (0, i)), grad_out],
+        )
+        (c["in_grad"],) = call(
+            rank_kernel, (4,), (info,), ranks + [masks, (lhs_one, (None, span, block), in_stack_full)], [grad_out]
+        )
+        (c["grad"],) = call(
             functools.partial(final_kernel, width), (4,), (info,),
-            [
-                (c["n_own"], (span, block), in_half),
-                (c["n_got"], (span, block), in_half),
-                (c["n_own"], (span, 2 * rank), lambda i, info: (0, half // (2 * rank))),
-                (c["n_got"], (span, 2 * rank), lambda i, info: (0, half // (2 * rank))),
-                (c["d_own"], (span, block), in_half),
-                (c["d_got"], (span, block), in_half),
-                (c["d_own"], tail, lambda i, info: (0, half // rank)),
-                (c["d_got"], tail, lambda i, info: (0, half // rank)),
-                (c["hidden"], (span, block), in_full),
+            [(c["n_own"], (span, block), in_half), (c["n_got"], (span, block), in_half)]
+            + ranks
+            + [
                 (c["gh"], (span, block), in_full),
                 (x_full, (None, span, block), in_stack_full),
-                (lhs_one, (None, span, block), in_stack_full),
-                (lhs_one, (None,) + tail, lambda i, info, k=k: (k, 0, width // rank)),
+                (lhs_one, (None, span, rank), lambda i, info, k=k: (k, 0, width // rank)),
                 (scale, (None, span, 128), lambda i, info, k=k: (k, 0, 0)),
-                (mask, (None,) + tail, lambda i, info, k=k: (k, 0, 0)),
-                (glhs, (None, span, block), in_stack_full),
+                masks,
                 (gain_one, (1, block), lambda i, info: (0, info[2] * 4 + i)),
                 (input_adapter_shrink, (block, rank), lambda i, info: (info[2] * 4 + i, 0)),
-                (down_adapter_expand, (rank, block), lambda i, info: (0, info[2] * 4 + i)),
             ],
-            [
-                ((span, half), bf16, (span, block), lambda i, info: (0, i)),
-                ((span, half), f32, (span, block), lambda i, info: (0, i)),
-                ((rank, half), f32, (rank, block), lambda i, info: (0, i)),
-                ((rank, half), f32, (rank, block), lambda i, info: (0, i)),
-            ],
+            [((span, half), f32, (span, block), lambda i, info: (0, i))],
         )
     block_output = jnp.concatenate([c["out"] for c in chunks], axis=0)
     input_grad = jnp.concatenate([c["grad"] for c in chunks], axis=0)
 
-    def summed(name):
-        return sum(c[name] for c in chunks).astype(bf16)
-
-    def reduced(*parts):
-        return lax.psum(parts, ("dp", "ctx"))
-
-    def joined(part):
-        got = swap_tensor(part)
-        first = jnp.where(tens == 0, part, got)
-        second = jnp.where(tens == 0, got, part)
-        return jnp.concatenate([first, second], axis=1).astype(f32)
-
-    feed, ffn_grad, second_grad, mixer, in_grad, down_grad = reduced(
-        summed("feed_grads"), summed("ffn_grad"), summed("second_grad"), summed("mixer_grads"), summed("in_grad"), summed("down_grad")
-    )
+    if special:
+        early_halves, early_others = [summed("ffn_grad"), summed("second_grad")], [summed("mixer_grads")]
+        late_halves = [summed("in_grad"), summed("down_grad")]
+        early = jnp.concatenate([cut(early_halves), cut(early_others)], axis=3)
+        early = scatter_z(scatter_x(scatter_core(early)))
+        late = scatter_z(scatter_x(scatter_core(cut(late_halves))))
+        h = 3 * rank * half // (4 * pieces * half)
+        early = jnp.concatenate([joined(early[:h], swap_tensor(early[:h]), 0), early[h:]], axis=0)
+        late = joined(late, swap_tensor(late), 0)
+        feed = gather_chip(gather_z(feed_sum)).reshape(feed.shape)
+        early = gather_chip(gather_z(early)).reshape(4 * pieces, -1, half)
+        late = gather_chip(gather_z(late)).reshape(4 * pieces, -1, half)
+        both = both_halves(early, h)
+        ffn_grad, second_grad = both[: 2 * rank], both[2 * rank :]
+        mixer = early[:, 2 * h :].reshape(4, rank, half)
+        both = both_halves(late, late.shape[1] // 2)
+        in_grad, down_grad = both[:rank], both[rank:]
+    else:
+        feed, mixer, ffn_grad, second_grad, in_grad, down_grad = plain(
+            feed, summed("mixer_grads"), summed("ffn_grad"), summed("second_grad"), summed("in_grad"), summed("down_grad")
+        )
+        ffn_grad, second_grad, in_grad, down_grad = (
+            joined(v, swap_tensor(v), 1) for v in (ffn_grad, second_grad, in_grad, down_grad)
+        )
     return (
         block_output,
         input_grad,
-        joined(in_grad).T,
+        in_grad.astype(f32).T,
         mixer[:3].astype(f32),
         mixer[3].astype(f32).T,
-        joined(second_grad),
-        joined(ffn_grad).T,
+        second_grad.astype(f32),
+        ffn_grad.astype(f32).T,
         feed[1:].astype(f32),
         feed[0].astype(f32).T,
-        joined(down_grad),
+        down_grad.astype(f32),
     )
 
 

time: 760 us -> 668 us (0.88)
  waiting for transfers between devices: 381 us -> 140 us
  starting transfers between devices: 34.8 us -> 87.5 us
  Pallas kernels: 253 us -> 301 us
  local copies, waits for them, and re-layouts: 26.5 us -> 63.6 us
  other arithmetic: 27.8 us -> 47.7 us
    psum x1 -> x0, waiting for transfers between devices: 110 us -> none  [reduced(): return lax.psum(parts, ('dp', 'ctx'))]
    ppermute x22 -> x73, waiting for transfers between devices: 210 us -> 123 us  [the longest x43 91.9 us: begin(): return lax.ppermute(after(array, *gates), axis, route)]
    ppermute x22 -> x73, starting transfers between devices: 17.5 us -> 76.7 us  [the longest x43 38.2 us: begin(): return lax.ppermute(after(array, *gates), axis, route)]
    pallas_call x12 -> x16, Pallas kernels: 253 us -> 301 us  [call(): pl.pallas_call(kernel, grid_spec=pltpu.PrefetchScalarGridSpec(num_scalar_...]
    ppermute x15 -> x10, waiting for transfers between devices: 59.7 us -> 16.1 us  [swap_tensor(): return lax.ppermute(array, 'tensor', [(0, 1), (1, 0)])]
    dynamic_update_slice x0 -> x10, local copies, waits for them, and re-layouts: none -> 14.5 us  [gather_z(): lax.dynamic_update_index_in_dim(total, piece, (ctx + pieces - k) % pieces...]
    slice x1 -> x17, local copies, waits for them, and re-layouts: 0.9 us -> 11.9 us  [the longest x2 5.72 us: feed_piece(): gateup_weight[:, :, at]]
    select_n x4 -> x11, other arithmetic: 3.12 us -> 12.7 us  [the longest x9 12.7 us: gather_pair(): return jnp.where(bit == 0, jnp.stack([total, got]), jnp.stack([got, total]))]
  transfers between devices with their start and end apart: 38 -> 87, of which waited for: 17 -> 28; matrix products, arithmetic and copies ran while one was open for 4% -> 13% of each run, Pallas kernels for 32% -> 45%
where the time goes in v3:
time: 668 us; the launch traced here: 663 us
  Pallas kernels  301 us (45%)
  waiting for transfers between devices  140 us (21%)
  starting transfers between devices  87.5 us (13%)
  local copies, waits for them, and re-layouts  63.6 us (10%)
  other arithmetic  47.7 us (7%)
  between operations  15.5 us (2%)
  blocking collectives  7.19 us (1%)
    pallas_call x16, Pallas kernels, call(): pl.pallas_call(kernel, grid_spec=pltpu.PrefetchScalarGridSpec(num_scalar_...  301 us
    ppermute x43, waiting for transfers between devices, begin(): return lax.ppermute(after(array, *gates), axis, route)  91.9 us
    ppermute x43, starting transfers between devices, begin(): return lax.ppermute(after(array, *gates), axis, route)  38.2 us
    unnamed x141, local copies, waits for them, and re-layouts  20.4 us
    ppermute x9, waiting for transfers between devices, gather_z(): got = [total] + [lax.ppermute(total, 'ctx', route) for route in shifts]  16.5 us
    ppermute x10, waiting for transfers between devices, swap_tensor(): return lax.ppermute(array, 'tensor', [(0, 1), (1, 0)])  16.1 us
    ppermute x9, starting transfers between devices, scatter_z(): lax.ppermute(take(total, (ctx + k) % pieces), 'ctx', route)  15.5 us
    dynamic_update_slice x10, local copies, waits for them, and re-layouts, gather_z(): lax.dynamic_update_index_in_dim(total, piece, (ctx + pieces - k) % pieces...  14.5 us
  transfers between devices with their start and end apart: 87, of which 28 were waited for; matrix products, arithmetic and copies ran while one was open for 13% of the time, Pallas kernels for 45%

profile of v3, /device:TPU:0, one launch (start us, length us, event | category | flops | bytes accessed | tf_op | source)
XLA Modules:
  0.0 662.8 jit_solution(9193894620356225492)
XLA Ops:
  9.2 7.2 %all-gather = bf16[16,8,1024]{2,1,0:T(8,128)(2,1)S(1)} all-gather(bf16[4,8,1024]{2,1,0:T(8,128)(2,1)S(1)} %pad_maximum_fusion.13), channel_id=2, replica_groups=mesh['dp'=4,'ctx'=4,'tensor'=2] {'dp'}, dimensions={0}, use_global_device_ids=true | all-gather | bytes 327680 | tf_op jit(solution)/shard_map/all_gather | solution.py:587
  29.0 4.5 collective-permute-start.2
  35.7 6.8 %collective-permute-done.got_first = bf16[384,1024]{1,0:T(8,128)(2,1)} collective-permute-done((bf16[384,1024]{1,0:T(8,128)(2,1)}, bf16[384,1024]{1,0:T(8,128)(2,1)}, u32[]{:S(2)}, u32[]{:S(2)}) %collective-permute-start) | collective-permute-done | bytes 786464 | tf_op jit(solution)/shard_map/ppermute | solution.py:546
  47.8 4.6 fusion.33
  60.3 18.4 %collective-permute-done.5.halo_got = bf16[2,2,16,1024]{3,2,1,0:T(8,128)(2,1)S(1)} collective-permute-done((bf16[2,2,16,1024]{3,2,1,0:T(8,128)(2,1)S(1)}, bf16[2,2,16,1024]{3,2,1,0:T(8,128)(2,1)S(1)}, u32[]{:S(2)}, u32[]{:S(2)}) %collective-permute-start.5) | collective-permute-done | bytes 131104 | tf_op jit(solution)/shard_map/ppermute | solution.py:546
  88.4 11.7 %shard_map.269 = (bf16[2,400,2048]{2,1,0:T(8,128)(2,1)}, bf16[2,400,2176]{2,1,0:T(8,128)(2,1)}, f32[2,400,128]{2,1,0:T(8,128)}) custom-call(s32[24]{0:T(128)} %stack.210.info, bf16[768,1024]{1,0:T(8,128)(2,1)} %own.2, bf16[384,1024]{1,0:T(8,128)(2,1)} %collective-permute-done.got_first, bf16[384,1024]{1,0:T(8,128)(2,1)} %collective-permute-done.4.got_second, ...), custom_call_target="tpu_custom_call" | custom-call | flops 1 | bytes 1 | tf_op jit(solution)/shard_map/pallas_call | solution.py:65
  111.6 20.3 %shard_map.270 = (f32[400,1024]{1,0:T(8,128)}, f32[400,1024]{1,0:T(8,128)}, f32[400,1024]{1,0:T(8,128)}, f32[400,1024]{1,0:T(8,128)}, bf16[400,1024]{1,0:T(8,128...) custom-call(bf16[2,400,2176]{2,1,0:T(8,128)(2,1)} %get-tuple-element.138.lhs.lhs_one.low.normed, ...), custom_call_target="tpu_custom_call" | custom-call | flops 7130316800 | bytes 1 | tf_op jit(solution)/shard_map/pallas_call | solution.py:65
  138.2 23.0 %shard_map.271 = (f32[400,1024]{1,0:T(8,128)}, f32[400,1024]{1,0:T(8,128)}, f32[400,1024]{1,0:T(8,128)}, f32[400,1024]{1,0:T(8,128)}, bf16[400,1024]{1,0:T(8,128...) custom-call(bf16[2,400,2176]{2,1,0:T(8,128)(2,1)} %get-tuple-element.138.lhs.lhs_one.low.normed, ...), custom_call_target="tpu_custom_call" | custom-call | flops 7130316800 | bytes 1 | tf_op jit(solution)/shard_map/pallas_call | solution.py:65
  167.3 15.3 %collective-permute-done.26.refs_10_ = bf16[3,256,512]{2,1,0:T(8,128)(2,1)S(1)} collective-permute-done((bf16[3,256,512]{2,1,0:T(8,128)(2,1)}, bf16[3,256,512]{2,1,0:T(8,128)(2,1)S(1)}, u32[]{:S(2)}, u32[]{:S(2)}) %collective-permute-start.26) | collective-permute-done | bytes 786464 | tf_op jit(solution)/shard_map/ppermute | solution.py:546
  190.6 5.4 shard_map.272.glhs.g
  196.0 7.4 %collective-permute-done.31.refs_11_ = bf16[3,256,512]{2,1,0:T(8,128)(2,1)S(1)} collective-permute-done((bf16[3,256,512]{2,1,0:T(8,128)(2,1)}, bf16[3,256,512]{2,1,0:T(8,128)(2,1)S(1)}, u32[]{:S(2)}, u32[]{:S(2)}) %collective-permute-start.31) | collective-permute-done | bytes 786464 | tf_op jit(solution)/shard_map/ppermute | solution.py:546
  209.1 9.9 %collective-permute-done.34.refs_7_ = bf16[3,256,256]{2,1,0:T(8,128)(2,1)S(1)} collective-permute-done((bf16[3,256,256]{2,1,0:T(8,128)(2,1)S(1)}, bf16[3,256,256]{2,1,0:T(8,128)(2,1)S(1)}, u32[]{:S(2)}, u32[]{:S(2)}) %collective-permute-start.34) | collective-permute-done | bytes 393248 | tf_op jit(solution)/shard_map/ppermute | solution.py:546
  219.0 7.6 %collective-permute-done.35.refs_12_ = bf16[3,256,512]{2,1,0:T(8,128)(2,1)S(1)} collective-permute-done((bf16[3,256,512]{2,1,0:T(8,128)(2,1)}, bf16[3,256,512]{2,1,0:T(8,128)(2,1)S(1)}, u32[]{:S(2)}, u32[]{:S(2)}) %collective-permute-start.35) | collective-permute-done | bytes 786464 | tf_op jit(solution)/shard_map/ppermute | solution.py:546
  227.8 10.5 %collective-permute-done.38.refs_13_ = bf16[3,256,256]{2,1,0:T(8,128)(2,1)} collective-permute-done((bf16[3,256,256]{2,1,0:T(8,128)(2,1)S(1)}, bf16[3,256,256]{2,1,0:T(8,128)(2,1)}, u32[]{:S(2)}, u32[]{:S(2)}) %collective-permute-start.38) | collective-permute-done | bytes 393248 | tf_op jit(solution)/shard_map/ppermute | solution.py:546
  242.1 68.4 %shard_map.273 = (bf16[400,2304]{1,0:T(8,128)(2,1)}, bf16[384,1152]{1,0:T(8,128)(2,1)}, bf16[384,1152]{1,0:T(8,128)(2,1)}, f32[400,2048]{1,0:T(8,128)}, bf16[400...) custom-call(s32[24]{0:T(128)} %stack.210.info, bf16[2,400,2048]{2,1,0:T(8,128)(2,1)} %get-tuple-element.137.x, ...), custom_call_target="tpu_custom_call" | custom-call | flops 31142707200 | bytes 1 | tf_op jit(solution)/shard_map/pallas_call | solution.py:65
  312.9 57.8 %shard_map.275 = (bf16[400,2304]{1,0:T(8,128)(2,1)}, bf16[384,1152]{1,0:T(8,128)(2,1)}, bf16[384,1152]{1,0:T(8,128)(2,1)}, f32[400,2048]{1,0:T(8,128)}, bf16[400...) custom-call(s32[24]{0:T(128)} %stack.210.info, bf16[2,400,2048]{2,1,0:T(8,128)(2,1)} %get-tuple-element.137.x, ...), custom_call_target="tpu_custom_call" | custom-call | flops 31142707200 | bytes 1 | tf_op jit(solution)/shard_map/pallas_call | solution.py:65
  370.6 3.9 add_convert_fusion
  374.6 4.0 reshape_reshape.7
  380.4 38.5 %shard_map.274 = (bf16[384,1024]{1,0:T(8,128)(2,1)}, bf16[384,1024]{1,0:T(8,128)(2,1)}, bf16[384,256]{1,0:T(8,128)(2,1)}, f32[400,2048]{1,0:T(8,128)}, f32[256,1...) custom-call(s32[24]{0:T(128)} %stack.210.info, bf16[400,2304]{1,0:T(8,128)(2,1)} %get-tuple-element.178.part, ...), custom_call_target="tpu_custom_call" | custom-call | flops 7130316800 | bytes 1 | tf_op jit(solution)/shard_map/pallas_call | solution.py:65
  420.3 6.5 collective-permute-done.49.rank_got.got
  433.4 4.6 shard_map.281
  438.0 9.6 %collective-permute-done.50.got = bf16[384,1024]{1,0:T(8,128)(2,1)} collective-permute-done((bf16[384,1024]{1,0:T(8,128)(2,1)}, bf16[384,1024]{1,0:T(8,128)(2,1)}, u32[]{:S(2)}, u32[]{:S(2)}) %collective-permute-start.50) | collective-permute-done | bytes 786464 | tf_op jit(solution)/shard_map/ppermute | solution.py:477
  447.6 6.0 shard_map.279
  453.8 39.1 %shard_map.276 = (bf16[384,1024]{1,0:T(8,128)(2,1)}, bf16[384,1024]{1,0:T(8,128)(2,1)}, bf16[384,256]{1,0:T(8,128)(2,1)}, f32[400,2048]{1,0:T(8,128)}, f32[256,1...) custom-call(s32[24]{0:T(128)} %stack.210.info, bf16[400,2304]{1,0:T(8,128)(2,1)} %get-tuple-element.190.part, ...), custom_call_target="tpu_custom_call" | custom-call | flops 7130316800 | bytes 1 | tf_op jit(solution)/shard_map/pallas_call | solution.py:65
  502.0 5.3 shard_map.277
  507.3 5.4 shard_map.278
  514.5 4.6 shard_map.282
  540.6 3.6 dynamic_update_slice.47
  579.7 6.8 %collective-permute-done.65 = bf16[4,56,1024]{2,1,0:T(8,128)(2,1)S(1)} collective-permute-done((bf16[4,56,1024]{2,1,0:T(8,128)(2,1)S(1)}, bf16[4,56,1024]{2,1,0:T(8,128)(2,1)S(1)}, u32[]{:S(2)}, u32[]{:S(2)}) %collective-permute-start.65) | collective-permute-done | bytes 458784 | tf_op jit(solution)/shard_map/ppermute | solution.py:838
  592.9 6.1 shard_map.280
  608.6 4.3 collective-permute-done.70
  612.9 6.3 collective-permute-done.71
  (439 shorter events, 213.7 us)
Async XLA Ops:
  7.2 38.4 %all-gather.10.cloned.1.call-start = ((), (), s32[]{:S(2)}) async-start(), calls=%async_computation | async-start | bytes 9437184 | tf_op jit(solution)/shard_map/all_gather | solution.py:574
  8.0 72.1 %all-gather.12.cloned.1.call-start = ((), (), s32[]{:S(2)}) async-start(), calls=%async_computation.1 | async-start | bytes 3145728 | tf_op jit(solution)/shard_map/all_gather | solution.py:574
  19.9 25.7 %collective-permute-start.3 = (bf16[4,256,512]{2,1,0:T(8,128)(2,1)}, bf16[4,256,512]{2,1,0:T(8,128)(2,1)}, u32[]{:S(2)}, u32[]{:S(2)}) collective-permute-start(bf16[4,256,512]{2,1,0:T(8,128)(2,1)} %pad_maximum_fusion.2), channel_id=1, source_target_pairs={{0,16},{16,0},{8,24},{24,8},{1,17},{17,1},{9,25},{25,9},{2,18},{18... | collective-permute-start | bytes 3145736 | tf_op jit(solution)/shard_map/ppermute | solution.py:546
  45.7 196.4 %all-gather.16.cloned.1.call-start = ((), (), s32[]{:S(2)}) async-start(), calls=%async_computation.3 | async-start | bytes 8650752 | tf_op jit(solution)/shard_map/all_gather | solution.py:574
  52.5 26.2 %collective-permute-start.7 = (bf16[4,256,512]{2,1,0:T(8,128)(2,1)}, bf16[4,256,512]{2,1,0:T(8,128)(2,1)S(1)}, u32[]{:S(2)}, u32[]{:S(2)}) collective-permute-start(bf16[4,256,512]{2,1,0:T(8,128)(2,1)} %collective-permute-done.3.refs_2_), channel_id=1, source_target_pairs={{0,2},{2,0},{4,6},{6,4},{1,3},{3,1},{5,7},{7,5},{8,10},{10,8},{12,... | collective-permute-start | bytes 3145736 | tf_op jit(solution)/shard_map/ppermute | solution.py:546
  54.2 24.6 %collective-permute-start.8 = (bf16[4,256,512]{2,1,0:T(8,128)(2,1)}, bf16[4,256,512]{2,1,0:T(8,128)(2,1)}, u32[]{:S(2)}, u32[]{:S(2)}) collective-permute-start(bf16[4,256,512]{2,1,0:T(8,128)(2,1)} %collective-permute-done.3.refs_2_), channel_id=1, source_target_pairs={{0,8},{8,0},{16,24},{24,16},{1,9},{9,1},{17,25},{25,17},{2,10},{10... | collective-permute-start | bytes 3145736 | tf_op jit(solution)/shard_map/ppermute | solution.py:546
  54.2 25.9 %collective-permute-start.6 = (bf16[4,256,512]{2,1,0:T(8,128)(2,1)}, bf16[4,256,512]{2,1,0:T(8,128)(2,1)}, u32[]{:S(2)}, u32[]{:S(2)}) collective-permute-start(bf16[4,256,512]{2,1,0:T(8,128)(2,1)} %pad_maximum_fusion.3), channel_id=1, source_target_pairs={{0,16},{16,0},{8,24},{24,8},{1,17},{17,1},{9,25},{25,9},{2,18},{18... | collective-permute-start | bytes 3145736 | tf_op jit(solution)/shard_map/ppermute | solution.py:546
  80.1 23.1 %collective-permute-start.10 = (bf16[4,256,512]{2,1,0:T(8,128)(2,1)}, bf16[4,256,512]{2,1,0:T(8,128)(2,1)S(1)}, u32[]{:S(2)}, u32[]{:S(2)}) collective-permute-start(bf16[4,256,512]{2,1,0:T(8,128)(2,1)} %collective-permute-done.6.refs_3_), channel_id=1, source_target_pairs={{0,8},{8,0},{16,24},{24,16},{1,9},{9,1},{17,25},{25,17},{2,10},{10... | collective-permute-start | bytes 3145736 | tf_op jit(solution)/shard_map/ppermute | solution.py:546
  80.1 25.8 %collective-permute-start.9 = (bf16[4,256,512]{2,1,0:T(8,128)(2,1)}, bf16[4,256,512]{2,1,0:T(8,128)(2,1)S(1)}, u32[]{:S(2)}, u32[]{:S(2)}) collective-permute-start(bf16[4,256,512]{2,1,0:T(8,128)(2,1)} %collective-permute-done.6.refs_3_), channel_id=1, source_target_pairs={{0,2},{2,0},{4,6},{6,4},{1,3},{3,1},{5,7},{7,5},{8,10},{10,8},{12,... | collective-permute-start | bytes 3145736 | tf_op jit(solution)/shard_map/ppermute | solution.py:546
  106.0 26.9 %collective-permute-start.17 = (bf16[3,256,512]{2,1,0:T(8,128)(2,1)}, bf16[3,256,512]{2,1,0:T(8,128)(2,1)}, u32[]{:S(2)}, u32[]{:S(2)}) collective-permute-start(bf16[3,256,512]{2,1,0:T(8,128)(2,1)} %collective-permute-done.13.refs_2_), channel_id=1, source_target_pairs={{0,2},{2,0},{4,6},{6,4},{1,3},{3,1},{5,7},{7,5},{8,10},{10,8},{12,... | collective-permute-start | bytes 2359304 | tf_op jit(solution)/shard_map/ppermute | solution.py:546
  106.5 26.4 %collective-permute-start.18 = (bf16[3,256,512]{2,1,0:T(8,128)(2,1)}, bf16[3,256,512]{2,1,0:T(8,128)(2,1)}, u32[]{:S(2)}, u32[]{:S(2)}) collective-permute-start(bf16[3,256,512]{2,1,0:T(8,128)(2,1)} %collective-permute-done.13.refs_2_), channel_id=1, source_target_pairs={{0,8},{8,0},{16,24},{24,16},{1,9},{9,1},{17,25},{25,17},{2,10},{10... | collective-permute-start | bytes 2359304 | tf_op jit(solution)/shard_map/ppermute | solution.py:546
  106.7 25.2 %collective-permute-start.15 = (bf16[384,1024]{1,0:T(8,128)(2,1)}, bf16[384,1024]{1,0:T(8,128)(2,1)S(1)}, u32[]{:S(2)}, u32[]{:S(2)}) collective-permute-start(bf16[384,1024]{1,0:T(8,128)(2,1)} %get-tuple-element.151), channel_id=1, source_target_pairs={{0,1},{1,0},{2,3},{3,2},{4,5},{5,4},{6,7},{7,6},{8,9},{9,8},{10,11... | collective-permute-start | bytes 2359304 | tf_op jit(solution)/shard_map/ppermute | solution.py:546
  108.2 24.7 %collective-permute-start.16 = (bf16[3,256,512]{2,1,0:T(8,128)(2,1)S(1)}, bf16[3,256,512]{2,1,0:T(8,128)(2,1)}, u32[]{:S(2)}, u32[]{:S(2)}) collective-permute-start(bf16[3,256,512]{2,1,0:T(8,128)(2,1)S(1)} %pad_maximum_fusion.5), channel_id=1, source_target_pairs={{0,16},{16,0},{8,24},{24,8},{1,17},{17,1},{9,25},{25,9},{2,18},{18... | collective-permute-start | bytes 2359304 | tf_op jit(solution)/shard_map/ppermute | solution.py:546
  132.9 109.1 %all-gather.14.cloned.1.call-start = ((), (), s32[]{:S(2)}) async-start(), calls=%async_computation.2 | async-start | bytes 17301504 | tf_op jit(solution)/shard_map/all_gather | solution.py:574
  134.8 26.4 %collective-permute-start.19 = (bf16[192,2176]{1,0:T(8,128)(2,1)S(1)}, bf16[192,2176]{1,0:T(8,128)(2,1)S(1)}, u32[]{:S(2)}, u32[]{:S(2)}) collective-permute-start(bf16[192,2176]{1,0:T(8,128)(2,1)S(1)} %copy-done.52), channel_id=1, source_target_pairs={{0,1},{1,0},{2,3},{3,2},{4,5},{5,4},{6,7},{7,6},{8,9},{9,8},{10,11... | collective-permute-start | bytes 2506760 | tf_op jit(solution)/shard_map/ppermute | solution.py:546
  135.4 25.9 %collective-permute-start.21 = (bf16[3,256,512]{2,1,0:T(8,128)(2,1)}, bf16[3,256,512]{2,1,0:T(8,128)(2,1)S(1)}, u32[]{:S(2)}, u32[]{:S(2)}) collective-permute-start(bf16[3,256,512]{2,1,0:T(8,128)(2,1)} %collective-permute-done.16.refs_3_), channel_id=1, source_target_pairs={{0,2},{2,0},{4,6},{6,4},{1,3},{3,1},{5,7},{7,5},{8,10},{10,8},{12,... | collective-permute-start | bytes 2359304 | tf_op jit(solution)/shard_map/ppermute | solution.py:546
  137.0 24.2 %collective-permute-start.22 = (bf16[3,256,512]{2,1,0:T(8,128)(2,1)}, bf16[3,256,512]{2,1,0:T(8,128)(2,1)}, u32[]{:S(2)}, u32[]{:S(2)}) collective-permute-start(bf16[3,256,512]{2,1,0:T(8,128)(2,1)} %collective-permute-done.16.refs_3_), channel_id=1, source_target_pairs={{0,8},{8,0},{16,24},{24,16},{1,9},{9,1},{17,25},{25,17},{2,10},{10... | collective-permute-start | bytes 2359304 | tf_op jit(solution)/shard_map/ppermute | solution.py:546
  137.0 24.2 %collective-permute-start.23 = (bf16[3,256,512]{2,1,0:T(8,128)(2,1)}, bf16[3,256,512]{2,1,0:T(8,128)(2,1)}, u32[]{:S(2)}, u32[]{:S(2)}) collective-permute-start(bf16[3,256,512]{2,1,0:T(8,128)(2,1)} %collective-permute-done.17.refs_8_), channel_id=1, source_target_pairs={{0,8},{8,0},{16,24},{24,16},{1,9},{9,1},{17,25},{25,17},{2,10},{10... | collective-permute-start | bytes 2359304 | tf_op jit(solution)/shard_map/ppermute | solution.py:546
  137.6 23.7 %collective-permute-start.20 = (bf16[3,256,512]{2,1,0:T(8,128)(2,1)S(1)}, bf16[3,256,512]{2,1,0:T(8,128)(2,1)}, u32[]{:S(2)}, u32[]{:S(2)}) collective-permute-start(bf16[3,256,512]{2,1,0:T(8,128)(2,1)S(1)} %copy-done.31), channel_id=1, source_target_pairs={{0,16},{16,0},{8,24},{24,8},{1,17},{17,1},{9,25},{25,9},{2,18},{18... | collective-permute-start | bytes 2359304 | tf_op jit(solution)/shard_map/ppermute | solution.py:546
  240.5 71.4 %collective-permute-start.44 = (bf16[208,2176]{1,0:T(8,128)(2,1)S(1)}, bf16[208,2176]{1,0:T(8,128)(2,1)S(1)}, u32[]{:S(2)}, u32[]{:S(2)}) collective-permute-start(bf16[208,2176]{1,0:T(8,128)(2,1)S(1)} %copy-done.49), channel_id=1, source_target_pairs={{0,1},{1,0},{2,3},{3,2},{4,5},{5,4},{6,7},{7,6},{8,9},{9,8},{10,11... | collective-permute-start | bytes 2715656 | tf_op jit(solution)/shard_map/ppermute | solution.py:546
  310.5 64.1 %collective-permute-start.42 = (bf16[400,2304]{1,0:T(8,128)(2,1)}, bf16[400,2304]{1,0:T(8,128)(2,1)}, u32[]{:S(2)}, u32[]{:S(2)}) collective-permute-start(bf16[400,2304]{1,0:T(8,128)(2,1)} %get-tuple-element.178.part), channel_id=1, source_target_pairs={{0,1},{1,0},{2,3},{3,2},{4,5},{5,4},{6,7},{7,6},{8,9},{9,8},{10,11... | collective-permute-start | bytes 5529608 | tf_op jit(solution)/shard_map/ppermute | solution.py:477
  379.6 48.0 %collective-permute-start.46 = (bf16[2,4,66,1024]{3,1,2,0:T(4,128)(2,1)S(1)}, bf16[2,4,66,1024]{3,1,2,0:T(4,128)(2,1)}, u32[]{:S(2)}, u32[]{:S(2)}) collective-permute-start(bf16[2,4,66,1024]{3,1,2,0:T(4,128)(2,1)S(1)} %bitcast.226), channel_id=1, source_target_pairs={{0,8},{8,0},{16,24},{24,16},{1,9},{9,1},{17,25},{25,17},{2,10},{10... | collective-permute-start | bytes 3244040 | tf_op jit(solution)/shard_map/ppermute | solution.py:835
  379.7 74.2 %collective-permute-start.45 = (bf16[400,2304]{1,0:T(8,128)(2,1)}, bf16[400,2304]{1,0:T(8,128)(2,1)}, u32[]{:S(2)}, u32[]{:S(2)}) collective-permute-start(bf16[400,2304]{1,0:T(8,128)(2,1)} %get-tuple-element.190.part), channel_id=1, source_target_pairs={{0,1},{1,0},{2,3},{3,2},{4,5},{5,4},{6,7},{7,6},{8,9},{9,8},{10,11... | collective-permute-start | bytes 5529608 | tf_op jit(solution)/shard_map/ppermute | solution.py:477
  429.8 23.8 %collective-permute-start.47 = (bf16[4,66,1024]{2,0,1:T(4,128)(2,1)S(1)}, bf16[4,66,1024]{2,0,1:T(4,128)(2,1)S(1)}, u32[]{:S(2)}, u32[]{:S(2)}) collective-permute-start(bf16[4,66,1024]{2,0,1:T(4,128)(2,1)S(1)} %bitcast.233), channel_id=1, source_target_pairs={{0,16},{16,0},{8,24},{24,8},{1,17},{17,1},{9,25},{25,9},{2,18},{18... | collective-permute-start | bytes 1622024 | tf_op jit(solution)/shard_map/ppermute | solution.py:838
  431.3 66.6 %collective-permute-start.43 = (bf16[384,1152]{1,0:T(8,128)(2,1)}, bf16[384,1152]{1,0:T(8,128)(2,1)S(1)}, u32[]{:S(2)}, u32[]{:S(2)}) collective-permute-start(bf16[384,1152]{1,0:T(8,128)(2,1)} %get-tuple-element.188), channel_id=1, source_target_pairs={{0,1},{1,0},{2,3},{3,2},{4,5},{5,4},{6,7},{7,6},{8,9},{9,8},{10,11... | collective-permute-start | bytes 2654216 | tf_op jit(solution)/shard_map/ppermute | solution.py:477
  432.6 67.5 %collective-permute-start.48 = (bf16[384,1152]{1,0:T(8,128)(2,1)}, bf16[384,1152]{1,0:T(8,128)(2,1)S(1)}, u32[]{:S(2)}, u32[]{:S(2)}) collective-permute-start(bf16[384,1152]{1,0:T(8,128)(2,1)} %get-tuple-element.209), channel_id=1, source_target_pairs={{0,1},{1,0},{2,3},{3,2},{4,5},{5,4},{6,7},{7,6},{8,9},{9,8},{10,11... | collective-permute-start | bytes 2654216 | tf_op jit(solution)/shard_map/ppermute | solution.py:477
  494.5 34.2 %collective-permute-start.75 = (bf16[66,1024]{1,0:T(8,128)(2,1)}, bf16[66,1024]{1,0:T(8,128)(2,1)S(1)}, u32[]{:S(2)}, u32[]{:S(2)}) collective-permute-start(bf16[66,1024]{1,0:T(8,128)(2,1)} %get-tuple-element.306), channel_id=1, source_target_pairs={{0,2},{2,4},{4,6},{6,0},{1,3},{3,5},{5,7},{7,1},{8,10},{10,12},{12... | collective-permute-start | bytes 405512 | tf_op jit(solution)/shard_map/ppermute | solution.py:841
  495.1 34.5 %collective-permute-start.76 = (bf16[66,1024]{1,0:T(8,128)(2,1)S(1)}, bf16[66,1024]{1,0:T(8,128)(2,1)S(1)}, u32[]{:S(2)}, u32[]{:S(2)}) collective-permute-start(bf16[66,1024]{1,0:T(8,128)(2,1)S(1)} %get-tuple-element.308), channel_id=1, source_target_pairs={{0,4},{2,6},{4,0},{6,2},{1,5},{3,7},{5,1},{7,3},{8,12},{10,14},{12... | collective-permute-start | bytes 405512 | tf_op jit(solution)/shard_map/ppermute | solution.py:841
  497.9 34.6 %collective-permute-start.77 = (bf16[66,1024]{1,0:T(8,128)(2,1)S(1)}, bf16[66,1024]{1,0:T(8,128)(2,1)S(1)}, u32[]{:S(2)}, u32[]{:S(2)}) collective-permute-start(bf16[66,1024]{1,0:T(8,128)(2,1)S(1)} %get-tuple-element.307), channel_id=1, source_target_pairs={{0,6},{2,0},{4,2},{6,4},{1,7},{3,1},{5,3},{7,5},{8,14},{10,8},{12,... | collective-permute-start | bytes 405512 | tf_op jit(solution)/shard_map/ppermute | solution.py:841
  525.5 45.5 %collective-permute-start.64 = (bf16[2,4,56,1024]{3,2,1,0:T(8,128)(2,1)}, bf16[2,4,56,1024]{3,2,1,0:T(8,128)(2,1)}, u32[]{:S(2)}, u32[]{:S(2)}) collective-permute-start(bf16[2,4,56,1024]{3,2,1,0:T(8,128)(2,1)} %fusion.4), channel_id=1, source_target_pairs={{0,8},{8,0},{16,24},{24,16},{1,9},{9,1},{17,25},{25,17},{2,10},{10... | collective-permute-start | bytes 2752520 | tf_op jit(solution)/shard_map/ppermute | solution.py:835
  544.3 48.5 %collective-permute-start.52 = (bf16[384,1024]{1,0:T(8,128)(2,1)}, bf16[384,1024]{1,0:T(8,128)(2,1)}, u32[]{:S(2)}, u32[]{:S(2)}) collective-permute-start(bf16[384,1024]{1,0:T(8,128)(2,1)} %get-tuple-element.219), channel_id=1, source_target_pairs={{0,1},{1,0},{2,3},{3,2},{4,5},{5,4},{6,7},{7,6},{8,9},{9,8},{10,11... | collective-permute-start | bytes 2359304 | tf_op jit(solution)/shard_map/ppermute | solution.py:477
  575.8 52.0 %collective-permute-start.82 = (bf16[2,4,66,1024]{3,1,2,0:T(4,128)(2,1)}, bf16[2,4,66,1024]{3,1,2,0:T(4,128)(2,1)}, u32[]{:S(2)}, u32[]{:S(2)}) collective-permute-start(bf16[2,4,66,1024]{3,1,2,0:T(4,128)(2,1)} %maximum_select_fusion.5), channel_id=1, source_target_pairs={{0,8},{8,0},{16,24},{24,16},{1,9},{9,1},{17,25},{25,17},{2,10},{10... | collective-permute-start | bytes 3244040 | tf_op jit(solution)/shard_map/ppermute | solution.py:852
  (122 other events, 1637.1 us)
Sparse Core Ops, SparseCore 0:
  9.6 19.4 all-gather.9
  45.8 12.6 all-gather.11
  133.0 15.4 all-gather.15
  150.0 25.4 all-gather.13

commit v4 on v3

--- a/solution.py
+++ b/solution.py
@@ -44,10 +44,12 @@
     return pl.ds(pl.multiple_of(index * width, width), width)
 
 
-def call(kernel, grid, scalars, ins, outs, scratch=(), flops=0):
+def call(kernel, grid, scalars, ins, outs, scratch=(), flops=0, aliases=None):
     in_specs = []
     for array, block, index in ins:
-        if block is None:
+        if block == "any":
+            in_specs.append(pl.BlockSpec(memory_space=pl.ANY))
+        elif block is None:
             zeros = (0,) * array.ndim
             in_specs.append(
                 pl.BlockSpec(array.shape, lambda *_, z=zeros: z, pipeline_mode=pl.Buffered(1))
@@ -72,6 +74,7 @@
             scratch_shapes=list(scratch),
         ),
         out_shape=out_shape,
+        input_output_aliases=aliases or {},
         compiler_params=pltpu.CompilerParams(
             dimension_semantics=("arbitrary",) * len(grid), vmem_limit_bytes=VMEM_BYTES
         ),
@@ -247,63 +250,97 @@
         part_second[...] = acc[cut:, :].astype(bf16)
 
 
-def feed_kernel(cuts, span, info, x, part_first, part_second, got_first, got_second, glhs, mask, gain, out_second, ffn_first, ffn_expand, down_shrink, *refs):
+def blocks_across(ref, value):
+    for i in range(value.shape[1] // 128):
+        ref[i] = value[:, i * 128 : (i + 1) * 128]
+
+
+def blocks_down(ref, value):
+    for i in range(value.shape[0] // 128):
+        ref[i] = value[i * 128 : (i + 1) * 128, :]
+
+
+def middle_kernel(info, x, part_first, part_second, got_first, got_second, mask, gain, out_second, ffn_first,
+                  hidden_ref, lhs, low_ref, both_ref, added, first_rel, second_rel, gain_rel):
+    width = x.shape[1]
+    block = width // 8
+    rank = mask.shape[1]
+    for r in range(8):
+        at = lanes_at(info[ACTUAL + r], block)
+        here = slice(r * block, (r + 1) * block)
+        first_rel[here, :] = ffn_first[at, :]
+        second_rel[:, here] = out_second[:, at]
+        gain_rel[:, here] = gain[:, at]
+    cut = part_first.shape[0]
+    for own, got, base in ((part_first, got_first, 0), (part_second, got_second, cut)):
+        both_ref[base : base + own.shape[0], :] = own[...].astype(f32) + got[...].astype(f32)
+    low = both_ref[:, width:].astype(bf16) * mask[...]
+    low_ref[...] = low
+    added[...] = dot(low, second_rel[...])
+
+    def visit(at):
+        hidden = x[at, :].astype(f32) + (both_ref[at, :width] + adapter_scale * added[at, :])
+        hidden_ref[at, :] = hidden
+        scale = lax.rsqrt(jnp.mean(hidden * hidden, axis=-1, keepdims=True) + norm_eps)
+        lhs[at, :width] = (hidden * scale * gain_rel[0:1, :]).astype(bf16)
+
+    over_row_blocks(x.shape[0], 16, visit)
+    low = dot(lhs[:, :width], first_rel[...]).astype(bf16)
+    lhs[:, width : width + rank] = low[:, :rank] * mask[...]
+    lhs[:, width + rank :] = low[:, rank:] * mask[...]
+
+
+def feed_kernel(cuts, span, info, lhs, glhs, ffn_expand, down_shrink, *refs):
     if len(cuts) == 1:
         gu_parts, down_parts, refs = [[refs[0].at[0], refs[0].at[1]]], [refs[1]], refs[2:]
+        arrived = lambda: None
     else:
         gu_parts = [[refs[0].at[k, j] for j in range(2)] for k in range(2)]
         down_parts = [refs[1].at[k] for k in range(2)]
         count = len(FEED_CUTS)
         far, refs = refs[2 : 2 + 4 * count], refs[2 + 4 * count :]
-        here, refs = refs[-1], refs[:-1]
-        for i, (low, top) in enumerate(FEED_CUTS):
-
-            @pl.when((pl.program_id(0) >= low) & (pl.program_id(0) < top))
-            def _(i=i):
-                for k in range(4):
-                    here[k] = far[k * count + i][...]
-
+        slots, sems, refs = refs[-2], refs[-1], refs[:-2]
+        step, steps = pl.program_id(0), FEED_CUTS[-1][1]
+
+        def fetch(tile):
+            for i, (low, top) in enumerate(FEED_CUTS):
+
+                @pl.when((tile >= low) & (tile < top))
+                def _(i=i, low=low):
+                    at = pl.ds(pl.multiple_of((tile - low) * TILE, TILE), TILE)
+                    for k in range(4):
+                        slot = lax.rem(tile, 2)
+                        pltpu.make_async_copy(far[k * count + i].at[:, :, at], slots.at[slot, k], sems.at[slot, k]).start()
+
+        @pl.when(step == 0)
+        def _():
+            fetch(step)
+
+        @pl.when(step + 1 < steps)
+        def _():
+            fetch(step + 1)
+
+        slot = lax.rem(step, 2)
+        here = slots.at[slot]
         for k in range(4):
             gu_parts.append([here.at[k, 0], here.at[k, 1]])
             down_parts.append(here.at[k, 2])
-    (f_ref, own_ref, send_ref, hidden_ref, lhs, low_ref, grads,
-     acc_d, acc_f, first_rel, second_rel, gain_rel) = refs
+
+        def arrived():
+            for k in range(4):
+                pltpu.make_async_copy(far[k * count].at[:, :, :TILE], slots.at[slot, k], sems.at[slot, k]).wait()
+    f_ref, own_ref, send_ref, grads, acc_d, acc_f = refs
     width = cuts[-1][1]
     half = width // 2
-    block = width // 8
-    rank = mask.shape[1]
+    rank = down_shrink.shape[1]
     step = pl.program_id(0)
 
     @pl.when(step == 0)
     def _():
-        for r in range(8):
-            at = lanes_at(info[ACTUAL + r], block)
-            here = slice(r * block, (r + 1) * block)
-            first_rel[here, :] = ffn_first[at, :]
-            second_rel[:, here] = out_second[:, at]
-            gain_rel[:, here] = gain[:, at]
-        cut = part_first.shape[0]
-        for own, got, base in ((part_first, got_first, 0), (part_second, got_second, cut)):
-            n = own.shape[0]
-            acc_d[base : base + n, :] = own[...].astype(f32) + got[...].astype(f32)
-        low = acc_d[:, width:].astype(bf16) * mask[...]
-        low_ref[...] = low
-        acc_f[:, :width] = dot(low, second_rel[...])
-
-        def visit(at):
-            both = acc_d[at, :width]
-            hidden = x[at, :].astype(f32) + (both + adapter_scale * acc_f[at, :width])
-            hidden_ref[at, :] = hidden
-            scale = lax.rsqrt(jnp.mean(hidden * hidden, axis=-1, keepdims=True) + norm_eps)
-            lhs[at, :width] = (hidden * scale * gain_rel[0:1, :]).astype(bf16)
-
-        over_row_blocks(x.shape[0], 16, visit)
-        low = dot(lhs[:, :width], first_rel[...]).astype(bf16)
-        lhs[:, width : width + rank] = low[:, :rank] * mask[...]
-        lhs[:, width + rank :] = low[:, rank:] * mask[...]
         acc_d[...] = jnp.zeros_like(acc_d)
         acc_f[...] = jnp.zeros_like(acc_f)
 
+    arrived()
     lows = [lhs[:, width : width + rank], lhs[:, width + rank :]]
     half_scale = jnp.asarray(adapter_scale, bf16)
 
@@ -330,9 +367,9 @@
         acc_f[:, low:top] += dot_nt(gg, w[0][...]) + dot_nt(gu, w[1][...])
     acc_f[:, width : width + rank] += dot_nt(gg, ffn_expand[0] * half_scale)
     acc_f[:, width + rank :] += dot_nt(gu, ffn_expand[1] * half_scale)
-    grads[0] = dot_tn(g_low[:span], act[:span])
-    grads[1] = adapter_scale * dot_tn(lows[0][:span], gg[:span])
-    grads[2] = adapter_scale * dot_tn(lows[1][:span], gu[:span])
+    blocks_down(grads.at[0], dot_tn(act[:span], g_low[:span]))
+    blocks_across(grads.at[1], adapter_scale * dot_tn(lows[0][:span], gg[:span]))
+    blocks_across(grads.at[2], adapter_scale * dot_tn(lows[1][:span], gu[:span]))
 
     @pl.when(step == pl.num_programs(0) - 1)
     def _():
@@ -385,9 +422,10 @@
         branch[:, width:] = b_low.astype(bf16) * mask[...]
         for i in range(4):
             at = lanes_at(place * 4 + info[INNER + i], block)
-            here = slice(i * block, (i + 1) * block)
-            ffn_grad[:, here] = dot_tn(low[:span], lhs_two[:span, at])
-            second_grad[:, here] = adapter_scale * dot_tn(out_low[:span, :], branch[:span, at])
+            value = dot_tn(lhs_two[:span, at], low[:span])
+            for k in range(2):
+                blocks_down(ffn_grad.at[i, k], value[:, k * 128 : (k + 1) * 128])
+            blocks_across(second_grad.at[i], adapter_scale * dot_tn(out_low[:span, :], branch[:span, at]))
         acc[...] = jnp.zeros_like(acc)
 
     total = dot_nt(branch[:, width:], out_shrink[...])
@@ -418,8 +456,8 @@
     )
     low_one = lhs_one[:span, width:]
     for j in range(3):
-        grads[j] = adapter_scale * dot_tn(low_one, proj[j])
-    grads[3] = dot_tn(branch[:span, width:], gated_ref[:span, :])
+        blocks_across(grads.at[j], adapter_scale * dot_tn(low_one, proj[j]))
+    blocks_down(grads.at[3], dot_tn(gated_ref[:span, :], branch[:span, width:]))
 
     @pl.when(step == pl.num_programs(0) - 1)
     def _():
@@ -446,19 +484,27 @@
     return sums[:, :rank].astype(bf16) * mask[...], sums[:, rank:]
 
 
-def output_kernel(info, own, got, rank_own, rank_got, hidden, mask, g, second, out_ref, grad_ref):
+def output_kernel(info, *refs):
+    output_rows(info, *refs[:8], *refs[-2:])
+
+
+def output_rows(info, own, got, rank_own, rank_got, hidden, mask, g, second, out_ref, grad_ref):
     low, _ = rank_rows(rank_own, rank_got, mask)
     down = own[...].astype(f32) + got[...].astype(f32)
     out_ref[...] = (hidden[...] + (down + adapter_scale * dot(low, second[...]))).astype(bf16)
-    grad_ref[...] = adapter_scale * dot_tn(low, g[...])
+    blocks_across(grad_ref, adapter_scale * dot_tn(low, g[...]))
 
 
 def rank_kernel(info, own, got, mask, normed, grad_ref):
     low, _ = rank_rows(own, got, mask)
-    grad_ref[...] = dot_tn(low, normed[...])
-
-
-def final_kernel(width, info, own, got, rank_own, rank_got, gh, x, low, scale, mask, gain, first, grad_ref):
+    blocks_down(grad_ref, dot_tn(normed[...], low))
+
+
+def final_kernel(width, info, *refs):
+    final_rows(width, info, *refs[:11], refs[-1])
+
+
+def final_rows(width, info, own, got, rank_own, rank_got, gh, x, low, scale, mask, gain, first, grad_ref):
     n_low, stat = rank_rows(rank_own, rank_got, mask)
     stat = jnp.sum(stat, axis=-1, keepdims=True)
     stat = stat + jnp.sum(n_low.astype(f32) * low[...].astype(f32), axis=-1, keepdims=True)
@@ -467,6 +513,86 @@
     unit = x[...].astype(f32) * scale_rows
     grad = own[...].astype(f32) + got[...].astype(f32) + dot_nt(n_low, first[...])
     grad_ref[...] = gh[...] + scale_rows * (grad * gain[0:1, :].astype(f32) - unit * stat)
+
+
+def places(info, pieces):
+    me, ctx = info[0], info[1]
+    for place in range(4 * pieces):
+        c, x, z = place // (2 * pieces), place // pieces % 2, place % pieces
+        far_c, far_x = (me % 2) ^ c, (me // 2) ^ x
+        yield place, 2 * far_c + far_x, lax.rem(ctx + pieces - z, pieces)
+
+
+def unpack_feed_kernel(tiles, total, expand_ref, first_ref):
+    for h in range(tiles):
+        for k in range(2):
+            column = h * 256 + k * 128
+            for j in range(3):
+                row = ((h * 3 + j) * 2 + k) * 128
+                value = total[row : row + 128, :].astype(f32)
+                if j:
+                    expand_ref[j - 1, :, column : column + 128] = value
+                else:
+                    first_ref[column : column + 128, :] = value
+
+
+def gather_feed_kernel(pieces, tiles, info, own, x, c, cx, expand_ref, first_ref, kept):
+    n = own.shape[1]
+    for place, which, distance in places(info, pieces):
+        for k, part in enumerate((own, x, c, cx)):
+
+            @pl.when(which == k)
+            def _(part=part, place=place, distance=distance):
+                kept[place * n : (place + 1) * n, :] = part[distance]
+
+    unpack_feed_kernel(tiles, kept, expand_ref, first_ref)
+
+
+def gather_rows_kernel(pieces, info, own, x, c, cx, out):
+    for place, which, distance in places(info, pieces):
+        for k, part in enumerate((own, x, c, cx)):
+
+            @pl.when(which == k)
+            def _(part=part, place=place, distance=distance):
+                out[place] = part[distance]
+
+
+def unpack_early_kernel(pieces, info, own, x, c, cx, ffn_ref, second_ref, expand_ref, out_ref, kept):
+    gather_rows_kernel(pieces, info, own, x, c, cx, kept)
+    tens = info[2]
+    for place in range(4 * pieces):
+        i, k, part = place // 4, place // 2 % 2, place % 2
+        for t in range(2):
+            base = pl.multiple_of(jnp.where(tens == t, 0, 192), 64)
+            ffn_ref[t * 1024 + i * 256 + part * 128 : t * 1024 + i * 256 + part * 128 + 128, k * 128 : (k + 1) * 128] = (
+                kept[place, pl.ds(base, 128), :].astype(f32)
+            )
+            column = t * 1024 + i * 256 + k * 128
+            second_ref[part * 64 : part * 64 + 64, column : column + 128] = kept[
+                place, pl.ds(pl.multiple_of(base + 128, 64), 64), :
+            ].astype(f32)
+        h, j = place // 4, place % 4
+        for k in range(2):
+            value = kept[place, 384 + k * 128 : 512 + k * 128, :].astype(f32)
+            column = h * 256 + k * 128
+            if j < 3:
+                expand_ref[j, :, column : column + 128] = value
+            else:
+                out_ref[column : column + 128, :] = value
+
+
+def unpack_late_kernel(pieces, info, own, x, c, cx, first_ref, second_ref, kept):
+    gather_rows_kernel(pieces, info, own, x, c, cx, kept)
+    tens = info[2]
+    for place in range(4 * pieces):
+        for t in range(2):
+            base = pl.multiple_of(jnp.where(tens == t, 0, 128), 128)
+            row = t * 1024 + place * 64
+            first_ref[row : row + 64, :] = kept[place, pl.ds(base, 64), :].astype(f32)
+            row, column = place % 2 * 64, t * 1024 + place // 2 * 128
+            second_ref[row : row + 64, column : column + 128] = kept[
+                place, pl.ds(pl.multiple_of(base + 64, 64), 64), :
+            ].astype(f32)
 
 
 def after(array, *gates):
@@ -747,6 +873,22 @@
             if special:
                 feed_step(2)
                 down_own = chip_pair(down_weight)
+    def middle(i):
+        c = chunks[i]
+        c["hidden"], c["lhs"], c["low"] = call(
+            middle_kernel, (1,), (info,),
+            [picked(x_full, i)] + [(w, None, None) for w in (*c["part"], *c["got"])]
+            + [picked(mask, i), (gain_two, None, None), (output_adapter_expand, None, None), (ffn_shrink, None, None)],
+            [((rows, width), f32, None, None), ((rows, ext_two), bf16, None, None), ((rows, rank), bf16, None, None)],
+            [
+                pltpu.VMEM((rows, ext_one), f32),
+                pltpu.VMEM((rows, width), f32),
+                pltpu.VMEM((width, 2 * rank), bf16),
+                pltpu.VMEM((rank, width), bf16),
+                pltpu.VMEM((1, width), f32),
+            ],
+        )
+
     wait(*stage, *chunks[1]["part"])
     chunks[0]["got"][1] = over_y(chunks[0]["part"][1])
     stage = [chunks[0]["got"][1]]
@@ -766,59 +908,44 @@
 
     wait(*stage, glhs)
     chunks[1]["got"][1] = over_y(chunks[1]["part"][1])
-    stage = []
+    stage = [chunks[1]["got"][1]]
+    middle(0)
+    middle(1)
     if special:
         feed_step(5)
-        wait(*stage)
-        stage = []
+        wait(*stage, chunks[0]["lhs"])
+        stage = [chunks[1]["lhs"]]
         feed_step(6)
         wait(*stage)
         feed_step(7)
         whole = [(gu_own, (2, 2, gu_own.shape[2], TILE), lambda h, *_: (0, 0, 0, h)),
                  (down_own, (2, TILE, down_own.shape[2]), lambda h, *_: (0, h, 0))]
-        feed_inputs = whole + [
-            (w, (3, TILE, TILE), lambda h, *_, low=low, top=top: (0, 0, jnp.clip(h - low, 0, top - low - 1)))
-            for part in (feed_x, feed_z, feed_xc, feed_zc)
-            for w, (low, top) in zip(part, FEED_CUTS)
-        ]
+        feed_inputs = whole + [(w, "any", None) for part in (feed_x, feed_z, feed_xc, feed_zc) for w in part]
     else:
         feed_inputs = [columns(gu_parts[0]), row_tiles(down_parts[0])]
 
     for i, c in enumerate(chunks):
-        f_part, d_own, d_send, hidden, lhs_two, out_low, grads = call(
+        f_part, d_own, d_send, grads = call(
             functools.partial(feed_kernel, cuts, span), (feed_steps,), (info,),
-            [picked(x_full, i)] + [(w, None, None) for w in (*c["part"], *c["got"])] + [picked(glhs, i), picked(mask, i),
-             (gain_two, None, None), (output_adapter_expand, None, None), (ffn_shrink, None, None),
-             columns(ffn_expand), row_tiles(down_shrink)]
+            [(c["lhs"], None, None), picked(glhs, i), columns(ffn_expand), row_tiles(down_shrink)]
             + feed_inputs,
             [
                 ((rows, ext_two), bf16, None, None),
                 ((span, half + rank), bf16, None, None),
                 ((span, half + rank), bf16, None, None),
-                ((rows, width), f32, None, None),
-                ((rows, ext_two), bf16, None, None),
-                ((rows, rank), bf16, None, None),
-                ((3, rank, hidden_units), f32, (3, rank, TILE), lambda h, *_: (0, 0, h)),
+                ((feed_steps, 3, 2, 128, 128), f32, (None, 3, 2, 128, 128), lambda h, *_: (h, 0, 0, 0, 0)),
             ],
             [
                 pltpu.VMEM((rows, ext_one), f32),
                 pltpu.VMEM((rows, ext_two), f32),
-                pltpu.VMEM((width, 2 * rank), bf16),
-                pltpu.VMEM((rank, width), bf16),
-                pltpu.VMEM((1, width), f32),
             ]
-            + ([pltpu.VMEM((4, 3, TILE, TILE), bf16)] if special else []),
+            + ([pltpu.VMEM((2, 4, 3, TILE, TILE), bf16), pltpu.SemaphoreType.DMA((2, 4))] if special else []),
             flops=2 * rows * hidden_units * ext_two * 6,
         )
-        c.update(f_own=f_part, d_own=d_own, d_send=d_send, hidden=hidden, lhs=lhs_two, low=out_low, feed_grads=grads)
+        c.update(f_own=f_part, d_own=d_own, d_send=d_send, feed_grads=grads)
     def summed(name):
         return sum(c[name] for c in chunks).astype(bf16)
 
-    def joined(own, got, axis):
-        first = jnp.where(tens == 0, own, got)
-        second = jnp.where(tens == 0, got, own)
-        return jnp.concatenate([first, second], axis=axis)
-
     def take(array, i):
         return lax.dynamic_index_in_dim(array, i, 0, keepdims=False)
 
@@ -828,8 +955,8 @@
     core_bit, x_bit = me % 2, me // 2
     shifts = [[(i, (i + k) % pieces) for i in range(pieces)] for k in range(1, pieces)]
 
-    def cut(arrays):
-        return jnp.concatenate([a.reshape(-1, half) for a in arrays], axis=0).reshape(2, 2, pieces, -1, half)
+    def cut(*arrays):
+        return jnp.concatenate([a.reshape(2, 2, pieces, -1, 128) for a in arrays], axis=3)
 
     def scatter_core(total):
         return add(take(total, core_bit), lax.ppermute(take(total, 1 - core_bit), "dp", core_route))
@@ -842,32 +969,19 @@
         return add(take(total, ctx), *sent)
 
     def gather_z(total):
-        got = [total] + [lax.ppermute(total, "ctx", route) for route in shifts]
-        total = jnp.zeros((pieces,) + total.shape, bf16)
-        for k, piece in enumerate(got):
-            total = lax.dynamic_update_index_in_dim(total, piece, (ctx + pieces - k) % pieces, 0)
-        return total
-
-    def gather_pair(total, route, bit):
-        got = lax.ppermute(total, "dp", route)
-        return jnp.where(bit == 0, jnp.stack([total, got]), jnp.stack([got, total]))
+        return jnp.stack([total] + [lax.ppermute(total, "ctx", route) for route in shifts])
 
     def gather_chip(total):
-        return gather_pair(gather_pair(total, x_route, x_bit), core_route, core_bit)
-
-    def both_halves(total, h):
-        return total[:, : 2 * h].reshape(4 * pieces, 2, h, half).transpose(0, 2, 1, 3).reshape(-1, width)
-
-    def plain(*arrays):
-        return lax.psum(arrays, ("dp", "ctx"))
+        over_x = lax.ppermute(total, "dp", x_route)
+        return [total, over_x] + [lax.ppermute(v, "dp", core_route) for v in (total, over_x)]
 
     for c in chunks:
         c["f_got"] = swap_tensor(c["f_own"])
     feed = summed("feed_grads")
     if special:
-        feed_sum = scatter_core(cut([after(feed, chunks[0]["f_got"])]))
+        feed_sum = scatter_core(cut(after(feed, chunks[0]["f_got"])))
     for i, c in enumerate(chunks):
-        f_got = after(c["f_got"], feed_sum) if special and i == 1 else c["f_got"]
+        f_got = after(c["f_got"], *([feed_sum] if special and i == 0 else []), *([chunks[0]["n_rank"]] if i else []))
         n_own, n_send, n_rank, grad_hidden, ffn_grad, second_grad, grads = call(
             functools.partial(back_kernel, cuts, span), (mixer_steps,), (info,),
             [(c["f_own"], None, None), (f_got, None, None), (c["hidden"], None, None), picked(glhs, i),
@@ -881,9 +995,9 @@
                 ((span, half), bf16, None, None),
                 ((span, 2 * rank), bf16, None, None),
                 ((rows, width), f32, None, None),
-                ((2 * rank, half), f32, None, None),
-                ((rank, half), f32, None, None),
-                ((4, rank, half), f32, (4, rank, TILE), lambda h, *_: (0, 0, h)),
+                ((4, 2, 2, 128, 128), f32, None, None),
+                ((4, 2, 128, 128), f32, None, None),
+                ((mixer_steps, 4, 2, 128, 128), f32, (None, 4, 2, 128, 128), lambda h, *_: (h, 0, 0, 0, 0)),
             ],
             [
                 pltpu.VMEM((rows, ext_one), f32),
@@ -895,23 +1009,31 @@
             flops=2 * rows * half * ext_one * 4,
         )
         c.update(n_own=n_own, n_send=n_send, n_rank=n_rank, gh=grad_hidden, ffn_grad=ffn_grad, second_grad=second_grad, mixer_grads=grads)
-        c["rank_got"] = swap_tensor(n_rank)
-        c["n_got"] = swap_tensor(after(n_send, c["rank_got"]))
         if special:
-            feed_sum = scatter_x(after(feed_sum, n_rank)) if i == 0 else scatter_z(after(feed_sum, n_rank))
+            feed_sum = scatter_x(feed_sum) if i == 0 else feed_sum
     for c in chunks:
-        c["d_got"] = swap_tensor(after(c["d_send"], chunks[0]["n_rank"]))
+        c["d_got"] = swap_tensor(after(c["d_send"], chunks[0]["f_got"]))
+    chunks[1]["rank_got"] = swap_tensor(chunks[1]["n_rank"])
+    chunks[0]["rank_got"] = swap_tensor(after(chunks[0]["n_rank"], chunks[1]["n_rank"]))
+    for c in chunks:
+        c["n_got"] = swap_tensor(after(c["n_send"], chunks[1]["rank_got"]))
+    if special:
+        feed_sum = scatter_z(feed_sum)
+        early = cut(after(summed("ffn_grad"), feed_sum, *(c["d_got"] for c in chunks)), summed("second_grad"), summed("mixer_grads"))
+        early = scatter_core(early)
+        first_step = (early,)
+    else:
+        first_step = ()
 
     block = half // 4
     in_half = lambda i, info: (0, info[INNER + i])
     in_full = lambda i, info: (0, info[3] * 4 + info[INNER + i])
     whole_block = lambda i, info: (0, 0)
-    grad_out = ((rank, half), f32, (rank, block), lambda i, info: (0, i))
+    grad_out = ((4, 2, 128, 128), f32, (None, 2, 128, 128), lambda i, info: (i, 0, 0, 0))
     for k, c in enumerate(chunks):
         in_stack_full = lambda i, info, k=k: (k, 0, info[3] * 4 + info[INNER + i])
         masks = (mask, (None, span, rank), lambda i, info, k=k: (k, 0, 0))
-        ranks = [(c[name], (span, 2 * rank), whole_block) for name in ("n_rank", "rank_got")]
-        d_got = after(c["d_got"], chunks[1]["n_rank"])
+        d_got = after(c["d_got"], *first_step)
         c["out"], c["down_grad"] = call(
             output_kernel, (4,), (info,),
             [
@@ -923,15 +1045,45 @@
                 masks,
                 (glhs, (None, span, block), in_stack_full),
                 (down_adapter_expand, (rank, block), lambda i, info: (0, info[2] * 4 + i)),
-            ],
-            [((span, half), bf16, (span, block), lambda i, info: (0, i)), grad_out],
+            ]
+            + ([(chunks[0]["out"], "any", None)] if k else []),
+            [((tok_count, half), bf16, (span, block), lambda i, info, k=k: (k, i)), grad_out],
+            flops=5 * 10**9,
+            aliases={9: 0} if k else None,
         )
+    wait()
+    if special:
+        feed_sum = gather_z(after(feed_sum, early))
+        early = after(scatter_x(early), feed_sum, chunks[-1]["out"])
+        second_step = (early,)
+    else:
+        second_step = ()
+    for k, c in enumerate(chunks):
+        in_stack_full = lambda i, info, k=k: (k, 0, info[3] * 4 + info[INNER + i])
+        masks = (mask, (None, span, rank), lambda i, info, k=k: (k, 0, 0))
+        ranks = [(w, (span, 2 * rank), whole_block) for w in (c["n_rank"], after(c["rank_got"], *second_step))]
         (c["in_grad"],) = call(
-            rank_kernel, (4,), (info,), ranks + [masks, (lhs_one, (None, span, block), in_stack_full)], [grad_out]
+            rank_kernel, (4,), (info,), ranks + [masks, (lhs_one, (None, span, block), in_stack_full)], [grad_out],
+            flops=5 * 10**9,
         )
+    if special:
+        feed_parts = [feed_sum, begin("dp", x_route, after(feed_sum, early))]
+        early = after(scatter_z(early), feed_parts[1], *(c["in_grad"] for c in chunks))
+        feed_parts += [begin("dp", core_route, v) for v in feed_parts]
+        late = scatter_core(cut(summed("in_grad"), summed("down_grad")))
+        h = 3 * 1024 // (4 * pieces)
+        early = jnp.concatenate([early[:h], swap_tensor(early[:h]), early[h:]], axis=0)
+        third_step = (early,)
+    else:
+        third_step = ()
+    for k, c in enumerate(chunks):
+        in_stack_full = lambda i, info, k=k: (k, 0, info[3] * 4 + info[INNER + i])
+        masks = (mask, (None, span, rank), lambda i, info, k=k: (k, 0, 0))
+        ranks = [(w, (span, 2 * rank), whole_block) for w in (c["n_rank"], c["rank_got"])]
+        n_got = after(c["n_got"], *third_step)
         (c["grad"],) = call(
             functools.partial(final_kernel, width), (4,), (info,),
-            [(c["n_own"], (span, block), in_half), (c["n_got"], (span, block), in_half)]
+            [(c["n_own"], (span, block), in_half), (n_got, (span, block), in_half)]
             + ranks
             + [
                 (c["gh"], (span, block), in_full),
@@ -941,47 +1093,70 @@
                 masks,
                 (gain_one, (1, block), lambda i, info: (0, info[2] * 4 + i)),
                 (input_adapter_shrink, (block, rank), lambda i, info: (info[2] * 4 + i, 0)),
-            ],
-            [((span, half), f32, (span, block), lambda i, info: (0, i))],
+            ]
+            + ([(chunks[0]["grad"], "any", None)] if k else []),
+            [((tok_count, half), f32, (span, block), lambda i, info, k=k: (k, i))],
+            flops=6 * 10**9,
+            aliases={12: 0} if k else None,
         )
-    block_output = jnp.concatenate([c["out"] for c in chunks], axis=0)
-    input_grad = jnp.concatenate([c["grad"] for c in chunks], axis=0)
-
-    if special:
-        early_halves, early_others = [summed("ffn_grad"), summed("second_grad")], [summed("mixer_grads")]
-        late_halves = [summed("in_grad"), summed("down_grad")]
-        early = jnp.concatenate([cut(early_halves), cut(early_others)], axis=3)
-        early = scatter_z(scatter_x(scatter_core(early)))
-        late = scatter_z(scatter_x(scatter_core(cut(late_halves))))
-        h = 3 * rank * half // (4 * pieces * half)
-        early = jnp.concatenate([joined(early[:h], swap_tensor(early[:h]), 0), early[h:]], axis=0)
-        late = joined(late, swap_tensor(late), 0)
-        feed = gather_chip(gather_z(feed_sum)).reshape(feed.shape)
-        early = gather_chip(gather_z(early)).reshape(4 * pieces, -1, half)
-        late = gather_chip(gather_z(late)).reshape(4 * pieces, -1, half)
-        both = both_halves(early, h)
-        ffn_grad, second_grad = both[: 2 * rank], both[2 * rank :]
-        mixer = early[:, 2 * h :].reshape(4, rank, half)
-        both = both_halves(late, late.shape[1] // 2)
-        in_grad, down_grad = both[:rank], both[rank:]
+    block_output, input_grad = chunks[-1]["out"], chunks[-1]["grad"]
+
+    if special:
+        late = scatter_x(after(late, early))
+        gathered = gather_z(early)
+        late = scatter_z(after(late, gathered))
+        late = jnp.concatenate([late, swap_tensor(late)], axis=0)
+        n = 4 * pieces
+        parts = gather_chip(gathered)
+        ffn_grad, second_grad, mixer_grad, out_grad = call(
+            functools.partial(unpack_early_kernel, pieces), (1,), (info,), [(v, None, None) for v in parts],
+            [((width, 2 * rank), f32, None, None), ((rank, width), f32, None, None), ((3, rank, half), f32, None, None),
+             ((half, rank), f32, None, None)],
+            [pltpu.VMEM((n,) + early.shape, bf16)],
+        )
+        feed_outs = [((2, rank, hidden_units), f32, None, None), ((hidden_units, rank), f32, None, None)]
+        expand_grad, first_grad = call(
+            functools.partial(gather_feed_kernel, pieces, feed_steps), (1,), (info,), [(v, None, None) for v in feed_parts],
+            feed_outs, [pltpu.VMEM((feed.size // 128, 128), bf16)],
+        )
+        parts = gather_chip(gather_z(late))
+        in_grad, down_grad = call(
+            functools.partial(unpack_late_kernel, pieces), (1,), (info,), [(v, None, None) for v in parts],
+            [((width, rank), f32, None, None), ((rank, width), f32, None, None)],
+            [pltpu.VMEM((n,) + late.shape, bf16)],
+        )
     else:
-        feed, mixer, ffn_grad, second_grad, in_grad, down_grad = plain(
-            feed, summed("mixer_grads"), summed("ffn_grad"), summed("second_grad"), summed("in_grad"), summed("down_grad")
+        names = ("mixer_grads", "ffn_grad", "second_grad", "in_grad", "down_grad")
+        feed, mixer, ffn_grad, second_grad, in_grad, down_grad = lax.psum(
+            (feed, *(summed(name) for name in names)), ("dp", "ctx")
         )
-        ffn_grad, second_grad, in_grad, down_grad = (
-            joined(v, swap_tensor(v), 1) for v in (ffn_grad, second_grad, in_grad, down_grad)
-        )
+
+        def whole(part, axis):
+            got = swap_tensor(part)
+            pair = [jnp.where(tens == 0, part, got), jnp.where(tens == 0, got, part)]
+            return jnp.concatenate(pair, axis=axis).astype(f32)
+
+        def across(blocks):
+            return blocks.reshape(-1, 128, 128).transpose(1, 0, 2).reshape(128, -1)
+
+        ffn_grad = whole(ffn_grad.transpose(0, 2, 3, 1, 4).reshape(half, 2 * rank), 0)
+        second_grad, down_grad = whole(across(second_grad), 1), whole(across(down_grad), 1)
+        in_grad = whole(in_grad.reshape(half, rank), 0)
+        mixer_grad = jnp.stack([across(mixer[:, j]) for j in range(3)]).astype(f32)
+        out_grad = mixer[:, 3].reshape(half, rank).astype(f32)
+        expand_grad = jnp.stack([across(feed[:, j]) for j in (1, 2)]).astype(f32)
+        first_grad = feed[:, 0].reshape(hidden_units, rank).astype(f32)
     return (
         block_output,
         input_grad,
-        in_grad.astype(f32).T,
-        mixer[:3].astype(f32),
-        mixer[3].astype(f32).T,
-        second_grad.astype(f32),
-        ffn_grad.astype(f32).T,
-        feed[1:].astype(f32),
-        feed[0].astype(f32).T,
-        down_grad.astype(f32),
+        in_grad,
+        mixer_grad,
+        out_grad,
+        second_grad,
+        ffn_grad,
+        expand_grad,
+        first_grad,
+        down_grad,
     )
 
 

time: 668 us -> 569 us (0.85)
  local copies, waits for them, and re-layouts: 63.6 us -> 30.1 us
  other arithmetic: 47.7 us -> 20.7 us
  waiting for transfers between devices: 140 us -> 113 us
  starting transfers between devices: 87.5 us -> 76.1 us
    ppermute x43 -> x46, waiting for transfers between devices: 91.9 us -> 70.2 us  [begin(): return lax.ppermute(after(array, *gates), axis, route)]
    dynamic_update_slice x10 -> x0, local copies, waits for them, and re-layouts: 14.5 us -> none  [gather_z(): lax.dynamic_update_index_in_dim(total, piece, (ctx + pieces - k) % pieces...]
    select_n x11 -> x0, other arithmetic: 12.7 us -> none  [the longest x9 12.7 us: gather_pair(): return jnp.where(bit == 0, jnp.stack([total, got]), jnp.stack([got, total]))]
    ppermute x9, waiting for transfers between devices: 1.28 us -> 13.8 us  [scatter_z(): lax.ppermute(take(total, (ctx + k) % pieces), 'ctx', route)]
    ppermute x3, waiting for transfers between devices: 9.81 us -> 0.43 us  [scatter_x(): lax.ppermute(take(total, 1 - x_bit), 'dp', x_route)]
    ppermute x10, waiting for transfers between devices: 16.1 us -> 7.45 us  [swap_tensor(): return lax.ppermute(array, 'tensor', [(0, 1), (1, 0)])]
    unnamed x141 -> x170, local copies, waits for them, and re-layouts: 20.4 us -> 14.3 us
    pallas_call x16 -> x21, Pallas kernels: 301 us -> 297 us  [call(): pl.pallas_call(kernel, grid_spec=pltpu.PrefetchScalarGridSpec(num_scalar_...]
  transfers between devices with their start and end apart: 87 -> 90, of which waited for: 28 -> 32; matrix products, arithmetic and copies ran while one was open for 13% -> 6% of each run, Pallas kernels for 45% -> 44%
where the time goes in v4:
time: 569 us; the launch traced here: 560 us
  Pallas kernels  297 us (52%)
  waiting for transfers between devices  113 us (20%)
  starting transfers between devices  76.1 us (13%)
  local copies, waits for them, and re-layouts  30.1 us (5%)
  other arithmetic  20.7 us (4%)
  between operations  15.7 us (3%)
  blocking collectives  7.19 us (1%)
    pallas_call x21, Pallas kernels, call(): pl.pallas_call(kernel, grid_spec=pltpu.PrefetchScalarGridSpec(num_scalar_...  297 us
    ppermute x46, waiting for transfers between devices, begin(): return lax.ppermute(after(array, *gates), axis, route)  70.2 us
    ppermute x46, starting transfers between devices, begin(): return lax.ppermute(after(array, *gates), axis, route)  39 us
    ppermute x9, waiting for transfers between devices, gather_z(): lax.ppermute(total, 'ctx', route)  17.9 us
    unnamed x170, local copies, waits for them, and re-layouts  14.3 us
    ppermute x9, waiting for transfers between devices, scatter_z(): lax.ppermute(take(total, (ctx + k) % pieces), 'ctx', route)  13.8 us
  transfers between devices with their start and end apart: 90, of which 32 were waited for; matrix products, arithmetic and copies ran while one was open for 6% of the time, Pallas kernels for 44%

profile of v4, /device:TPU:0, one launch (start us, length us, event | category | flops | bytes accessed | tf_op | source)
XLA Modules:
  0.0 560.4 jit_solution(2545987335140990927)
XLA Ops:
  10.0 7.2 %all-gather = bf16[16,8,1024]{2,1,0:T(8,128)(2,1)S(1)} all-gather(bf16[4,8,1024]{2,1,0:T(8,128)(2,1)S(1)} %pad_maximum_fusion.13), channel_id=2, replica_groups=mesh['dp'=4,'ctx'=4,'tensor'=2] {'dp'}, dimensions={0}, use_global_device_ids=true | all-gather | bytes 327680 | tf_op jit(solution)/shard_map/all_gather | solution.py:713
  30.3 4.5 collective-permute-start.2
  36.5 7.2 %collective-permute-done.got_first = bf16[384,1024]{1,0:T(8,128)(2,1)} collective-permute-done((bf16[384,1024]{1,0:T(8,128)(2,1)}, bf16[384,1024]{1,0:T(8,128)(2,1)}, u32[]{:S(2)}, u32[]{:S(2)}) %collective-permute-start) | collective-permute-done | bytes 786464 | tf_op jit(solution)/shard_map/ppermute | solution.py:672
  48.8 4.6 fusion.35
  62.3 17.4 %collective-permute-done.5.halo_got = bf16[2,2,16,1024]{3,2,1,0:T(8,128)(2,1)S(1)} collective-permute-done((bf16[2,2,16,1024]{3,2,1,0:T(8,128)(2,1)S(1)}, bf16[2,2,16,1024]{3,2,1,0:T(8,128)(2,1)S(1)}, u32[]{:S(2)}, u32[]{:S(2)}) %collective-permute-start.5) | collective-permute-done | bytes 131104 | tf_op jit(solution)/shard_map/ppermute | solution.py:672
  91.4 11.6 %shard_map.269 = (bf16[2,400,2048]{2,1,0:T(8,128)(2,1)}, bf16[2,400,2176]{2,1,0:T(8,128)(2,1)}, f32[2,400,128]{2,1,0:T(8,128)}) custom-call(s32[24]{0:T(128)} %stack.153.info, bf16[768,1024]{1,0:T(8,128)(2,1)} %own.2, bf16[384,1024]{1,0:T(8,128)(2,1)} %collective-permute-done.got_first, bf16[384,1024]{1,0:T(8,128)(2,1)} %collective-permute-done.4.got_second, ...), custom_call_target="tpu_custom_call" | custom-call | flops 1 | bytes 1 | tf_op jit(solution)/shard_map/pallas_call | solution.py:67
  112.8 20.3 %shard_map.271 = (f32[400,1024]{1,0:T(8,128)}, f32[400,1024]{1,0:T(8,128)}, f32[400,1024]{1,0:T(8,128)}, f32[400,1024]{1,0:T(8,128)}, bf16[400,1024]{1,0:T(8,128...) custom-call(bf16[2,400,2176]{2,1,0:T(8,128)(2,1)} %get-tuple-element.157.lhs.lhs_one.normed.refs_6_, ...), custom_call_target="tpu_custom_call" | custom-call | flops 7130316800 | bytes 1 | tf_op jit(solution)/shard_map/pallas_call | solution.py:67
  139.1 22.2 %shard_map.270 = (f32[400,1024]{1,0:T(8,128)}, f32[400,1024]{1,0:T(8,128)}, f32[400,1024]{1,0:T(8,128)}, f32[400,1024]{1,0:T(8,128)}, bf16[400,1024]{1,0:T(8,128...) custom-call(bf16[2,400,2176]{2,1,0:T(8,128)(2,1)} %get-tuple-element.157.lhs.lhs_one.normed.refs_6_, ...), custom_call_target="tpu_custom_call" | custom-call | flops 7130316800 | bytes 1 | tf_op jit(solution)/shard_map/pallas_call | solution.py:67
  165.6 18.1 %collective-permute-done.25.refs_5_ = bf16[3,256,512]{2,1,0:T(8,128)(2,1)} collective-permute-done((bf16[3,256,512]{2,1,0:T(8,128)(2,1)S(1)}, bf16[3,256,512]{2,1,0:T(8,128)(2,1)}, u32[]{:S(2)}, u32[]{:S(2)}) %collective-permute-start.25) | collective-permute-done | bytes 786464 | tf_op jit(solution)/shard_map/ppermute | solution.py:672
  191.1 5.4 shard_map.272.glhs.refs_6_
  196.6 10.7 %collective-permute-done.30.refs_6_ = bf16[3,256,512]{2,1,0:T(8,128)(2,1)S(1)} collective-permute-done((bf16[3,256,512]{2,1,0:T(8,128)(2,1)S(1)}, bf16[3,256,512]{2,1,0:T(8,128)(2,1)S(1)}, u32[]{:S(2)}, u32[]{:S(2)}) %collective-permute-start.30) | collective-permute-done | bytes 786464 | tf_op jit(solution)/shard_map/ppermute | solution.py:672
  212.3 10.5 %shard_map.274 = (f32[400,2048]{1,0:T(8,128)}, bf16[400,2304]{1,0:T(8,128)(2,1)}, bf16[400,128]{1,0:T(8,128)(2,1)}) custom-call(s32[24]{0:T(128)} %stack.153.info, bf16[2,400,2048]{2,1,0:T(8,128)(2,1)} %get-tuple-element.156.x.refs_5_, bf16[192,2176]{1,0:T(8,128)(2,1)} %get-tuple-element.175.part_first, bf16[208,2176]{1,0:T(8,128)(2,1)} %get-tuple-element.179.part_second, ...), custom_call_target="tpu_custom_call" | custom-call | flops 1 | bytes 1 | tf_op jit(solution)/shard_map/pallas_call | solution.py:67
  222.8 6.0 %collective-permute-done.36.refs_12_ = bf16[3,256,512]{2,1,0:T(8,128)(2,1)S(1)} collective-permute-done((bf16[3,256,512]{2,1,0:T(8,128)(2,1)}, bf16[3,256,512]{2,1,0:T(8,128)(2,1)S(1)}, u32[]{:S(2)}, u32[]{:S(2)}) %collective-permute-start.36) | collective-permute-done | bytes 786464 | tf_op jit(solution)/shard_map/ppermute | solution.py:672
  230.9 10.5 %shard_map.273 = (f32[400,2048]{1,0:T(8,128)}, bf16[400,2304]{1,0:T(8,128)(2,1)}, bf16[400,128]{1,0:T(8,128)(2,1)}) custom-call(s32[24]{0:T(128)} %stack.153.info, bf16[2,400,2048]{2,1,0:T(8,128)(2,1)} %get-tuple-element.156.x.refs_5_, bf16[192,2176]{1,0:T(8,128)(2,1)} %get-tuple-element.183.part_first, bf16[208,2176]{1,0:T(8,128)(2,1)} %get-tuple-element.187.part_second, ...), custom_call_target="tpu_custom_call" | custom-call | flops 1 | bytes 1 | tf_op jit(solution)/shard_map/pallas_call | solution.py:67
  244.1 44.3 %shard_map.276 = (bf16[400,2304]{1,0:T(8,128)(2,1)}, bf16[384,1152]{1,0:T(8,128)(2,1)}, bf16[384,1152]{1,0:T(8,128)(2,1)}, f32[11,3,2,128,128]{4,3,2,1,0:T(8,128)}) custom-call(s32[24]{0:T(128)} %stack.153.info, bf16[400,2304]{1,0:T(8,128)(2,1)} %get-tuple-element.194.lhs.lhs_two, bf16[2,400,2176]{2,1,0:T(8,128)(2,1)} %shard_map.272.glhs.refs_6_, ...), custom_call_target="tpu_custom_call" | custom-call | flops 31142707200 | bytes 1 | tf_op jit(solution)/shard_map/pallas_call | solution.py:67
  289.9 44.7 %shard_map.275 = (bf16[400,2304]{1,0:T(8,128)(2,1)}, bf16[384,1152]{1,0:T(8,128)(2,1)}, bf16[384,1152]{1,0:T(8,128)(2,1)}, f32[11,3,2,128,128]{4,3,2,1,0:T(8,128)}) custom-call(s32[24]{0:T(128)} %stack.153.info, bf16[400,2304]{1,0:T(8,128)(2,1)} %get-tuple-element.188.lhs.lhs_two, bf16[2,400,2176]{2,1,0:T(8,128)(2,1)} %shard_map.272.glhs.refs_6_, ...), custom_call_target="tpu_custom_call" | custom-call | flops 31142707200 | bytes 1 | tf_op jit(solution)/shard_map/pallas_call | solution.py:67
  334.6 3.2 add_convert_fusion
  342.3 38.8 %shard_map.277 = (bf16[384,1024]{1,0:T(8,128)(2,1)}, bf16[384,1024]{1,0:T(8,128)(2,1)}, bf16[384,256]{1,0:T(8,128)(2,1)}, f32[400,2048]{1,0:T(8,128)}, f32[4,2,2...) custom-call(s32[24]{0:T(128)} %stack.153.info, ...), custom_call_target="tpu_custom_call" | custom-call | flops 7130316800 | bytes 1 | tf_op jit(solution)/shard_map/pallas_call | solution.py:67
  382.9 38.7 %shard_map.278 = (bf16[384,1024]{1,0:T(8,128)(2,1)}, bf16[384,1024]{1,0:T(8,128)(2,1)}, bf16[384,256]{1,0:T(8,128)(2,1)}, f32[400,2048]{1,0:T(8,128)}, f32[4,2,2...) custom-call(s32[24]{0:T(128)} %stack.153.info, ...), custom_call_target="tpu_custom_call" | custom-call | flops 7130316800 | bytes 1 | tf_op jit(solution)/shard_map/pallas_call | solution.py:67
  424.2 3.4 collective-permute-start.50
  431.6 7.4 %collective-permute-done.49 = bf16[528,128]{1,0:T(8,128)(2,1)S(1)} collective-permute-done((bf16[528,128]{1,0:T(8,128)(2,1)S(1)}, bf16[528,128]{1,0:T(8,128)(2,1)S(1)}, u32[]{:S(2)}, u32[]{:S(2)}) %collective-permute-start.49) | collective-permute-done | bytes 135200 | tf_op jit(solution)/shard_map/ppermute | solution.py:968
  447.9 5.3 shard_map.279
  453.2 5.4 shard_map.280
  467.2 4.7 shard_map.281
  472.5 4.7 shard_map.282
  488.0 3.6 collective-permute-done.70
  491.6 8.7 %collective-permute-done.69 = bf16[640,128]{1,0:T(8,128)(2,1)S(1)} collective-permute-done((bf16[640,128]{1,0:T(8,128)(2,1)S(1)}, bf16[640,128]{1,0:T(8,128)(2,1)S(1)}, u32[]{:S(2)}, u32[]{:S(2)}) %collective-permute-start.69) | collective-permute-done | bytes 163872 | tf_op jit(solution)/shard_map/ppermute | solution.py:972
  522.3 5.9 %shard_map.283.refs_11_ = f32[768,1024]{1,0:T(8,128)} custom-call(s32[24]{0:T(128)} %stack.153.info, bf16[384,1024]{1,0:T(8,128)(2,1)} %get-tuple-element.251.refs_0_, bf16[384,1024]{1,0:T(8,128)(2,1)} %copy-done.71, bf16[384,256]{1,0:T(8,128)(2,1)} %get-tuple-element.244.own.refs_2_, bf16[384,256]{1,0:T(8,128)(2,1)} %copy-done.84, ...), custom_call_target="tpu_custom_call" | custom-call | flops 6000000000 | bytes 1 | tf_op jit(solution)/shard_map/pallas_call | solution.py:67
  529.7 5.9 %shard_map.284 = f32[768,1024]{1,0:T(8,128)} custom-call(s32[24]{0:T(128)} %stack.153.info, bf16[384,1024]{1,0:T(8,128)(2,1)} %get-tuple-element.237.refs_0_, bf16[384,1024]{1,0:T(8,128)(2,1)} %copy-done.75, bf16[384,256]{1,0:T(8,128)(2,1)} %get-tuple-element.239.own.refs_2_, bf16[384,256]{1,0:T(8,128)(2,1)} %copy-done.83, ...), custom_call_target="tpu_custom_call", output_to_operand_aliasing={{}: (12, {})} | custom-call | flops 6000000000 | bytes 1 | tf_op jit(solution)/shard_map/pallas_call | solution.py:67
  536.5 4.9 shard_map.287
  542.8 3.6 shard_map.285
  548.2 5.3 shard_map.286
  (431 shorter events, 150.1 us)
Async XLA Ops:
  7.2 39.5 %all-gather.10.cloned.1.call-start = ((), (), s32[]{:S(2)}) async-start(), calls=%async_computation | async-start | bytes 9437184 | tf_op jit(solution)/shard_map/all_gather | solution.py:700
  8.0 73.1 %all-gather.12.cloned.1.call-start = ((), (), s32[]{:S(2)}) async-start(), calls=%async_computation.1 | async-start | bytes 3145728 | tf_op jit(solution)/shard_map/all_gather | solution.py:700
  21.0 25.7 %collective-permute-start.3 = (bf16[4,256,512]{2,1,0:T(8,128)(2,1)}, bf16[4,256,512]{2,1,0:T(8,128)(2,1)}, u32[]{:S(2)}, u32[]{:S(2)}) collective-permute-start(bf16[4,256,512]{2,1,0:T(8,128)(2,1)} %pad_maximum_fusion.1), channel_id=1, source_target_pairs={{0,16},{16,0},{8,24},{24,8},{1,17},{17,1},{9,25},{25,9},{2,18},{18... | collective-permute-start | bytes 3145736 | tf_op jit(solution)/shard_map/ppermute | solution.py:672
  46.8 196.5 %all-gather.16.cloned.1.call-start = ((), (), s32[]{:S(2)}) async-start(), calls=%async_computation.3 | async-start | bytes 8650752 | tf_op jit(solution)/shard_map/all_gather | solution.py:700
  53.4 27.6 %collective-permute-start.7 = (bf16[4,256,512]{2,1,0:T(8,128)(2,1)}, bf16[4,256,512]{2,1,0:T(8,128)(2,1)S(1)}, u32[]{:S(2)}, u32[]{:S(2)}) collective-permute-start(bf16[4,256,512]{2,1,0:T(8,128)(2,1)} %collective-permute-done.3.refs_2_), channel_id=1, source_target_pairs={{0,2},{2,0},{4,6},{6,4},{1,3},{3,1},{5,7},{7,5},{8,10},{10,8},{12,... | collective-permute-start | bytes 3145736 | tf_op jit(solution)/shard_map/ppermute | solution.py:672
  55.1 25.9 %collective-permute-start.8 = (bf16[4,256,512]{2,1,0:T(8,128)(2,1)}, bf16[4,256,512]{2,1,0:T(8,128)(2,1)}, u32[]{:S(2)}, u32[]{:S(2)}) collective-permute-start(bf16[4,256,512]{2,1,0:T(8,128)(2,1)} %collective-permute-done.3.refs_2_), channel_id=1, source_target_pairs={{0,8},{8,0},{16,24},{24,16},{1,9},{9,1},{17,25},{25,17},{2,10},{10... | collective-permute-start | bytes 3145736 | tf_op jit(solution)/shard_map/ppermute | solution.py:672
  55.1 25.9 %collective-permute-start.6 = (bf16[4,256,512]{2,1,0:T(8,128)(2,1)}, bf16[4,256,512]{2,1,0:T(8,128)(2,1)}, u32[]{:S(2)}, u32[]{:S(2)}) collective-permute-start(bf16[4,256,512]{2,1,0:T(8,128)(2,1)} %pad_maximum_fusion.2), channel_id=1, source_target_pairs={{0,16},{16,0},{8,24},{24,8},{1,17},{17,1},{9,25},{25,9},{2,18},{18... | collective-permute-start | bytes 3145736 | tf_op jit(solution)/shard_map/ppermute | solution.py:672
  56.9 22.8 %collective-permute-start.4 = (bf16[384,1024]{1,0:T(8,128)(2,1)}, bf16[384,1024]{1,0:T(8,128)(2,1)}, u32[]{:S(2)}, u32[]{:S(2)}) collective-permute-start(bf16[384,1024]{1,0:T(8,128)(2,1)} %get-tuple-element.151), channel_id=1, source_target_pairs={{0,1},{1,0},{2,3},{3,2},{4,5},{5,4},{6,7},{7,6},{8,9},{9,8},{10,11... | collective-permute-start | bytes 2359304 | tf_op jit(solution)/shard_map/ppermute | solution.py:672
  81.1 25.1 %collective-permute-start.9 = (bf16[4,256,512]{2,1,0:T(8,128)(2,1)}, bf16[4,256,512]{2,1,0:T(8,128)(2,1)S(1)}, u32[]{:S(2)}, u32[]{:S(2)}) collective-permute-start(bf16[4,256,512]{2,1,0:T(8,128)(2,1)} %collective-permute-done.6.refs_3_), channel_id=1, source_target_pairs={{0,2},{2,0},{4,6},{6,4},{1,3},{3,1},{5,7},{7,5},{8,10},{10,8},{12,... | collective-permute-start | bytes 3145736 | tf_op jit(solution)/shard_map/ppermute | solution.py:672
  81.6 24.6 %collective-permute-start.10 = (bf16[4,256,512]{2,1,0:T(8,128)(2,1)}, bf16[4,256,512]{2,1,0:T(8,128)(2,1)S(1)}, u32[]{:S(2)}, u32[]{:S(2)}) collective-permute-start(bf16[4,256,512]{2,1,0:T(8,128)(2,1)} %collective-permute-done.6.refs_3_), channel_id=1, source_target_pairs={{0,8},{8,0},{16,24},{24,16},{1,9},{9,1},{17,25},{25,17},{2,10},{10... | collective-permute-start | bytes 3145736 | tf_op jit(solution)/shard_map/ppermute | solution.py:672
  81.6 24.6 %collective-permute-start.11 = (bf16[4,256,512]{2,1,0:T(8,128)(2,1)S(1)}, bf16[4,256,512]{2,1,0:T(8,128)(2,1)S(1)}, u32[]{:S(2)}, u32[]{:S(2)}) collective-permute-start(bf16[4,256,512]{2,1,0:T(8,128)(2,1)S(1)} %collective-permute-done.7.refs_4_), channel_id=1, source_target_pairs={{0,8},{8,0},{16,24},{24,16},{1,9},{9,1},{17,25},{25,17},{2,10},{10... | collective-permute-start | bytes 3145736 | tf_op jit(solution)/shard_map/ppermute | solution.py:672
  107.2 25.9 %collective-permute-start.17 = (bf16[3,256,512]{2,1,0:T(8,128)(2,1)}, bf16[3,256,512]{2,1,0:T(8,128)(2,1)S(1)}, u32[]{:S(2)}, u32[]{:S(2)}) collective-permute-start(bf16[3,256,512]{2,1,0:T(8,128)(2,1)} %collective-permute-done.13.refs_2_), channel_id=1, source_target_pairs={{0,2},{2,0},{4,6},{6,4},{1,3},{3,1},{5,7},{7,5},{8,10},{10,8},{12,... | collective-permute-start | bytes 2359304 | tf_op jit(solution)/shard_map/ppermute | solution.py:672
  107.7 25.4 %collective-permute-start.18 = (bf16[3,256,512]{2,1,0:T(8,128)(2,1)}, bf16[3,256,512]{2,1,0:T(8,128)(2,1)S(1)}, u32[]{:S(2)}, u32[]{:S(2)}) collective-permute-start(bf16[3,256,512]{2,1,0:T(8,128)(2,1)} %collective-permute-done.13.refs_2_), channel_id=1, source_target_pairs={{0,8},{8,0},{16,24},{24,16},{1,9},{9,1},{17,25},{25,17},{2,10},{10... | collective-permute-start | bytes 2359304 | tf_op jit(solution)/shard_map/ppermute | solution.py:672
  107.7 25.3 %collective-permute-start.15 = (bf16[384,1024]{1,0:T(8,128)(2,1)}, bf16[384,1024]{1,0:T(8,128)(2,1)S(1)}, u32[]{:S(2)}, u32[]{:S(2)}) collective-permute-start(bf16[384,1024]{1,0:T(8,128)(2,1)} %get-tuple-element.172), channel_id=1, source_target_pairs={{0,1},{1,0},{2,3},{3,2},{4,5},{5,4},{6,7},{7,6},{8,9},{9,8},{10,11... | collective-permute-start | bytes 2359304 | tf_op jit(solution)/shard_map/ppermute | solution.py:672
  109.3 23.8 %collective-permute-start.16 = (bf16[3,256,512]{2,1,0:T(8,128)(2,1)}, bf16[3,256,512]{2,1,0:T(8,128)(2,1)}, u32[]{:S(2)}, u32[]{:S(2)}) collective-permute-start(bf16[3,256,512]{2,1,0:T(8,128)(2,1)} %pad_maximum_fusion.4), channel_id=1, source_target_pairs={{0,16},{16,0},{8,24},{24,8},{1,17},{17,1},{9,25},{25,9},{2,18},{18... | collective-permute-start | bytes 2359304 | tf_op jit(solution)/shard_map/ppermute | solution.py:672
  134.6 108.7 %all-gather.14.cloned.1.call-start = ((), (), s32[]{:S(2)}) async-start(), calls=%async_computation.2 | async-start | bytes 17301504 | tf_op jit(solution)/shard_map/all_gather | solution.py:700
  136.1 25.3 %collective-permute-start.19 = (bf16[192,2176]{1,0:T(8,128)(2,1)S(1)}, bf16[192,2176]{1,0:T(8,128)(2,1)S(1)}, u32[]{:S(2)}, u32[]{:S(2)}) collective-permute-start(bf16[192,2176]{1,0:T(8,128)(2,1)S(1)} %copy-done.30), channel_id=1, source_target_pairs={{0,1},{1,0},{2,3},{3,2},{4,5},{5,4},{6,7},{7,6},{8,9},{9,8},{10,11... | collective-permute-start | bytes 2506760 | tf_op jit(solution)/shard_map/ppermute | solution.py:672
  136.6 24.7 %collective-permute-start.21 = (bf16[3,256,512]{2,1,0:T(8,128)(2,1)}, bf16[3,256,512]{2,1,0:T(8,128)(2,1)S(1)}, u32[]{:S(2)}, u32[]{:S(2)}) collective-permute-start(bf16[3,256,512]{2,1,0:T(8,128)(2,1)} %collective-permute-done.16.refs_3_), channel_id=1, source_target_pairs={{0,2},{2,0},{4,6},{6,4},{1,3},{3,1},{5,7},{7,5},{8,10},{10,8},{12,... | collective-permute-start | bytes 2359304 | tf_op jit(solution)/shard_map/ppermute | solution.py:672
  138.2 23.1 %collective-permute-start.22 = (bf16[3,256,512]{2,1,0:T(8,128)(2,1)}, bf16[3,256,512]{2,1,0:T(8,128)(2,1)}, u32[]{:S(2)}, u32[]{:S(2)}) collective-permute-start(bf16[3,256,512]{2,1,0:T(8,128)(2,1)} %collective-permute-done.16.refs_3_), channel_id=1, source_target_pairs={{0,8},{8,0},{16,24},{24,16},{1,9},{9,1},{17,25},{25,17},{2,10},{10... | collective-permute-start | bytes 2359304 | tf_op jit(solution)/shard_map/ppermute | solution.py:672
  138.2 23.0 %collective-permute-start.20 = (bf16[3,256,512]{2,1,0:T(8,128)(2,1)S(1)}, bf16[3,256,512]{2,1,0:T(8,128)(2,1)}, u32[]{:S(2)}, u32[]{:S(2)}) collective-permute-start(bf16[3,256,512]{2,1,0:T(8,128)(2,1)S(1)} %copy-done.36), channel_id=1, source_target_pairs={{0,16},{16,0},{8,24},{24,8},{1,17},{17,1},{9,25},{25,9},{2,18},{18... | collective-permute-start | bytes 2359304 | tf_op jit(solution)/shard_map/ppermute | solution.py:672
  138.8 22.6 %collective-permute-start.23 = (bf16[3,256,512]{2,1,0:T(8,128)(2,1)}, bf16[3,256,512]{2,1,0:T(8,128)(2,1)}, u32[]{:S(2)}, u32[]{:S(2)}) collective-permute-start(bf16[3,256,512]{2,1,0:T(8,128)(2,1)} %copy-done.63), channel_id=1, source_target_pairs={{0,8},{8,0},{16,24},{24,16},{1,9},{9,1},{17,25},{25,17},{2,10},{10... | collective-permute-start | bytes 2359304 | tf_op jit(solution)/shard_map/ppermute | solution.py:672
  162.2 22.4 %collective-permute-start.24 = (bf16[208,2176]{1,0:T(8,128)(2,1)S(1)}, bf16[208,2176]{1,0:T(8,128)(2,1)S(1)}, u32[]{:S(2)}, u32[]{:S(2)}) collective-permute-start(bf16[208,2176]{1,0:T(8,128)(2,1)S(1)} %copy-done.26), channel_id=1, source_target_pairs={{0,1},{1,0},{2,3},{3,2},{4,5},{5,4},{6,7},{7,6},{8,9},{9,8},{10,11... | collective-permute-start | bytes 2715656 | tf_op jit(solution)/shard_map/ppermute | solution.py:672
  184.6 23.5 %collective-permute-start.29 = (bf16[192,2176]{1,0:T(8,128)(2,1)S(1)}, bf16[192,2176]{1,0:T(8,128)(2,1)S(1)}, u32[]{:S(2)}, u32[]{:S(2)}) collective-permute-start(bf16[192,2176]{1,0:T(8,128)(2,1)S(1)} %copy-done.31), channel_id=1, source_target_pairs={{0,1},{1,0},{2,3},{3,2},{4,5},{5,4},{6,7},{7,6},{8,9},{9,8},{10,11... | collective-permute-start | bytes 2506760 | tf_op jit(solution)/shard_map/ppermute | solution.py:672
  288.4 49.4 %collective-permute-start.43 = (bf16[400,2304]{1,0:T(8,128)(2,1)}, bf16[400,2304]{1,0:T(8,128)(2,1)}, u32[]{:S(2)}, u32[]{:S(2)}) collective-permute-start(bf16[400,2304]{1,0:T(8,128)(2,1)} %get-tuple-element.200.part), channel_id=1, source_target_pairs={{0,1},{1,0},{2,3},{3,2},{4,5},{5,4},{6,7},{7,6},{8,9},{9,8},{10,11... | collective-permute-start | bytes 5529608 | tf_op jit(solution)/shard_map/ppermute | solution.py:603
  337.9 43.4 %collective-permute-start.46 = (bf16[400,2304]{1,0:T(8,128)(2,1)}, bf16[400,2304]{1,0:T(8,128)(2,1)}, u32[]{:S(2)}, u32[]{:S(2)}) collective-permute-start(bf16[400,2304]{1,0:T(8,128)(2,1)} %get-tuple-element.214.part), channel_id=1, source_target_pairs={{0,1},{1,0},{2,3},{3,2},{4,5},{5,4},{6,7},{7,6},{8,9},{9,8},{10,11... | collective-permute-start | bytes 5529608 | tf_op jit(solution)/shard_map/ppermute | solution.py:603
  338.6 100.5 %collective-permute-start.44 = (bf16[384,1152]{1,0:T(8,128)(2,1)}, bf16[384,1152]{1,0:T(8,128)(2,1)}, u32[]{:S(2)}, u32[]{:S(2)}) collective-permute-start(bf16[384,1152]{1,0:T(8,128)(2,1)} %get-tuple-element.201), channel_id=1, source_target_pairs={{0,1},{1,0},{2,3},{3,2},{4,5},{5,4},{6,7},{7,6},{8,9},{9,8},{10,11... | collective-permute-start | bytes 2654216 | tf_op jit(solution)/shard_map/ppermute | solution.py:603
  340.0 99.0 %collective-permute-start.51 = (bf16[384,1152]{1,0:T(8,128)(2,1)}, bf16[384,1152]{1,0:T(8,128)(2,1)}, u32[]{:S(2)}, u32[]{:S(2)}) collective-permute-start(bf16[384,1152]{1,0:T(8,128)(2,1)} %get-tuple-element.226), channel_id=1, source_target_pairs={{0,1},{1,0},{2,3},{3,2},{4,5},{5,4},{6,7},{7,6},{8,9},{9,8},{10,11... | collective-permute-start | bytes 2654216 | tf_op jit(solution)/shard_map/ppermute | solution.py:603
  381.4 42.6 %collective-permute-start.47 = (bf16[4,528,128]{2,1,0:T(8,128)(2,1)S(1)}, bf16[4,528,128]{2,1,0:T(8,128)(2,1)S(1)}, u32[]{:S(2)}, u32[]{:S(2)}) collective-permute-start(bf16[4,528,128]{2,1,0:T(8,128)(2,1)S(1)} %dynamic-slice_bitcast_fusion.2), channel_id=1, source_target_pairs={{0,16},{16,0},{8,24},{24,8},{1,17},{17,1},{9,25},{25,9},{2,18},{18... | collective-permute-start | bytes 1622024 | tf_op jit(solution)/shard_map/ppermute | solution.py:965
  440.0 31.8 %collective-permute-start.53 = (bf16[384,256]{1,0:T(8,128)(2,1)S(1)}, bf16[384,256]{1,0:T(8,128)(2,1)S(1)}, u32[]{:S(2)}, u32[]{:S(2)}) collective-permute-start(bf16[384,256]{1,0:T(8,128)(2,1)S(1)} %copy-done.81), channel_id=1, source_target_pairs={{0,1},{1,0},{2,3},{3,2},{4,5},{5,4},{6,7},{7,6},{8,9},{9,8},{10,11... | collective-permute-start | bytes 589832 | tf_op jit(solution)/shard_map/ppermute | solution.py:603
  483.7 32.0 %collective-permute-start.65 = (bf16[384,1024]{1,0:T(8,128)(2,1)S(1)}, bf16[384,1024]{1,0:T(8,128)(2,1)S(1)}, u32[]{:S(2)}, u32[]{:S(2)}) collective-permute-start(bf16[384,1024]{1,0:T(8,128)(2,1)S(1)} %copy-done.62), channel_id=1, source_target_pairs={{0,1},{1,0},{2,3},{3,2},{4,5},{5,4},{6,7},{7,6},{8,9},{9,8},{10,11... | collective-permute-start | bytes 2359304 | tf_op jit(solution)/shard_map/ppermute | solution.py:603
  520.9 25.6 %collective-permute-start.82 = (bf16[4,640,128]{2,1,0:T(8,128)(2,1)S(1)}, bf16[4,640,128]{2,1,0:T(8,128)(2,1)S(1)}, u32[]{:S(2)}, u32[]{:S(2)}) collective-permute-start(bf16[4,640,128]{2,1,0:T(8,128)(2,1)S(1)} %pad_maximum_fusion.8.own), channel_id=1, source_target_pairs={{0,8},{8,0},{16,24},{24,16},{1,9},{9,1},{17,25},{25,17},{2,10},{10... | collective-permute-start | bytes 1966088 | tf_op jit(solution)/shard_map/ppermute | solution.py:976
  522.3 24.2 %collective-permute-start.83 = (bf16[4,640,128]{2,1,0:T(8,128)(2,1)S(1)}, bf16[4,640,128]{2,1,0:T(8,128)(2,1)S(1)}, u32[]{:S(2)}, u32[]{:S(2)}) collective-permute-start(bf16[4,640,128]{2,1,0:T(8,128)(2,1)S(1)} %collective-permute-done.81.x), channel_id=1, source_target_pairs={{0,8},{8,0},{16,24},{24,16},{1,9},{9,1},{17,25},{25,17},{2,10},{10... | collective-permute-start | bytes 1966088 | tf_op jit(solution)/shard_map/ppermute | solution.py:976
  (143 other events, 1619.8 us)
Sparse Core Ops, SparseCore 0:
  9.6 19.4 all-gather.9
  46.9 12.5 all-gather.11
  134.7 15.3 all-gather.15
  151.5 25.0 all-gather.13

commit v5 on v4

--- a/solution.py
+++ b/solution.py
@@ -37,7 +37,7 @@
         visit(pl.ds(pl.multiple_of(i * step, step), step))
         return carry
 
-    lax.fori_loop(0, rows // step, one, 0)
+    lax.fori_loop(0, rows // step, one, 0, unroll=5 if rows % (5 * step) == 0 else 2)
 
 
 def lanes_at(index, width):
@@ -710,6 +710,15 @@
     digit_rows = jnp.zeros((groups, 2, half), bf16).at[0, 0, : digits.shape[0]].set(digits)
     edges = jnp.concatenate([x_blocks[:, :2], g_blocks[:, :2], x_blocks[:, sub - 2 :], digit_rows], axis=1)
 
+    if special:
+        in_own = chip_pair(in_weight)
+        mixer_x, mixer_z, mixer_xc, mixer_zc = ([None] * 2 for _ in range(4))
+        feed_x, feed_z, feed_xc, feed_zc = ([None] * len(FEED_CUTS) for _ in range(4))
+        mixer_packed = [mixer_piece(k) for k in range(2)]
+        feed_packed = [feed_piece(k) for k in range(len(FEED_CUTS))]
+    x_got = [over_y(block_input[:span]), None]
+    if special:
+        mixer_x[0] = over_x(mixer_packed[0])
     all_edges = lax.all_gather(edges, "dp", axis=0, tiled=False)
     digits = all_edges[:, 0, 6, : 2 * numbers.shape[0]].astype(jnp.int32)
     table = digits[:, : numbers.shape[0]] * 64 + digits[:, numbers.shape[0] :]
@@ -732,18 +741,16 @@
             ((groups, 2, half), bf16, None, None),
         ],
     )
-    if special:
-        in_own = chip_pair(in_weight)
-        mixer_x, mixer_z, mixer_xc, mixer_zc = ([None] * 2 for _ in range(4))
-        feed_x, feed_z, feed_xc, feed_zc = ([None] * len(FEED_CUTS) for _ in range(4))
-        mixer_packed = [mixer_piece(k) for k in range(2)]
-        feed_packed = [feed_piece(k) for k in range(len(FEED_CUTS))]
-    wait(all_edges)
-    x_got = [over_y(block_input[:span]), None]
-    if special:
-        mixer_x[0] = over_x(mixer_packed[0])
+    stage = [all_edges, x_got[0]] + ([mixer_x[0], in_own, mixer_packed[1], feed_packed[0]] if special else [])
+    wait(*stage)
     from_next = begin("ctx", [(i + 1, i) for i in range(pieces - 1)], first_heads)
     from_prev = begin("ctx", [(i, i + 1) for i in range(pieces - 1)], last_tails)
+    x_got[1] = over_y(block_input[span:])
+    stage = [from_next, from_prev, x_got[1]]
+    if special:
+        mixer_x[1], mixer_z[0] = over_x(mixer_packed[1]), over_z(mixer_x[0])
+        out_own = chip_pair(out_weight)
+        stage += [mixer_x[1], mixer_z[0], out_own]
     deal_all = table[:, :groups]
     at_end = (deal_all[:, groups - 1] == me)[:, None, None]
     at_start = (deal_all[:, 0] == me)[:, None, None]
@@ -753,23 +760,17 @@
     halo_g = jnp.concatenate([jnp.zeros_like(prev_rows), next_rows[:, 2:]], axis=1)
     halo_own = jnp.stack([halo_x, halo_g]).reshape(2, CHUNKS, 4 * nb, half)
     halo_own = jnp.pad(halo_own, ((0, 0), (0, 0), (0, halo - 4 * nb), (0, 0)))
-    stage = [from_next, from_prev, x_got[0]] + ([mixer_x[0], in_own, mixer_packed[1]] if special else [])
     wait(*stage)
     halo_got = over_y(halo_own)
-    x_got[1] = over_y(block_input[span:])
-    stage = [halo_got, x_got[1]]
-    if special:
-        mixer_x[1], mixer_z[0], mixer_xc[0] = over_x(mixer_packed[1]), over_z(mixer_x[0]), core(mixer_x[0])
-        out_own = chip_pair(out_weight)
-        stage += [mixer_x[1], mixer_z[0], mixer_xc[0], out_own, feed_packed[0]]
-    wait(*stage)
-    g_got = [over_y(cotangent[:span]), None]
+    g_got = [over_y(after(cotangent[:span], halo_got)), None]
     stage = [g_got[0]]
     if special:
         feed_x[0], mixer_z[1] = over_x(feed_packed[0]), over_z(mixer_x[1])
-        mixer_xc[1], mixer_zc[0] = core(mixer_x[1]), core(mixer_z[0])
+        mixer_xc[0] = core(mixer_x[0])
+        mixer_xc[1] = core(after(mixer_x[1], mixer_xc[0]))
+        mixer_zc[0] = core(after(mixer_z[0], mixer_xc[1]))
         gu_own = chip_pair(gateup_weight)
-        stage += [feed_x[0], mixer_z[1], mixer_xc[1], mixer_zc[0], feed_packed[1]]
+        stage += [feed_x[0], mixer_z[1], mixer_xc[0], mixer_xc[1], mixer_zc[0], feed_packed[1]]
 
     gain_one, gain_two = mixer_gain[None, :].astype(f32), ffn_gain[None, :].astype(f32)
     ext_one, ext_two = width + rank, width + 2 * rank
@@ -981,7 +982,7 @@
     if special:
         feed_sum = scatter_core(cut(after(feed, chunks[0]["f_got"])))
     for i, c in enumerate(chunks):
-        f_got = after(c["f_got"], *([feed_sum] if special and i == 0 else []), *([chunks[0]["n_rank"]] if i else []))
+        f_got = after(c["f_got"], *([feed_sum] if special else []), *([chunks[0]["n_rank"]] if i else []))
         n_own, n_send, n_rank, grad_hidden, ffn_grad, second_grad, grads = call(
             functools.partial(back_kernel, cuts, span), (mixer_steps,), (info,),
             [(c["f_own"], None, None), (f_got, None, None), (c["hidden"], None, None), picked(glhs, i),
@@ -1013,10 +1014,7 @@
             feed_sum = scatter_x(feed_sum) if i == 0 else feed_sum
     for c in chunks:
         c["d_got"] = swap_tensor(after(c["d_send"], chunks[0]["f_got"]))
-    chunks[1]["rank_got"] = swap_tensor(chunks[1]["n_rank"])
-    chunks[0]["rank_got"] = swap_tensor(after(chunks[0]["n_rank"], chunks[1]["n_rank"]))
-    for c in chunks:
-        c["n_got"] = swap_tensor(after(c["n_send"], chunks[1]["rank_got"]))
+    chunks[0]["n_got"] = swap_tensor(chunks[0]["n_send"])
     if special:
         feed_sum = scatter_z(feed_sum)
         early = cut(after(summed("ffn_grad"), feed_sum, *(c["d_got"] for c in chunks)), summed("second_grad"), summed("mixer_grads"))
@@ -1054,14 +1052,16 @@
     wait()
     if special:
         feed_sum = gather_z(after(feed_sum, early))
-        early = after(scatter_x(early), feed_sum, chunks[-1]["out"])
+        early = after(scatter_x(early), feed_sum, chunks[-1]["out"], chunks[0]["n_got"])
         second_step = (early,)
     else:
         second_step = ()
+    for c in chunks[::-1]:
+        c["rank_got"] = swap_tensor(after(c["n_rank"], *second_step))
     for k, c in enumerate(chunks):
         in_stack_full = lambda i, info, k=k: (k, 0, info[3] * 4 + info[INNER + i])
         masks = (mask, (None, span, rank), lambda i, info, k=k: (k, 0, 0))
-        ranks = [(w, (span, 2 * rank), whole_block) for w in (c["n_rank"], after(c["rank_got"], *second_step))]
+        ranks = [(w, (span, 2 * rank), whole_block) for w in (c["n_rank"], c["rank_got"])]
         (c["in_grad"],) = call(
             rank_kernel, (4,), (info,), ranks + [masks, (lhs_one, (None, span, block), in_stack_full)], [grad_out],
             flops=5 * 10**9,
@@ -1069,13 +1069,13 @@
     if special:
         feed_parts = [feed_sum, begin("dp", x_route, after(feed_sum, early))]
         early = after(scatter_z(early), feed_parts[1], *(c["in_grad"] for c in chunks))
-        feed_parts += [begin("dp", core_route, v) for v in feed_parts]
         late = scatter_core(cut(summed("in_grad"), summed("down_grad")))
         h = 3 * 1024 // (4 * pieces)
         early = jnp.concatenate([early[:h], swap_tensor(early[:h]), early[h:]], axis=0)
         third_step = (early,)
     else:
         third_step = ()
+    chunks[1]["n_got"] = swap_tensor(after(chunks[1]["n_send"], *third_step))
     for k, c in enumerate(chunks):
         in_stack_full = lambda i, info, k=k: (k, 0, info[3] * 4 + info[INNER + i])
         masks = (mask, (None, span, rank), lambda i, info, k=k: (k, 0, 0))
@@ -1103,21 +1103,26 @@
 
     if special:
         late = scatter_x(after(late, early))
-        gathered = gather_z(early)
+        gathered = after(gather_z(early), chunks[0]["grad"], chunks[1]["n_got"])
         late = scatter_z(after(late, gathered))
+        n = 4 * pieces
+        feed_parts = [after(v, gathered) for v in feed_parts]
+        feed_parts += [lax.ppermute(v, "dp", core_route) for v in feed_parts]
+        expand_grad, first_grad = call(
+            functools.partial(gather_feed_kernel, pieces, feed_steps), (1,), (info,),
+            [(v, None, None) for v in feed_parts],
+            [((2, rank, hidden_units), f32, None, None), ((hidden_units, rank), f32, None, None)],
+            [pltpu.VMEM((feed.size // 128, 128), bf16)],
+            flops=5 * 10**9,
+        )
         late = jnp.concatenate([late, swap_tensor(late)], axis=0)
-        n = 4 * pieces
-        parts = gather_chip(gathered)
+        over = after(lax.ppermute(gathered, "dp", x_route), expand_grad, chunks[1]["grad"])
+        parts = [gathered, over] + [lax.ppermute(v, "dp", core_route) for v in (gathered, over)]
         ffn_grad, second_grad, mixer_grad, out_grad = call(
             functools.partial(unpack_early_kernel, pieces), (1,), (info,), [(v, None, None) for v in parts],
             [((width, 2 * rank), f32, None, None), ((rank, width), f32, None, None), ((3, rank, half), f32, None, None),
              ((half, rank), f32, None, None)],
             [pltpu.VMEM((n,) + early.shape, bf16)],
-        )
-        feed_outs = [((2, rank, hidden_units), f32, None, None), ((hidden_units, rank), f32, None, None)]
-        expand_grad, first_grad = call(
-            functools.partial(gather_feed_kernel, pieces, feed_steps), (1,), (info,), [(v, None, None) for v in feed_parts],
-            feed_outs, [pltpu.VMEM((feed.size // 128, 128), bf16)],
         )
         parts = gather_chip(gather_z(late))
         in_grad, down_grad = call(

time: 569 us -> 550 us (0.967)
  Pallas kernels: 297 us -> 281 us
  blocking collectives: 7.19 us -> 21.7 us
  waiting for transfers between devices: 113 us -> 105 us
  local copies, waits for them, and re-layouts: 30.1 us -> 23.6 us
    pallas_call x21, Pallas kernels: 297 us -> 281 us  [call(): pl.pallas_call(kernel, grid_spec=pltpu.PrefetchScalarGridSpec(num_scalar_...]
    all_gather x1, blocking collectives: 7.19 us -> 21.7 us  [body(): all_edges = lax.all_gather(edges, 'dp', axis=0, tiled=False)]
    ppermute x9, waiting for transfers between devices: 17.9 us -> 7.31 us  [gather_z(): lax.ppermute(total, 'ctx', route)]
    ppermute x9, waiting for transfers between devices: 13.8 us -> 3.17 us  [scatter_z(): lax.ppermute(take(total, (ctx + k) % pieces), 'ctx', route)]
    ppermute x2 -> x1, waiting for transfers between devices: 0.78 us -> 7.55 us  [gather_chip(): over_x = lax.ppermute(total, 'dp', x_route)]
    ppermute x10, waiting for transfers between devices: 7.45 us -> 13.2 us  [swap_tensor(): return lax.ppermute(array, 'tensor', [(0, 1), (1, 0)])]
    unnamed x170 -> x158, local copies, waits for them, and re-layouts: 14.3 us -> 10.4 us
    ppermute x46 -> x44, starting transfers between devices: 39 us -> 35.6 us  [begin(): return lax.ppermute(after(array, *gates), axis, route)]
  transfers between devices with their start and end apart: 90 -> 90, of which waited for: 32 -> 29; matrix products, arithmetic and copies ran while one was open for 6% -> 6% of each run, Pallas kernels for 44% -> 43%
where the time goes in v5:
time: 550 us; the launch traced here: 541 us
  Pallas kernels  281 us (51%)
  waiting for transfers between devices  105 us (19%)
  starting transfers between devices  74.4 us (14%)
  local copies, waits for them, and re-layouts  23.6 us (4%)
  blocking collectives  21.7 us (4%)
  other arithmetic  19.7 us (4%)
  between operations  15.5 us (3%)
    pallas_call x21, Pallas kernels, call(): pl.pallas_call(kernel, grid_spec=pltpu.PrefetchScalarGridSpec(num_scalar_...  281 us
    ppermute x44, waiting for transfers between devices, begin(): return lax.ppermute(after(array, *gates), axis, route)  70.5 us
    ppermute x44, starting transfers between devices, begin(): return lax.ppermute(after(array, *gates), axis, route)  35.6 us
    all_gather x1, blocking collectives, body(): all_edges = lax.all_gather(edges, 'dp', axis=0, tiled=False)  21.7 us
    ppermute x10, waiting for transfers between devices, swap_tensor(): return lax.ppermute(array, 'tensor', [(0, 1), (1, 0)])  13.2 us
    ppermute x9, starting transfers between devices, scatter_z(): lax.ppermute(take(total, (ctx + k) % pieces), 'ctx', route)  12.4 us
  transfers between devices with their start and end apart: 90, of which 29 were waited for; matrix products, arithmetic and copies ran while one was open for 6% of the time, Pallas kernels for 43%

profile of v5, /device:TPU:0, one launch (start us, length us, event | category | flops | bytes accessed | tf_op | source)
XLA Modules:
  0.0 541.1 jit_solution(6630522537186521180)
XLA Ops:
  20.0 21.7 %all-gather = bf16[16,8,1024]{2,1,0:T(8,128)(2,1)S(1)} all-gather(bf16[4,8,1024]{2,1,0:T(8,128)(2,1)S(1)} %pad_maximum_fusion.13), channel_id=2, replica_groups=mesh['dp'=4,'ctx'=4,'tensor'=2] {'dp'}, dimensions={0}, use_global_device_ids=true | all-gather | bytes 327680 | tf_op jit(solution)/shard_map/all_gather | solution.py:722
  55.2 4.5 collective-permute-start.3
  59.8 12.6 %collective-permute-done.3 = bf16[4,2,1024]{2,1,0:T(2,128)(2,1)S(1)} collective-permute-done((bf16[4,2,1024]{2,1,0:T(2,128)(2,1)}, bf16[4,2,1024]{2,1,0:T(2,128)(2,1)S(1)}, u32[]{:S(2)}, u32[]{:S(2)}) %collective-permute-start.3) | collective-permute-done | bytes 16416 | tf_op jit(solution)/shard_map/ppermute | solution.py:672
  90.9 7.7 %shard_map.269 = (bf16[2,400,2048]{2,1,0:T(8,128)(2,1)}, bf16[2,400,2176]{2,1,0:T(8,128)(2,1)}, f32[2,400,128]{2,1,0:T(8,128)}) custom-call(s32[24]{0:T(128)} %stack.153.info, bf16[768,1024]{1,0:T(8,128)(2,1)} %own.2, bf16[384,1024]{1,0:T(8,128)(2,1)} %collective-permute-done.got_first, bf16[384,1024]{1,0:T(8,128)(2,1)} %collective-permute-done.2.got_second, ...), custom_call_target="tpu_custom_call" | custom-call | flops 1 | bytes 1 | tf_op jit(solution)/shard_map/pallas_call | solution.py:67
  98.6 5.1 collective-permute-done.13.refs_2_
  111.1 20.3 %shard_map.271 = (f32[400,1024]{1,0:T(8,128)}, f32[400,1024]{1,0:T(8,128)}, f32[400,1024]{1,0:T(8,128)}, f32[400,1024]{1,0:T(8,128)}, bf16[400,1024]{1,0:T(8,128...) custom-call(bf16[2,400,2176]{2,1,0:T(8,128)(2,1)} %get-tuple-element.163.lhs.lhs_one.normed.refs_6_, ...), custom_call_target="tpu_custom_call" | custom-call | flops 7130316800 | bytes 1 | tf_op jit(solution)/shard_map/pallas_call | solution.py:67
  137.4 22.3 %shard_map.270 = (f32[400,1024]{1,0:T(8,128)}, f32[400,1024]{1,0:T(8,128)}, f32[400,1024]{1,0:T(8,128)}, f32[400,1024]{1,0:T(8,128)}, bf16[400,1024]{1,0:T(8,128...) custom-call(bf16[2,400,2176]{2,1,0:T(8,128)(2,1)} %get-tuple-element.163.lhs.lhs_one.normed.refs_6_, ...), custom_call_target="tpu_custom_call" | custom-call | flops 7130316800 | bytes 1 | tf_op jit(solution)/shard_map/pallas_call | solution.py:67
  162.4 19.4 %collective-permute-done.25.refs_5_ = bf16[3,256,512]{2,1,0:T(8,128)(2,1)} collective-permute-done((bf16[3,256,512]{2,1,0:T(8,128)(2,1)S(1)}, bf16[3,256,512]{2,1,0:T(8,128)(2,1)}, u32[]{:S(2)}, u32[]{:S(2)}) %collective-permute-start.25) | collective-permute-done | bytes 786464 | tf_op jit(solution)/shard_map/ppermute | solution.py:672
  186.9 5.4 %shard_map.272.glhs.refs_6_ = bf16[2,400,2176]{2,1,0:T(8,128)(2,1)} custom-call(s32[24]{0:T(128)} %stack.153.info, bf16[768,1024]{1,0:T(8,128)(2,1)} %own.3, bf16[384,1024]{1,0:T(8,128)(2,1)} %copy-done.30, bf16[384,1024]{1,0:T(8,128)(2,1)} %copy-done.31, bf16[2,2,16,1024]{3,2,1,0:T(8,128)(2,1)} %copy-done.15, bf16[2,2,16,1024]{3,2,1,0:T(8,128)(2,1)} %copy-done.37, ...), custom_call_target="tpu_custom_call" | custom-call | flops 1 | bytes 1 | tf_op jit(solution)/shard_map/pallas_call | solution.py:67
  192.4 11.9 %collective-permute-done.30.refs_6_ = bf16[3,256,512]{2,1,0:T(8,128)(2,1)} collective-permute-done((bf16[3,256,512]{2,1,0:T(8,128)(2,1)S(1)}, bf16[3,256,512]{2,1,0:T(8,128)(2,1)}, u32[]{:S(2)}, u32[]{:S(2)}) %collective-permute-start.30) | collective-permute-done | bytes 786464 | tf_op jit(solution)/shard_map/ppermute | solution.py:672
  208.7 8.8 %shard_map.274 = (f32[400,2048]{1,0:T(8,128)}, bf16[400,2304]{1,0:T(8,128)(2,1)}, bf16[400,128]{1,0:T(8,128)(2,1)}) custom-call(s32[24]{0:T(128)} %stack.153.info, bf16[2,400,2048]{2,1,0:T(8,128)(2,1)} %get-tuple-element.162.x.refs_5_, bf16[192,2176]{1,0:T(8,128)(2,1)} %get-tuple-element.183.part_first, bf16[208,2176]{1,0:T(8,128)(2,1)} %get-tuple-element.187.part_second, ...), custom_call_target="tpu_custom_call" | custom-call | flops 1 | bytes 1 | tf_op jit(solution)/shard_map/pallas_call | solution.py:67
  218.8 6.6 %collective-permute-done.36.refs_12_ = bf16[3,256,512]{2,1,0:T(8,128)(2,1)S(1)} collective-permute-done((bf16[3,256,512]{2,1,0:T(8,128)(2,1)}, bf16[3,256,512]{2,1,0:T(8,128)(2,1)S(1)}, u32[]{:S(2)}, u32[]{:S(2)}) %collective-permute-start.36) | collective-permute-done | bytes 786464 | tf_op jit(solution)/shard_map/ppermute | solution.py:672
  228.2 8.6 %shard_map.273 = (f32[400,2048]{1,0:T(8,128)}, bf16[400,2304]{1,0:T(8,128)(2,1)}, bf16[400,128]{1,0:T(8,128)(2,1)}) custom-call(s32[24]{0:T(128)} %stack.153.info, bf16[2,400,2048]{2,1,0:T(8,128)(2,1)} %get-tuple-element.162.x.refs_5_, bf16[192,2176]{1,0:T(8,128)(2,1)} %get-tuple-element.191.part_first, bf16[208,2176]{1,0:T(8,128)(2,1)} %get-tuple-element.195.part_second, ...), custom_call_target="tpu_custom_call" | custom-call | flops 1 | bytes 1 | tf_op jit(solution)/shard_map/pallas_call | solution.py:67
  241.4 44.6 %shard_map.276 = (bf16[400,2304]{1,0:T(8,128)(2,1)}, bf16[384,1152]{1,0:T(8,128)(2,1)}, bf16[384,1152]{1,0:T(8,128)(2,1)}, f32[11,3,2,128,128]{4,3,2,1,0:T(8,128)}) custom-call(s32[24]{0:T(128)} %stack.153.info, bf16[400,2304]{1,0:T(8,128)(2,1)} %get-tuple-element.202.lhs.lhs_two, bf16[2,400,2176]{2,1,0:T(8,128)(2,1)} %shard_map.272.glhs.refs_6_, ...), custom_call_target="tpu_custom_call" | custom-call | flops 31142707200 | bytes 1 | tf_op jit(solution)/shard_map/pallas_call | solution.py:67
  287.1 44.8 %shard_map.275 = (bf16[400,2304]{1,0:T(8,128)(2,1)}, bf16[384,1152]{1,0:T(8,128)(2,1)}, bf16[384,1152]{1,0:T(8,128)(2,1)}, f32[11,3,2,128,128]{4,3,2,1,0:T(8,128)}) custom-call(s32[24]{0:T(128)} %stack.153.info, bf16[400,2304]{1,0:T(8,128)(2,1)} %get-tuple-element.196.lhs.lhs_two, bf16[2,400,2176]{2,1,0:T(8,128)(2,1)} %shard_map.272.glhs.refs_6_, ...), custom_call_target="tpu_custom_call" | custom-call | flops 31142707200 | bytes 1 | tf_op jit(solution)/shard_map/pallas_call | solution.py:67
  331.9 3.2 add_convert_fusion
  340.3 33.9 %shard_map.277 = (bf16[384,1024]{1,0:T(8,128)(2,1)}, bf16[384,1024]{1,0:T(8,128)(2,1)}, bf16[384,256]{1,0:T(8,128)(2,1)}, f32[400,2048]{1,0:T(8,128)}, f32[4,2,2...) custom-call(s32[24]{0:T(128)} %stack.153.info, ...), custom_call_target="tpu_custom_call" | custom-call | flops 7130316800 | bytes 1 | tf_op jit(solution)/shard_map/pallas_call | solution.py:67
  374.3 4.3 collective-permute-done.46.got
  383.4 34.2 %shard_map.278 = (bf16[384,1024]{1,0:T(8,128)(2,1)}, bf16[384,1024]{1,0:T(8,128)(2,1)}, bf16[384,256]{1,0:T(8,128)(2,1)}, f32[400,2048]{1,0:T(8,128)}, f32[4,2,2...) custom-call(s32[24]{0:T(128)} %stack.153.info, ...), custom_call_target="tpu_custom_call" | custom-call | flops 7130316800 | bytes 1 | tf_op jit(solution)/shard_map/pallas_call | solution.py:67
  429.3 5.3 shard_map.279
  434.6 5.3 shard_map.280
  449.7 4.7 shard_map.281
  455.2 4.7 shard_map.282
  471.7 5.9 %shard_map.283.refs_11_ = f32[768,1024]{1,0:T(8,128)} custom-call(s32[24]{0:T(128)} %stack.153.info, bf16[384,1024]{1,0:T(8,128)(2,1)} %get-tuple-element.259.refs_0_, bf16[384,1024]{1,0:T(8,128)(2,1)} %copy-done.59, bf16[384,256]{1,0:T(8,128)(2,1)} %get-tuple-element.251.own.refs_2_, bf16[384,256]{1,0:T(8,128)(2,1)} %copy-done.76, ...), custom_call_target="tpu_custom_call" | custom-call | flops 6000000000 | bytes 1 | tf_op jit(solution)/shard_map/pallas_call | solution.py:67
  477.7 5.9 %collective-permute-done.69 = bf16[640,128]{1,0:T(8,128)(2,1)S(1)} collective-permute-done((bf16[640,128]{1,0:T(8,128)(2,1)S(1)}, bf16[640,128]{1,0:T(8,128)(2,1)S(1)}, u32[]{:S(2)}, u32[]{:S(2)}) %collective-permute-start.69) | collective-permute-done | bytes 163872 | tf_op jit(solution)/shard_map/ppermute | solution.py:973
  483.7 4.2 collective-permute-done.65.refs_1_
  487.9 3.6 collective-permute-start.73
  498.4 5.9 %shard_map.284 = f32[768,1024]{1,0:T(8,128)} custom-call(s32[24]{0:T(128)} %stack.153.info, bf16[384,1024]{1,0:T(8,128)(2,1)} %get-tuple-element.245.refs_0_, bf16[384,1024]{1,0:T(8,128)(2,1)} %copy-done.65, bf16[384,256]{1,0:T(8,128)(2,1)} %get-tuple-element.253.own.refs_2_, bf16[384,256]{1,0:T(8,128)(2,1)} %copy-done.75, ...), custom_call_target="tpu_custom_call", output_to_operand_aliasing={{}: (12, {})} | custom-call | flops 6000000000 | bytes 1 | tf_op jit(solution)/shard_map/pallas_call | solution.py:67
  507.7 4.9 shard_map.286
  514.0 7.6 %collective-permute-done.78.x = bf16[4,256,128]{2,1,0:T(8,128)(2,1)S(1)} collective-permute-done((bf16[4,256,128]{2,1,0:T(8,128)(2,1)S(1)}, bf16[4,256,128]{2,1,0:T(8,128)(2,1)S(1)}, u32[]{:S(2)}, u32[]{:S(2)}) %collective-permute-start.78) | collective-permute-done | bytes 262176 | tf_op jit(solution)/shard_map/ppermute | solution.py:976
  523.8 3.6 shard_map.285
  529.1 5.3 shard_map.287
  (421 shorter events, 139.0 us)
Async XLA Ops:
  7.2 38.7 %all-gather.10.cloned.1.call-start = ((), (), s32[]{:S(2)}) async-start(), calls=%async_computation | async-start | bytes 9437184 | tf_op jit(solution)/shard_map/all_gather | solution.py:700
  7.9 65.7 %all-gather.12.cloned.1.call-start = ((), (), s32[]{:S(2)}) async-start(), calls=%async_computation.1 | async-start | bytes 3145728 | tf_op jit(solution)/shard_map/all_gather | solution.py:700
  9.8 36.1 %collective-permute-start = (bf16[384,1024]{1,0:T(8,128)(2,1)}, bf16[384,1024]{1,0:T(8,128)(2,1)}, u32[]{:S(2)}, u32[]{:S(2)}) collective-permute-start(bf16[384,1024]{1,0:T(8,128)(2,1)} %get-tuple-element.299), channel_id=1, source_target_pairs={{0,1},{1,0},{2,3},{3,2},{4,5},{5,4},{6,7},{7,6},{8,9},{9,8},{10,11... | collective-permute-start | bytes 2359304 | tf_op jit(solution)/shard_map/ppermute | solution.py:672
  14.7 31.2 %collective-permute-start.1 = (bf16[4,256,512]{2,1,0:T(8,128)(2,1)S(1)}, bf16[4,256,512]{2,1,0:T(8,128)(2,1)}, u32[]{:S(2)}, u32[]{:S(2)}) collective-permute-start(bf16[4,256,512]{2,1,0:T(8,128)(2,1)S(1)} %pad_maximum_fusion.1), channel_id=1, source_target_pairs={{0,16},{16,0},{8,24},{24,8},{1,17},{17,1},{9,25},{25,9},{2,18},{18... | collective-permute-start | bytes 3145736 | tf_op jit(solution)/shard_map/ppermute | solution.py:672
  45.9 195.4 %all-gather.16.cloned.1.call-start = ((), (), s32[]{:S(2)}) async-start(), calls=%async_computation.3 | async-start | bytes 8650752 | tf_op jit(solution)/shard_map/all_gather | solution.py:700
  46.0 27.6 %collective-permute-start.5 = (bf16[4,256,512]{2,1,0:T(8,128)(2,1)}, bf16[4,256,512]{2,1,0:T(8,128)(2,1)S(1)}, u32[]{:S(2)}, u32[]{:S(2)}) collective-permute-start(bf16[4,256,512]{2,1,0:T(8,128)(2,1)} %pad_maximum_fusion.2), channel_id=1, source_target_pairs={{0,16},{16,0},{8,24},{24,8},{1,17},{17,1},{9,25},{25,9},{2,18},{18... | collective-permute-start | bytes 3145736 | tf_op jit(solution)/shard_map/ppermute | solution.py:672
  47.5 26.1 %collective-permute-start.6 = (bf16[4,256,512]{2,1,0:T(8,128)(2,1)}, bf16[4,256,512]{2,1,0:T(8,128)(2,1)}, u32[]{:S(2)}, u32[]{:S(2)}) collective-permute-start(bf16[4,256,512]{2,1,0:T(8,128)(2,1)} %collective-permute-done.1.refs_2_), channel_id=1, source_target_pairs={{0,2},{2,0},{4,6},{6,4},{1,3},{3,1},{5,7},{7,5},{8,10},{10,8},{12,... | collective-permute-start | bytes 3145736 | tf_op jit(solution)/shard_map/ppermute | solution.py:672
  49.1 24.5 %collective-permute-start.2 = (bf16[384,1024]{1,0:T(8,128)(2,1)}, bf16[384,1024]{1,0:T(8,128)(2,1)}, u32[]{:S(2)}, u32[]{:S(2)}) collective-permute-start(bf16[384,1024]{1,0:T(8,128)(2,1)} %get-tuple-element.150), channel_id=1, source_target_pairs={{0,1},{1,0},{2,3},{3,2},{4,5},{5,4},{6,7},{7,6},{8,9},{9,8},{10,11... | collective-permute-start | bytes 2359304 | tf_op jit(solution)/shard_map/ppermute | solution.py:672
  80.9 25.1 %collective-permute-start.8 = (bf16[4,256,512]{2,1,0:T(8,128)(2,1)S(1)}, bf16[4,256,512]{2,1,0:T(8,128)(2,1)S(1)}, u32[]{:S(2)}, u32[]{:S(2)}) collective-permute-start(bf16[4,256,512]{2,1,0:T(8,128)(2,1)S(1)} %collective-permute-done.5.refs_3_), channel_id=1, source_target_pairs={{0,2},{2,0},{4,6},{6,4},{1,3},{3,1},{5,7},{7,5},{8,10},{10,8},{12,... | collective-permute-start | bytes 3145736 | tf_op jit(solution)/shard_map/ppermute | solution.py:672
  82.2 23.9 %collective-permute-start.11 = (bf16[4,256,512]{2,1,0:T(8,128)(2,1)}, bf16[4,256,512]{2,1,0:T(8,128)(2,1)S(1)}, u32[]{:S(2)}, u32[]{:S(2)}) collective-permute-start(bf16[4,256,512]{2,1,0:T(8,128)(2,1)} %collective-permute-done.6.refs_4_), channel_id=1, source_target_pairs={{0,8},{8,0},{16,24},{24,16},{1,9},{9,1},{17,25},{25,17},{2,10},{10... | collective-permute-start | bytes 3145736 | tf_op jit(solution)/shard_map/ppermute | solution.py:672
  106.2 25.2 %collective-permute-start.17 = (bf16[3,256,512]{2,1,0:T(8,128)(2,1)}, bf16[3,256,512]{2,1,0:T(8,128)(2,1)}, u32[]{:S(2)}, u32[]{:S(2)}) collective-permute-start(bf16[3,256,512]{2,1,0:T(8,128)(2,1)} %collective-permute-done.13.refs_2_), channel_id=1, source_target_pairs={{0,2},{2,0},{4,6},{6,4},{1,3},{3,1},{5,7},{7,5},{8,10},{10,8},{12,... | collective-permute-start | bytes 2359304 | tf_op jit(solution)/shard_map/ppermute | solution.py:672
  107.5 23.9 %collective-permute-start.18 = (bf16[3,256,512]{2,1,0:T(8,128)(2,1)}, bf16[3,256,512]{2,1,0:T(8,128)(2,1)}, u32[]{:S(2)}, u32[]{:S(2)}) collective-permute-start(bf16[3,256,512]{2,1,0:T(8,128)(2,1)} %collective-permute-done.13.refs_2_), channel_id=1, source_target_pairs={{0,8},{8,0},{16,24},{24,16},{1,9},{9,1},{17,25},{25,17},{2,10},{10... | collective-permute-start | bytes 2359304 | tf_op jit(solution)/shard_map/ppermute | solution.py:672
  107.7 23.6 %collective-permute-start.15 = (bf16[384,1024]{1,0:T(8,128)(2,1)}, bf16[384,1024]{1,0:T(8,128)(2,1)S(1)}, u32[]{:S(2)}, u32[]{:S(2)}) collective-permute-start(bf16[384,1024]{1,0:T(8,128)(2,1)} %get-tuple-element.180), channel_id=1, source_target_pairs={{0,1},{1,0},{2,3},{3,2},{4,5},{5,4},{6,7},{7,6},{8,9},{9,8},{10,11... | collective-permute-start | bytes 2359304 | tf_op jit(solution)/shard_map/ppermute | solution.py:672
  108.6 22.8 %collective-permute-start.16 = (bf16[3,256,512]{2,1,0:T(8,128)(2,1)}, bf16[3,256,512]{2,1,0:T(8,128)(2,1)}, u32[]{:S(2)}, u32[]{:S(2)}) collective-permute-start(bf16[3,256,512]{2,1,0:T(8,128)(2,1)} %pad_maximum_fusion.4), channel_id=1, source_target_pairs={{0,16},{16,0},{8,24},{24,8},{1,17},{17,1},{9,25},{25,9},{2,18},{18... | collective-permute-start | bytes 2359304 | tf_op jit(solution)/shard_map/ppermute | solution.py:672
  131.5 109.9 %all-gather.14.cloned.1.call-start = ((), (), s32[]{:S(2)}) async-start(), calls=%async_computation.2 | async-start | bytes 17301504 | tf_op jit(solution)/shard_map/all_gather | solution.py:700
  133.6 26.2 %collective-permute-start.19 = (bf16[192,2176]{1,0:T(8,128)(2,1)S(1)}, bf16[192,2176]{1,0:T(8,128)(2,1)S(1)}, u32[]{:S(2)}, u32[]{:S(2)}) collective-permute-start(bf16[192,2176]{1,0:T(8,128)(2,1)S(1)} %copy-done.26), channel_id=1, source_target_pairs={{0,1},{1,0},{2,3},{3,2},{4,5},{5,4},{6,7},{7,6},{8,9},{9,8},{10,11... | collective-permute-start | bytes 2506760 | tf_op jit(solution)/shard_map/ppermute | solution.py:672
  134.7 25.0 %collective-permute-start.21 = (bf16[3,256,512]{2,1,0:T(8,128)(2,1)}, bf16[3,256,512]{2,1,0:T(8,128)(2,1)S(1)}, u32[]{:S(2)}, u32[]{:S(2)}) collective-permute-start(bf16[3,256,512]{2,1,0:T(8,128)(2,1)} %collective-permute-done.16.refs_3_), channel_id=1, source_target_pairs={{0,2},{2,0},{4,6},{6,4},{1,3},{3,1},{5,7},{7,5},{8,10},{10,8},{12,... | collective-permute-start | bytes 2359304 | tf_op jit(solution)/shard_map/ppermute | solution.py:672
  135.6 24.2 %collective-permute-start.22 = (bf16[3,256,512]{2,1,0:T(8,128)(2,1)}, bf16[3,256,512]{2,1,0:T(8,128)(2,1)S(1)}, u32[]{:S(2)}, u32[]{:S(2)}) collective-permute-start(bf16[3,256,512]{2,1,0:T(8,128)(2,1)} %collective-permute-done.16.refs_3_), channel_id=1, source_target_pairs={{0,8},{8,0},{16,24},{24,16},{1,9},{9,1},{17,25},{25,17},{2,10},{10... | collective-permute-start | bytes 2359304 | tf_op jit(solution)/shard_map/ppermute | solution.py:672
  135.6 24.2 %collective-permute-start.20 = (bf16[3,256,512]{2,1,0:T(8,128)(2,1)S(1)}, bf16[3,256,512]{2,1,0:T(8,128)(2,1)}, u32[]{:S(2)}, u32[]{:S(2)}) collective-permute-start(bf16[3,256,512]{2,1,0:T(8,128)(2,1)S(1)} %copy-done.32), channel_id=1, source_target_pairs={{0,16},{16,0},{8,24},{24,8},{1,17},{17,1},{9,25},{25,9},{2,18},{18... | collective-permute-start | bytes 2359304 | tf_op jit(solution)/shard_map/ppermute | solution.py:672
  137.1 22.7 %collective-permute-start.23 = (bf16[3,256,512]{2,1,0:T(8,128)(2,1)}, bf16[3,256,512]{2,1,0:T(8,128)(2,1)}, u32[]{:S(2)}, u32[]{:S(2)}) collective-permute-start(bf16[3,256,512]{2,1,0:T(8,128)(2,1)} %collective-permute-done.17.refs_8_), channel_id=1, source_target_pairs={{0,8},{8,0},{16,24},{24,16},{1,9},{9,1},{17,25},{25,17},{2,10},{10... | collective-permute-start | bytes 2359304 | tf_op jit(solution)/shard_map/ppermute | solution.py:672
  159.9 22.3 %collective-permute-start.24 = (bf16[208,2176]{1,0:T(8,128)(2,1)S(1)}, bf16[208,2176]{1,0:T(8,128)(2,1)S(1)}, u32[]{:S(2)}, u32[]{:S(2)}) collective-permute-start(bf16[208,2176]{1,0:T(8,128)(2,1)S(1)} %copy-done.22), channel_id=1, source_target_pairs={{0,1},{1,0},{2,3},{3,2},{4,5},{5,4},{6,7},{7,6},{8,9},{9,8},{10,11... | collective-permute-start | bytes 2715656 | tf_op jit(solution)/shard_map/ppermute | solution.py:672
  182.2 23.0 %collective-permute-start.29 = (bf16[192,2176]{1,0:T(8,128)(2,1)S(1)}, bf16[192,2176]{1,0:T(8,128)(2,1)S(1)}, u32[]{:S(2)}, u32[]{:S(2)}) collective-permute-start(bf16[192,2176]{1,0:T(8,128)(2,1)S(1)} %copy-done.27), channel_id=1, source_target_pairs={{0,1},{1,0},{2,3},{3,2},{4,5},{5,4},{6,7},{7,6},{8,9},{9,8},{10,11... | collective-permute-start | bytes 2506760 | tf_op jit(solution)/shard_map/ppermute | solution.py:672
  205.2 21.8 %collective-permute-start.34 = (bf16[208,2176]{1,0:T(8,128)(2,1)S(1)}, bf16[208,2176]{1,0:T(8,128)(2,1)S(1)}, u32[]{:S(2)}, u32[]{:S(2)}) collective-permute-start(bf16[208,2176]{1,0:T(8,128)(2,1)S(1)} %copy-done.23), channel_id=1, source_target_pairs={{0,1},{1,0},{2,3},{3,2},{4,5},{5,4},{6,7},{7,6},{8,9},{9,8},{10,11... | collective-permute-start | bytes 2715656 | tf_op jit(solution)/shard_map/ppermute | solution.py:672
  286.0 49.1 %collective-permute-start.43 = (bf16[400,2304]{1,0:T(8,128)(2,1)}, bf16[400,2304]{1,0:T(8,128)(2,1)}, u32[]{:S(2)}, u32[]{:S(2)}) collective-permute-start(bf16[400,2304]{1,0:T(8,128)(2,1)} %get-tuple-element.208.part), channel_id=1, source_target_pairs={{0,1},{1,0},{2,3},{3,2},{4,5},{5,4},{6,7},{7,6},{8,9},{9,8},{10,11... | collective-permute-start | bytes 5529608 | tf_op jit(solution)/shard_map/ppermute | solution.py:603
  335.3 43.4 %collective-permute-start.46 = (bf16[400,2304]{1,0:T(8,128)(2,1)}, bf16[400,2304]{1,0:T(8,128)(2,1)}, u32[]{:S(2)}, u32[]{:S(2)}) collective-permute-start(bf16[400,2304]{1,0:T(8,128)(2,1)} %get-tuple-element.222.part), channel_id=1, source_target_pairs={{0,1},{1,0},{2,3},{3,2},{4,5},{5,4},{6,7},{7,6},{8,9},{9,8},{10,11... | collective-permute-start | bytes 5529608 | tf_op jit(solution)/shard_map/ppermute | solution.py:603
  336.3 85.5 %collective-permute-start.44 = (bf16[384,1152]{1,0:T(8,128)(2,1)}, bf16[384,1152]{1,0:T(8,128)(2,1)S(1)}, u32[]{:S(2)}, u32[]{:S(2)}) collective-permute-start(bf16[384,1152]{1,0:T(8,128)(2,1)} %get-tuple-element.209), channel_id=1, source_target_pairs={{0,1},{1,0},{2,3},{3,2},{4,5},{5,4},{6,7},{7,6},{8,9},{9,8},{10,11... | collective-permute-start | bytes 2654216 | tf_op jit(solution)/shard_map/ppermute | solution.py:603
  337.4 84.4 %collective-permute-start.51 = (bf16[384,1152]{1,0:T(8,128)(2,1)}, bf16[384,1152]{1,0:T(8,128)(2,1)S(1)}, u32[]{:S(2)}, u32[]{:S(2)}) collective-permute-start(bf16[384,1152]{1,0:T(8,128)(2,1)} %get-tuple-element.234), channel_id=1, source_target_pairs={{0,1},{1,0},{2,3},{3,2},{4,5},{5,4},{6,7},{7,6},{8,9},{9,8},{10,11... | collective-permute-start | bytes 2654216 | tf_op jit(solution)/shard_map/ppermute | solution.py:603
  339.9 34.3 %collective-permute-start.47 = (bf16[4,528,128]{2,1,0:T(8,128)(2,1)S(1)}, bf16[4,528,128]{2,1,0:T(8,128)(2,1)S(1)}, u32[]{:S(2)}, u32[]{:S(2)}) collective-permute-start(bf16[4,528,128]{2,1,0:T(8,128)(2,1)S(1)} %dynamic-slice_bitcast_fusion.2), channel_id=1, source_target_pairs={{0,16},{16,0},{8,24},{24,8},{1,17},{17,1},{9,25},{25,9},{2,18},{18... | collective-permute-start | bytes 1622024 | tf_op jit(solution)/shard_map/ppermute | solution.py:966
  378.7 42.9 %collective-permute-start.50 = (bf16[528,128]{1,0:T(8,128)(2,1)S(1)}, bf16[528,128]{1,0:T(8,128)(2,1)S(1)}, u32[]{:S(2)}, u32[]{:S(2)}) collective-permute-start(bf16[528,128]{1,0:T(8,128)(2,1)S(1)} %get-tuple-element.303), channel_id=1, source_target_pairs={{0,6},{2,0},{4,2},{6,4},{1,7},{3,1},{5,3},{7,5},{8,14},{10,8},{12,... | collective-permute-start | bytes 405512 | tf_op jit(solution)/shard_map/ppermute | solution.py:969
  381.7 39.9 %collective-permute-start.49 = (bf16[528,128]{1,0:T(8,128)(2,1)S(1)}, bf16[528,128]{1,0:T(8,128)(2,1)S(1)}, u32[]{:S(2)}, u32[]{:S(2)}) collective-permute-start(bf16[528,128]{1,0:T(8,128)(2,1)S(1)} %get-tuple-element.304), channel_id=1, source_target_pairs={{0,4},{2,6},{4,0},{6,2},{1,5},{3,7},{5,1},{7,3},{8,12},{10,14},{12... | collective-permute-start | bytes 405512 | tf_op jit(solution)/shard_map/ppermute | solution.py:969
  381.7 39.9 %collective-permute-start.48 = (bf16[528,128]{1,0:T(8,128)(2,1)S(1)}, bf16[528,128]{1,0:T(8,128)(2,1)S(1)}, u32[]{:S(2)}, u32[]{:S(2)}) collective-permute-start(bf16[528,128]{1,0:T(8,128)(2,1)S(1)} %get-tuple-element.302), channel_id=1, source_target_pairs={{0,2},{2,4},{4,6},{6,0},{1,3},{3,5},{5,7},{7,1},{8,10},{10,12},{12... | collective-permute-start | bytes 405512 | tf_op jit(solution)/shard_map/ppermute | solution.py:969
  493.6 33.9 %collective-permute-start.84 = (bf16[4,640,128]{2,1,0:T(8,128)(2,1)S(1)}, bf16[4,640,128]{2,1,0:T(8,128)(2,1)S(1)}, u32[]{:S(2)}, u32[]{:S(2)}) collective-permute-start(bf16[4,640,128]{2,1,0:T(8,128)(2,1)S(1)} %pad_maximum_fusion.8.own), channel_id=1, source_target_pairs={{0,8},{8,0},{16,24},{24,16},{1,9},{9,1},{17,25},{25,17},{2,10},{10... | collective-permute-start | bytes 1966088 | tf_op jit(solution)/shard_map/ppermute | solution.py:1120
  (137 other events, 1514.7 us)
Sparse Core Ops, SparseCore 0:
  9.6 19.4 all-gather.9
  46.1 11.4 all-gather.11
  131.6 16.0 all-gather.15
  149.1 25.0 all-gather.13

commit v6 on v5

--- a/solution.py
+++ b/solution.py
@@ -250,14 +250,18 @@
         part_second[...] = acc[cut:, :].astype(bf16)
 
 
-def blocks_across(ref, value):
+def blocks_across(ref, value, earlier=None, *at):
     for i in range(value.shape[1] // 128):
-        ref[i] = value[:, i * 128 : (i + 1) * 128]
-
-
-def blocks_down(ref, value):
+        block = value[:, i * 128 : (i + 1) * 128]
+        block = block if earlier is None else block + earlier[(*at, i)]
+        ref[(*at, i)] = block.astype(ref.dtype)
+
+
+def blocks_down(ref, value, earlier=None, *at):
     for i in range(value.shape[0] // 128):
-        ref[i] = value[i * 128 : (i + 1) * 128, :]
+        block = value[i * 128 : (i + 1) * 128, :]
+        block = block if earlier is None else block + earlier[(*at, i)]
+        ref[(*at, i)] = block.astype(ref.dtype)
 
 
 def middle_kernel(info, x, part_first, part_second, got_first, got_second, mask, gain, out_second, ffn_first,
@@ -290,7 +294,9 @@
     lhs[:, width + rank :] = low[:, rank:] * mask[...]
 
 
-def feed_kernel(cuts, span, info, lhs, glhs, ffn_expand, down_shrink, *refs):
+def feed_kernel(cuts, span, later, info, lhs, glhs, ffn_expand, down_shrink, *refs):
+    earlier = refs[0] if later else None
+    refs = refs[1:] if later else refs
     if len(cuts) == 1:
         gu_parts, down_parts, refs = [[refs[0].at[0], refs[0].at[1]]], [refs[1]], refs[2:]
         arrived = lambda: None
@@ -367,9 +373,9 @@
         acc_f[:, low:top] += dot_nt(gg, w[0][...]) + dot_nt(gu, w[1][...])
     acc_f[:, width : width + rank] += dot_nt(gg, ffn_expand[0] * half_scale)
     acc_f[:, width + rank :] += dot_nt(gu, ffn_expand[1] * half_scale)
-    blocks_down(grads.at[0], dot_tn(act[:span], g_low[:span]))
-    blocks_across(grads.at[1], adapter_scale * dot_tn(lows[0][:span], gg[:span]))
-    blocks_across(grads.at[2], adapter_scale * dot_tn(lows[1][:span], gu[:span]))
+    blocks_down(grads, dot_tn(act[:span], g_low[:span]), earlier, 0)
+    blocks_across(grads, adapter_scale * dot_tn(lows[0][:span], gg[:span]), earlier, 1)
+    blocks_across(grads, adapter_scale * dot_tn(lows[1][:span], gu[:span]), earlier, 2)
 
     @pl.when(step == pl.num_programs(0) - 1)
     def _():
@@ -381,9 +387,11 @@
         send_ref[:, half:] = acc_d[:span, width:].astype(bf16)
 
 
-def back_kernel(cuts, span, info, part, got, hidden, glhs, lhs_two, out_low, lhs_one, mask, gain, out_second, ffn_first,
+def back_kernel(cuts, span, later, info, part, got, hidden, glhs, lhs_two, out_low, lhs_one, mask, gain, out_second, ffn_first,
                 one, two, taps, in_expand, out_shrink, b_ref, c_ref, v_ref, conv_ref, gated_ref, *refs):
     in_parts, out_parts, refs = mixer_parts(refs, cuts)
+    ffn_earlier, second_earlier, grads_earlier = refs[:3] if later else (None,) * 3
+    refs = refs[3:] if later else refs
     (own_ref, send_ref, rank_ref, gh_ref, ffn_grad, second_grad, grads,
      acc, branch, first_rel, second_rel, gain_rel) = refs
     width = cuts[-1][1]
@@ -424,8 +432,8 @@
             at = lanes_at(place * 4 + info[INNER + i], block)
             value = dot_tn(lhs_two[:span, at], low[:span])
             for k in range(2):
-                blocks_down(ffn_grad.at[i, k], value[:, k * 128 : (k + 1) * 128])
-            blocks_across(second_grad.at[i], adapter_scale * dot_tn(out_low[:span, :], branch[:span, at]))
+                blocks_down(ffn_grad, value[:, k * 128 : (k + 1) * 128], ffn_earlier, i, k)
+            blocks_across(second_grad, adapter_scale * dot_tn(out_low[:span, :], branch[:span, at]), second_earlier, i)
         acc[...] = jnp.zeros_like(acc)
 
     total = dot_nt(branch[:, width:], out_shrink[...])
@@ -456,8 +464,8 @@
     )
     low_one = lhs_one[:span, width:]
     for j in range(3):
-        blocks_across(grads.at[j], adapter_scale * dot_tn(low_one, proj[j]))
-    blocks_down(grads.at[3], dot_tn(gated_ref[:span, :], branch[:span, width:]))
+        blocks_across(grads, adapter_scale * dot_tn(low_one, proj[j]), grads_earlier, j)
+    blocks_down(grads, dot_tn(gated_ref[:span, :], branch[:span, width:]), grads_earlier, 3)
 
     @pl.when(step == pl.num_programs(0) - 1)
     def _():
@@ -927,14 +935,15 @@
 
     for i, c in enumerate(chunks):
         f_part, d_own, d_send, grads = call(
-            functools.partial(feed_kernel, cuts, span), (feed_steps,), (info,),
+            functools.partial(feed_kernel, cuts, span, i > 0), (feed_steps,), (info,),
             [(c["lhs"], None, None), picked(glhs, i), columns(ffn_expand), row_tiles(down_shrink)]
+            + ([(chunks[0]["feed_grads"], (None, 3, 2, 128, 128), lambda h, *_: (h, 0, 0, 0, 0))] if i else [])
             + feed_inputs,
             [
                 ((rows, ext_two), bf16, None, None),
                 ((span, half + rank), bf16, None, None),
                 ((span, half + rank), bf16, None, None),
-                ((feed_steps, 3, 2, 128, 128), f32, (None, 3, 2, 128, 128), lambda h, *_: (h, 0, 0, 0, 0)),
+                ((feed_steps, 3, 2, 128, 128), bf16 if i else f32, (None, 3, 2, 128, 128), lambda h, *_: (h, 0, 0, 0, 0)),
             ],
             [
                 pltpu.VMEM((rows, ext_one), f32),
@@ -978,27 +987,29 @@
 
     for c in chunks:
         c["f_got"] = swap_tensor(c["f_own"])
-    feed = summed("feed_grads")
+    feed = chunks[-1]["feed_grads"]
     if special:
         feed_sum = scatter_core(cut(after(feed, chunks[0]["f_got"])))
     for i, c in enumerate(chunks):
         f_got = after(c["f_got"], *([feed_sum] if special else []), *([chunks[0]["n_rank"]] if i else []))
         n_own, n_send, n_rank, grad_hidden, ffn_grad, second_grad, grads = call(
-            functools.partial(back_kernel, cuts, span), (mixer_steps,), (info,),
+            functools.partial(back_kernel, cuts, span, i > 0), (mixer_steps,), (info,),
             [(c["f_own"], None, None), (f_got, None, None), (c["hidden"], None, None), picked(glhs, i),
              (c["lhs"], None, None), (c["low"], None, None), picked(lhs_one, i), picked(mask, i),
              (gain_two, None, None), (output_adapter_expand, None, None), (ffn_shrink, None, None),
              picked(one, i), picked(two, i), columns(conv_taps), columns(in_expand), row_tiles(out_shrink),
              columns(c["b"]), columns(c["c"]), columns(c["v"]), columns(c["conv"]), columns(c["gated"])]
-            + mixer_inputs(),
+            + mixer_inputs()
+            + ([(chunks[0]["ffn_grad"], None, None), (chunks[0]["second_grad"], None, None),
+                (chunks[0]["mixer_grads"], (None, 4, 2, 128, 128), lambda h, *_: (h, 0, 0, 0, 0))] if i else []),
             [
                 ((span, half), bf16, None, None),
                 ((span, half), bf16, None, None),
                 ((span, 2 * rank), bf16, None, None),
                 ((rows, width), f32, None, None),
-                ((4, 2, 2, 128, 128), f32, None, None),
-                ((4, 2, 128, 128), f32, None, None),
-                ((mixer_steps, 4, 2, 128, 128), f32, (None, 4, 2, 128, 128), lambda h, *_: (h, 0, 0, 0, 0)),
+                ((4, 2, 2, 128, 128), bf16 if i else f32, None, None),
+                ((4, 2, 128, 128), bf16 if i else f32, None, None),
+                ((mixer_steps, 4, 2, 128, 128), bf16 if i else f32, (None, 4, 2, 128, 128), lambda h, *_: (h, 0, 0, 0, 0)),
             ],
             [
                 pltpu.VMEM((rows, ext_one), f32),
@@ -1017,7 +1028,8 @@
     chunks[0]["n_got"] = swap_tensor(chunks[0]["n_send"])
     if special:
         feed_sum = scatter_z(feed_sum)
-        early = cut(after(summed("ffn_grad"), feed_sum, *(c["d_got"] for c in chunks)), summed("second_grad"), summed("mixer_grads"))
+        last = chunks[-1]
+        early = cut(after(last["ffn_grad"], feed_sum, *(c["d_got"] for c in chunks)), last["second_grad"], last["mixer_grads"])
         early = scatter_core(early)
         first_step = (early,)
     else:
@@ -1124,16 +1136,19 @@
              ((half, rank), f32, None, None)],
             [pltpu.VMEM((n,) + early.shape, bf16)],
         )
-        parts = gather_chip(gather_z(late))
+        late = gather_z(late)
+        over = after(lax.ppermute(late, "dp", x_route), ffn_grad)
+        parts = [late, over] + [lax.ppermute(v, "dp", core_route) for v in (late, over)]
         in_grad, down_grad = call(
             functools.partial(unpack_late_kernel, pieces), (1,), (info,), [(v, None, None) for v in parts],
             [((width, rank), f32, None, None), ((rank, width), f32, None, None)],
-            [pltpu.VMEM((n,) + late.shape, bf16)],
+            [pltpu.VMEM((n,) + late.shape[1:], bf16)],
         )
     else:
-        names = ("mixer_grads", "ffn_grad", "second_grad", "in_grad", "down_grad")
+        last = chunks[-1]
         feed, mixer, ffn_grad, second_grad, in_grad, down_grad = lax.psum(
-            (feed, *(summed(name) for name in names)), ("dp", "ctx")
+            (feed, last["mixer_grads"], last["ffn_grad"], last["second_grad"], summed("in_grad"), summed("down_grad")),
+            ("dp", "ctx"),
         )
 
         def whole(part, axis):

time: 550 us -> 544 us (0.989)
    ppermute x3 -> x1, waiting for transfers between devices: 9.07 us -> 0.01 us  [body(): over = after(lax.ppermute(late, 'dp', x_route), ffn_grad)]
    convert_element_type x6 -> x2, other arithmetic: 7.89 us -> 1.15 us  [summed(): return sum((c[name] for c in chunks)).astype(bf16)]
  transfers between devices with their start and end apart: 90 -> 90, of which waited for: 29 -> 30; matrix products, arithmetic and copies ran while one was open for 6% -> 5% of each run, Pallas kernels for 43% -> 43%
where the time goes in v6:
time: 544 us; the launch traced here: 536 us
  Pallas kernels  281 us (52%)
  waiting for transfers between devices  102 us (19%)
  starting transfers between devices  75.7 us (14%)
  local copies, waits for them, and re-layouts  24.5 us (5%)
  blocking collectives  21.7 us (4%)
  between operations  15.4 us (3%)
  other arithmetic  15.1 us (3%)
    pallas_call x21, Pallas kernels, call(): pl.pallas_call(kernel, grid_spec=pltpu.PrefetchScalarGridSpec(num_scalar_...  281 us
    ppermute x44, waiting for transfers between devices, begin(): return lax.ppermute(after(array, *gates), axis, route)  70.8 us
    ppermute x44, starting transfers between devices, begin(): return lax.ppermute(after(array, *gates), axis, route)  35.5 us
    all_gather x1, blocking collectives, body(): all_edges = lax.all_gather(edges, 'dp', axis=0, tiled=False)  21.7 us
    ppermute x10, waiting for transfers between devices, swap_tensor(): return lax.ppermute(array, 'tensor', [(0, 1), (1, 0)])  16.1 us
    ppermute x9, starting transfers between devices, scatter_z(): lax.ppermute(take(total, (ctx + k) % pieces), 'ctx', route)  12.7 us
    ppermute x9, waiting for transfers between devices, gather_z(): lax.ppermute(total, 'ctx', route)  12.5 us
    ppermute x9, starting transfers between devices, gather_z(): lax.ppermute(total, 'ctx', route)  11.5 us
  transfers between devices with their start and end apart: 90, of which 30 were waited for; matrix products, arithmetic and copies ran while one was open for 5% of the time, Pallas kernels for 43%

profile of v6, /device:TPU:0, one launch (start us, length us, event | category | flops | bytes accessed | tf_op | source)
XLA Modules:
  0.0 535.7 jit_solution(1554494627038710480)
XLA Ops:
  19.9 21.7 %all-gather = bf16[16,8,1024]{2,1,0:T(8,128)(2,1)S(1)} all-gather(bf16[4,8,1024]{2,1,0:T(8,128)(2,1)S(1)} %pad_maximum_fusion.13), channel_id=2, replica_groups=mesh['dp'=4,'ctx'=4,'tensor'=2] {'dp'}, dimensions={0}, use_global_device_ids=true | all-gather | bytes 327680 | tf_op jit(solution)/shard_map/all_gather | solution.py:730
  55.2 4.5 collective-permute-start.3
  59.8 12.6 %collective-permute-done.3 = bf16[4,2,1024]{2,1,0:T(2,128)(2,1)S(1)} collective-permute-done((bf16[4,2,1024]{2,1,0:T(2,128)(2,1)}, bf16[4,2,1024]{2,1,0:T(2,128)(2,1)S(1)}, u32[]{:S(2)}, u32[]{:S(2)}) %collective-permute-start.3) | collective-permute-done | bytes 16416 | tf_op jit(solution)/shard_map/ppermute | solution.py:680
  90.9 7.6 %shard_map.269 = (bf16[2,400,2048]{2,1,0:T(8,128)(2,1)}, bf16[2,400,2176]{2,1,0:T(8,128)(2,1)}, f32[2,400,128]{2,1,0:T(8,128)}) custom-call(s32[24]{0:T(128)} %stack.153.info, bf16[768,1024]{1,0:T(8,128)(2,1)} %own.2, bf16[384,1024]{1,0:T(8,128)(2,1)} %collective-permute-done.got_first, bf16[384,1024]{1,0:T(8,128)(2,1)} %collective-permute-done.2.got_second, ...), custom_call_target="tpu_custom_call" | custom-call | flops 1 | bytes 1 | tf_op jit(solution)/shard_map/pallas_call | solution.py:67
  98.6 5.2 collective-permute-done.13.refs_2_.refs_3_
  111.2 20.3 %shard_map.271 = (f32[400,1024]{1,0:T(8,128)}, f32[400,1024]{1,0:T(8,128)}, f32[400,1024]{1,0:T(8,128)}, f32[400,1024]{1,0:T(8,128)}, bf16[400,1024]{1,0:T(8,128...) custom-call(bf16[2,400,2176]{2,1,0:T(8,128)(2,1)} %get-tuple-element.164.lhs.lhs_one.normed.refs_6_, ...), custom_call_target="tpu_custom_call" | custom-call | flops 7130316800 | bytes 1 | tf_op jit(solution)/shard_map/pallas_call | solution.py:67
  137.6 22.4 %shard_map.270 = (f32[400,1024]{1,0:T(8,128)}, f32[400,1024]{1,0:T(8,128)}, f32[400,1024]{1,0:T(8,128)}, f32[400,1024]{1,0:T(8,128)}, bf16[400,1024]{1,0:T(8,128...) custom-call(bf16[2,400,2176]{2,1,0:T(8,128)(2,1)} %get-tuple-element.164.lhs.lhs_one.normed.refs_6_, ...), custom_call_target="tpu_custom_call" | custom-call | flops 7130316800 | bytes 1 | tf_op jit(solution)/shard_map/pallas_call | solution.py:67
  162.6 19.4 %collective-permute-done.25.refs_5_.refs_6_ = bf16[3,256,512]{2,1,0:T(8,128)(2,1)} collective-permute-done((bf16[3,256,512]{2,1,0:T(8,128)(2,1)S(1)}, bf16[3,256,512]{2,1,0:T(8,128)(2,1)}, u32[]{:S(2)}, u32[]{:S(2)}) %collective-permute-start.25) | collective-permute-done | bytes 786464 | tf_op jit(solution)/shard_map/ppermute | solution.py:680
  187.2 5.4 %shard_map.272.glhs.refs_6_ = bf16[2,400,2176]{2,1,0:T(8,128)(2,1)} custom-call(s32[24]{0:T(128)} %stack.153.info, bf16[768,1024]{1,0:T(8,128)(2,1)} %own.3, bf16[384,1024]{1,0:T(8,128)(2,1)} %copy-done.28, bf16[384,1024]{1,0:T(8,128)(2,1)} %copy-done.29, bf16[2,2,16,1024]{3,2,1,0:T(8,128)(2,1)} %copy-done.14, bf16[2,2,16,1024]{3,2,1,0:T(8,128)(2,1)} %copy-done.35, ...), custom_call_target="tpu_custom_call" | custom-call | flops 1 | bytes 1 | tf_op jit(solution)/shard_map/pallas_call | solution.py:67
  192.6 11.9 %collective-permute-done.30.refs_6_.refs_7_ = bf16[3,256,512]{2,1,0:T(8,128)(2,1)} collective-permute-done((bf16[3,256,512]{2,1,0:T(8,128)(2,1)S(1)}, bf16[3,256,512]{2,1,0:T(8,128)(2,1)}, u32[]{:S(2)}, u32[]{:S(2)}) %collective-permute-start.30) | collective-permute-done | bytes 786464 | tf_op jit(solution)/shard_map/ppermute | solution.py:680
  208.9 8.6 %shard_map.274 = (f32[400,2048]{1,0:T(8,128)}, bf16[400,2304]{1,0:T(8,128)(2,1)}, bf16[400,128]{1,0:T(8,128)(2,1)}) custom-call(s32[24]{0:T(128)} %stack.153.info, bf16[2,400,2048]{2,1,0:T(8,128)(2,1)} %get-tuple-element.163.x.refs_5_, bf16[192,2176]{1,0:T(8,128)(2,1)} %get-tuple-element.184.part_first, bf16[208,2176]{1,0:T(8,128)(2,1)} %get-tuple-element.188.part_second, ...), custom_call_target="tpu_custom_call" | custom-call | flops 1 | bytes 1 | tf_op jit(solution)/shard_map/pallas_call | solution.py:67
  219.0 6.6 %collective-permute-done.36.refs_12_.refs_13_ = bf16[3,256,512]{2,1,0:T(8,128)(2,1)S(1)} collective-permute-done((bf16[3,256,512]{2,1,0:T(8,128)(2,1)}, bf16[3,256,512]{2,1,0:T(8,128)(2,1)S(1)}, u32[]{:S(2)}, u32[]{:S(2)}) %collective-permute-start.36) | collective-permute-done | bytes 786464 | tf_op jit(solution)/shard_map/ppermute | solution.py:680
  228.4 8.7 %shard_map.273 = (f32[400,2048]{1,0:T(8,128)}, bf16[400,2304]{1,0:T(8,128)(2,1)}, bf16[400,128]{1,0:T(8,128)(2,1)}) custom-call(s32[24]{0:T(128)} %stack.153.info, bf16[2,400,2048]{2,1,0:T(8,128)(2,1)} %get-tuple-element.163.x.refs_5_, bf16[192,2176]{1,0:T(8,128)(2,1)} %get-tuple-element.192.part_first, bf16[208,2176]{1,0:T(8,128)(2,1)} %get-tuple-element.196.part_second, ...), custom_call_target="tpu_custom_call" | custom-call | flops 1 | bytes 1 | tf_op jit(solution)/shard_map/pallas_call | solution.py:67
  241.6 44.7 %shard_map.275 = (bf16[400,2304]{1,0:T(8,128)(2,1)}, bf16[384,1152]{1,0:T(8,128)(2,1)}, bf16[384,1152]{1,0:T(8,128)(2,1)}, f32[11,3,2,128,128]{4,3,2,1,0:T(8,128)}) custom-call(s32[24]{0:T(128)} %stack.153.info, bf16[400,2304]{1,0:T(8,128)(2,1)} %get-tuple-element.198.lhs.lhs_two, bf16[2,400,2176]{2,1,0:T(8,128)(2,1)} %shard_map.272.glhs.refs_6_, ...), custom_call_target="tpu_custom_call" | custom-call | flops 31142707200 | bytes 1 | tf_op jit(solution)/shard_map/pallas_call | solution.py:67
  287.5 44.2 %shard_map.276 = (bf16[400,2304]{1,0:T(8,128)(2,1)}, bf16[384,1152]{1,0:T(8,128)(2,1)}, bf16[384,1152]{1,0:T(8,128)(2,1)}, bf16[11,3,2,128,128]{4,3,2,1,0:T(8,128)(2,1)}) custom-call(s32[24]{0:T(128)} %stack.153.info, bf16[400,2304]{1,0:T(8,128)(2,1)} %get-tuple-element.197.lhs.lhs_two, bf16[2,400,2176]{2,1,0:T(8,128)(2,1)} %shard_map.272.glhs.refs_6_, ...), custom_call_target="tpu_custom_call" | custom-call | flops 31142707200 | bytes 1 | tf_op jit(solution)/shard_map/pallas_call | solution.py:67
  338.2 34.0 %shard_map.277 = (bf16[384,1024]{1,0:T(8,128)(2,1)}, bf16[384,1024]{1,0:T(8,128)(2,1)}, bf16[384,256]{1,0:T(8,128)(2,1)}, f32[400,2048]{1,0:T(8,128)}, f32[4,2,2...) custom-call(s32[24]{0:T(128)} %stack.153.info, ...), custom_call_target="tpu_custom_call" | custom-call | flops 7130316800 | bytes 1 | tf_op jit(solution)/shard_map/pallas_call | solution.py:67
  372.4 4.3 collective-permute-done.45.got
  381.4 34.4 %shard_map.278 = (bf16[384,1024]{1,0:T(8,128)(2,1)}, bf16[384,1024]{1,0:T(8,128)(2,1)}, bf16[384,256]{1,0:T(8,128)(2,1)}, f32[400,2048]{1,0:T(8,128)}, bf16[4,2,...) custom-call(s32[24]{0:T(128)} %stack.153.info, ...), custom_call_target="tpu_custom_call" | custom-call | flops 7130316800 | bytes 1 | tf_op jit(solution)/shard_map/pallas_call | solution.py:67
  424.8 5.3 shard_map.279
  430.1 5.3 shard_map.280
  444.8 4.7 shard_map.281
  450.4 4.7 shard_map.282
  467.1 5.9 %shard_map.283.refs_11_ = f32[768,1024]{1,0:T(8,128)} custom-call(s32[24]{0:T(128)} %stack.153.info, bf16[384,1024]{1,0:T(8,128)(2,1)} %get-tuple-element.260.refs_0_, bf16[384,1024]{1,0:T(8,128)(2,1)} %copy-done.55, bf16[384,256]{1,0:T(8,128)(2,1)} %get-tuple-element.252.own.refs_2_, bf16[384,256]{1,0:T(8,128)(2,1)} %copy-done.72, ...), custom_call_target="tpu_custom_call" | custom-call | flops 6000000000 | bytes 1 | tf_op jit(solution)/shard_map/pallas_call | solution.py:67
  473.1 5.9 %collective-permute-done.69 = bf16[640,128]{1,0:T(8,128)(2,1)S(1)} collective-permute-done((bf16[640,128]{1,0:T(8,128)(2,1)S(1)}, bf16[640,128]{1,0:T(8,128)(2,1)S(1)}, u32[]{:S(2)}, u32[]{:S(2)}) %collective-permute-start.69) | collective-permute-done | bytes 163872 | tf_op jit(solution)/shard_map/ppermute | solution.py:982
  479.1 4.2 collective-permute-done.65.refs_1_
  484.6 3.2 collective-permute-start.73
  488.4 5.9 %shard_map.284 = f32[768,1024]{1,0:T(8,128)} custom-call(s32[24]{0:T(128)} %stack.153.info, bf16[384,1024]{1,0:T(8,128)(2,1)} %get-tuple-element.246.refs_0_, bf16[384,1024]{1,0:T(8,128)(2,1)} %copy-done.62, bf16[384,256]{1,0:T(8,128)(2,1)} %get-tuple-element.254.own.refs_2_, bf16[384,256]{1,0:T(8,128)(2,1)} %copy-done.71, ...), custom_call_target="tpu_custom_call", output_to_operand_aliasing={{}: (12, {})} | custom-call | flops 6000000000 | bytes 1 | tf_op jit(solution)/shard_map/pallas_call | solution.py:67
  496.0 5.1 shard_map.285
  505.3 3.1 collective-permute-start.77
  510.6 3.1 collective-permute-done.76
  517.6 5.3 shard_map.286
  525.3 3.6 shard_map.287
  (409 shorter events, 138.5 us)
Async XLA Ops:
  7.2 38.8 %all-gather.10.cloned.1.call-start = ((), (), s32[]{:S(2)}) async-start(), calls=%async_computation | async-start | bytes 9437184 | tf_op jit(solution)/shard_map/all_gather | solution.py:708
  7.9 65.8 %all-gather.12.cloned.1.call-start = ((), (), s32[]{:S(2)}) async-start(), calls=%async_computation.1 | async-start | bytes 3145728 | tf_op jit(solution)/shard_map/all_gather | solution.py:708
  9.8 36.1 %collective-permute-start = (bf16[384,1024]{1,0:T(8,128)(2,1)}, bf16[384,1024]{1,0:T(8,128)(2,1)}, u32[]{:S(2)}, u32[]{:S(2)}) collective-permute-start(bf16[384,1024]{1,0:T(8,128)(2,1)} %get-tuple-element.301), channel_id=1, source_target_pairs={{0,1},{1,0},{2,3},{3,2},{4,5},{5,4},{6,7},{7,6},{8,9},{9,8},{10,11... | collective-permute-start | bytes 2359304 | tf_op jit(solution)/shard_map/ppermute | solution.py:680
  14.7 31.3 %collective-permute-start.1 = (bf16[4,256,512]{2,1,0:T(8,128)(2,1)S(1)}, bf16[4,256,512]{2,1,0:T(8,128)(2,1)}, u32[]{:S(2)}, u32[]{:S(2)}) collective-permute-start(bf16[4,256,512]{2,1,0:T(8,128)(2,1)S(1)} %pad_maximum_fusion.1), channel_id=1, source_target_pairs={{0,16},{16,0},{8,24},{24,8},{1,17},{17,1},{9,25},{25,9},{2,18},{18... | collective-permute-start | bytes 3145736 | tf_op jit(solution)/shard_map/ppermute | solution.py:680
  46.0 195.6 %all-gather.16.cloned.1.call-start = ((), (), s32[]{:S(2)}) async-start(), calls=%async_computation.3 | async-start | bytes 8650752 | tf_op jit(solution)/shard_map/all_gather | solution.py:708
  46.0 27.6 %collective-permute-start.5 = (bf16[4,256,512]{2,1,0:T(8,128)(2,1)}, bf16[4,256,512]{2,1,0:T(8,128)(2,1)S(1)}, u32[]{:S(2)}, u32[]{:S(2)}) collective-permute-start(bf16[4,256,512]{2,1,0:T(8,128)(2,1)} %pad_maximum_fusion.2), channel_id=1, source_target_pairs={{0,16},{16,0},{8,24},{24,8},{1,17},{17,1},{9,25},{25,9},{2,18},{18... | collective-permute-start | bytes 3145736 | tf_op jit(solution)/shard_map/ppermute | solution.py:680
  47.6 26.1 %collective-permute-start.6 = (bf16[4,256,512]{2,1,0:T(8,128)(2,1)}, bf16[4,256,512]{2,1,0:T(8,128)(2,1)}, u32[]{:S(2)}, u32[]{:S(2)}) collective-permute-start(bf16[4,256,512]{2,1,0:T(8,128)(2,1)} %collective-permute-done.1.refs_2_), channel_id=1, source_target_pairs={{0,2},{2,0},{4,6},{6,4},{1,3},{3,1},{5,7},{7,5},{8,10},{10,8},{12,... | collective-permute-start | bytes 3145736 | tf_op jit(solution)/shard_map/ppermute | solution.py:680
  49.2 24.5 %collective-permute-start.2 = (bf16[384,1024]{1,0:T(8,128)(2,1)}, bf16[384,1024]{1,0:T(8,128)(2,1)}, u32[]{:S(2)}, u32[]{:S(2)}) collective-permute-start(bf16[384,1024]{1,0:T(8,128)(2,1)} %get-tuple-element.151), channel_id=1, source_target_pairs={{0,1},{1,0},{2,3},{3,2},{4,5},{5,4},{6,7},{7,6},{8,9},{9,8},{10,11... | collective-permute-start | bytes 2359304 | tf_op jit(solution)/shard_map/ppermute | solution.py:680
  81.0 25.1 %collective-permute-start.8 = (bf16[4,256,512]{2,1,0:T(8,128)(2,1)S(1)}, bf16[4,256,512]{2,1,0:T(8,128)(2,1)S(1)}, u32[]{:S(2)}, u32[]{:S(2)}) collective-permute-start(bf16[4,256,512]{2,1,0:T(8,128)(2,1)S(1)} %collective-permute-done.5.refs_3_), channel_id=1, source_target_pairs={{0,2},{2,0},{4,6},{6,4},{1,3},{3,1},{5,7},{7,5},{8,10},{10,8},{12,... | collective-permute-start | bytes 3145736 | tf_op jit(solution)/shard_map/ppermute | solution.py:680
  82.2 23.9 %collective-permute-start.11 = (bf16[4,256,512]{2,1,0:T(8,128)(2,1)}, bf16[4,256,512]{2,1,0:T(8,128)(2,1)S(1)}, u32[]{:S(2)}, u32[]{:S(2)}) collective-permute-start(bf16[4,256,512]{2,1,0:T(8,128)(2,1)} %collective-permute-done.6.refs_4_), channel_id=1, source_target_pairs={{0,8},{8,0},{16,24},{24,16},{1,9},{9,1},{17,25},{25,17},{2,10},{10... | collective-permute-start | bytes 3145736 | tf_op jit(solution)/shard_map/ppermute | solution.py:680
  106.3 25.3 %collective-permute-start.17 = (bf16[3,256,512]{2,1,0:T(8,128)(2,1)}, bf16[3,256,512]{2,1,0:T(8,128)(2,1)}, u32[]{:S(2)}, u32[]{:S(2)}) collective-permute-start(bf16[3,256,512]{2,1,0:T(8,128)(2,1)} %collective-permute-done.13.refs_2_.refs_3_), channel_id=1, source_target_pairs={{0,2},{2,0},{4,6},{6,4},{1,3},{3,1},{5,7},{7,5},{8,10},{10,8},{12,... | collective-permute-start | bytes 2359304 | tf_op jit(solution)/shard_map/ppermute | solution.py:680
  107.6 24.0 %collective-permute-start.18 = (bf16[3,256,512]{2,1,0:T(8,128)(2,1)}, bf16[3,256,512]{2,1,0:T(8,128)(2,1)}, u32[]{:S(2)}, u32[]{:S(2)}) collective-permute-start(bf16[3,256,512]{2,1,0:T(8,128)(2,1)} %collective-permute-done.13.refs_2_.refs_3_), channel_id=1, source_target_pairs={{0,8},{8,0},{16,24},{24,16},{1,9},{9,1},{17,25},{25,17},{2,10},{10... | collective-permute-start | bytes 2359304 | tf_op jit(solution)/shard_map/ppermute | solution.py:680
  107.8 23.7 %collective-permute-start.15 = (bf16[384,1024]{1,0:T(8,128)(2,1)}, bf16[384,1024]{1,0:T(8,128)(2,1)S(1)}, u32[]{:S(2)}, u32[]{:S(2)}) collective-permute-start(bf16[384,1024]{1,0:T(8,128)(2,1)} %get-tuple-element.181), channel_id=1, source_target_pairs={{0,1},{1,0},{2,3},{3,2},{4,5},{5,4},{6,7},{7,6},{8,9},{9,8},{10,11... | collective-permute-start | bytes 2359304 | tf_op jit(solution)/shard_map/ppermute | solution.py:680
  108.7 22.9 %collective-permute-start.16 = (bf16[3,256,512]{2,1,0:T(8,128)(2,1)}, bf16[3,256,512]{2,1,0:T(8,128)(2,1)}, u32[]{:S(2)}, u32[]{:S(2)}) collective-permute-start(bf16[3,256,512]{2,1,0:T(8,128)(2,1)} %pad_maximum_fusion.4), channel_id=1, source_target_pairs={{0,16},{16,0},{8,24},{24,8},{1,17},{17,1},{9,25},{25,9},{2,18},{18... | collective-permute-start | bytes 2359304 | tf_op jit(solution)/shard_map/ppermute | solution.py:680
  131.6 109.9 %all-gather.14.cloned.1.call-start = ((), (), s32[]{:S(2)}) async-start(), calls=%async_computation.2 | async-start | bytes 17301504 | tf_op jit(solution)/shard_map/all_gather | solution.py:708
  133.8 26.3 %collective-permute-start.19 = (bf16[192,2176]{1,0:T(8,128)(2,1)S(1)}, bf16[192,2176]{1,0:T(8,128)(2,1)S(1)}, u32[]{:S(2)}, u32[]{:S(2)}) collective-permute-start(bf16[192,2176]{1,0:T(8,128)(2,1)S(1)} %copy-done.24), channel_id=1, source_target_pairs={{0,1},{1,0},{2,3},{3,2},{4,5},{5,4},{6,7},{7,6},{8,9},{9,8},{10,11... | collective-permute-start | bytes 2506760 | tf_op jit(solution)/shard_map/ppermute | solution.py:680
  135.0 25.1 %collective-permute-start.21 = (bf16[3,256,512]{2,1,0:T(8,128)(2,1)}, bf16[3,256,512]{2,1,0:T(8,128)(2,1)S(1)}, u32[]{:S(2)}, u32[]{:S(2)}) collective-permute-start(bf16[3,256,512]{2,1,0:T(8,128)(2,1)} %collective-permute-done.16.refs_3_.refs_4_), channel_id=1, source_target_pairs={{0,2},{2,0},{4,6},{6,4},{1,3},{3,1},{5,7},{7,5},{8,10},{10,8},{12,... | collective-permute-start | bytes 2359304 | tf_op jit(solution)/shard_map/ppermute | solution.py:680
  135.8 24.2 %collective-permute-start.22 = (bf16[3,256,512]{2,1,0:T(8,128)(2,1)}, bf16[3,256,512]{2,1,0:T(8,128)(2,1)S(1)}, u32[]{:S(2)}, u32[]{:S(2)}) collective-permute-start(bf16[3,256,512]{2,1,0:T(8,128)(2,1)} %collective-permute-done.16.refs_3_.refs_4_), channel_id=1, source_target_pairs={{0,8},{8,0},{16,24},{24,16},{1,9},{9,1},{17,25},{25,17},{2,10},{10... | collective-permute-start | bytes 2359304 | tf_op jit(solution)/shard_map/ppermute | solution.py:680
  135.8 24.2 %collective-permute-start.20 = (bf16[3,256,512]{2,1,0:T(8,128)(2,1)S(1)}, bf16[3,256,512]{2,1,0:T(8,128)(2,1)}, u32[]{:S(2)}, u32[]{:S(2)}) collective-permute-start(bf16[3,256,512]{2,1,0:T(8,128)(2,1)S(1)} %copy-done.30), channel_id=1, source_target_pairs={{0,16},{16,0},{8,24},{24,8},{1,17},{17,1},{9,25},{25,9},{2,18},{18... | collective-permute-start | bytes 2359304 | tf_op jit(solution)/shard_map/ppermute | solution.py:680
  137.3 22.8 %collective-permute-start.23 = (bf16[3,256,512]{2,1,0:T(8,128)(2,1)}, bf16[3,256,512]{2,1,0:T(8,128)(2,1)}, u32[]{:S(2)}, u32[]{:S(2)}) collective-permute-start(bf16[3,256,512]{2,1,0:T(8,128)(2,1)} %collective-permute-done.17.refs_8_.refs_9_), channel_id=1, source_target_pairs={{0,8},{8,0},{16,24},{24,16},{1,9},{9,1},{17,25},{25,17},{2,10},{10... | collective-permute-start | bytes 2359304 | tf_op jit(solution)/shard_map/ppermute | solution.py:680
  160.1 22.3 %collective-permute-start.24 = (bf16[208,2176]{1,0:T(8,128)(2,1)S(1)}, bf16[208,2176]{1,0:T(8,128)(2,1)S(1)}, u32[]{:S(2)}, u32[]{:S(2)}) collective-permute-start(bf16[208,2176]{1,0:T(8,128)(2,1)S(1)} %copy-done.20), channel_id=1, source_target_pairs={{0,1},{1,0},{2,3},{3,2},{4,5},{5,4},{6,7},{7,6},{8,9},{9,8},{10,11... | collective-permute-start | bytes 2715656 | tf_op jit(solution)/shard_map/ppermute | solution.py:680
  182.4 23.0 %collective-permute-start.29 = (bf16[192,2176]{1,0:T(8,128)(2,1)S(1)}, bf16[192,2176]{1,0:T(8,128)(2,1)S(1)}, u32[]{:S(2)}, u32[]{:S(2)}) collective-permute-start(bf16[192,2176]{1,0:T(8,128)(2,1)S(1)} %copy-done.25), channel_id=1, source_target_pairs={{0,1},{1,0},{2,3},{3,2},{4,5},{5,4},{6,7},{7,6},{8,9},{9,8},{10,11... | collective-permute-start | bytes 2506760 | tf_op jit(solution)/shard_map/ppermute | solution.py:680
  205.4 21.8 %collective-permute-start.34 = (bf16[208,2176]{1,0:T(8,128)(2,1)S(1)}, bf16[208,2176]{1,0:T(8,128)(2,1)S(1)}, u32[]{:S(2)}, u32[]{:S(2)}) collective-permute-start(bf16[208,2176]{1,0:T(8,128)(2,1)S(1)} %copy-done.21), channel_id=1, source_target_pairs={{0,1},{1,0},{2,3},{3,2},{4,5},{5,4},{6,7},{7,6},{8,9},{9,8},{10,11... | collective-permute-start | bytes 2715656 | tf_op jit(solution)/shard_map/ppermute | solution.py:680
  286.3 45.4 %collective-permute-start.43 = (bf16[400,2304]{1,0:T(8,128)(2,1)}, bf16[400,2304]{1,0:T(8,128)(2,1)}, u32[]{:S(2)}, u32[]{:S(2)}) collective-permute-start(bf16[400,2304]{1,0:T(8,128)(2,1)} %get-tuple-element.210.part), channel_id=1, source_target_pairs={{0,1},{1,0},{2,3},{3,2},{4,5},{5,4},{6,7},{7,6},{8,9},{9,8},{10,11... | collective-permute-start | bytes 5529608 | tf_op jit(solution)/shard_map/ppermute | solution.py:611
  333.3 43.4 %collective-permute-start.45 = (bf16[400,2304]{1,0:T(8,128)(2,1)}, bf16[400,2304]{1,0:T(8,128)(2,1)}, u32[]{:S(2)}, u32[]{:S(2)}) collective-permute-start(bf16[400,2304]{1,0:T(8,128)(2,1)} %get-tuple-element.212.part), channel_id=1, source_target_pairs={{0,1},{1,0},{2,3},{3,2},{4,5},{5,4},{6,7},{7,6},{8,9},{9,8},{10,11... | collective-permute-start | bytes 5529608 | tf_op jit(solution)/shard_map/ppermute | solution.py:611
  334.3 81.7 %collective-permute-start.44 = (bf16[384,1152]{1,0:T(8,128)(2,1)}, bf16[384,1152]{1,0:T(8,128)(2,1)S(1)}, u32[]{:S(2)}, u32[]{:S(2)}) collective-permute-start(bf16[384,1152]{1,0:T(8,128)(2,1)} %get-tuple-element.211), channel_id=1, source_target_pairs={{0,1},{1,0},{2,3},{3,2},{4,5},{5,4},{6,7},{7,6},{8,9},{9,8},{10,11... | collective-permute-start | bytes 2654216 | tf_op jit(solution)/shard_map/ppermute | solution.py:611
  335.4 80.6 %collective-permute-start.51 = (bf16[384,1152]{1,0:T(8,128)(2,1)}, bf16[384,1152]{1,0:T(8,128)(2,1)S(1)}, u32[]{:S(2)}, u32[]{:S(2)}) collective-permute-start(bf16[384,1152]{1,0:T(8,128)(2,1)} %get-tuple-element.237), channel_id=1, source_target_pairs={{0,1},{1,0},{2,3},{3,2},{4,5},{5,4},{6,7},{7,6},{8,9},{9,8},{10,11... | collective-permute-start | bytes 2654216 | tf_op jit(solution)/shard_map/ppermute | solution.py:611
  337.9 34.3 %collective-permute-start.47 = (bf16[4,528,128]{2,1,0:T(8,128)(2,1)S(1)}, bf16[4,528,128]{2,1,0:T(8,128)(2,1)S(1)}, u32[]{:S(2)}, u32[]{:S(2)}) collective-permute-start(bf16[4,528,128]{2,1,0:T(8,128)(2,1)S(1)} %dynamic-slice_bitcast_fusion.2), channel_id=1, source_target_pairs={{0,16},{16,0},{8,24},{24,8},{1,17},{17,1},{9,25},{25,9},{2,18},{18... | collective-permute-start | bytes 1622024 | tf_op jit(solution)/shard_map/ppermute | solution.py:975
  376.7 39.1 %collective-permute-start.50 = (bf16[528,128]{1,0:T(8,128)(2,1)S(1)}, bf16[528,128]{1,0:T(8,128)(2,1)S(1)}, u32[]{:S(2)}, u32[]{:S(2)}) collective-permute-start(bf16[528,128]{1,0:T(8,128)(2,1)S(1)} %get-tuple-element.305), channel_id=1, source_target_pairs={{0,6},{2,0},{4,2},{6,4},{1,7},{3,1},{5,3},{7,5},{8,14},{10,8},{12,... | collective-permute-start | bytes 405512 | tf_op jit(solution)/shard_map/ppermute | solution.py:978
  379.7 36.2 %collective-permute-start.49 = (bf16[528,128]{1,0:T(8,128)(2,1)S(1)}, bf16[528,128]{1,0:T(8,128)(2,1)S(1)}, u32[]{:S(2)}, u32[]{:S(2)}) collective-permute-start(bf16[528,128]{1,0:T(8,128)(2,1)S(1)} %get-tuple-element.306), channel_id=1, source_target_pairs={{0,4},{2,6},{4,0},{6,2},{1,5},{3,7},{5,1},{7,3},{8,12},{10,14},{12... | collective-permute-start | bytes 405512 | tf_op jit(solution)/shard_map/ppermute | solution.py:978
  379.7 36.2 %collective-permute-start.48 = (bf16[528,128]{1,0:T(8,128)(2,1)S(1)}, bf16[528,128]{1,0:T(8,128)(2,1)S(1)}, u32[]{:S(2)}, u32[]{:S(2)}) collective-permute-start(bf16[528,128]{1,0:T(8,128)(2,1)S(1)} %get-tuple-element.304), channel_id=1, source_target_pairs={{0,2},{2,4},{4,6},{6,0},{1,3},{3,5},{5,7},{7,1},{8,10},{10,12},{12... | collective-permute-start | bytes 405512 | tf_op jit(solution)/shard_map/ppermute | solution.py:978
  484.6 31.3 %collective-permute-start.82 = (bf16[4,640,128]{2,1,0:T(8,128)(2,1)S(1)}, bf16[4,640,128]{2,1,0:T(8,128)(2,1)S(1)}, u32[]{:S(2)}, u32[]{:S(2)}) collective-permute-start(bf16[4,640,128]{2,1,0:T(8,128)(2,1)S(1)} %pad_maximum_fusion.8.own), channel_id=1, source_target_pairs={{0,8},{8,0},{16,24},{24,16},{1,9},{9,1},{17,25},{25,17},{2,10},{10... | collective-permute-start | bytes 1966088 | tf_op jit(solution)/shard_map/ppermute | solution.py:1132
  (133 other events, 1407.1 us)
Sparse Core Ops, SparseCore 0:
  9.6 19.4 all-gather.9
  46.1 11.4 all-gather.11
  131.7 16.0 all-gather.15
  149.3 25.0 all-gather.13

commit v7 on v6

--- a/solution.py
+++ b/solution.py
@@ -212,6 +212,44 @@
     return ins, outs, refs[10:]
 
 
+def held_mixer_parts(refs, cuts):
+    if len(cuts) == 1:
+        return *mixer_parts(refs, cuts), lambda: None
+    in_own, out_own, *far = refs[:10]
+    *refs, near, out_near, distant, sems = refs[10:]
+    step = pl.program_id(0)
+
+    def copies(tile):
+        at = pl.ds(tile * TILE, TILE)
+        yield pltpu.make_async_copy(in_own.at[:, :, :, at], near.at[:, :, :, at], sems.at[tile, 0])
+        yield pltpu.make_async_copy(out_own.at[:, at, :], out_near.at[:, at, :], sems.at[tile, 1])
+        for k in range(4):
+            part = far[2 * k + tile // 2].at[:, :, pl.ds(tile % 2 * TILE, TILE)]
+            yield pltpu.make_async_copy(part, distant.at[k, :, :, at], sems.at[tile, 2 + k])
+
+    @pl.when(step == 0)
+    def _():
+        for tile in range(4):
+            for copy in copies(tile):
+                copy.start()
+
+    def arrived():
+        for tile in range(4):
+
+            @pl.when(step == tile)
+            def _(tile=tile):
+                for copy in copies(tile):
+                    copy.wait()
+
+    at = pl.ds(pl.multiple_of(step * TILE, TILE), TILE)
+    ins = [[near.at[k, j, :, at] for j in range(3)] for k in range(2)]
+    outs = [out_near.at[k, at, :] for k in range(2)]
+    for k in range(4):
+        ins.append([distant.at[k, j, :, at] for j in range(3)])
+        outs.append(distant.at[k, 3, :, at])
+    return ins, outs, refs, arrived
+
+
 def mixer_kernel(cuts, lhs, one, two, taps, in_expand, out_shrink, *refs):
     in_parts, out_parts, refs = mixer_parts(refs, cuts)
     b_ref, c_ref, v_ref, conv_ref, gated_ref, part_first, part_second, acc = refs
@@ -389,7 +427,7 @@
 
 def back_kernel(cuts, span, later, info, part, got, hidden, glhs, lhs_two, out_low, lhs_one, mask, gain, out_second, ffn_first,
                 one, two, taps, in_expand, out_shrink, b_ref, c_ref, v_ref, conv_ref, gated_ref, *refs):
-    in_parts, out_parts, refs = mixer_parts(refs, cuts)
+    in_parts, out_parts, refs, arrived = held_mixer_parts(refs, cuts)
     ffn_earlier, second_earlier, grads_earlier = refs[:3] if later else (None,) * 3
     refs = refs[3:] if later else refs
     (own_ref, send_ref, rank_ref, gh_ref, ffn_grad, second_grad, grads,
@@ -436,6 +474,7 @@
             blocks_across(second_grad, adapter_scale * dot_tn(out_low[:span, :], branch[:span, at]), second_earlier, i)
         acc[...] = jnp.zeros_like(acc)
 
+    arrived()
     total = dot_nt(branch[:, width:], out_shrink[...])
     for (low, top), w in zip(cuts, out_parts):
         total = total + dot_nt(branch[:, low:top], w[...])
@@ -990,6 +1029,16 @@
     feed = chunks[-1]["feed_grads"]
     if special:
         feed_sum = scatter_core(cut(after(feed, chunks[0]["f_got"])))
+    held_scratch = []
+    if special:
+        held = [in_own, out_own] + [w for part in (mixer_x, mixer_z, mixer_xc, mixer_zc) for w in part]
+        held_inputs = [(w, "any", None) for w in held]
+        held_scratch = [
+            pltpu.VMEM(in_own.shape, bf16),
+            pltpu.VMEM(out_own.shape, bf16),
+            pltpu.VMEM((4, 4, TILE, half), bf16),
+            pltpu.SemaphoreType.DMA((4, 6)),
+        ]
     for i, c in enumerate(chunks):
         f_got = after(c["f_got"], *([feed_sum] if special else []), *([chunks[0]["n_rank"]] if i else []))
         n_own, n_send, n_rank, grad_hidden, ffn_grad, second_grad, grads = call(
@@ -999,7 +1048,7 @@
              (gain_two, None, None), (output_adapter_expand, None, None), (ffn_shrink, None, None),
              picked(one, i), picked(two, i), columns(conv_taps), columns(in_expand), row_tiles(out_shrink),
              columns(c["b"]), columns(c["c"]), columns(c["v"]), columns(c["conv"]), columns(c["gated"])]
-            + mixer_inputs()
+            + (held_inputs if special else mixer_inputs())
             + ([(chunks[0]["ffn_grad"], None, None), (chunks[0]["second_grad"], None, None),
                 (chunks[0]["mixer_grads"], (None, 4, 2, 128, 128), lambda h, *_: (h, 0, 0, 0, 0))] if i else []),
             [
@@ -1017,7 +1066,8 @@
                 pltpu.VMEM((width, 2 * rank), bf16),
                 pltpu.VMEM((rank, width), bf16),
                 pltpu.VMEM((1, width), f32),
-            ],
+            ]
+            + held_scratch,
             flops=2 * rows * half * ext_one * 4,
         )
         c.update(n_own=n_own, n_send=n_send, n_rank=n_rank, gh=grad_hidden, ffn_grad=ffn_grad, second_grad=second_grad, mixer_grads=grads)

time: 544 us -> 542 us (level)
  transfers between devices with their start and end apart: 90 -> 90, of which waited for: 30 -> 29; matrix products, arithmetic and copies ran while one was open for 5% -> 5% of each run, Pallas kernels for 43% -> 43%
where the time goes in v7:
time: 542 us; the launch traced here: 534 us
  Pallas kernels  276 us (51%)
  waiting for transfers between devices  103 us (19%)
  starting transfers between devices  78 us (14%)
  local copies, waits for them, and re-layouts  24.2 us (4%)
  blocking collectives  21.7 us (4%)
  between operations  15.7 us (3%)
  other arithmetic  15 us (3%)
    pallas_call x21, Pallas kernels, call(): pl.pallas_call(kernel, grid_spec=pltpu.PrefetchScalarGridSpec(num_scalar_...  276 us
    ppermute x44, waiting for transfers between devices, begin(): return lax.ppermute(after(array, *gates), axis, route)  70.8 us
    ppermute x44, starting transfers between devices, begin(): return lax.ppermute(after(array, *gates), axis, route)  35 us
    all_gather x1, blocking collectives, body(): all_edges = lax.all_gather(edges, 'dp', axis=0, tiled=False)  21.7 us
    ppermute x10, waiting for transfers between devices, swap_tensor(): return lax.ppermute(array, 'tensor', [(0, 1), (1, 0)])  16.9 us
    ppermute x9, starting transfers between devices, scatter_z(): lax.ppermute(take(total, (ctx + k) % pieces), 'ctx', route)  13.7 us
    ppermute x9, starting transfers between devices, gather_z(): lax.ppermute(total, 'ctx', route)  13.6 us
    ppermute x9, waiting for transfers between devices, gather_z(): lax.ppermute(total, 'ctx', route)  11.3 us
  transfers between devices with their start and end apart: 90, of which 29 were waited for; matrix products, arithmetic and copies ran while one was open for 5% of the time, Pallas kernels for 43%

profile of v7, /device:TPU:0, one launch (start us, length us, event | category | flops | bytes accessed | tf_op | source)
XLA Modules:
  0.0 533.5 jit_solution(1815727084965132105)
XLA Ops:
  19.9 21.7 %all-gather = bf16[16,8,1024]{2,1,0:T(8,128)(2,1)S(1)} all-gather(bf16[4,8,1024]{2,1,0:T(8,128)(2,1)S(1)} %pad_maximum_fusion.13), channel_id=2, replica_groups=mesh['dp'=4,'ctx'=4,'tensor'=2] {'dp'}, dimensions={0}, use_global_device_ids=true | all-gather | bytes 327680 | tf_op jit(solution)/shard_map/all_gather | solution.py:769
  55.2 4.5 collective-permute-start.3
  59.8 12.6 %collective-permute-done.3 = bf16[4,2,1024]{2,1,0:T(2,128)(2,1)S(1)} collective-permute-done((bf16[4,2,1024]{2,1,0:T(2,128)(2,1)}, bf16[4,2,1024]{2,1,0:T(2,128)(2,1)S(1)}, u32[]{:S(2)}, u32[]{:S(2)}) %collective-permute-start.3) | collective-permute-done | bytes 16416 | tf_op jit(solution)/shard_map/ppermute | solution.py:719
  90.9 7.6 %shard_map.269 = (bf16[2,400,2048]{2,1,0:T(8,128)(2,1)}, bf16[2,400,2176]{2,1,0:T(8,128)(2,1)}, f32[2,400,128]{2,1,0:T(8,128)}) custom-call(s32[24]{0:T(128)} %stack.153.info, bf16[768,1024]{1,0:T(8,128)(2,1)} %own.2, bf16[384,1024]{1,0:T(8,128)(2,1)} %collective-permute-done.got_first, bf16[384,1024]{1,0:T(8,128)(2,1)} %collective-permute-done.2.got_second, ...), custom_call_target="tpu_custom_call" | custom-call | flops 1 | bytes 1 | tf_op jit(solution)/shard_map/pallas_call | solution.py:67
  98.6 5.2 collective-permute-done.13.refs_2_.refs_3_
  111.2 20.3 %shard_map.271 = (f32[400,1024]{1,0:T(8,128)}, f32[400,1024]{1,0:T(8,128)}, f32[400,1024]{1,0:T(8,128)}, f32[400,1024]{1,0:T(8,128)}, bf16[400,1024]{1,0:T(8,128...) custom-call(bf16[2,400,2176]{2,1,0:T(8,128)(2,1)} %get-tuple-element.164.lhs.lhs_one.normed.refs_6_, ...), custom_call_target="tpu_custom_call" | custom-call | flops 7130316800 | bytes 1 | tf_op jit(solution)/shard_map/pallas_call | solution.py:67
  137.6 22.4 %shard_map.270 = (f32[400,1024]{1,0:T(8,128)}, f32[400,1024]{1,0:T(8,128)}, f32[400,1024]{1,0:T(8,128)}, f32[400,1024]{1,0:T(8,128)}, bf16[400,1024]{1,0:T(8,128...) custom-call(bf16[2,400,2176]{2,1,0:T(8,128)(2,1)} %get-tuple-element.164.lhs.lhs_one.normed.refs_6_, ...), custom_call_target="tpu_custom_call" | custom-call | flops 7130316800 | bytes 1 | tf_op jit(solution)/shard_map/pallas_call | solution.py:67
  162.6 19.4 %collective-permute-done.25.refs_5_.refs_6_ = bf16[3,256,512]{2,1,0:T(8,128)(2,1)} collective-permute-done((bf16[3,256,512]{2,1,0:T(8,128)(2,1)S(1)}, bf16[3,256,512]{2,1,0:T(8,128)(2,1)}, u32[]{:S(2)}, u32[]{:S(2)}) %collective-permute-start.25) | collective-permute-done | bytes 786464 | tf_op jit(solution)/shard_map/ppermute | solution.py:719
  187.2 5.4 %shard_map.272.glhs.refs_6_ = bf16[2,400,2176]{2,1,0:T(8,128)(2,1)} custom-call(s32[24]{0:T(128)} %stack.153.info, bf16[768,1024]{1,0:T(8,128)(2,1)} %own.3, bf16[384,1024]{1,0:T(8,128)(2,1)} %copy-done.28, bf16[384,1024]{1,0:T(8,128)(2,1)} %copy-done.29, bf16[2,2,16,1024]{3,2,1,0:T(8,128)(2,1)} %copy-done.14, bf16[2,2,16,1024]{3,2,1,0:T(8,128)(2,1)} %copy-done.35, ...), custom_call_target="tpu_custom_call" | custom-call | flops 1 | bytes 1 | tf_op jit(solution)/shard_map/pallas_call | solution.py:67
  192.6 11.9 %collective-permute-done.30.refs_6_.refs_7_ = bf16[3,256,512]{2,1,0:T(8,128)(2,1)} collective-permute-done((bf16[3,256,512]{2,1,0:T(8,128)(2,1)S(1)}, bf16[3,256,512]{2,1,0:T(8,128)(2,1)}, u32[]{:S(2)}, u32[]{:S(2)}) %collective-permute-start.30) | collective-permute-done | bytes 786464 | tf_op jit(solution)/shard_map/ppermute | solution.py:719
  208.9 8.6 %shard_map.274 = (f32[400,2048]{1,0:T(8,128)}, bf16[400,2304]{1,0:T(8,128)(2,1)}, bf16[400,128]{1,0:T(8,128)(2,1)}) custom-call(s32[24]{0:T(128)} %stack.153.info, bf16[2,400,2048]{2,1,0:T(8,128)(2,1)} %get-tuple-element.163.x.refs_5_, bf16[192,2176]{1,0:T(8,128)(2,1)} %get-tuple-element.184.part_first, bf16[208,2176]{1,0:T(8,128)(2,1)} %get-tuple-element.188.part_second, ...), custom_call_target="tpu_custom_call" | custom-call | flops 1 | bytes 1 | tf_op jit(solution)/shard_map/pallas_call | solution.py:67
  219.0 6.6 %collective-permute-done.36.refs_12_.refs_13_ = bf16[3,256,512]{2,1,0:T(8,128)(2,1)S(1)} collective-permute-done((bf16[3,256,512]{2,1,0:T(8,128)(2,1)}, bf16[3,256,512]{2,1,0:T(8,128)(2,1)S(1)}, u32[]{:S(2)}, u32[]{:S(2)}) %collective-permute-start.36) | collective-permute-done | bytes 786464 | tf_op jit(solution)/shard_map/ppermute | solution.py:719
  228.4 8.7 %shard_map.273 = (f32[400,2048]{1,0:T(8,128)}, bf16[400,2304]{1,0:T(8,128)(2,1)}, bf16[400,128]{1,0:T(8,128)(2,1)}) custom-call(s32[24]{0:T(128)} %stack.153.info, bf16[2,400,2048]{2,1,0:T(8,128)(2,1)} %get-tuple-element.163.x.refs_5_, bf16[192,2176]{1,0:T(8,128)(2,1)} %get-tuple-element.192.part_first, bf16[208,2176]{1,0:T(8,128)(2,1)} %get-tuple-element.196.part_second, ...), custom_call_target="tpu_custom_call" | custom-call | flops 1 | bytes 1 | tf_op jit(solution)/shard_map/pallas_call | solution.py:67
  241.6 44.4 %shard_map.275 = (bf16[400,2304]{1,0:T(8,128)(2,1)}, bf16[384,1152]{1,0:T(8,128)(2,1)}, bf16[384,1152]{1,0:T(8,128)(2,1)}, f32[11,3,2,128,128]{4,3,2,1,0:T(8,128)}) custom-call(s32[24]{0:T(128)} %stack.153.info, bf16[400,2304]{1,0:T(8,128)(2,1)} %get-tuple-element.198.lhs.lhs_two, bf16[2,400,2176]{2,1,0:T(8,128)(2,1)} %shard_map.272.glhs.refs_6_, ...), custom_call_target="tpu_custom_call" | custom-call | flops 31142707200 | bytes 1 | tf_op jit(solution)/shard_map/pallas_call | solution.py:67
  287.2 44.2 %shard_map.276 = (bf16[400,2304]{1,0:T(8,128)(2,1)}, bf16[384,1152]{1,0:T(8,128)(2,1)}, bf16[384,1152]{1,0:T(8,128)(2,1)}, bf16[11,3,2,128,128]{4,3,2,1,0:T(8,128)(2,1)}) custom-call(s32[24]{0:T(128)} %stack.153.info, bf16[400,2304]{1,0:T(8,128)(2,1)} %get-tuple-element.197.lhs.lhs_two, bf16[2,400,2176]{2,1,0:T(8,128)(2,1)} %shard_map.272.glhs.refs_6_, ...), custom_call_target="tpu_custom_call" | custom-call | flops 31142707200 | bytes 1 | tf_op jit(solution)/shard_map/pallas_call | solution.py:67
  337.9 32.1 %shard_map.277 = (bf16[384,1024]{1,0:T(8,128)(2,1)}, bf16[384,1024]{1,0:T(8,128)(2,1)}, bf16[384,256]{1,0:T(8,128)(2,1)}, f32[400,2048]{1,0:T(8,128)}, f32[4,2,2...) custom-call(s32[24]{0:T(128)} %stack.153.info, ...), custom_call_target="tpu_custom_call" | custom-call | flops 7130316800 | bytes 1 | tf_op jit(solution)/shard_map/pallas_call | solution.py:67
  370.1 6.2 %collective-permute-done.45.got = bf16[400,2304]{1,0:T(8,128)(2,1)} collective-permute-done((bf16[400,2304]{1,0:T(8,128)(2,1)}, bf16[400,2304]{1,0:T(8,128)(2,1)}, u32[]{:S(2)}, u32[]{:S(2)}) %collective-permute-start.45) | collective-permute-done | bytes 1843232 | tf_op jit(solution)/shard_map/ppermute | solution.py:650
  381.1 32.3 %shard_map.278 = (bf16[384,1024]{1,0:T(8,128)(2,1)}, bf16[384,1024]{1,0:T(8,128)(2,1)}, bf16[384,256]{1,0:T(8,128)(2,1)}, f32[400,2048]{1,0:T(8,128)}, bf16[4,2,...) custom-call(s32[24]{0:T(128)} %stack.153.info, ...), custom_call_target="tpu_custom_call" | custom-call | flops 7130316800 | bytes 1 | tf_op jit(solution)/shard_map/pallas_call | solution.py:67
  423.8 5.3 shard_map.279
  429.1 5.3 shard_map.280
  443.1 4.7 shard_map.281
  448.4 4.7 shard_map.282
  458.7 3.4 collective-permute-start.70
  464.8 5.9 %shard_map.283.refs_11_ = f32[768,1024]{1,0:T(8,128)} custom-call(s32[24]{0:T(128)} %stack.153.info, bf16[384,1024]{1,0:T(8,128)(2,1)} %get-tuple-element.260.refs_0_, bf16[384,1024]{1,0:T(8,128)(2,1)} %copy-done.55, bf16[384,256]{1,0:T(8,128)(2,1)} %get-tuple-element.252.own.refs_2_, bf16[384,256]{1,0:T(8,128)(2,1)} %copy-done.72, ...), custom_call_target="tpu_custom_call" | custom-call | flops 6000000000 | bytes 1 | tf_op jit(solution)/shard_map/pallas_call | solution.py:67
  470.8 6.0 %collective-permute-done.69 = bf16[640,128]{1,0:T(8,128)(2,1)S(1)} collective-permute-done((bf16[640,128]{1,0:T(8,128)(2,1)S(1)}, bf16[640,128]{1,0:T(8,128)(2,1)S(1)}, u32[]{:S(2)}, u32[]{:S(2)}) %collective-permute-start.69) | collective-permute-done | bytes 163872 | tf_op jit(solution)/shard_map/ppermute | solution.py:1021
  477.0 4.3 collective-permute-done.65.refs_1_
  482.3 3.6 collective-permute-start.73
  486.5 5.9 %shard_map.284 = f32[768,1024]{1,0:T(8,128)} custom-call(s32[24]{0:T(128)} %stack.153.info, bf16[384,1024]{1,0:T(8,128)(2,1)} %get-tuple-element.246.refs_0_, bf16[384,1024]{1,0:T(8,128)(2,1)} %copy-done.62, bf16[384,256]{1,0:T(8,128)(2,1)} %get-tuple-element.254.own.refs_2_, bf16[384,256]{1,0:T(8,128)(2,1)} %copy-done.71, ...), custom_call_target="tpu_custom_call", output_to_operand_aliasing={{}: (12, {})} | custom-call | flops 6000000000 | bytes 1 | tf_op jit(solution)/shard_map/pallas_call | solution.py:67
  493.6 4.9 shard_map.285
  508.1 3.6 collective-permute-done.76
  515.2 5.3 shard_map.286
  522.9 3.6 shard_map.287
  (409 shorter events, 137.4 us)
Async XLA Ops:
  7.2 38.8 %all-gather.10.cloned.1.call-start = ((), (), s32[]{:S(2)}) async-start(), calls=%async_computation | async-start | bytes 9437184 | tf_op jit(solution)/shard_map/all_gather | solution.py:747
  7.9 65.8 %all-gather.12.cloned.1.call-start = ((), (), s32[]{:S(2)}) async-start(), calls=%async_computation.1 | async-start | bytes 3145728 | tf_op jit(solution)/shard_map/all_gather | solution.py:747
  9.8 36.1 %collective-permute-start = (bf16[384,1024]{1,0:T(8,128)(2,1)}, bf16[384,1024]{1,0:T(8,128)(2,1)}, u32[]{:S(2)}, u32[]{:S(2)}) collective-permute-start(bf16[384,1024]{1,0:T(8,128)(2,1)} %get-tuple-element.301), channel_id=1, source_target_pairs={{0,1},{1,0},{2,3},{3,2},{4,5},{5,4},{6,7},{7,6},{8,9},{9,8},{10,11... | collective-permute-start | bytes 2359304 | tf_op jit(solution)/shard_map/ppermute | solution.py:719
  14.7 31.3 %collective-permute-start.1 = (bf16[4,256,512]{2,1,0:T(8,128)(2,1)S(1)}, bf16[4,256,512]{2,1,0:T(8,128)(2,1)}, u32[]{:S(2)}, u32[]{:S(2)}) collective-permute-start(bf16[4,256,512]{2,1,0:T(8,128)(2,1)S(1)} %pad_maximum_fusion.1), channel_id=1, source_target_pairs={{0,16},{16,0},{8,24},{24,8},{1,17},{17,1},{9,25},{25,9},{2,18},{18... | collective-permute-start | bytes 3145736 | tf_op jit(solution)/shard_map/ppermute | solution.py:719
  46.0 195.6 %all-gather.16.cloned.1.call-start = ((), (), s32[]{:S(2)}) async-start(), calls=%async_computation.3 | async-start | bytes 8650752 | tf_op jit(solution)/shard_map/all_gather | solution.py:747
  46.0 27.6 %collective-permute-start.5 = (bf16[4,256,512]{2,1,0:T(8,128)(2,1)}, bf16[4,256,512]{2,1,0:T(8,128)(2,1)S(1)}, u32[]{:S(2)}, u32[]{:S(2)}) collective-permute-start(bf16[4,256,512]{2,1,0:T(8,128)(2,1)} %pad_maximum_fusion.2), channel_id=1, source_target_pairs={{0,16},{16,0},{8,24},{24,8},{1,17},{17,1},{9,25},{25,9},{2,18},{18... | collective-permute-start | bytes 3145736 | tf_op jit(solution)/shard_map/ppermute | solution.py:719
  47.6 26.1 %collective-permute-start.6 = (bf16[4,256,512]{2,1,0:T(8,128)(2,1)}, bf16[4,256,512]{2,1,0:T(8,128)(2,1)}, u32[]{:S(2)}, u32[]{:S(2)}) collective-permute-start(bf16[4,256,512]{2,1,0:T(8,128)(2,1)} %collective-permute-done.1.refs_2_), channel_id=1, source_target_pairs={{0,2},{2,0},{4,6},{6,4},{1,3},{3,1},{5,7},{7,5},{8,10},{10,8},{12,... | collective-permute-start | bytes 3145736 | tf_op jit(solution)/shard_map/ppermute | solution.py:719
  49.2 24.5 %collective-permute-start.2 = (bf16[384,1024]{1,0:T(8,128)(2,1)}, bf16[384,1024]{1,0:T(8,128)(2,1)}, u32[]{:S(2)}, u32[]{:S(2)}) collective-permute-start(bf16[384,1024]{1,0:T(8,128)(2,1)} %get-tuple-element.151), channel_id=1, source_target_pairs={{0,1},{1,0},{2,3},{3,2},{4,5},{5,4},{6,7},{7,6},{8,9},{9,8},{10,11... | collective-permute-start | bytes 2359304 | tf_op jit(solution)/shard_map/ppermute | solution.py:719
  81.0 25.1 %collective-permute-start.8 = (bf16[4,256,512]{2,1,0:T(8,128)(2,1)S(1)}, bf16[4,256,512]{2,1,0:T(8,128)(2,1)S(1)}, u32[]{:S(2)}, u32[]{:S(2)}) collective-permute-start(bf16[4,256,512]{2,1,0:T(8,128)(2,1)S(1)} %collective-permute-done.5.refs_3_), channel_id=1, source_target_pairs={{0,2},{2,0},{4,6},{6,4},{1,3},{3,1},{5,7},{7,5},{8,10},{10,8},{12,... | collective-permute-start | bytes 3145736 | tf_op jit(solution)/shard_map/ppermute | solution.py:719
  82.2 23.9 %collective-permute-start.11 = (bf16[4,256,512]{2,1,0:T(8,128)(2,1)}, bf16[4,256,512]{2,1,0:T(8,128)(2,1)S(1)}, u32[]{:S(2)}, u32[]{:S(2)}) collective-permute-start(bf16[4,256,512]{2,1,0:T(8,128)(2,1)} %collective-permute-done.6.refs_4_), channel_id=1, source_target_pairs={{0,8},{8,0},{16,24},{24,16},{1,9},{9,1},{17,25},{25,17},{2,10},{10... | collective-permute-start | bytes 3145736 | tf_op jit(solution)/shard_map/ppermute | solution.py:719
  106.3 25.3 %collective-permute-start.17 = (bf16[3,256,512]{2,1,0:T(8,128)(2,1)}, bf16[3,256,512]{2,1,0:T(8,128)(2,1)}, u32[]{:S(2)}, u32[]{:S(2)}) collective-permute-start(bf16[3,256,512]{2,1,0:T(8,128)(2,1)} %collective-permute-done.13.refs_2_.refs_3_), channel_id=1, source_target_pairs={{0,2},{2,0},{4,6},{6,4},{1,3},{3,1},{5,7},{7,5},{8,10},{10,8},{12,... | collective-permute-start | bytes 2359304 | tf_op jit(solution)/shard_map/ppermute | solution.py:719
  107.6 24.0 %collective-permute-start.18 = (bf16[3,256,512]{2,1,0:T(8,128)(2,1)}, bf16[3,256,512]{2,1,0:T(8,128)(2,1)}, u32[]{:S(2)}, u32[]{:S(2)}) collective-permute-start(bf16[3,256,512]{2,1,0:T(8,128)(2,1)} %collective-permute-done.13.refs_2_.refs_3_), channel_id=1, source_target_pairs={{0,8},{8,0},{16,24},{24,16},{1,9},{9,1},{17,25},{25,17},{2,10},{10... | collective-permute-start | bytes 2359304 | tf_op jit(solution)/shard_map/ppermute | solution.py:719
  107.8 23.8 %collective-permute-start.15 = (bf16[384,1024]{1,0:T(8,128)(2,1)}, bf16[384,1024]{1,0:T(8,128)(2,1)S(1)}, u32[]{:S(2)}, u32[]{:S(2)}) collective-permute-start(bf16[384,1024]{1,0:T(8,128)(2,1)} %get-tuple-element.181), channel_id=1, source_target_pairs={{0,1},{1,0},{2,3},{3,2},{4,5},{5,4},{6,7},{7,6},{8,9},{9,8},{10,11... | collective-permute-start | bytes 2359304 | tf_op jit(solution)/shard_map/ppermute | solution.py:719
  108.7 22.9 %collective-permute-start.16 = (bf16[3,256,512]{2,1,0:T(8,128)(2,1)}, bf16[3,256,512]{2,1,0:T(8,128)(2,1)}, u32[]{:S(2)}, u32[]{:S(2)}) collective-permute-start(bf16[3,256,512]{2,1,0:T(8,128)(2,1)} %pad_maximum_fusion.4), channel_id=1, source_target_pairs={{0,16},{16,0},{8,24},{24,8},{1,17},{17,1},{9,25},{25,9},{2,18},{18... | collective-permute-start | bytes 2359304 | tf_op jit(solution)/shard_map/ppermute | solution.py:719
  131.6 109.9 %all-gather.14.cloned.1.call-start = ((), (), s32[]{:S(2)}) async-start(), calls=%async_computation.2 | async-start | bytes 17301504 | tf_op jit(solution)/shard_map/all_gather | solution.py:747
  133.8 26.3 %collective-permute-start.19 = (bf16[192,2176]{1,0:T(8,128)(2,1)S(1)}, bf16[192,2176]{1,0:T(8,128)(2,1)S(1)}, u32[]{:S(2)}, u32[]{:S(2)}) collective-permute-start(bf16[192,2176]{1,0:T(8,128)(2,1)S(1)} %copy-done.24), channel_id=1, source_target_pairs={{0,1},{1,0},{2,3},{3,2},{4,5},{5,4},{6,7},{7,6},{8,9},{9,8},{10,11... | collective-permute-start | bytes 2506760 | tf_op jit(solution)/shard_map/ppermute | solution.py:719
  135.0 25.1 %collective-permute-start.21 = (bf16[3,256,512]{2,1,0:T(8,128)(2,1)}, bf16[3,256,512]{2,1,0:T(8,128)(2,1)S(1)}, u32[]{:S(2)}, u32[]{:S(2)}) collective-permute-start(bf16[3,256,512]{2,1,0:T(8,128)(2,1)} %collective-permute-done.16.refs_3_.refs_4_), channel_id=1, source_target_pairs={{0,2},{2,0},{4,6},{6,4},{1,3},{3,1},{5,7},{7,5},{8,10},{10,8},{12,... | collective-permute-start | bytes 2359304 | tf_op jit(solution)/shard_map/ppermute | solution.py:719
  135.8 24.2 %collective-permute-start.22 = (bf16[3,256,512]{2,1,0:T(8,128)(2,1)}, bf16[3,256,512]{2,1,0:T(8,128)(2,1)S(1)}, u32[]{:S(2)}, u32[]{:S(2)}) collective-permute-start(bf16[3,256,512]{2,1,0:T(8,128)(2,1)} %collective-permute-done.16.refs_3_.refs_4_), channel_id=1, source_target_pairs={{0,8},{8,0},{16,24},{24,16},{1,9},{9,1},{17,25},{25,17},{2,10},{10... | collective-permute-start | bytes 2359304 | tf_op jit(solution)/shard_map/ppermute | solution.py:719
  135.8 24.2 %collective-permute-start.20 = (bf16[3,256,512]{2,1,0:T(8,128)(2,1)S(1)}, bf16[3,256,512]{2,1,0:T(8,128)(2,1)}, u32[]{:S(2)}, u32[]{:S(2)}) collective-permute-start(bf16[3,256,512]{2,1,0:T(8,128)(2,1)S(1)} %copy-done.30), channel_id=1, source_target_pairs={{0,16},{16,0},{8,24},{24,8},{1,17},{17,1},{9,25},{25,9},{2,18},{18... | collective-permute-start | bytes 2359304 | tf_op jit(solution)/shard_map/ppermute | solution.py:719
  137.3 22.8 %collective-permute-start.23 = (bf16[3,256,512]{2,1,0:T(8,128)(2,1)}, bf16[3,256,512]{2,1,0:T(8,128)(2,1)}, u32[]{:S(2)}, u32[]{:S(2)}) collective-permute-start(bf16[3,256,512]{2,1,0:T(8,128)(2,1)} %collective-permute-done.17.refs_8_.refs_9_), channel_id=1, source_target_pairs={{0,8},{8,0},{16,24},{24,16},{1,9},{9,1},{17,25},{25,17},{2,10},{10... | collective-permute-start | bytes 2359304 | tf_op jit(solution)/shard_map/ppermute | solution.py:719
  160.1 22.3 %collective-permute-start.24 = (bf16[208,2176]{1,0:T(8,128)(2,1)S(1)}, bf16[208,2176]{1,0:T(8,128)(2,1)S(1)}, u32[]{:S(2)}, u32[]{:S(2)}) collective-permute-start(bf16[208,2176]{1,0:T(8,128)(2,1)S(1)} %copy-done.20), channel_id=1, source_target_pairs={{0,1},{1,0},{2,3},{3,2},{4,5},{5,4},{6,7},{7,6},{8,9},{9,8},{10,11... | collective-permute-start | bytes 2715656 | tf_op jit(solution)/shard_map/ppermute | solution.py:719
  182.4 23.0 %collective-permute-start.29 = (bf16[192,2176]{1,0:T(8,128)(2,1)S(1)}, bf16[192,2176]{1,0:T(8,128)(2,1)S(1)}, u32[]{:S(2)}, u32[]{:S(2)}) collective-permute-start(bf16[192,2176]{1,0:T(8,128)(2,1)S(1)} %copy-done.25), channel_id=1, source_target_pairs={{0,1},{1,0},{2,3},{3,2},{4,5},{5,4},{6,7},{7,6},{8,9},{9,8},{10,11... | collective-permute-start | bytes 2506760 | tf_op jit(solution)/shard_map/ppermute | solution.py:719
  205.4 21.8 %collective-permute-start.34 = (bf16[208,2176]{1,0:T(8,128)(2,1)S(1)}, bf16[208,2176]{1,0:T(8,128)(2,1)S(1)}, u32[]{:S(2)}, u32[]{:S(2)}) collective-permute-start(bf16[208,2176]{1,0:T(8,128)(2,1)S(1)} %copy-done.21), channel_id=1, source_target_pairs={{0,1},{1,0},{2,3},{3,2},{4,5},{5,4},{6,7},{7,6},{8,9},{9,8},{10,11... | collective-permute-start | bytes 2715656 | tf_op jit(solution)/shard_map/ppermute | solution.py:719
  286.1 45.3 %collective-permute-start.43 = (bf16[400,2304]{1,0:T(8,128)(2,1)}, bf16[400,2304]{1,0:T(8,128)(2,1)}, u32[]{:S(2)}, u32[]{:S(2)}) collective-permute-start(bf16[400,2304]{1,0:T(8,128)(2,1)} %get-tuple-element.210.part), channel_id=1, source_target_pairs={{0,1},{1,0},{2,3},{3,2},{4,5},{5,4},{6,7},{7,6},{8,9},{9,8},{10,11... | collective-permute-start | bytes 5529608 | tf_op jit(solution)/shard_map/ppermute | solution.py:650
  333.0 43.4 %collective-permute-start.45 = (bf16[400,2304]{1,0:T(8,128)(2,1)}, bf16[400,2304]{1,0:T(8,128)(2,1)}, u32[]{:S(2)}, u32[]{:S(2)}) collective-permute-start(bf16[400,2304]{1,0:T(8,128)(2,1)} %get-tuple-element.212.part), channel_id=1, source_target_pairs={{0,1},{1,0},{2,3},{3,2},{4,5},{5,4},{6,7},{7,6},{8,9},{9,8},{10,11... | collective-permute-start | bytes 5529608 | tf_op jit(solution)/shard_map/ppermute | solution.py:650
  334.0 79.6 %collective-permute-start.44 = (bf16[384,1152]{1,0:T(8,128)(2,1)}, bf16[384,1152]{1,0:T(8,128)(2,1)S(1)}, u32[]{:S(2)}, u32[]{:S(2)}) collective-permute-start(bf16[384,1152]{1,0:T(8,128)(2,1)} %get-tuple-element.211), channel_id=1, source_target_pairs={{0,1},{1,0},{2,3},{3,2},{4,5},{5,4},{6,7},{7,6},{8,9},{9,8},{10,11... | collective-permute-start | bytes 2654216 | tf_op jit(solution)/shard_map/ppermute | solution.py:650
  335.0 78.6 %collective-permute-start.51 = (bf16[384,1152]{1,0:T(8,128)(2,1)}, bf16[384,1152]{1,0:T(8,128)(2,1)S(1)}, u32[]{:S(2)}, u32[]{:S(2)}) collective-permute-start(bf16[384,1152]{1,0:T(8,128)(2,1)} %get-tuple-element.237), channel_id=1, source_target_pairs={{0,1},{1,0},{2,3},{3,2},{4,5},{5,4},{6,7},{7,6},{8,9},{9,8},{10,11... | collective-permute-start | bytes 2654216 | tf_op jit(solution)/shard_map/ppermute | solution.py:650
  337.6 32.4 %collective-permute-start.47 = (bf16[4,528,128]{2,1,0:T(8,128)(2,1)S(1)}, bf16[4,528,128]{2,1,0:T(8,128)(2,1)S(1)}, u32[]{:S(2)}, u32[]{:S(2)}) collective-permute-start(bf16[4,528,128]{2,1,0:T(8,128)(2,1)S(1)} %dynamic-slice_bitcast_fusion.2), channel_id=1, source_target_pairs={{0,16},{16,0},{8,24},{24,8},{1,17},{17,1},{9,25},{25,9},{2,18},{18... | collective-permute-start | bytes 1622024 | tf_op jit(solution)/shard_map/ppermute | solution.py:1014
  376.4 37.1 %collective-permute-start.50 = (bf16[528,128]{1,0:T(8,128)(2,1)S(1)}, bf16[528,128]{1,0:T(8,128)(2,1)S(1)}, u32[]{:S(2)}, u32[]{:S(2)}) collective-permute-start(bf16[528,128]{1,0:T(8,128)(2,1)S(1)} %get-tuple-element.305), channel_id=1, source_target_pairs={{0,6},{2,0},{4,2},{6,4},{1,7},{3,1},{5,3},{7,5},{8,14},{10,8},{12,... | collective-permute-start | bytes 405512 | tf_op jit(solution)/shard_map/ppermute | solution.py:1017
  379.4 34.0 %collective-permute-start.49 = (bf16[528,128]{1,0:T(8,128)(2,1)S(1)}, bf16[528,128]{1,0:T(8,128)(2,1)S(1)}, u32[]{:S(2)}, u32[]{:S(2)}) collective-permute-start(bf16[528,128]{1,0:T(8,128)(2,1)S(1)} %get-tuple-element.306), channel_id=1, source_target_pairs={{0,4},{2,6},{4,0},{6,2},{1,5},{3,7},{5,1},{7,3},{8,12},{10,14},{12... | collective-permute-start | bytes 405512 | tf_op jit(solution)/shard_map/ppermute | solution.py:1017
  379.4 34.0 %collective-permute-start.48 = (bf16[528,128]{1,0:T(8,128)(2,1)S(1)}, bf16[528,128]{1,0:T(8,128)(2,1)S(1)}, u32[]{:S(2)}, u32[]{:S(2)}) collective-permute-start(bf16[528,128]{1,0:T(8,128)(2,1)S(1)} %get-tuple-element.304), channel_id=1, source_target_pairs={{0,2},{2,4},{4,6},{6,0},{1,3},{3,5},{5,7},{7,1},{8,10},{10,12},{12... | collective-permute-start | bytes 405512 | tf_op jit(solution)/shard_map/ppermute | solution.py:1017
  482.3 31.2 %collective-permute-start.82 = (bf16[4,640,128]{2,1,0:T(8,128)(2,1)S(1)}, bf16[4,640,128]{2,1,0:T(8,128)(2,1)S(1)}, u32[]{:S(2)}, u32[]{:S(2)}) collective-permute-start(bf16[4,640,128]{2,1,0:T(8,128)(2,1)S(1)} %pad_maximum_fusion.8.own), channel_id=1, source_target_pairs={{0,8},{8,0},{16,24},{24,16},{1,9},{9,1},{17,25},{25,17},{2,10},{10... | collective-permute-start | bytes 1966088 | tf_op jit(solution)/shard_map/ppermute | solution.py:1182
  (133 other events, 1401.7 us)
Sparse Core Ops, SparseCore 0:
  9.6 19.4 all-gather.9
  46.1 11.4 all-gather.11
  131.7 16.0 all-gather.15
  149.3 25.0 all-gather.13
